TPU v7x, 32 devices: a whole 2x2x4 slice. The times are simulated.
32 devices in a mesh: section: 2 (over core), fsdp: 4 (over y, x), ctx: 4 (over z).
Axes of the slice: x: 2, y: 2, z: 4, core: 2. Of those that a mesh axis runs over, the one named last changes fastest.
Arguments:
- inputs: bfloat16 [2, 4, 1024, 1088], P(None, 'fsdp', 'ctx'), may hold values from -6 to 6
- segments: int32 [2, 4, 1024], P(None, 'fsdp'), may hold values from 0 to 3, never falling along the last dimension, each value on 1 to 512 neighbouring positions
- cotangent: bfloat16 [2, 4, 1024, 1088], P(None, 'fsdp', 'ctx'), may hold values from -6 to 6
- qkv_weight: bfloat16 [2, 1088, 3264], P('section', 'fsdp'), may hold values from -0.1875 to 0.1875
- out_weight: bfloat16 [2, 1088, 1088], P('section', 'fsdp'), may hold values from -0.75 to 0.75
- up_weight: bfloat16 [2, 1088, 4352], P('section', 'fsdp'), may hold values from -0.1875 to 0.1875
- down_weight: bfloat16 [2, 4352, 1088], P('section', 'fsdp'), may hold values from -0.09375 to 0.09375
- norm_gains: bfloat16 [2, 2, 1088], P('section', None, 'fsdp'), may hold values from 0.5 to 1.5
- biases: bfloat16 [2, 6, 1088], P('section', None, 'fsdp'), may hold values from -3 to 3
- ff_bias: bfloat16 [2, 4352], P('section', 'fsdp'), may hold values from -3 to 3
Outputs:
- section_out: bfloat16 [2, 2, 4, 1024, 1088], P('section', None, 'fsdp', 'ctx')
- input_grad: float32 [2, 2, 4, 1024, 1088], P('section', None, 'fsdp', 'ctx')
- qkv_grad: float32 [2, 1088, 3264], P('section', 'fsdp')
- out_grad: float32 [2, 1088, 1088], P('section', 'fsdp')
- up_grad: float32 [2, 1088, 4352], P('section', 'fsdp')
- down_grad: float32 [2, 4352, 1088], P('section', 'fsdp')
- gain_grad: float32 [2, 2, 1088], P('section', None, 'fsdp')
- bias_grad: float32 [2, 6, 1088], P('section', None, 'fsdp')
- ff_bias_grad: float32 [2, 4352], P('section', 'fsdp')
Inputs may be any that keep to these rules, and one draw needn't show every extreme that they name: `segments`: along each sequence the segment numbers never fall, every number appears, and one document covers exactly 512 positions, none more.
All inputs are finite; a program needn't handle non-finite values.
Results may differ from a plain program's by a relative error of at most 0.018.
Values may be sent and summed in bfloat16 or wider, within the bound.
A program may use at most 320 MiB of HBM per device.

v0:
```python
import math

import jax
import jax.numpy as jnp
from jax import lax
from jax.sharding import PartitionSpec as P

D = 1088
HEADS = 17
HD = 64
MICRO = 2


def from_behind(value, axis, steps):
    count = lax.axis_size(axis)
    first, last = (max(0, -steps), min(count, count - steps))
    return lax.ppermute(value, axis, [(source, source + steps) for source in range(first, last)])


def shortened(shard):
    return jax.tree.map(lambda a: a.astype(jnp.bfloat16) if a.dtype == jnp.float32 else a, shard)


def normalize(values, gain_row, shift_row):
    center = jnp.mean(values, axis=-1, keepdims=True)
    offset = values - center
    spread = jnp.mean(offset * offset, axis=-1, keepdims=True)
    return offset * lax.rsqrt(spread + 1e-05) * gain_row + shift_row


def exact_gelu(values):
    return jax.nn.gelu(values, approximate=False)


def split_heads(values):
    return values.reshape(values.shape[0], values.shape[1], HEADS, HD)


def prepare(gathered):
    qkv_w, out_w, up_w, down_w, gain_rows, bias_rows, hidden_bias = gathered
    return (
        qkv_w,
        out_w,
        up_w,
        down_w,
        gain_rows.astype(jnp.float32),
        bias_rows.astype(jnp.float32),
        hidden_bias.astype(jnp.float32),
    )


def forward_layer(layer_in, allowed, weights):
    qkv_w, out_w, up_w, down_w, gain_rows, bias_rows, hidden_bias = weights
    seqs_here, rows_here = (layer_in.shape[0], layer_in.shape[1])
    scale = 1.0 / math.sqrt(HD)
    normed_b = normalize(layer_in, gain_rows[0], bias_rows[0]).astype(jnp.bfloat16)
    qkv_out = jnp.dot(normed_b, qkv_w, preferred_element_type=jnp.float32)
    query_b = (qkv_out[..., :D] + bias_rows[1]).astype(jnp.bfloat16)
    key_b = qkv_out[..., D : 2 * D].astype(jnp.bfloat16)
    value_b = (qkv_out[..., 2 * D :] + bias_rows[2]).astype(jnp.bfloat16)
    key_all, value_all = (
        lax.all_gather(key_b, "ctx", axis=1, tiled=True),
        lax.all_gather(value_b, "ctx", axis=1, tiled=True),
    )
    scores = (
        jnp.einsum(
            "sqhd,skhd->shqk",
            split_heads(query_b),
            split_heads(key_all),
            preferred_element_type=jnp.float32,
        )
        * scale
    )
    sum_exp = jnp.sum(jnp.where(allowed, jnp.exp(scores), 0.0), axis=-1, keepdims=True)
    log_sum = jnp.log(sum_exp)
    prob_b = jnp.where(allowed, jnp.exp(scores - log_sum), 0.0).astype(jnp.bfloat16)
    attended = jnp.einsum(
        "shqk,skhd->sqhd", prob_b, split_heads(value_all), preferred_element_type=jnp.float32
    )
    attended_b = attended.reshape(seqs_here, rows_here, D).astype(jnp.bfloat16)
    residual = (
        layer_in + jnp.dot(attended_b, out_w, preferred_element_type=jnp.float32) + bias_rows[3]
    )
    second_b = normalize(residual, gain_rows[1], bias_rows[4]).astype(jnp.bfloat16)
    hidden = jnp.dot(second_b, up_w, preferred_element_type=jnp.float32) + hidden_bias
    active_b = exact_gelu(hidden).astype(jnp.bfloat16)
    layer_out = (
        residual + jnp.dot(active_b, down_w, preferred_element_type=jnp.float32) + bias_rows[5]
    )
    kept = (
        layer_in,
        normed_b,
        query_b,
        key_all,
        value_all,
        log_sum,
        attended_b,
        residual,
        second_b,
        hidden,
        active_b,
    )
    return (layer_out, kept)


def backward_layer(upstream, kept, allowed, weights):
    qkv_w, out_w, up_w, down_w, gain_rows, bias_rows, hidden_bias = weights
    (
        layer_in,
        normed_b,
        query_b,
        key_all,
        value_all,
        log_sum,
        attended_b,
        residual,
        second_b,
        hidden,
        active_b,
    ) = kept
    seqs_here, rows_here = (upstream.shape[0], upstream.shape[1])
    scale = 1.0 / math.sqrt(HD)
    upstream_b = upstream.astype(jnp.bfloat16)
    grad_active = jnp.einsum("scd,fd->scf", upstream_b, down_w, preferred_element_type=jnp.float32)
    grad_hidden = jax.vjp(exact_gelu, hidden)[1](grad_active)[0]
    hidden_grad_b = grad_hidden.astype(jnp.bfloat16)
    grad_second = jnp.einsum("scf,df->scd", hidden_grad_b, up_w, preferred_element_type=jnp.float32)
    second_pull = jax.vjp(normalize, residual, gain_rows[1], bias_rows[4])[1]
    grad_resid_norm, grad_gain_two, grad_shift_two = second_pull(grad_second)
    grad_resid = upstream + grad_resid_norm
    resid_grad_b = grad_resid.astype(jnp.bfloat16)
    grad_att_b = jnp.einsum(
        "sce,de->scd", resid_grad_b, out_w, preferred_element_type=jnp.float32
    ).astype(jnp.bfloat16)
    query_heads = split_heads(query_b)
    key_heads = split_heads(key_all)
    value_heads = split_heads(value_all)
    grad_att_heads = split_heads(grad_att_b)
    scores = (
        jnp.einsum("sqhd,skhd->shqk", query_heads, key_heads, preferred_element_type=jnp.float32)
        * scale
    )
    probs = jnp.where(allowed, jnp.exp(scores - log_sum), 0.0)
    grad_prob = jnp.einsum(
        "sqhd,skhd->shqk", grad_att_heads, value_heads, preferred_element_type=jnp.float32
    )
    row_dot = jnp.sum(probs * grad_prob, axis=-1, keepdims=True)
    grad_score_b = (probs * (grad_prob - row_dot)).astype(jnp.bfloat16)
    grad_query = (
        jnp.einsum("shqk,skhd->sqhd", grad_score_b, key_heads, preferred_element_type=jnp.float32)
        * scale
    )
    grad_query_b = grad_query.reshape(seqs_here, rows_here, D).astype(jnp.bfloat16)
    key_term = (
        jnp.einsum("shqk,sqhd->skhd", grad_score_b, query_heads, preferred_element_type=jnp.float32)
        * scale
    )
    value_term = jnp.einsum(
        "shqk,sqhd->skhd",
        probs.astype(jnp.bfloat16),
        grad_att_heads,
        preferred_element_type=jnp.float32,
    )
    full_rows = key_all.shape[1]
    grad_key, grad_value = (
        lax.psum_scatter(
            key_term.reshape(seqs_here, full_rows, D), "ctx", scatter_dimension=1, tiled=True
        ),
        lax.psum_scatter(
            value_term.reshape(seqs_here, full_rows, D), "ctx", scatter_dimension=1, tiled=True
        ),
    )
    grad_value_b = grad_value.astype(jnp.bfloat16)
    grad_qkv_b = jnp.concatenate(
        [grad_query_b, grad_key.astype(jnp.bfloat16), grad_value_b], axis=-1
    )
    grad_normed = jnp.einsum("sce,de->scd", grad_qkv_b, qkv_w, preferred_element_type=jnp.float32)
    first_pull = jax.vjp(normalize, layer_in, gain_rows[0], bias_rows[0])[1]
    grad_in_norm, grad_gain_one, grad_shift_one = first_pull(grad_normed)
    layer_grad = grad_resid + grad_in_norm
    bias_terms = jnp.stack(
        [
            grad_shift_one,
            jnp.sum(grad_query_b.astype(jnp.float32), axis=(0, 1)),
            jnp.sum(grad_value_b.astype(jnp.float32), axis=(0, 1)),
            jnp.sum(grad_resid, axis=(0, 1)),
            grad_shift_two,
            jnp.sum(upstream, axis=(0, 1)),
        ]
    )
    terms = (
        jnp.einsum("scd,sce->de", normed_b, grad_qkv_b, preferred_element_type=jnp.float32),
        jnp.einsum("scd,sce->de", attended_b, resid_grad_b, preferred_element_type=jnp.float32),
        jnp.einsum("scd,scf->df", second_b, hidden_grad_b, preferred_element_type=jnp.float32),
        jnp.einsum("scf,scd->fd", active_b, upstream_b, preferred_element_type=jnp.float32),
        jnp.stack([grad_gain_one, grad_gain_two]),
        bias_terms,
        jnp.sum(grad_hidden, axis=(0, 1)),
    )
    return (layer_grad, terms)


def on_device(
    inputs,
    segments,
    cotangent,
    qkv_weight,
    out_weight,
    up_weight,
    down_weight,
    norm_gains,
    biases,
    ff_bias,
):
    rows_here = inputs.shape[2]
    ctx_start = lax.axis_index("ctx") * rows_here
    section_idx = lax.axis_index("section")
    is_first = section_idx == 0
    shards = (
        qkv_weight[0],
        out_weight[0],
        up_weight[0],
        down_weight[0],
        norm_gains[0],
        biases[0],
        ff_bias[0],
    )

    def allowed_for(micro_idx):
        seq_seg = lax.dynamic_index_in_dim(segments, micro_idx, 0, keepdims=False)
        query_seg = lax.dynamic_slice_in_dim(seq_seg, ctx_start, rows_here, 1)
        query_pos = ctx_start + jnp.arange(rows_here, dtype=jnp.int32)
        key_pos = jnp.arange(seq_seg.shape[1], dtype=jnp.int32)
        allowed = (query_seg[:, :, None] == seq_seg[:, None, :]) & (
            key_pos[None, None, :] <= query_pos[None, :, None]
        )
        return allowed[:, None]

    inbound = jnp.zeros(inputs.shape[1:], jnp.float32)
    saved = []
    produced = []
    for tick_index in range(MICRO + 1):
        current = prepare(
            (
                lax.all_gather(shards[0], "fsdp", axis=0, tiled=True),
                lax.all_gather(shards[1], "fsdp", axis=0, tiled=True),
                lax.all_gather(shards[2], "fsdp", axis=0, tiled=True),
                lax.all_gather(shards[3], "fsdp", axis=0, tiled=True),
                lax.all_gather(shards[4], "fsdp", axis=1, tiled=True),
                lax.all_gather(shards[5], "fsdp", axis=1, tiled=True),
                lax.all_gather(shards[6], "fsdp", axis=0, tiled=True),
            )
        )
        own_in = inputs[min(tick_index, MICRO - 1)].astype(jnp.float32)
        layer_in = jnp.where(is_first, own_in, inbound)
        micro_idx = jnp.clip(tick_index - section_idx, 0, MICRO - 1)
        layer_out, kept = forward_layer(layer_in, allowed_for(micro_idx), current)
        out_low = layer_out.astype(jnp.bfloat16)
        saved.append(kept)
        produced.append(out_low)
        if tick_index < MICRO:
            inbound = from_behind(out_low, "section", 1).astype(jnp.float32)
    section_out = jnp.stack(
        [jnp.where(is_first, produced[micro], produced[micro + 1]) for micro in range(MICRO)]
    )
    grad_in = jnp.zeros(inputs.shape[1:], jnp.float32)
    totals = None
    derived = []
    for tick_index in range(MICRO + 1):
        current = prepare(
            (
                lax.all_gather(shards[0], "fsdp", axis=0, tiled=True),
                lax.all_gather(shards[1], "fsdp", axis=0, tiled=True),
                lax.all_gather(shards[2], "fsdp", axis=0, tiled=True),
                lax.all_gather(shards[3], "fsdp", axis=0, tiled=True),
                lax.all_gather(shards[4], "fsdp", axis=1, tiled=True),
                lax.all_gather(shards[5], "fsdp", axis=1, tiled=True),
                lax.all_gather(shards[6], "fsdp", axis=0, tiled=True),
            )
        )
        micro_raw = tick_index - 1 + section_idx
        valid = (micro_raw >= 0) & (micro_raw < MICRO)
        micro_idx = jnp.clip(micro_raw, 0, MICRO - 1)
        kept = jax.tree.map(
            lambda early_val, late_val: jnp.where(is_first, early_val, late_val),
            saved[max(tick_index - 1, 0)],
            saved[min(tick_index + 1, MICRO)],
        )
        own_cot = cotangent[min(tick_index, MICRO - 1)].astype(jnp.float32)
        upstream = jnp.where(is_first, grad_in, own_cot)
        layer_grad, terms = backward_layer(upstream, kept, allowed_for(micro_idx), current)
        terms = tuple((jnp.where(valid, term_val, 0.0) for term_val in terms))
        totals = (
            terms
            if totals is None
            else tuple((old_val + new_val for old_val, new_val in zip(totals, terms)))
        )
        derived.append(layer_grad)
        if tick_index < MICRO:
            grad_in = from_behind(layer_grad.astype(jnp.bfloat16), "section", -1).astype(
                jnp.float32
            )
    totals = (
        lax.psum_scatter(
            totals[0].astype(jnp.bfloat16), "fsdp", scatter_dimension=0, tiled=True
        ).astype(jnp.float32),
        lax.psum_scatter(
            totals[1].astype(jnp.bfloat16), "fsdp", scatter_dimension=0, tiled=True
        ).astype(jnp.float32),
        lax.psum_scatter(
            totals[2].astype(jnp.bfloat16), "fsdp", scatter_dimension=0, tiled=True
        ).astype(jnp.float32),
        lax.psum_scatter(
            totals[3].astype(jnp.bfloat16), "fsdp", scatter_dimension=0, tiled=True
        ).astype(jnp.float32),
        lax.psum_scatter(
            totals[4].astype(jnp.bfloat16), "fsdp", scatter_dimension=1, tiled=True
        ).astype(jnp.float32),
        lax.psum_scatter(
            totals[5].astype(jnp.bfloat16), "fsdp", scatter_dimension=1, tiled=True
        ).astype(jnp.float32),
        lax.psum_scatter(
            totals[6].astype(jnp.bfloat16), "fsdp", scatter_dimension=0, tiled=True
        ).astype(jnp.float32),
    )
    summed = jax.tree.map(lambda part: part.astype(jnp.float32), lax.psum(shortened(totals), "ctx"))
    input_grad = jnp.stack(
        [jnp.where(is_first, derived[micro + 1], derived[micro]) for micro in range(MICRO)]
    )
    grad_qkv, grad_out, grad_up, grad_down, grad_gain, grad_bias, grad_ffb = summed
    return (
        section_out[None],
        input_grad[None],
        grad_qkv[None],
        grad_out[None],
        grad_up[None],
        grad_down[None],
        grad_gain[None],
        grad_bias[None],
        grad_ffb[None],
    )


def solution(mesh):
    return jax.shard_map(
        on_device,
        mesh=mesh,
        in_specs=(
            P(None, "fsdp", "ctx", None),
            P(None, "fsdp", None),
            P(None, "fsdp", "ctx", None),
            P("section", "fsdp", None),
            P("section", "fsdp", None),
            P("section", "fsdp", None),
            P("section", "fsdp", None),
            P("section", None, "fsdp"),
            P("section", None, "fsdp"),
            P("section", "fsdp"),
        ),
        out_specs=(
            P("section", None, "fsdp", "ctx", None),
            P("section", None, "fsdp", "ctx", None),
            P("section", "fsdp", None),
            P("section", "fsdp", None),
            P("section", "fsdp", None),
            P("section", "fsdp", None),
            P("section", None, "fsdp"),
            P("section", None, "fsdp"),
            P("section", "fsdp"),
        ),
        check_vma=False,
    )
```

profile of v0, /device:TPU:0, one launch (start us, length us, event | category | flops | bytes accessed | tf_op | source)
XLA Modules:
  0.0 2044.8 jit_solution(3308660674128787533)
XLA Ops:
  8.8 11.7 all-gather
  21.3 15.5 all-gather.1
  37.9 17.8 slice_reduce_fusion.2
  55.7 18.6 slice_reduce_fusion
  74.4 19.9 all-gather.30.cloned.1.call-done
  109.6 15.3 dynamic-update-slice
  124.9 15.0 all-reduce
  162.7 38.3 %all-gather.18.cloned.1.call-done = bf16[1,1024,1088]{1,2,0:T(8,128)(2,1)} async-done(((bf16[1,256,1088]{1,2,0:T(8,128)(2,1)}), bf16[1,1024,1088]{1,2,0:T(8,128)(2,1)}) %all-gather.18.cloned.1.call-update) | async-done | bytes 2228240 | tf_op jit(solution)/shard_map/all_gather | solution.py:63
  210.5 29.0 %all-gather.32.cloned.1.call-done = bf16[1,1088,1088]{2,1,0:T(8,128)(2,1)} async-done(((bf16[1,272,1088]{2,1,0:T(8,128)(2,1)}), bf16[1,1088,1088]{2,1,0:T(8,128)(2,1)}) %all-gather.32.cloned.1.call-update) | async-done | bytes 2367504 | tf_op jit(solution)/shard_map/all_gather | solution.py:246
  242.8 94.8 %all-gather.34.cloned.1.call-done = bf16[1,1088,4352]{2,1,0:T(8,128)(2,1)} async-done(((bf16[1,272,4352]{2,1,0:T(8,128)(2,1)}), bf16[1,1088,4352]{2,1,0:T(8,128)(2,1)}) %all-gather.34.cloned.1.call-update) | async-done | bytes 9469968 | tf_op jit(solution)/shard_map/all_gather | solution.py:247
  337.6 16.9 fusion.80
  354.5 86.0 %all-gather.36.cloned.1.call-done = bf16[1,4352,1088]{2,1,0:T(8,128)(2,1)} async-done(((bf16[1,1088,1088]{2,1,0:T(8,128)(2,1)}), bf16[1,4352,1088]{2,1,0:T(8,128)(2,1)}) %all-gather.36.cloned.1.call-update) | async-done | bytes 9469968 | tf_op jit(solution)/shard_map/all_gather | solution.py:248
  464.4 45.6 %all-gather.24.cloned.1.call-done = bf16[1,1024,1088]{1,2,0:T(8,128)(2,1)} async-done(((bf16[1,256,1088]{1,2,0:T(8,128)(2,1)}), bf16[1,1024,1088]{1,2,0:T(8,128)(2,1)}) %all-gather.24.cloned.1.call-update) | async-done | bytes 2228240 | tf_op jit(solution)/shard_map/all_gather | solution.py:62
  510.1 10.6 select_reduce_fusion.1
  520.7 38.1 %all-gather.22.cloned.1.call-done = bf16[1,1024,1088]{1,2,0:T(8,128)(2,1)} async-done(((bf16[1,256,1088]{1,2,0:T(8,128)(2,1)}), bf16[1,1024,1088]{1,2,0:T(8,128)(2,1)}) %all-gather.22.cloned.1.call-update) | async-done | bytes 2228240 | tf_op jit(solution)/shard_map/all_gather | solution.py:63
  569.2 16.8 fusion.83
  613.1 17.2 fusion.356
  630.3 27.5 %all-gather.28.cloned.1.call-done = bf16[1,1024,1088]{1,2,0:T(8,128)(2,1)} async-done(((bf16[1,256,1088]{1,2,0:T(8,128)(2,1)}), bf16[1,1024,1088]{1,2,0:T(8,128)(2,1)}) %all-gather.28.cloned.1.call-update) | async-done | bytes 2228240 | tf_op jit(solution)/shard_map/all_gather | solution.py:62
  657.8 12.4 select_reduce_fusion
  670.9 35.0 %all-gather.26.cloned.1.call-done = bf16[1,1024,1088]{1,2,0:T(8,128)(2,1)} async-done(((bf16[1,256,1088]{1,2,0:T(8,128)(2,1)}), bf16[1,1024,1088]{1,2,0:T(8,128)(2,1)}) %all-gather.26.cloned.1.call-update) | async-done | bytes 2228240 | tf_op jit(solution)/shard_map/all_gather | solution.py:63
  743.5 14.2 multiply_reduce_fusion.2
  757.7 12.0 multiply_convert_fusion.2
  774.6 10.8 fusion.39
  796.9 57.0 %reduce-scatter.15.cloned.1.call-done = f32[1,256,1088]{1,2,0:T(8,128)} async-done(((f32[1,1024,1088]{1,2,0:T(8,128)}), f32[1,256,1088]{1,2,0:T(8,128)}) %reduce-scatter.15.cloned.1.call-update) | async-done | bytes 1114128 | tf_op jit(solution)/shard_map/reduce_scatter | solution.py:166
  856.0 81.6 %reduce-scatter.17.cloned.1.call-done = f32[1,256,1088]{1,2,0:T(8,128)} async-done(((f32[1,1024,1088]{1,2,0:T(8,128)}), f32[1,256,1088]{1,2,0:T(8,128)}) %reduce-scatter.17.cloned.1.call-update) | async-done | bytes 1114128 | tf_op jit(solution)/shard_map/reduce_scatter | solution.py:169
  948.7 15.4 fusion.86
  964.2 15.3 fusion.355
  998.8 13.9 multiply_reduce_fusion.1
  1012.7 12.0 multiply_convert_fusion.1
  1048.0 64.0 %reduce-scatter.19.cloned.1.call-done = f32[1,256,1088]{1,2,0:T(8,128)} async-done(((f32[1,1024,1088]{1,2,0:T(8,128)}), f32[1,256,1088]{1,2,0:T(8,128)}) %reduce-scatter.19.cloned.1.call-update) | async-done | bytes 1114128 | tf_op jit(solution)/shard_map/reduce_scatter | solution.py:166
  1113.3 83.0 %reduce-scatter.21.cloned.1.call-done = f32[1,256,1088]{1,2,0:T(8,128)} async-done(((f32[1,1024,1088]{1,2,0:T(8,128)}), f32[1,256,1088]{1,2,0:T(8,128)}) %reduce-scatter.21.cloned.1.call-update) | async-done | bytes 1114128 | tf_op jit(solution)/shard_map/reduce_scatter | solution.py:169
  1210.6 15.3 fusion.354
  1245.7 13.5 multiply_reduce_fusion
  1259.2 12.2 multiply_convert_fusion
  1287.7 11.2 convolution_select_fusion.5
  1304.2 11.8 convolution_select_fusion.3
  1316.0 18.5 fusion.6
  1335.8 11.1 convolution_select_fusion.1
  1346.9 12.1 fusion
  1359.0 13.6 fusion.7
  1397.9 44.3 %reduce-scatter.25.cloned.1.call-done = f32[1,256,1088]{1,2,0:T(8,128)} async-done(((f32[1,1024,1088]{1,2,0:T(8,128)}), f32[1,256,1088]{1,2,0:T(8,128)}) %reduce-scatter.25.cloned.1.call-update) | async-done | bytes 1114128 | tf_op jit(solution)/shard_map/reduce_scatter | solution.py:169
  1453.4 31.5 %reduce-scatter.33.cloned.1.call-done = bf16[272,1088]{1,0:T(8,128)(2,1)} async-done(((bf16[1088,1088]{1,0:T(8,128)(2,1)}), bf16[272,1088]{1,0:T(8,128)(2,1)}) %reduce-scatter.33.cloned.1.call-update) | async-done | bytes 591888
  1485.0 102.7 %reduce-scatter.31.cloned.1.call-done = bf16[1088,1088]{1,0:T(8,128)(2,1)} async-done(((bf16[4352,1088]{1,0:T(8,128)(2,1)}), bf16[1088,1088]{1,0:T(8,128)(2,1)}) %reduce-scatter.31.cloned.1.call-update) | async-done | bytes 2367504 | tf_op jit(solution)/shard_map/reduce_scatter | solution.py:313
  1587.7 99.6 %reduce-scatter.29.cloned.1.call-done = bf16[272,4352]{1,0:T(8,128)(2,1)} async-done(((bf16[1088,4352]{1,0:T(8,128)(2,1)}), bf16[272,4352]{1,0:T(8,128)(2,1)}) %reduce-scatter.29.cloned.1.call-update) | async-done | bytes 2367504 | tf_op jit(solution)/shard_map/reduce_scatter | solution.py:310
  1687.3 80.9 %reduce-scatter.27.cloned.1.call-done = bf16[272,3264]{1,0:T(8,128)(2,1)} async-done(((bf16[1088,3264]{1,0:T(8,128)(2,1)}), bf16[272,3264]{1,0:T(8,128)(2,1)}) %reduce-scatter.27.cloned.1.call-update) | async-done | bytes 1775632 | tf_op jit(solution)/shard_map/reduce_scatter | solution.py:304
  1804.7 15.9 all-reduce.7
  1820.8 21.1 %all-reduce.5 = (bf16[1,6,272]{2,1,0:T(8,128)(2,1)S(1)}, bf16[1,2,272]{2,1,0:T(2,128)(2,1)S(1)}, bf16[1,1088]{1,0:T(2,128)(2,1)S(1)}) all-reduce(bf16[1,6,272]{2,1,0:T(8,128)(2,1)S(1)} %dynamic-slice_bitcast_fusion, bf16[1,2,272]{2,1,0:T(2,128)(2,1)S(1)} %dynamic-slice_bitcast_fusion.1, ...), channel_id=1, replica_groups=mesh['section'=2,'fsdp'=4,'ctx'=4] {'ctx'}, use_global_device_ids=true, to_apply=%region_83.84 | all-reduce | flops 3264 | bytes 13056 | tf_op jit(solution)/shard_map/psum | solution.py:326
  1847.0 180.5 %all-reduce.10.cloned.1.call-done = (bf16[1,272,3264]{2,1,0:T(8,128)(2,1)}, bf16[1,272,1088]{2,1,0:T(8,128)(2,1)}, bf16[1,272,4352]{2,1,0:T(8,128)(2,1)}, bf16[1,1088,1088]{2,1,0:T(8,128)(2,1)}) async-done(((bf16[1,272,3264]{2,1,0:T(8,128)(2,1)}, bf16[1,272,1088]{2,1,0:T(8,128)(2,1)}, bf16[1,272,4352]{2,1,0:T(8,128)(2,1)}, bf16[1,1088,1088]{2,1,0:T(8,128)(2,1)}), (bf16[1,272,3264]{2,1,0:T(8,128)(2,1)}, ...) | async-done | bytes 7102480 | tf_op jit(solution)/shard_map/psum | solution.py:326
  (583 shorter events, 369.1 us)
Async XLA Ops:
  7.2 30.2 %copy-start.7 = (bf16[2,1,256,1088]{2,3,1,0:T(8,128)(2,1)S(1)}, bf16[2,1,256,1088]{2,3,1,0:T(8,128)(2,1)}, u32[]{:S(2)}) copy-start(bf16[2,1,256,1088]{2,3,1,0:T(8,128)(2,1)} %param.10) | copy-start | bytes 3342340
  7.2 87.1 %all-gather.30.cloned.1.call-start = ((), (), s32[]{:S(2)}) async-start(), calls=%async_computation.25 | async-start | bytes 9052160 | tf_op jit(solution)/shard_map/all_gather | solution.py:245
  7.9 144.2 %all-gather.20.cloned.1.call-start = ((), (), s32[]{:S(2)}) async-start(), calls=%async_computation.11 | async-start | bytes 2785280 | tf_op jit(solution)/shard_map/all_gather | solution.py:62
  37.6 63.4 %copy-start.138 = (f32[256]{0:T(256)}, f32[256]{0:T(256)S(1)}, u32[]{:S(2)}) copy-start(f32[256]{0:T(256)S(1)} %broadcast_multiply_fusion.14) | copy-start | bytes 3076
  37.9 63.1 %copy-start.151 = (f32[256]{0:T(256)}, f32[256]{0:T(256)S(1)}, u32[]{:S(2)}) copy-start(f32[256]{0:T(256)S(1)} %add_rsqrt_fusion.5) | copy-start | bytes 3076
  55.7 1149.4 %copy-start.100 = (f32[1088]{0:T(1024)}, f32[1088]{0:T(1024)S(1)}, u32[]{:S(2)}) copy-start(f32[1088]{0:T(1024)S(1)} %get-tuple-element.67) | copy-start | bytes 13060
  74.3 511.8 %copy-start.146 = (f32[1088]{0:T(1024)}, f32[1088]{0:T(1024)S(1)}, u32[]{:S(2)}) copy-start(f32[1088]{0:T(1024)S(1)} %get-tuple-element.60) | copy-start | bytes 13060
  74.3 526.2 %copy-start.108 = (f32[1088]{0:T(1024)}, f32[1088]{0:T(1024)S(1)}, u32[]{:S(2)}) copy-start(f32[1088]{0:T(1024)S(1)} %get-tuple-element.65) | copy-start | bytes 13060
  74.4 643.6 %copy-start.90 = (f32[1088]{0:T(1024)}, f32[1088]{0:T(1024)S(1)}, u32[]{:S(2)}) copy-start(f32[1088]{0:T(1024)S(1)} %get-tuple-element.61) | copy-start | bytes 13060
  103.6 97.3 %all-gather.18.cloned.1.call-start = ((), (), s32[]{:S(2)}) async-start(), calls=%async_computation.10 | async-start | bytes 2785280 | tf_op jit(solution)/shard_map/all_gather | solution.py:63
  106.4 352.9 %copy-start.53 = (bf16[1,256,1088]{1,2,0:T(8,128)(2,1)}, bf16[1,256,1088]{1,2,0:T(8,128)(2,1)S(1)}, u32[]{:S(2)}) copy-start(bf16[1,256,1088]{1,2,0:T(8,128)(2,1)S(1)} %get-tuple-element.112) | copy-start | bytes 1671172
  106.4 33.5 %copy-start.103 = (s32[2,1,1024]{2,1,0:T(1,128)S(1)}, s32[2,1,1024]{2,1,0:T(1,128)}, u32[]{:S(2)}) copy-start(s32[2,1,1024]{2,1,0:T(1,128)} %param.11) | copy-start | bytes 24580
  106.4 133.0 %all-gather.32.cloned.1.call-start = ((), (), s32[]{:S(2)}) async-start(), calls=%async_computation.26 | async-start | bytes 3133440 | tf_op jit(solution)/shard_map/all_gather | solution.py:246
  107.0 230.6 %all-gather.34.cloned.1.call-start = ((), (), s32[]{:S(2)}) async-start(), calls=%async_computation.27 | async-start | bytes 11837440 | tf_op jit(solution)/shard_map/all_gather | solution.py:247
  107.6 332.8 %all-gather.36.cloned.1.call-start = ((), (), s32[]{:S(2)}) async-start(), calls=%async_computation.28 | async-start | bytes 12533760 | tf_op jit(solution)/shard_map/all_gather | solution.py:248
  108.2 401.9 %all-gather.24.cloned.1.call-start = ((), (), s32[]{:S(2)}) async-start(), calls=%async_computation.13 | async-start | bytes 2785280 | tf_op jit(solution)/shard_map/all_gather | solution.py:62
  162.6 47.8 %copy-start.106 = (f32[17,256]{1,0:T(8,128)}, f32[17,256]{1,0:T(8,128)S(1)}, u32[]{:S(2)}) copy-start(f32[17,256]{1,0:T(8,128)S(1)} %get-tuple-element.169) | copy-start | bytes 52228
  242.5 475.4 %copy-start.5 = (f32[256,1088]{0,1:T(8,128)}, f32[256,1088]{0,1:T(8,128)S(1)}, u32[]{:S(2)}) copy-start(f32[256,1088]{0,1:T(8,128)S(1)} %get-tuple-element.172) | copy-start | bytes 3342340
  242.6 111.9 %copy-start.110 = (f32[256]{0:T(256)}, f32[256]{0:T(256)S(1)}, u32[]{:S(2)}) copy-start(f32[256]{0:T(256)S(1)} %broadcast_multiply_fusion.13) | copy-start | bytes 3076
  242.8 111.7 %copy-start.116 = (f32[256]{0:T(256)}, f32[256]{0:T(256)S(1)}, u32[]{:S(2)}) copy-start(f32[256]{0:T(256)S(1)} %add_rsqrt_fusion.4) | copy-start | bytes 3076
  448.9 3.1 collective-permute-start
  461.5 59.2 %copy-start.78 = (bf16[1,256,1088]{1,2,0:T(8,128)(2,1)}, bf16[1,256,1088]{1,2,0:T(8,128)(2,1)S(1)}, u32[]{:S(2)}) copy-start(bf16[1,256,1088]{1,2,0:T(8,128)(2,1)S(1)} %get-tuple-element.107) | copy-start | bytes 1671172
  461.5 97.3 %all-gather.22.cloned.1.call-start = ((), (), s32[]{:S(2)}) async-start(), calls=%async_computation.12 | async-start | bytes 2785280 | tf_op jit(solution)/shard_map/all_gather | solution.py:63
  464.0 193.9 %all-gather.28.cloned.1.call-start = ((), (), s32[]{:S(2)}) async-start(), calls=%async_computation.15 | async-start | bytes 2785280 | tf_op jit(solution)/shard_map/all_gather | solution.py:62
  510.0 48.7 %copy-start.102 = (pred[256,1024]{1,0:T(8,128)(4,1)S(1)}, pred[256,1024]{1,0:T(8,128)(4,1)}, u32[]{:S(2)}) copy-start(pred[256,1024]{1,0:T(8,128)(4,1)} %get-tuple-element.157) | copy-start | bytes 786436
  569.0 149.0 %copy-start.3 = (f32[1,256,1088]{1,2,0:T(8,128)}, f32[1,256,1088]{1,2,0:T(8,128)S(1)}, u32[]{:S(2)}) copy-start(f32[1,256,1088]{1,2,0:T(8,128)S(1)} %get-tuple-element.178) | copy-start | bytes 3342340
  594.8 2.9 collective-permute-start.1
  610.6 95.2 %all-gather.26.cloned.1.call-start = ((), (), s32[]{:S(2)}) async-start(), calls=%async_computation.14 | async-start | bytes 2785280 | tf_op jit(solution)/shard_map/all_gather | solution.py:63
  613.0 240.9 %reduce-scatter.15.cloned.1.call-start = ((), (), s32[]{:S(2)}) async-start(), calls=%async_computation.16 | async-start | bytes 5570560 | tf_op jit(solution)/shard_map/reduce_scatter | solution.py:166
  774.5 163.1 %reduce-scatter.17.cloned.1.call-start = ((), (), s32[]{:S(2)}) async-start(), calls=%async_computation.17 | async-start | bytes 5570560 | tf_op jit(solution)/shard_map/reduce_scatter | solution.py:169
  785.4 326.5 %reduce-scatter.19.cloned.1.call-start = ((), (), s32[]{:S(2)}) async-start(), calls=%async_computation.18 | async-start | bytes 5570560 | tf_op jit(solution)/shard_map/reduce_scatter | solution.py:166
  947.0 17.1 collective-permute-start.2
  964.1 22.7 %copy-start.54 = (bf16[1,256,1088]{1,2,0:T(8,128)(2,1)}, bf16[1,256,1088]{1,2,0:T(8,128)(2,1)S(1)}, u32[]{:S(2)}) copy-start(bf16[1,256,1088]{1,2,0:T(8,128)(2,1)S(1)} %collective-permute-done.2) | copy-start | bytes 1671172
  1029.4 166.8 %reduce-scatter.21.cloned.1.call-start = ((), (), s32[]{:S(2)}) async-start(), calls=%async_computation.19 | async-start | bytes 5570560 | tf_op jit(solution)/shard_map/reduce_scatter | solution.py:169
  1039.5 356.2 %reduce-scatter.23.cloned.1.call-start = ((), (), s32[]{:S(2)}) async-start(), calls=%async_computation.20 | async-start | bytes 5570560 | tf_op jit(solution)/shard_map/reduce_scatter | solution.py:166
  1048.0 150.4 %copy-start.43 = (f32[1,256,1088]{1,2,0:T(8,128)S(1)}, f32[1,256,1088]{1,2,0:T(8,128)}, u32[]{:S(2)}) copy-start(f32[1,256,1088]{1,2,0:T(8,128)} %get-tuple-element.126) | copy-start | bytes 3342340
  1048.0 150.4 %copy-start.95 = (bf16[17,64,256]{2,1,0:T(8,128)(2,1)S(1)}, bf16[17,64,256]{2,1,0:T(8,128)(2,1)}, u32[]{:S(2)}) copy-start(bf16[17,64,256]{2,1,0:T(8,128)(2,1)} %get-tuple-element.203) | copy-start | bytes 1671172
  1113.3 90.5 %copy-start.98 = (bf16[1,256,1088]{1,2,0:T(8,128)(2,1)}, bf16[1,256,1088]{1,2,0:T(8,128)(2,1)S(1)}, u32[]{:S(2)}) copy-start(bf16[1,256,1088]{1,2,0:T(8,128)(2,1)S(1)} %convert_element_type.571) | copy-start | bytes 1671172
  1206.7 3.9 collective-permute-start.3
  1210.6 22.7 %copy-start.81 = (bf16[1,256,1088]{1,2,0:T(8,128)(2,1)}, bf16[1,256,1088]{1,2,0:T(8,128)(2,1)S(1)}, u32[]{:S(2)}) copy-start(bf16[1,256,1088]{1,2,0:T(8,128)(2,1)S(1)} %collective-permute-done.3) | copy-start | bytes 1671172
  1276.1 166.0 %reduce-scatter.25.cloned.1.call-start = ((), (), s32[]{:S(2)}) async-start(), calls=%async_computation.21 | async-start | bytes 5570560 | tf_op jit(solution)/shard_map/reduce_scatter | solution.py:169
  1286.0 198.9 %reduce-scatter.33.cloned.1.call-start = ((), (), s32[]{:S(2)}) async-start(), calls=%async_computation.29 | async-start | bytes 3133440
  1303.7 284.0 %reduce-scatter.31.cloned.1.call-start = ((), (), s32[]{:S(2)}) async-start(), calls=%async_computation.24 | async-start | bytes 12533760 | tf_op jit(solution)/shard_map/reduce_scatter | solution.py:313
  1334.6 352.7 %reduce-scatter.29.cloned.1.call-start = ((), (), s32[]{:S(2)}) async-start(), calls=%async_computation.23 | async-start | bytes 11837440 | tf_op jit(solution)/shard_map/reduce_scatter | solution.py:310
  1372.6 395.5 %reduce-scatter.27.cloned.1.call-start = ((), (), s32[]{:S(2)}) async-start(), calls=%async_computation.22 | async-start | bytes 9052160 | tf_op jit(solution)/shard_map/reduce_scatter | solution.py:304
  1453.2 574.4 %all-reduce.10.cloned.1.call-start = ((), (), s32[]{:S(2)}) async-start(), calls=%async_computation.30 | async-start | bytes 14622720 | tf_op jit(solution)/shard_map/psum | solution.py:326
  1771.9 23.5 %copy-start.144 = (f32[256]{0:T(256)}, f32[256]{0:T(256)S(1)}, u32[]{:S(2)}) copy-start(f32[256]{0:T(256)S(1)} %broadcast_multiply_fusion.3) | copy-start | bytes 3076
  1801.1 43.4 %copy-start.26 = (f32[1,256,1088]{1,2,0:T(8,128)S(1)}, f32[1,256,1088]{1,2,0:T(8,128)}, u32[]{:S(2)}) copy-start(f32[1,256,1088]{1,2,0:T(8,128)} %copy-done.24) | copy-start | bytes 3342340
  (153 other events, 1035.5 us)
Sparse Core Ops, SparseCore 0:
  9.9 84.3 all-gather.29
  103.7 48.3 all-gather.19
  154.3 46.5 all-gather.17
  202.6 36.7 all-gather.31
  241.1 96.4 all-gather.33
  339.3 101.0 all-gather.35
  461.6 48.3 all-gather.23
  512.2 46.5 all-gather.21
  610.7 47.0 all-gather.27
  659.2 46.5 all-gather.25
  774.6 79.2 reduce-scatter.14
  856.1 81.5 reduce-scatter.16
  1029.6 82.3 reduce-scatter.18
  1114.7 81.5 reduce-scatter.20
  1276.3 81.5 reduce-scatter.22
  1360.6 81.5 reduce-scatter.24
  1445.6 39.3 reduce-scatter.32
  1488.0 99.6 reduce-scatter.30
  1590.8 96.4 reduce-scatter.28
  1690.2 77.8 reduce-scatter.26
  1770.8 256.7 all-reduce.9
where the time goes:
time: 2050 us; the launch traced here: 2040 us
  waiting for transfers between devices  1260 us (61%)
  matrix products  489 us (24%)
  other arithmetic  115 us (6%)
  blocking collectives  79.2 us (4%)
  local copies, waits for them, and re-layouts  77.5 us (4%)
    reduce_scatter x3, waiting for transfers between devices, backward_layer(): lax.psum_scatter(value_term.reshape(seqs_here, full_rows, D), 'ctx', scat...  209 us
    psum x1, waiting for transfers between devices, on_device(): lax.psum(shortened(totals), 'ctx')  181 us
    reduce_scatter x3, waiting for transfers between devices, backward_layer(): lax.psum_scatter(key_term.reshape(seqs_here, full_rows, D), 'ctx', scatte...  121 us
    all_gather x3, waiting for transfers between devices, forward_layer(): lax.all_gather(value_b, 'ctx', axis=1, tiled=True)  111 us
    reduce_scatter x1, waiting for transfers between devices, on_device(): lax.psum_scatter(totals[3].astype(jnp.bfloat16), 'fsdp', scatter_dimensio...  103 us
    reduce_scatter x1, waiting for transfers between devices, on_device(): lax.psum_scatter(totals[2].astype(jnp.bfloat16), 'fsdp', scatter_dimensio...  99.6 us
    all_gather x1, waiting for transfers between devices, on_device(): lax.all_gather(shards[2], 'fsdp', axis=0, tiled=True)  94.8 us
    all_gather x1, waiting for transfers between devices, on_device(): lax.all_gather(shards[3], 'fsdp', axis=0, tiled=True)  86 us
  transfers between devices with their start and end apart: 25, of which 23 were waited for; matrix products, arithmetic and copies ran while one was open for 18% of the time, Pallas kernels for 0%

commit v1 on v0

v1 whole, which is shorter than its diff:
```python
import math

import jax
import jax.numpy as jnp
from jax import lax
from jax.experimental import pallas as pl
from jax.experimental.pallas import tpu as pltpu
from jax.sharding import PartitionSpec as P

D = 1088
HEADS = 17
HD = 64
F32 = jnp.float32
BF = jnp.bfloat16
SCALE = 1.0 / math.sqrt(HD)
EXT = 3328
MESH = pl.DeviceIdType.MESH
SWAP = [(0, 1), (1, 0)]


def mm(a, b):
    return jnp.dot(a, b, preferred_element_type=F32)


def mm_nt(a, b):
    return lax.dot_general(a, b, (((1,), (1,)), ((), ())), preferred_element_type=F32)


def mm_tn(a, b):
    return lax.dot_general(a, b, (((0,), (0,)), ((), ())), preferred_element_type=F32)


def norm_parts(values):
    center = jnp.mean(values, axis=-1, keepdims=True)
    offset = values - center
    spread = jnp.mean(offset * offset, axis=-1, keepdims=True)
    inv = lax.rsqrt(spread + 1e-05)
    return offset * inv, inv


def norm_back(grad, gain, unit, inv):
    dn = grad * gain
    return inv * (
        dn
        - jnp.mean(dn, axis=-1, keepdims=True)
        - unit * jnp.mean(dn * unit, axis=-1, keepdims=True)
    )


def phi_parts(z):
    cdf = 0.5 * (1.0 + lax.erf(z * (1.0 / math.sqrt(2.0))))
    pdf = jnp.exp(-0.5 * z * z) * (1.0 / math.sqrt(2.0 * math.pi))
    return cdf, pdf


def plane_neighbours():
    f = lax.axis_index("fsdp")
    x = lax.rem(f, 2)
    y = f // 2
    return y * 2 + (1 - x), (1 - y) * 2 + x


def plane_barrier(xn, yn):
    barrier = pltpu.get_barrier_semaphore()
    for nb in (xn, yn):
        pl.semaphore_signal(barrier, inc=1, device_id={"fsdp": nb}, device_id_type=MESH)
    pl.semaphore_wait(barrier, 2)


def remote(src, dst, send, recv, nb):
    return pltpu.make_async_remote_copy(
        src_ref=src, dst_ref=dst, send_sem=send, recv_sem=recv,
        device_id={"fsdp": nb}, device_id_type=MESH,
    )


def gather_kernel(b_ref, out_ref, send, recv):
    xn, yn = plane_neighbours()
    half = b_ref.shape[0] // 2
    plane_barrier(xn, yn)
    to_x = remote(b_ref, out_ref.at[1], send.at[0], recv.at[0], xn)
    to_y = remote(b_ref, out_ref.at[2], send.at[1], recv.at[1], yn)
    to_x.start()
    to_y.start()
    out_ref[0] = b_ref[...]
    to_x.wait_recv()
    low = remote(
        out_ref.at[1, pl.ds(half, half)], out_ref.at[3, pl.ds(half, half)],
        send.at[3], recv.at[3], yn,
    )
    low.start()
    to_y.wait_recv()
    top = remote(
        out_ref.at[2, pl.ds(0, half)], out_ref.at[3, pl.ds(0, half)],
        send.at[2], recv.at[2], xn,
    )
    top.start()
    to_x.wait_send()
    to_y.wait_send()
    low.wait()
    top.wait()


def scatter_kernel(p_ref, out_ref, x1, y1, x2, y2, sum_x, sum_y, send, recv):
    xn, yn = plane_neighbours()
    half = p_ref.shape[1] // 2
    top = pl.ds(0, half)
    low = pl.ds(half, half)
    plane_barrier(xn, yn)
    first_x = remote(p_ref.at[3, top], x1, send.at[0], recv.at[0], xn)
    first_y = remote(p_ref.at[3, low], y1, send.at[1], recv.at[1], yn)
    own_x = remote(p_ref.at[1, top], x2.at[top], send.at[2], recv.at[2], xn)
    own_y = remote(p_ref.at[2, low], y2.at[low], send.at[3], recv.at[3], yn)
    for copy in (first_x, first_y, own_x, own_y):
        copy.start()
    first_x.wait_recv()
    sum_y[...] = (p_ref[2, top, :].astype(F32) + x1[...].astype(F32)).astype(BF)
    rest_y = remote(sum_y, y2.at[top], send.at[5], recv.at[5], yn)
    rest_y.start()
    first_y.wait_recv()
    sum_x[...] = (p_ref[1, low, :].astype(F32) + y1[...].astype(F32)).astype(BF)
    rest_x = remote(sum_x, x2.at[low], send.at[4], recv.at[4], xn)
    rest_x.start()
    own_x.wait_recv()
    own_y.wait_recv()
    rest_y.wait_recv()
    out_ref[top, :] = (
        p_ref[0, top, :].astype(F32) + x2[top, :].astype(F32) + y2[top, :].astype(F32)
    )
    rest_x.wait_recv()
    out_ref[low, :] = (
        p_ref[0, low, :].astype(F32) + x2[low, :].astype(F32) + y2[low, :].astype(F32)
    )
    for copy in (first_x, first_y, own_x, own_y, rest_x, rest_y):
        copy.wait_send()


VSPEC = pl.BlockSpec(memory_space=pltpu.VMEM)


def plane_gather(value):
    if lax.axis_size("fsdp") != 4:
        return lax.all_gather(value, "fsdp", axis=0, tiled=True)
    rows, width = value.shape
    out = pl.pallas_call(
        gather_kernel,
        out_shape=jax.ShapeDtypeStruct((4, rows, width), value.dtype),
        in_specs=[VSPEC],
        out_specs=VSPEC,
        scratch_shapes=[pltpu.SemaphoreType.DMA((4,)), pltpu.SemaphoreType.DMA((4,))],
        compiler_params=pltpu.CompilerParams(collective_id=1, has_side_effects=True),
        name="plane_gather",
    )(value)
    return out.reshape(4 * rows, width)


def plane_scatter(value, rows):
    if lax.axis_size("fsdp") != 4:
        return lax.psum_scatter(value, "fsdp", scatter_dimension=0, tiled=True).astype(F32)
    width = value.shape[-1]
    half = rows // 2
    return pl.pallas_call(
        scatter_kernel,
        out_shape=jax.ShapeDtypeStruct((rows, width), F32),
        in_specs=[VSPEC],
        out_specs=VSPEC,
        scratch_shapes=[
            pltpu.VMEM((half, width), BF),
            pltpu.VMEM((half, width), BF),
            pltpu.VMEM((rows, width), BF),
            pltpu.VMEM((rows, width), BF),
            pltpu.VMEM((half, width), BF),
            pltpu.VMEM((half, width), BF),
            pltpu.SemaphoreType.DMA((6,)),
            pltpu.SemaphoreType.DMA((6,)),
        ],
        compiler_params=pltpu.CompilerParams(collective_id=2, has_side_effects=True),
        name="plane_scatter",
    )(value.reshape(4, rows, width))


def shift(value, steps):
    count = lax.axis_size("ctx")
    pairs = [(i, i + steps) for i in range(count) if 0 <= i + steps < count]
    return lax.ppermute(value, "ctx", pairs)


def with_halo(own, chunks):
    parts = [own]
    for _ in range(chunks):
        parts.append(shift(parts[-1], 1))
    return jnp.concatenate(parts[::-1], axis=0)


def return_halo(halo, chunks, rows):
    carried = None
    for far in range(chunks):
        mine = halo[far * rows : (far + 1) * rows]
        carried = mine if carried is None else mine + carried
        carried = shift(carried.astype(BF), -1).astype(F32)
    return carried


def pick(s, first, second):
    return jnp.where(s == 0, first, second)


def on_chip(value):
    return lax.ppermute(value, "section", SWAP)


def both_layers(own, s):
    other = on_chip(own)
    return pick(s, own, other), pick(s, other, own)


def half_rows(own, s):
    half = own.shape[0] // 2
    halves = own.reshape(2, half, own.shape[1])
    keep = lax.dynamic_index_in_dim(halves, s, 0, keepdims=False)
    give = lax.dynamic_index_in_dim(halves, 1 - s, 0, keepdims=False)
    recv = on_chip(give)
    return pick(s, keep, recv), pick(s, recv, keep)


def heads(values):
    return values.reshape(values.shape[0], HEADS, HD)


def attention(q, k, v, allowed):
    scores = jnp.einsum("qhd,khd->hqk", heads(q), heads(k), preferred_element_type=F32) * SCALE
    total = jnp.sum(jnp.where(allowed, jnp.exp(scores), 0.0), axis=-1, keepdims=True)
    logs = jnp.log(total)
    prob = jnp.where(allowed, jnp.exp(scores - logs), 0.0).astype(BF)
    out = jnp.einsum("hqk,khd->qhd", prob, heads(v), preferred_element_type=F32)
    return out.reshape(q.shape[0], D).astype(BF), logs


def attention_back(q, k, v, logs, d_out, allowed):
    qh, kh, vh, gh = heads(q), heads(k), heads(v), heads(d_out)
    scores = jnp.einsum("qhd,khd->hqk", qh, kh, preferred_element_type=F32) * SCALE
    prob = jnp.where(allowed, jnp.exp(scores - logs), 0.0)
    d_prob = jnp.einsum("qhd,khd->hqk", gh, vh, preferred_element_type=F32)
    row = jnp.sum(prob * d_prob, axis=-1, keepdims=True)
    d_score = (prob * (d_prob - row)).astype(BF)
    dq = jnp.einsum("hqk,khd->qhd", d_score, kh, preferred_element_type=F32) * SCALE
    dk = jnp.einsum("hqk,qhd->khd", d_score, qh, preferred_element_type=F32) * SCALE
    dv = jnp.einsum("hqk,qhd->khd", prob.astype(BF), gh, preferred_element_type=F32)
    return (
        dq.reshape(q.shape[0], D).astype(BF),
        dk.reshape(k.shape[0], D).astype(BF),
        dv.reshape(k.shape[0], D).astype(BF),
    )


def on_device(
    inputs, segments, cotangent, qkv_weight, out_weight, up_weight, down_weight,
    norm_gains, biases, ff_bias,
):
    rows = inputs.shape[2]
    length = segments.shape[2]
    chunks = min((length // 2 - 1 + rows - 1) // rows, lax.axis_size("ctx") - 1)
    reach = chunks * rows
    s = lax.axis_index("section")
    f = lax.axis_index("fsdp")
    nf = lax.axis_size("fsdp")
    shard = D // nf
    ff_here = ff_bias.shape[1]
    per_row = ff_here // shard
    pair = ("fsdp", "section")

    own_in = lax.dynamic_index_in_dim(inputs, s, 0, keepdims=False)[0]
    own_cot = lax.dynamic_index_in_dim(cotangent, s, 0, keepdims=False)[0]
    seg = lax.dynamic_index_in_dim(segments, s, 0, keepdims=False)[0]
    start = lax.axis_index("ctx") * rows
    key_seg = lax.dynamic_slice_in_dim(
        jnp.pad(seg, (reach, 0), constant_values=-1), start, reach + rows, 0
    )
    allowed = (key_seg[reach:, None] == key_seg[None, :]) & (
        jnp.arange(reach + rows, dtype=jnp.int32)[None, :] - reach
        <= jnp.arange(rows, dtype=jnp.int32)[:, None]
    )

    small = jnp.concatenate(
        [norm_gains[0].T, biases[0].T, ff_bias[0].reshape(shard, per_row)], axis=1
    )
    qkv_own = jnp.concatenate(
        [qkv_weight[0], small, jnp.zeros((shard, EXT - 3 * D - 8 - per_row), BF)], axis=1
    )
    qkv_halves = half_rows(qkv_own, s)
    out_halves = half_rows(out_weight[0], s)
    up_own = lax.all_to_all(
        up_weight[0].reshape(shard, nf, ff_here), "fsdp", split_axis=1, concat_axis=0, tiled=True
    ).reshape(D, ff_here)
    up_w = both_layers(up_own, s)
    down_w = both_layers(down_weight[0], s)

    qkv_w, out_w, gains, shifts, ffb = [], [], [], [], []
    for layer in range(2):
        full = lax.all_gather(qkv_halves[layer], pair, axis=0, tiled=True)
        qkv_w.append(full)
        out_w.append(lax.all_gather(out_halves[layer], pair, axis=0, tiled=True))
        vectors = full[:, 3 * D : 3 * D + 8].T.astype(F32)
        gains.append(vectors[:2])
        shifts.append(vectors[2:])
        hidden = full[:, 3 * D + 8 : 3 * D + 8 + per_row].reshape(-1).astype(F32)
        ffb.append(lax.dynamic_slice_in_dim(hidden, f * ff_here, ff_here, 0))

    kept = []
    current = own_in
    produced = []
    for layer in range(2):
        gain, shift_rows = gains[layer], shifts[layer]
        wide = with_halo(current, chunks).astype(F32)
        n1, inv1 = norm_parts(wide)
        normed = (n1 * gain[0] + shift_rows[0]).astype(BF)
        q = (mm(normed[reach:], qkv_w[layer][:, :D]) + shift_rows[1]).astype(BF)
        k = mm(normed, qkv_w[layer][:, D : 2 * D]).astype(BF)
        v = (mm(normed, qkv_w[layer][:, 2 * D : 3 * D]) + shift_rows[2]).astype(BF)
        att, logs = attention(q, k, v, allowed)
        resid = current.astype(F32) + mm(att, out_w[layer]) + shift_rows[3]
        n2, inv2 = norm_parts(resid)
        second = (n2 * gain[1] + shift_rows[4]).astype(BF)
        second_all = plane_gather(second)
        z = mm(second_all, up_w[layer]) + ffb[layer]
        cdf, _ = phi_parts(z)
        active = (z * cdf).astype(BF)
        partial = mm(active, down_w[layer]).astype(BF)
        out = resid + plane_scatter(partial, rows) + shift_rows[5]
        low = out.astype(BF)
        produced.append(low)
        kept.append((wide, normed, q, k, v, att, logs, resid, second_all, z, active))
        current = low

    upstream = own_cot.astype(F32)
    derived = [None, None]
    totals = [None, None]
    for layer in (1, 0):
        wide, normed, q, k, v, att, logs, resid, second_all, z, active = kept[layer]
        gain = gains[layer]
        up_b = upstream.astype(BF)
        up_all = plane_gather(up_b)
        cdf, pdf = phi_parts(z)
        dz = mm_nt(up_all, down_w[layer]) * (cdf + z * pdf)
        dz_b = dz.astype(BF)
        d_second = plane_scatter(mm_nt(dz_b, up_w[layer]).astype(BF), rows)
        down_g = mm_tn(active, up_all)
        up_g = mm_tn(second_all, dz_b)
        ffb_g = jnp.sum(dz, axis=0)
        n2, inv2 = norm_parts(resid)
        d_resid = upstream + norm_back(d_second, gain[1], n2, inv2)
        c = d_resid.astype(BF)
        d_att = mm_nt(c, out_w[layer]).astype(BF)
        out_g = mm_tn(att, c)
        dq, dk, dv = attention_back(q, k, v, logs, d_att, allowed)
        w = qkv_w[layer]
        da_wide = mm_nt(dk, w[:, D : 2 * D]) + mm_nt(dv, w[:, 2 * D : 3 * D])
        da_own = da_wide[reach:] + mm_nt(dq, w[:, :D])
        da_halo = da_wide[:reach]
        n1, inv1 = norm_parts(wide)
        da = da_own + return_halo(da_halo, chunks, rows)
        d_in = d_resid + norm_back(da, gain[0], n1[reach:], inv1[reach:])
        derived[layer] = d_in
        upstream_next = d_in.astype(BF).astype(F32)
        vectors = jnp.stack(
            [
                jnp.sum(da_halo * n1[:reach], axis=0) + jnp.sum(da_own * n1[reach:], axis=0),
                jnp.sum(d_second * n2, axis=0),
                jnp.sum(da_halo, axis=0) + jnp.sum(da_own, axis=0),
                jnp.sum(dq.astype(F32), axis=0),
                jnp.sum(dv.astype(F32), axis=0),
                jnp.sum(d_resid, axis=0),
                jnp.sum(d_second, axis=0),
                jnp.sum(upstream, axis=0),
            ]
        )
        ffb_block = lax.dynamic_update_slice(
            jnp.zeros((D, per_row), BF),
            ffb_g.reshape(shard, per_row).astype(BF),
            (f * shard, 0),
        )
        qkv_g = jnp.concatenate(
            [
                mm_tn(normed[reach:], dq).astype(BF),
                mm_tn(normed, dk).astype(BF),
                mm_tn(normed, dv).astype(BF),
                vectors.T.astype(BF),
                ffb_block,
                jnp.zeros((D, EXT - 3 * D - 8 - per_row), BF),
            ],
            axis=1,
        )
        qkv_g = lax.psum_scatter(qkv_g, pair, scatter_dimension=0, tiled=True)
        out_g = lax.psum_scatter(out_g.astype(BF), pair, scatter_dimension=0, tiled=True)
        down_pair = down_g.astype(BF).reshape(2, ff_here // 2, D)
        up_pair = up_g.astype(BF).reshape(nf, 2, shard // 2, ff_here)
        give = (
            lax.dynamic_index_in_dim(down_pair, 1 - s, 0, keepdims=False),
            lax.dynamic_index_in_dim(up_pair, 1 - s, 1, keepdims=False),
        )
        keep = (
            lax.dynamic_index_in_dim(down_pair, s, 0, keepdims=False),
            lax.dynamic_index_in_dim(up_pair, s, 1, keepdims=False),
        )
        down_g, up_g = (
            (a.astype(F32) + on_chip(b).astype(F32)).astype(BF) for a, b in zip(keep, give)
        )
        up_g = lax.all_to_all(up_g, "fsdp", split_axis=0, concat_axis=0, tiled=True)
        totals[layer] = lax.psum((qkv_g, out_g, down_g, up_g), "ctx")
        upstream = upstream_next

    def settle(zero, one):
        mine = pick(s, zero, one)
        other = on_chip(pick(s, one, zero))
        return pick(s, mine, other).astype(F32), pick(s, other, mine).astype(F32)

    qkv_t, out_t, down_t, up_t = (settle(a, b) for a, b in zip(*totals))
    qkv_full = jnp.concatenate(qkv_t, axis=0)
    grad_up = jnp.concatenate(up_t, axis=1).transpose(1, 0, 2).reshape(shard, nf * ff_here)
    vectors = qkv_full[:, 3 * D : 3 * D + 8].T
    return (
        gather_micro(jnp.stack(produced), s),
        gather_micro(jnp.stack(derived), s),
        qkv_full[None, :, : 3 * D],
        jnp.concatenate(out_t, axis=0)[None],
        grad_up[None],
        jnp.concatenate(down_t, axis=0)[None],
        vectors[None, :2],
        vectors[None, 2:],
        qkv_full[:, 3 * D + 8 : 3 * D + 8 + per_row].reshape(1, ff_here),
    )


def gather_micro(layers, s):
    mine = lax.dynamic_index_in_dim(layers, s, 0, keepdims=False)
    other = on_chip(lax.dynamic_index_in_dim(layers, 1 - s, 0, keepdims=False))
    return jnp.stack([pick(s, mine, other), pick(s, other, mine)])[None, :, None]


def solution(mesh):
    return jax.shard_map(
        on_device,
        mesh=mesh,
        in_specs=(
            P(None, "fsdp", "ctx", None),
            P(None, "fsdp", None),
            P(None, "fsdp", "ctx", None),
            P("section", "fsdp", None),
            P("section", "fsdp", None),
            P("section", "fsdp", None),
            P("section", "fsdp", None),
            P("section", None, "fsdp"),
            P("section", None, "fsdp"),
            P("section", "fsdp"),
        ),
        out_specs=(
            P("section", None, "fsdp", "ctx", None),
            P("section", None, "fsdp", "ctx", None),
            P("section", "fsdp", None),
            P("section", "fsdp", None),
            P("section", "fsdp", None),
            P("section", "fsdp", None),
            P("section", None, "fsdp"),
            P("section", None, "fsdp"),
            P("section", "fsdp"),
        ),
        check_vma=False,
    )
```

time: 2050 us -> 1080 us (0.53)
  waiting for transfers between devices: 1260 us -> 366 us
  matrix products: 489 us -> 241 us
  Pallas kernels: 0 us -> 187 us
  blocking collectives: 79.2 us -> 0 us
  local copies, waits for them, and re-layouts: 77.5 us -> 129 us
  starting transfers between devices: 7.84 us -> 38.4 us
  other arithmetic: 115 us -> 90.7 us
    reduce_scatter x9 -> x2, waiting for transfers between devices: 613 us -> 1.8 us  [on_device(): qkv_g = lax.psum_scatter(qkv_g, pair, scatter_dimension=0, tiled=True)]
    all_gather x10 -> x4, waiting for transfers between devices: 424 us -> 2.28 us  [the longest x2 2.24 us: on_device(): full = lax.all_gather(qkv_halves[layer], pair, axis=0, tiled=True)]
    dot_general x57 -> x46, matrix products: 489 us -> 216 us  [the longest x12 58.4 us: mm_nt(): lax.dot_general(a, b, (((1,), (1,)), ((), ())), preferred_element_type=F32)]
    pallas_call x0 -> x8, Pallas kernels: none -> 187 us  [the longest x4 111 us: plane_gather(): pl.pallas_call(gather_kernel, out_shape=jax.ShapeDtypeStruct((4, rows, wi...]
    all_to_all x0 -> x3, waiting for transfers between devices: none -> 76.1 us  [the longest x2 44.1 us: on_device(): up_g = lax.all_to_all(up_g, 'fsdp', split_axis=0, concat_axis=0, tiled=True)]
    psum x1, waiting for transfers between devices: 181 us -> 250 us  [on_device(): totals[layer] = lax.psum((qkv_g, out_g, down_g, up_g), 'ctx')]
    unnamed x22 -> x11, waiting for transfers between devices: 34.1 us -> 0.82 us
    slice x3 -> x9, local copies, waits for them, and re-layouts: 37.3 us -> 6.03 us  [the longest x2 4.62 us: on_device(): out = resid + plane_scatter(partial, rows) + shift_rows[5]]
  transfers between devices with their start and end apart: 25 -> 34, of which waited for: 23 -> 13; matrix products, arithmetic and copies ran while one was open for 18% -> 32% of each run, Pallas kernels for 0% -> 12%
where the time goes in v1:
time: 1080 us; the launch traced here: 1070 us
  waiting for transfers between devices  366 us (34%)
  matrix products  241 us (22%)
  Pallas kernels  187 us (17%)
  local copies, waits for them, and re-layouts  129 us (12%)
  other arithmetic  90.7 us (8%)
  starting transfers between devices  38.4 us (4%)
  between operations  16 us (1%)
    psum x1, waiting for transfers between devices, on_device(): totals[layer] = lax.psum((qkv_g, out_g, down_g, up_g), 'ctx')  250 us
    pallas_call x4, Pallas kernels, plane_gather(): pl.pallas_call(gather_kernel, out_shape=jax.ShapeDtypeStruct((4, rows, wi...  111 us
    pallas_call x4, Pallas kernels, plane_scatter(): pl.pallas_call(scatter_kernel, out_shape=jax.ShapeDtypeStruct((rows, widt...  76 us
    dot_general x12, matrix products, mm_nt(): lax.dot_general(a, b, (((1,), (1,)), ((), ())), preferred_element_type=F32)  58.4 us
    dot_general x12, matrix products, mm(): return jnp.dot(a, b, preferred_element_type=F32)  53.2 us
    dot_general x12, matrix products, mm_tn(): lax.dot_general(a, b, (((0,), (0,)), ((), ())), preferred_element_type=F32)  48.6 us
    all_to_all x2, waiting for transfers between devices, on_device(): up_g = lax.all_to_all(up_g, 'fsdp', split_axis=0, concat_axis=0, tiled=True)  44.1 us
    all_to_all x1, waiting for transfers between devices, on_device(): lax.all_to_all(up_weight[0].reshape(shard, nf, ff_here), 'fsdp', split_ax...  32 us
  transfers between devices with their start and end apart: 34, of which 13 were waited for; matrix products, arithmetic and copies ran while one was open for 32% of the time, Pallas kernels for 12%

profile of v1, /device:TPU:0, one launch (start us, length us, event | category | flops | bytes accessed | tf_op | source)
XLA Modules:
  0.0 1067.5 jit_solution(6533998600080437299)
XLA Ops:
  25.4 5.6 collective-permute-start
  38.5 4.7 all-to-all-start
  49.3 9.6 collective-permute-done.1
  60.2 32.0 %all-to-all-done = bf16[272,4,1088]{2,0,1:T(8,128)(2,1)} async-done(((bf16[272,4,1088]{2,0,1:T(8,128)(2,1)}), bf16[272,4,1088]{2,0,1:T(8,128)(2,1)}, u32[]{:S(2)}, u32[]{:S(2)}) %all-to-all-start) | async-done | bytes 2367520 | tf_op jit(solution)/shard_map/all_to_all | solution.py:292
  102.6 4.4 convolution_convert_fusion.17
  109.5 12.5 %fusion.5 = f32[17,256,768]{2,1,0:T(8,128)} fusion(pred[256,768]{1,0:T(8,128)(4,1)S(1)} %fusion.101, bf16[256,17,64]{0,2,1:T(8,128)(2,1)S(1)} %bitcast.317, bf16[768,17,64]{0,2,1:T(8,128)(2,1)} %bitcast.300), kind=kOutput, calls=%fused_computation.7 | convolution fusion | flops 872354816 | bytes 15794176 | tf_op jit(solution)/shard_map/reduce_sum | solution.py:232
  122.1 7.0 fusion.85
  135.0 39.2 %plane_gather.4 = bf16[4,256,1088]{2,1,0:T(8,128)(2,1)} custom-call(bf16[256,1088]{1,0:T(8,128)(2,1)} %add_convert_fusion.5.b_ref), custom_call_target="tpu_custom_call" | custom-call | tf_op jit(solution)/shard_map/plane_gather/pallas_call | solution.py:145
  174.3 8.3 multiply_convert_fusion.3
  184.0 4.4 convolution_convert_fusion.15
  192.6 24.5 %plane_scatter.4 = f32[256,1088]{1,0:T(8,128)} custom-call(bf16[4,256,1088]{2,1,0:T(8,128)(2,1)} %bitcast.261), custom_call_target="tpu_custom_call" | custom-call | tf_op jit(solution)/shard_map/plane_scatter/pallas_call | solution.py:162
  224.7 23.4 %plane_gather.6 = bf16[4,256,1088]{2,1,0:T(8,128)(2,1)} custom-call(bf16[256,1088]{1,0:T(8,128)(2,1)} %bitcast.269), custom_call_target="tpu_custom_call" | custom-call | tf_op jit(solution)/shard_map/plane_gather/pallas_call | solution.py:145
  273.4 4.4 convolution_convert_fusion.16
  281.4 12.4 %fusion.3 = f32[17,256,768]{2,1,0:T(8,128)} fusion(pred[256,768]{1,0:T(8,128)(4,1)S(1)} %copy-done.63, bf16[256,17,64]{0,2,1:T(8,128)(2,1)S(1)} %bitcast.319, bf16[768,17,64]{0,2,1:T(8,128)(2,1)} %bitcast.304), kind=kOutput, calls=%fused_computation.4 | convolution fusion | flops 872354816 | bytes 15794176 | tf_op jit(solution)/shard_map/reduce_sum | solution.py:232
  293.8 7.5 fusion.88
  306.5 24.4 %plane_gather.5 = bf16[4,256,1088]{2,1,0:T(8,128)(2,1)} custom-call(bf16[256,1088]{1,0:T(8,128)(2,1)} %add_convert_fusion.3.b_ref), custom_call_target="tpu_custom_call" | custom-call | tf_op jit(solution)/shard_map/plane_gather/pallas_call | solution.py:145
  331.0 7.8 multiply_convert_fusion.2
  338.8 6.6 fusion.134
  346.7 6.1 convolution_convert_fusion.13
  357.0 17.7 %plane_scatter.6 = f32[256,1088]{1,0:T(8,128)} custom-call(bf16[4,256,1088]{2,1,0:T(8,128)(2,1)} %bitcast.262), custom_call_target="tpu_custom_call" | custom-call | tf_op jit(solution)/shard_map/plane_scatter/pallas_call | solution.py:162
  377.0 7.2 convolution_convert_fusion.14
  388.4 17.7 %plane_scatter.5 = f32[256,1088]{1,0:T(8,128)} custom-call(bf16[4,256,1088]{2,1,0:T(8,128)(2,1)} %bitcast.263), custom_call_target="tpu_custom_call" | custom-call | tf_op jit(solution)/shard_map/plane_scatter/pallas_call | solution.py:162
  413.3 6.3 fusion.133
  421.0 6.8 multiply_reduce_fusion.1
  427.9 6.4 multiply_convert_fusion.1
  436.9 5.1 fusion.62
  442.1 5.4 convolution_add_fusion.5
  450.9 12.0 %collective-permute-done.9 = bf16[256,1088]{0,1:T(8,128)(2,1)S(1)} collective-permute-done((bf16[256,1088]{0,1:T(8,128)(2,1)S(1)}, bf16[256,1088]{0,1:T(8,128)(2,1)S(1)}, u32[]{:S(2)}, u32[]{:S(2)}) %collective-permute-start.9) | collective-permute-done | bytes 557088 | tf_op jit(solution)/shard_map/ppermute | solution.py:185
  471.4 5.6 fusion.132
  486.6 24.2 %plane_gather.7 = bf16[4,256,1088]{2,1,0:T(8,128)(2,1)} custom-call(bf16[256,1088]{1,0:T(8,128)(2,1)} %get-tuple-element.90.b_ref), custom_call_target="tpu_custom_call" | custom-call | tf_op jit(solution)/shard_map/plane_gather/pallas_call | solution.py:145
  510.8 7.7 fusion.137
  519.9 6.1 convolution_convert_fusion.12
  530.1 16.1 %plane_scatter.7 = f32[256,1088]{1,0:T(8,128)} custom-call(bf16[4,256,1088]{2,1,0:T(8,128)(2,1)} %bitcast.264), custom_call_target="tpu_custom_call" | custom-call | tf_op jit(solution)/shard_map/plane_scatter/pallas_call | solution.py:162
  566.4 12.7 %concatenate.50 = bf16[1088,3328]{1,0:T(8,128)(2,1)} concatenate(bf16[1088,1088]{1,0:T(8,128)(2,1)} %convolution_convert_fusion.2, bf16[1088,1088]{1,0:T(8,128)(2,1)} %convolution_convert_fusion.9, bf16[1088,1088]{1,0:T(8,128)(2,1)} %convolution_convert_fusion.8, bf16[1088,8]{1,0:T(8,128)(2,1)S(1)} %bitcast.313, bf16[1088,4]{1,0:T(8,128)(2,1)S(1)} %constant_dynamic-update-slice_fusion, ...), dimensions={1} | concatenate | bytes 14483456 | tf_op jit(solution)/shard_map/concatenate | solution.py:382
  583.2 12.6 %multiply_reduce_fusion = (f32[17,256]{1,0:T(8,128)S(1)}, f32[17,256,768]{2,1,0:T(8,128)}) fusion(f32[17,256,768]{2,1,0:T(8,128)} %fusion.5, bf16[256,17,64]{0,2,1:T(8,128)(2,1)S(1)} %bitcast.270, bf16[768,17,64]{0,2,1:T(8,128)(2,1)S(1)} %bitcast.266), kind=kOutput, calls=%fused_computation.9 | convolution fusion | flops 434499328 | bytes 28984320 | tf_op jit(solution)/shard_map/qhd,khd->hqk/dot_general | solution.py:243
  595.9 6.3 multiply_convert_fusion
  620.0 5.8 fusion.135
  630.5 5.9 convolution_convert_fusion.10
  642.6 6.0 convolution_convert_fusion.11
  648.6 5.1 collective-permute-done.12
  655.2 5.4 multiply_reduce_fusion.5
  660.9 12.8 %concatenate.49 = bf16[1088,3328]{1,0:T(8,128)(2,1)} concatenate(bf16[1088,1088]{1,0:T(8,128)(2,1)} %convolution_convert_fusion.3, bf16[1088,1088]{1,0:T(8,128)(2,1)} %convolution_convert_fusion.11, bf16[1088,1088]{1,0:T(8,128)(2,1)} %convolution_convert_fusion.10, bf16[1088,8]{1,0:T(8,128)(2,1)S(1)} %bitcast.314, bf16[1088,4]{1,0:T(8,128)(2,1)S(1)} %constant_dynamic-update-slice_fusion.1, ...), dimensions={1} | concatenate | bytes 14483456 | tf_op jit(solution)/shard_map/concatenate | solution.py:382
  673.8 5.8 convolution_convert_fusion.6
  694.3 4.3 convolution_convert_fusion.5
  708.9 24.9 %all-to-all-done.2 = bf16[4,136,1088]{2,1,0:T(8,128)(2,1)S(1)} async-done(((bf16[4,136,1088]{2,1,0:T(8,128)(2,1)}), bf16[4,136,1088]{2,1,0:T(8,128)(2,1)S(1)}, u32[]{:S(2)}, u32[]{:S(2)}) %all-to-all-start.2) | async-done | bytes 1183776 | tf_op jit(solution)/shard_map/all_to_all | solution.py:408
  744.2 19.1 %all-to-all-done.1 = bf16[4,136,1088]{2,1,0:T(8,128)(2,1)} async-done(((bf16[4,136,1088]{2,1,0:T(8,128)(2,1)}), bf16[4,136,1088]{2,1,0:T(8,128)(2,1)}, u32[]{:S(2)}, u32[]{:S(2)}) %all-to-all-start.1) | async-done | bytes 1183776 | tf_op jit(solution)/shard_map/all_to_all | solution.py:408
  780.4 250.0 %all-reduce.6.cloned.1.call-done = (bf16[136,3328]{1,0:T(8,128)(2,1)}, bf16[136,3328]{1,0:T(8,128)(2,1)}, bf16[136,1088]{1,0:T(8,128)(2,1)}, bf16[136,1088]{1,0:...) async-done(((bf16[136,3328]{1,0:T(8,128)(2,1)}, ...) | async-done | bytes 7137296 | tf_op jit(solution)/shard_map/psum | solution.py:409
  1049.5 6.5 reshape.352
  (437 shorter events, 278.8 us)
Async XLA Ops:
  7.2 17.3 %copy-start = (bf16[2,1,256,1088]{2,3,1,0:T(8,128)(2,1)S(1)}, bf16[2,1,256,1088]{2,3,1,0:T(8,128)(2,1)}, u32[]{:S(2)}) copy-start(bf16[2,1,256,1088]{2,3,1,0:T(8,128)(2,1)} %param.10) | copy-start | bytes 3342340
  7.2 87.2 %all-gather.5.cloned.1.call-start = ((), (), s32[]{:S(2)}) async-start(), calls=%async_computation.7 | async-start | bytes 8146944 | tf_op jit(solution)/shard_map/all_gather | solution.py:300
  13.5 2.9 collective-permute-start.2
  19.0 111.8 %all-gather.7.cloned.1.call-start = ((), (), s32[]{:S(2)}) async-start(), calls=%async_computation.8 | async-start | bytes 2820096 | tf_op jit(solution)/shard_map/all_gather | solution.py:302
  20.2 1.7 collective-permute-start.3
  23.8 224.5 %all-gather.9.cloned.1.call-start = ((), (), s32[]{:S(2)}) async-start(), calls=%async_computation.9 | async-start | bytes 8146944 | tf_op jit(solution)/shard_map/all_gather | solution.py:300
  25.4 18.0 %collective-permute-start = (bf16[256,1088]{0,1:T(8,128)(2,1)}, bf16[256,1088]{0,1:T(8,128)(2,1)}, u32[]{:S(2)}, u32[]{:S(2)}) collective-permute-start(bf16[256,1088]{0,1:T(8,128)(2,1)} %fusion.206), channel_id=1, source_target_pairs={{0,1},{1,2},{2,3},{4,5},{5,6},{6,7},{8,9},{9,10},{10,11},{12,13},{... | collective-permute-start | bytes 1671176 | tf_op jit(solution)/shard_map/ppermute | solution.py:185
  38.5 53.7 %all-to-all-start = ((bf16[272,4,1088]{2,0,1:T(8,128)(2,1)}), bf16[272,4,1088]{2,0,1:T(8,128)(2,1)}, u32[]{:S(2)}, u32[]{:S(2)}) async-start(bf16[272,4,1088]{2,0,1:T(8,128)(2,1)} %copy.133), calls=%async_computation | async-start | bytes 5013504 | tf_op jit(solution)/shard_map/all_to_all | solution.py:292
  43.2 258.2 %all-gather.11.cloned.1.call-start = ((), (), s32[]{:S(2)}) async-start(), calls=%async_computation.10 | async-start | bytes 2820096 | tf_op jit(solution)/shard_map/all_gather | solution.py:302
  43.2 139.4 %collective-permute-start.5 = (bf16[1088,1088]{1,0:T(8,128)(2,1)}, bf16[1088,1088]{1,0:T(8,128)(2,1)}, u32[]{:S(2)}, u32[]{:S(2)}) collective-permute-start(bf16[1088,1088]{1,0:T(8,128)(2,1)} %bitcast.330), channel_id=1, source_target_pairs={{0,16},{16,0},{1,17},{17,1},{2,18},{18,2},{3,19},{19,3},{4,20},{20... | collective-permute-start | bytes 7102472 | tf_op jit(solution)/shard_map/ppermute | solution.py:209
  43.4 15.5 %collective-permute-start.1 = (bf16[256,1088]{0,1:T(8,128)(2,1)}, bf16[256,1088]{0,1:T(8,128)(2,1)S(1)}, u32[]{:S(2)}, u32[]{:S(2)}) collective-permute-start(bf16[256,1088]{0,1:T(8,128)(2,1)} %collective-permute-done), channel_id=1, source_target_pairs={{0,1},{1,2},{2,3},{4,5},{5,6},{6,7},{8,9},{9,10},{10,11},{12,13},{... | collective-permute-start | bytes 1671176 | tf_op jit(solution)/shard_map/ppermute | solution.py:185
  47.7 61.8 %copy-start.62 = (pred[256,768]{1,0:T(8,128)(4,1)}, pred[256,768]{1,0:T(8,128)(4,1)S(1)}, u32[]{:S(2)}) copy-start(pred[256,768]{1,0:T(8,128)(4,1)S(1)} %fusion.101) | copy-start | bytes 589828
  60.2 37.7 %copy-start.67 = (f32[768]{0:T(1024)}, f32[768]{0:T(1024)S(1)}, u32[]{:S(2)}) copy-start(f32[768]{0:T(1024)S(1)} %add_rsqrt_fusion.1) | copy-start | bytes 9220
  92.2 82.1 %collective-permute-start.4 = (bf16[1088,1088]{1,0:T(8,128)(2,1)}, bf16[1088,1088]{1,0:T(8,128)(2,1)}, u32[]{:S(2)}, u32[]{:S(2)}) collective-permute-start(bf16[1088,1088]{1,0:T(8,128)(2,1)} %bitcast.24), channel_id=1, source_target_pairs={{0,16},{16,0},{1,17},{17,1},{2,18},{18,2},{3,19},{19,3},{4,20},{20... | collective-permute-start | bytes 7102472 | tf_op jit(solution)/shard_map/ppermute | solution.py:209
  218.5 82.9 %copy-start.4 = (bf16[256,1088]{1,0:T(8,128)(2,1)}, bf16[256,1088]{1,0:T(8,128)(2,1)S(1)}, u32[]{:S(2)}) copy-start(bf16[256,1088]{1,0:T(8,128)(2,1)S(1)} %add_convert_fusion.4) | copy-start | bytes 1671172
  218.8 31.0 %collective-permute-start.6 = (bf16[256,1088]{0,1:T(8,128)(2,1)S(1)}, bf16[256,1088]{0,1:T(8,128)(2,1)}, u32[]{:S(2)}, u32[]{:S(2)}) collective-permute-start(bf16[256,1088]{0,1:T(8,128)(2,1)S(1)} %copy.135), channel_id=1, source_target_pairs={{0,1},{1,2},{2,3},{4,5},{5,6},{6,7},{8,9},{9,10},{10,11},{12,13},{... | collective-permute-start | bytes 1671176 | tf_op jit(solution)/shard_map/ppermute | solution.py:185
  248.2 515.2 %reduce-scatter.15.cloned.1.call-start = ((), (), s32[]{:S(2)}) async-start(), calls=%async_computation.14 | async-start | bytes 2820096
  249.7 11.1 %collective-permute-start.7 = (bf16[256,1088]{0,1:T(8,128)(2,1)}, bf16[256,1088]{0,1:T(8,128)(2,1)}, u32[]{:S(2)}, u32[]{:S(2)}) collective-permute-start(bf16[256,1088]{0,1:T(8,128)(2,1)} %collective-permute-done.6), channel_id=1, source_target_pairs={{0,1},{1,2},{2,3},{4,5},{5,6},{6,7},{8,9},{9,10},{10,11},{12,13},{... | collective-permute-start | bytes 1671176 | tf_op jit(solution)/shard_map/ppermute | solution.py:185
  388.4 17.7 %copy-start.17 = (bf16[1,1,256,1088]{3,2,1,0:T(8,128)(2,1)S(1)}, bf16[1,1,256,1088]{3,2,1,0:T(8,128)(2,1)}, u32[]{:S(2)}) copy-start(bf16[1,1,256,1088]{3,2,1,0:T(8,128)(2,1)} %copy.142) | copy-start | bytes 1671172
  388.4 31.2 %slice-start.4 = ((s8[13369344]{0:T(1024)(128)(4,1)}), s8[786432]{0:T(1024)(128)(4,1)S(1)}, s32[]{:S(2)}) async-start(s8[13369344]{0:T(1024)(128)(4,1)} %bitcast.255), calls=%async_computation.20 | async-start | bytes 1572864
  406.2 13.5 %slice-start.5 = ((s8[13369344]{0:T(1024)(128)(4,1)}), s8[4194304]{0:T(1024)(128)(4,1)S(1)}, s32[]{:S(2)}) async-start(s8[13369344]{0:T(1024)(128)(4,1)} %bitcast.255), calls=%async_computation.21 | async-start | bytes 8388608
  421.0 15.9 %copy-start.50 = (bf16[17,64,768]{2,1,0:T(8,128)(2,1)}, bf16[17,64,768]{2,1,0:T(8,128)(2,1)S(1)}, u32[]{:S(2)}) copy-start(bf16[17,64,768]{2,1,0:T(8,128)(2,1)S(1)} %get-tuple-element.140) | copy-start | bytes 5013508
  449.6 13.3 %collective-permute-start.9 = (bf16[256,1088]{0,1:T(8,128)(2,1)S(1)}, bf16[256,1088]{0,1:T(8,128)(2,1)S(1)}, u32[]{:S(2)}, u32[]{:S(2)}) collective-permute-start(bf16[256,1088]{0,1:T(8,128)(2,1)S(1)} %copy.147), channel_id=1, source_target_pairs={{1,0},{2,1},{3,2},{5,4},{6,5},{7,6},{9,8},{10,9},{11,10},{13,12},{... | collective-permute-start | bytes 1671176 | tf_op jit(solution)/shard_map/ppermute | solution.py:185
  466.2 11.8 %collective-permute-start.10 = (bf16[256,1088]{0,1:T(8,128)(2,1)S(1)}, bf16[256,1088]{0,1:T(8,128)(2,1)}, u32[]{:S(2)}, u32[]{:S(2)}) collective-permute-start(bf16[256,1088]{0,1:T(8,128)(2,1)S(1)} %copy.149), channel_id=1, source_target_pairs={{1,0},{2,1},{3,2},{5,4},{6,5},{7,6},{9,8},{10,9},{11,10},{13,12},{... | collective-permute-start | bytes 1671176 | tf_op jit(solution)/shard_map/ppermute | solution.py:185
  471.2 292.2 %reduce-scatter.13.cloned.1.call-start = ((), (), s32[]{:S(2)}) async-start(), calls=%async_computation.13 | async-start | bytes 2820096
  530.0 18.1 %copy-start.18 = (bf16[256,1088]{1,0:T(8,128)(2,1)S(1)}, bf16[256,1088]{1,0:T(8,128)(2,1)}, u32[]{:S(2)}) copy-start(bf16[256,1088]{1,0:T(8,128)(2,1)} %get-tuple-element.90.b_ref) | copy-start | bytes 1671172
  552.1 211.3 %reduce-scatter.11.cloned.1.call-start = ((), (), s32[]{:S(2)}) async-start(), calls=%async_computation.12 | async-start | bytes 8146944 | tf_op jit(solution)/shard_map/reduce_scatter | solution.py:393
  579.1 186.1 %reduce-scatter.9.cloned.1.call-start = ((), (), s32[]{:S(2)}) async-start(), calls=%async_computation.11 | async-start | bytes 8146944 | tf_op jit(solution)/shard_map/reduce_scatter | solution.py:393
  583.1 12.7 %slice-start = ((s8[13369344]{0:T(1024)(128)(4,1)}), s8[4194304]{0:T(1024)(128)(4,1)S(1)}, s32[]{:S(2)}) async-start(s8[13369344]{0:T(1024)(128)(4,1)} %bitcast.253), calls=%async_computation.16 | async-start | bytes 8388608
  583.2 12.7 %slice-start.1 = ((s8[13369344]{0:T(1024)(128)(4,1)}), s8[4194304]{0:T(1024)(128)(4,1)S(1)}, s32[]{:S(2)}) async-start(s8[13369344]{0:T(1024)(128)(4,1)} %bitcast.253), calls=%async_computation.17 | async-start | bytes 8388608
  583.2 12.6 %slice-start.2 = ((s8[13369344]{0:T(1024)(128)(4,1)}), s8[4194304]{0:T(1024)(128)(4,1)S(1)}, s32[]{:S(2)}) async-start(s8[13369344]{0:T(1024)(128)(4,1)} %bitcast.253), calls=%async_computation.18 | async-start | bytes 8388608
  583.2 12.6 %slice-start.3 = ((s8[13369344]{0:T(1024)(128)(4,1)}), s8[786432]{0:T(1024)(128)(4,1)S(1)}, s32[]{:S(2)}) async-start(s8[13369344]{0:T(1024)(128)(4,1)} %bitcast.253), calls=%async_computation.19 | async-start | bytes 1572864
  618.6 17.9 %collective-permute-start.11 = (bf16[256,1088]{0,1:T(8,128)(2,1)S(1)}, bf16[256,1088]{0,1:T(8,128)(2,1)}, u32[]{:S(2)}, u32[]{:S(2)}) collective-permute-start(bf16[256,1088]{0,1:T(8,128)(2,1)S(1)} %copy.155), channel_id=1, source_target_pairs={{1,0},{2,1},{3,2},{5,4},{6,5},{7,6},{9,8},{10,9},{11,10},{13,12},{... | collective-permute-start | bytes 1671176 | tf_op jit(solution)/shard_map/ppermute | solution.py:185
  641.2 12.5 %collective-permute-start.12 = (bf16[256,1088]{0,1:T(8,128)(2,1)S(1)}, bf16[256,1088]{0,1:T(8,128)(2,1)}, u32[]{:S(2)}, u32[]{:S(2)}) collective-permute-start(bf16[256,1088]{0,1:T(8,128)(2,1)S(1)} %copy.157), channel_id=1, source_target_pairs={{1,0},{2,1},{3,2},{5,4},{6,5},{7,6},{9,8},{10,9},{11,10},{13,12},{... | collective-permute-start | bytes 1671176 | tf_op jit(solution)/shard_map/ppermute | solution.py:185
  642.6 12.6 %copy-start.65 = (f32[1088]{0:T(1024)S(1)}, f32[1088]{0:T(1024)}, u32[]{:S(2)}) copy-start(f32[1088]{0:T(1024)} %copy-done.64) | copy-start | bytes 13060
  679.7 18.9 %collective-permute-start.17 = (bf16[4,136,1088]{2,1,0:T(8,128)(2,1)S(1)}, bf16[4,136,1088]{2,1,0:T(8,128)(2,1)S(1)}, u32[]{:S(2)}, u32[]{:S(2)}) collective-permute-start(bf16[4,136,1088]{2,1,0:T(8,128)(2,1)S(1)} %dynamic-slice_bitcast_fusion.2), channel_id=1, source_target_pairs={{0,16},{16,0},{1,17},{17,1},{2,18},{18,2},{3,19},{19,3},{4,20},{20... | collective-permute-start | bytes 3551240 | tf_op jit(solution)/shard_map/ppermute | solution.py:209
  687.3 51.2 %collective-permute-start.20 = (bf16[544,1088]{1,0:T(8,128)(2,1)}, bf16[544,1088]{1,0:T(8,128)(2,1)}, u32[]{:S(2)}, u32[]{:S(2)}) collective-permute-start(bf16[544,1088]{1,0:T(8,128)(2,1)} %dynamic-slice_bitcast_fusion), channel_id=1, source_target_pairs={{0,16},{16,0},{1,17},{17,1},{2,18},{18,2},{3,19},{19,3},{4,20},{20... | collective-permute-start | bytes 3551240 | tf_op jit(solution)/shard_map/ppermute | solution.py:209
  692.4 13.8 %collective-permute-start.16 = (bf16[4,136,1088]{2,1,0:T(8,128)(2,1)}, bf16[4,136,1088]{2,1,0:T(8,128)(2,1)}, u32[]{:S(2)}, u32[]{:S(2)}) collective-permute-start(bf16[4,136,1088]{2,1,0:T(8,128)(2,1)} %dynamic-slice_bitcast_fusion.3), channel_id=1, source_target_pairs={{0,16},{16,0},{1,17},{17,1},{2,18},{18,2},{3,19},{19,3},{4,20},{20... | collective-permute-start | bytes 3551240 | tf_op jit(solution)/shard_map/ppermute | solution.py:209
  700.0 33.8 %all-to-all-start.2 = ((bf16[4,136,1088]{2,1,0:T(8,128)(2,1)}), bf16[4,136,1088]{2,1,0:T(8,128)(2,1)S(1)}, u32[]{:S(2)}, u32[]{:S(2)}) async-start(bf16[4,136,1088]{2,1,0:T(8,128)(2,1)} %fusion.53), calls=%async_computation.4 | async-start | bytes 2506752 | tf_op jit(solution)/shard_map/all_to_all | solution.py:408
  706.2 35.4 %collective-permute-start.19 = (bf16[544,1088]{1,0:T(8,128)(2,1)}, bf16[544,1088]{1,0:T(8,128)(2,1)}, u32[]{:S(2)}, u32[]{:S(2)}) collective-permute-start(bf16[544,1088]{1,0:T(8,128)(2,1)} %dynamic-slice_bitcast_fusion.1), channel_id=1, source_target_pairs={{0,16},{16,0},{1,17},{17,1},{2,18},{18,2},{3,19},{19,3},{4,20},{20... | collective-permute-start | bytes 3551240 | tf_op jit(solution)/shard_map/ppermute | solution.py:209
  733.8 29.6 %all-to-all-start.1 = ((bf16[4,136,1088]{2,1,0:T(8,128)(2,1)}), bf16[4,136,1088]{2,1,0:T(8,128)(2,1)}, u32[]{:S(2)}, u32[]{:S(2)}) async-start(bf16[4,136,1088]{2,1,0:T(8,128)(2,1)} %fusion.54), calls=%async_computation.3 | async-start | bytes 2506752 | tf_op jit(solution)/shard_map/all_to_all | solution.py:408
  738.1 292.4 %all-reduce.6.cloned.1.call-start = ((), (), s32[]{:S(2)}) async-start(), calls=%async_computation.15 | async-start | bytes 14901248 | tf_op jit(solution)/shard_map/psum | solution.py:409
  770.1 4.7 collective-permute-start.8
  774.0 3.5 collective-permute-start.13
  1031.7 5.2 collective-permute-start.15
  1033.0 5.0 collective-permute-start.14
  1034.8 21.2 %collective-permute-start.21 = (bf16[544,1088]{1,0:T(8,128)(2,1)}, bf16[544,1088]{1,0:T(8,128)(2,1)}, u32[]{:S(2)}, u32[]{:S(2)}) collective-permute-start(bf16[544,1088]{1,0:T(8,128)(2,1)} %broadcast_select_fusion.6), channel_id=1, source_target_pairs={{0,16},{16,0},{1,17},{17,1},{2,18},{18,2},{3,19},{19,3},{4,20},{20... | collective-permute-start | bytes 3551240 | tf_op jit(solution)/shard_map/ppermute | solution.py:209
  1036.1 6.9 collective-permute-start.18
  (78 other events, 334.1 us)
Sparse Core Ops, SparseCore 0:
  19.1 75.2 all-gather.4
  96.9 27.9 all-gather.6
  127.4 62.5 all-gather.8
  248.3 26.7 all-gather.10
  471.3 46.9 reduce-scatter.14
  552.2 43.6 reduce-scatter.12
  599.4 68.8 reduce-scatter.10
  673.9 91.2 reduce-scatter.8
  768.8 261.6 all-reduce.5

commit v2 on v1

--- a/solution.py
+++ b/solution.py
@@ -13,6 +13,7 @@
 F32 = jnp.float32
 BF = jnp.bfloat16
 SCALE = 1.0 / math.sqrt(HD)
+WIDE = 1152
 EXT = 3328
 MESH = pl.DeviceIdType.MESH
 SWAP = [(0, 1), (1, 0)]
@@ -135,6 +136,293 @@
         copy.wait_send()
 
 
+def z_partners():
+    z = lax.axis_index("ctx")
+    return z + 1 - 2 * lax.rem(z, 2), 3 - z, (z == 1) | (z == 2)
+
+
+def add_rows(dst, one, two, rows, step):
+    @pl.loop(0, rows // step)
+    def _(i):
+        at = pl.ds(pl.multiple_of(i * step, 16), step)
+        dst[at, :] = (one[at, :].astype(F32) + two[at, :].astype(F32)).astype(dst.dtype)
+
+
+def reduce_kernel(
+    aq, ak, av, ao, down, up, a_out, m_out,
+    a_own, a_in, x1, y1, x2, y2, sx, sy, a_t, a_za, a_zb, a_fin,
+    m_own, m_in, m_za, m_zb, m_fin,
+    load, core_s, core_r, p_send, p_recv, z_send, z_recv, fin_s, fin_r,
+):
+    s = lax.axis_index("section")
+    f = lax.axis_index("fsdp")
+    xn, yn = plane_neighbours()
+    dn = 3 - f
+    side, across, inner = z_partners()
+    shard = a_t.shape[1]
+    cut = x1.shape[2]
+    wide = a_t.shape[2]
+    left = pl.ds(0, cut)
+    right = pl.ds(cut, wide - cut)
+
+    def to(src, dst, send, recv, **where):
+        return pltpu.make_async_remote_copy(
+            src_ref=src, dst_ref=dst, send_sem=send, recv_sem=recv,
+            device_id=where, device_id_type=MESH,
+        )
+
+    barrier = pltpu.get_barrier_semaphore()
+    partners = ({"section": 1 - s}, {"fsdp": xn}, {"fsdp": yn}, {"ctx": side}, {"ctx": across})
+    for where in partners:
+        pl.semaphore_signal(barrier, inc=1, device_id=where, device_id_type=MESH)
+    pl.semaphore_wait(barrier, 5)
+
+    def rows_of(half, k):
+        return pl.ds(pl.multiple_of(half * 2 * shard + k * shard, 16), shard)
+
+    def m_src(i):
+        return (down, up)[i // 2], i % 2
+
+    def m_copies(i):
+        ref, k = m_src(i)
+        return (
+            to(ref.at[rows_of(1 - s, k)], m_in.at[i], core_s.at[i], core_r.at[i], section=1 - s),
+            pltpu.make_async_copy(ref.at[rows_of(s, k)], m_own.at[i], load.at[i]),
+        )
+
+    def a_copies(j, give, keep):
+        return (
+            to(give, a_in.at[j], core_s.at[4 + j], core_r.at[4 + j], section=1 - s),
+            pltpu.make_async_copy(keep, a_own.at[j], load.at[4 + j]),
+        )
+
+    def start_a(j):
+        for half in range(2):
+
+            @pl.when(s == half)
+            def _(half=half):
+                pieces = (aq, ak, av, ao)
+                for copy in a_copies(j, pieces[2 - 2 * half + j], pieces[2 * half + j]):
+                    copy.start()
+
+    for i in range(4):
+        for copy in m_copies(i):
+            copy.start()
+        if i == 0:
+            start_a(0)
+            start_a(1)
+
+    def z_step(own, za, zb, fin, k):
+        return (
+            to(own, za, z_send.at[3 * k], z_recv.at[3 * k], ctx=side),
+            to(za, zb, z_send.at[3 * k + 1], z_recv.at[3 * k + 1], ctx=across),
+            to(fin, fin, z_send.at[3 * k + 2], z_recv.at[3 * k + 2], ctx=side),
+        )
+
+    def m_z(i):
+        return z_step(m_own.at[i], m_za.at[i], m_zb.at[i], m_fin.at[i], i)
+
+    def a_z(j):
+        return z_step(a_t.at[j], a_za.at[j], a_zb.at[j], a_fin.at[j], 4 + j)
+
+    def z_first(copies):
+        @pl.when(jnp.logical_not(inner))
+        def _():
+            copies[0].start()
+
+    def z_second(copies, own, za):
+        @pl.when(inner)
+        def _():
+            copies[0].wait_recv()
+            add_rows(za, own, za, shard, shard // 2 if shard % 32 == 0 else shard)
+            copies[1].start()
+
+    def z_third(copies, za, zb, fin):
+        @pl.when(inner)
+        def _():
+            copies[1].wait_recv()
+            add_rows(fin, za, zb, shard, shard // 2 if shard % 32 == 0 else shard)
+            copies[2].start()
+
+    def z_last(copies):
+        @pl.when(jnp.logical_not(inner))
+        def _():
+            copies[2].wait_recv()
+
+    def m_one(i):
+        far, near = m_copies(i)
+        far.wait_recv()
+        near.wait()
+        add_rows(m_own.at[i], m_own.at[i], m_in.at[i], shard, shard)
+        z_first(m_z(i))
+
+    def blk(owner):
+        return pl.ds(pl.multiple_of(owner * shard, 16), shard)
+
+    def plane(j):
+        own = a_own.at[j]
+        return (
+            to(own.at[blk(dn), left], x1.at[j], p_send.at[j, 0], p_recv.at[j, 0], fsdp=xn),
+            to(own.at[blk(dn), right], y1.at[j], p_send.at[j, 1], p_recv.at[j, 1], fsdp=yn),
+            to(own.at[blk(xn), left], x2.at[j, :, left], p_send.at[j, 2], p_recv.at[j, 2], fsdp=xn),
+            to(own.at[blk(yn), right], y2.at[j, :, right], p_send.at[j, 3], p_recv.at[j, 3], fsdp=yn),
+            to(sx.at[j], x2.at[j, :, right], p_send.at[j, 4], p_recv.at[j, 4], fsdp=xn),
+            to(sy.at[j], y2.at[j, :, left], p_send.at[j, 5], p_recv.at[j, 5], fsdp=yn),
+        )
+
+    def a_one(j):
+        far, near = a_copies(j, aq, aq)
+        far.wait_recv()
+        near.wait()
+        add_rows(a_own.at[j], a_own.at[j], a_in.at[j], 4 * shard, shard)
+        for copy in plane(j)[:4]:
+            copy.start()
+
+    def a_two(j):
+        copies = plane(j)
+        copies[0].wait_recv()
+        add_rows(sy.at[j], a_own.at[j, blk(yn), left], x1.at[j], shard, shard)
+        copies[5].start()
+        copies[1].wait_recv()
+        add_rows(sx.at[j], a_own.at[j, blk(xn), right], y1.at[j], shard, shard)
+        copies[4].start()
+
+    def a_three(j):
+        copies = plane(j)
+        for copy in copies[2:]:
+            copy.wait_recv()
+        a_t[j] = (
+            a_own[j, blk(f), :].astype(F32) + x2[j].astype(F32) + y2[j].astype(F32)
+        ).astype(BF)
+        z_first(a_z(j))
+
+    def m_two(i):
+        z_second(m_z(i), m_own.at[i], m_za.at[i])
+
+    def m_three(i):
+        z_third(m_z(i), m_za.at[i], m_zb.at[i], m_fin.at[i])
+
+    def fin_copy(i):
+        if i < 4:
+            k = i % 2
+            return to(
+                m_fin.at[i], m_out.at[i // 2, rows_of(s, k)], fin_s.at[i], fin_r.at[i], section=1 - s
+            )
+        return to(
+            a_fin.at[i - 4], a_out.at[s, i - 4], fin_s.at[i], fin_r.at[i], section=1 - s
+        )
+
+    def m_four(i):
+        z_last(m_z(i))
+        fin_copy(i).start()
+        m_out[i // 2, rows_of(s, i % 2), :] = m_fin[i]
+
+    def a_four(j):
+        z_last(a_z(j))
+        fin_copy(4 + j).start()
+        a_out[s, j] = a_fin[j]
+
+    m_one(0)
+    a_one(0)
+    m_one(1)
+    a_one(1)
+    m_one(2)
+    m_one(3)
+    m_two(0)
+    a_two(0)
+    m_two(1)
+    m_three(0)
+    a_two(1)
+    a_three(0)
+    m_two(2)
+    m_three(1)
+    m_four(0)
+    a_three(1)
+    m_two(3)
+    m_three(2)
+    m_four(1)
+    z_second(a_z(0), a_t.at[0], a_za.at[0])
+    m_three(3)
+    m_four(2)
+    z_second(a_z(1), a_t.at[1], a_za.at[1])
+    z_third(a_z(0), a_za.at[0], a_zb.at[0], a_fin.at[0])
+    m_four(3)
+    z_third(a_z(1), a_za.at[1], a_zb.at[1], a_fin.at[1])
+    a_four(0)
+    a_four(1)
+
+    for i in range(6):
+        fin_copy(i).wait()
+    for i in range(4):
+        m_copies(i)[0].wait_send()
+    for j in range(2):
+        a_copies(j, aq, aq)[0].wait_send()
+        for copy in plane(j):
+            copy.wait_send()
+    for copies in [m_z(i) for i in range(4)] + [a_z(j) for j in range(2)]:
+
+        @pl.when(inner)
+        def _(copies=copies):
+            copies[1].wait_send()
+            copies[2].wait_send()
+
+        @pl.when(jnp.logical_not(inner))
+        def _(copies=copies):
+            copies[0].wait_send()
+
+
+def reduce_layer(pieces, down, up):
+    shard = D // 4
+    cut = 640
+    dma = pltpu.SemaphoreType.DMA
+    any_spec = pl.BlockSpec(memory_space=pl.ANY)
+
+    def buf(*shape):
+        return pltpu.VMEM(shape, BF)
+
+    return pl.pallas_call(
+        reduce_kernel,
+        out_shape=(
+            jax.ShapeDtypeStruct((2, 2, shard, WIDE), BF),
+            jax.ShapeDtypeStruct((2, D, D), BF),
+        ),
+        in_specs=[any_spec] * 6,
+        out_specs=(VSPEC, VSPEC),
+        scratch_shapes=[
+            buf(2, D, WIDE), buf(2, D, WIDE),
+            buf(2, shard, cut), buf(2, shard, WIDE - cut),
+            buf(2, shard, WIDE), buf(2, shard, WIDE),
+            buf(2, shard, WIDE - cut), buf(2, shard, cut),
+            buf(2, shard, WIDE), buf(2, shard, WIDE), buf(2, shard, WIDE), buf(2, shard, WIDE),
+            buf(4, shard, D), buf(4, shard, D), buf(4, shard, D), buf(4, shard, D), buf(4, shard, D),
+            dma((6,)), dma((6,)), dma((6,)), dma((2, 6)), dma((2, 6)),
+            dma((18,)), dma((18,)), dma((6,)), dma((6,)),
+        ],
+        compiler_params=pltpu.CompilerParams(
+            collective_id=3, has_side_effects=True, vmem_limit_bytes=60 * 1024 * 1024
+        ),
+        name="reduce_layer",
+    )(*pieces, down, up)
+
+
+def reduce_plain(pieces, down, up):
+    s = lax.axis_index("section")
+    half = down.shape[0] // 2
+    both = jnp.stack([down, up]).reshape(2, 2, half, D)
+    keep = lax.dynamic_index_in_dim(both, s, 1, keepdims=False)
+    give = lax.dynamic_index_in_dim(both, 1 - s, 1, keepdims=False)
+    m = (keep.astype(F32) + on_chip(give).astype(F32)).astype(BF)
+    m = lax.psum(m, "ctx")
+    pair = ("fsdp", "section")
+    a = [lax.psum_scatter(p, pair, scatter_dimension=0, tiled=True) for p in pieces]
+    a, m = lax.optimization_barrier((a, m))
+    a = lax.psum(jnp.stack(a), "ctx")
+    a_far, m_far = on_chip(a), on_chip(m)
+    a = jnp.concatenate([pick(s, a, a_far), pick(s, a_far, a)], axis=1)
+    m = jnp.concatenate([pick(s, m, m_far), pick(s, m_far, m)], axis=1)
+    return a.reshape(2, 2, a.shape[1], WIDE), m
+
+
 VSPEC = pl.BlockSpec(memory_space=pltpu.VMEM)
 
 
@@ -221,6 +509,10 @@
     give = lax.dynamic_index_in_dim(halves, 1 - s, 0, keepdims=False)
     recv = on_chip(give)
     return pick(s, keep, recv), pick(s, recv, keep)
+
+
+def widen(values):
+    return jnp.pad(values, ((0, 0), (0, WIDE - D)))
 
 
 def heads(values):
@@ -351,7 +643,6 @@
         d_resid = upstream + norm_back(d_second, gain[1], n2, inv2)
         c = d_resid.astype(BF)
         d_att = mm_nt(c, out_w[layer]).astype(BF)
-        out_g = mm_tn(att, c)
         dq, dk, dv = attention_back(q, k, v, logs, d_att, allowed)
         w = qkv_w[layer]
         da_wide = mm_nt(dk, w[:, D : 2 * D]) + mm_nt(dv, w[:, 2 * D : 3 * D])
@@ -375,59 +666,45 @@
             ]
         )
         ffb_block = lax.dynamic_update_slice(
-            jnp.zeros((D, per_row), BF),
-            ffb_g.reshape(shard, per_row).astype(BF),
-            (f * shard, 0),
-        )
-        qkv_g = jnp.concatenate(
-            [
-                mm_tn(normed[reach:], dq).astype(BF),
-                mm_tn(normed, dk).astype(BF),
-                mm_tn(normed, dv).astype(BF),
-                vectors.T.astype(BF),
-                ffb_block,
-                jnp.zeros((D, EXT - 3 * D - 8 - per_row), BF),
-            ],
-            axis=1,
-        )
-        qkv_g = lax.psum_scatter(qkv_g, pair, scatter_dimension=0, tiled=True)
-        out_g = lax.psum_scatter(out_g.astype(BF), pair, scatter_dimension=0, tiled=True)
-        down_pair = down_g.astype(BF).reshape(2, ff_here // 2, D)
-        up_pair = up_g.astype(BF).reshape(nf, 2, shard // 2, ff_here)
-        give = (
-            lax.dynamic_index_in_dim(down_pair, 1 - s, 0, keepdims=False),
-            lax.dynamic_index_in_dim(up_pair, 1 - s, 1, keepdims=False),
-        )
-        keep = (
-            lax.dynamic_index_in_dim(down_pair, s, 0, keepdims=False),
-            lax.dynamic_index_in_dim(up_pair, s, 1, keepdims=False),
-        )
-        down_g, up_g = (
-            (a.astype(F32) + on_chip(b).astype(F32)).astype(BF) for a, b in zip(keep, give)
-        )
-        up_g = lax.all_to_all(up_g, "fsdp", split_axis=0, concat_axis=0, tiled=True)
-        totals[layer] = lax.psum((qkv_g, out_g, down_g, up_g), "ctx")
+            jnp.zeros((D, per_row), F32), ffb_g.reshape(shard, per_row), (f * shard, 0)
+        )
+        extra = jnp.pad(
+            jnp.concatenate([vectors.T, ffb_block], axis=1),
+            ((0, 0), (D, WIDE - D - 8 - per_row)),
+        )
+        pieces = (
+            mm_tn(normed[reach:], widen(dq)).astype(BF),
+            mm_tn(normed, widen(dk)).astype(BF),
+            mm_tn(normed, widen(dv)).astype(BF),
+            (mm_tn(att, widen(c)) + extra).astype(BF),
+        )
+        up_g = lax.all_to_all(
+            up_g.astype(BF).reshape(nf, shard, ff_here), "fsdp",
+            split_axis=0, concat_axis=0, tiled=True,
+        ).reshape(nf * shard, ff_here)
+        if nf != 4 or lax.axis_size("ctx") != 4 or layer == 1:
+            if ff_here != D:
+                up_g = up_g.reshape(ff_here, D)
+            totals[layer] = reduce_plain(pieces, down_g.astype(BF), up_g)
+        else:
+            totals[layer] = reduce_layer(pieces, down_g.astype(BF), up_g)
         upstream = upstream_next
 
-    def settle(zero, one):
-        mine = pick(s, zero, one)
-        other = on_chip(pick(s, one, zero))
-        return pick(s, mine, other).astype(F32), pick(s, other, mine).astype(F32)
-
-    qkv_t, out_t, down_t, up_t = (settle(a, b) for a, b in zip(*totals))
-    qkv_full = jnp.concatenate(qkv_t, axis=0)
-    grad_up = jnp.concatenate(up_t, axis=1).transpose(1, 0, 2).reshape(shard, nf * ff_here)
-    vectors = qkv_full[:, 3 * D : 3 * D + 8].T
+    a_tot = pick(s, totals[0][0], totals[1][0]).astype(F32)
+    m_tot = pick(s, totals[0][1], totals[1][1]).astype(F32)
+    a_tot = a_tot.reshape(4, shard, WIDE)
+    grad_up = m_tot[1].reshape(nf, shard, ff_here).transpose(1, 0, 2).reshape(shard, nf * ff_here)
+    vectors = a_tot[3, :, D : D + 8].T
     return (
         gather_micro(jnp.stack(produced), s),
         gather_micro(jnp.stack(derived), s),
-        qkv_full[None, :, : 3 * D],
-        jnp.concatenate(out_t, axis=0)[None],
+        jnp.concatenate([a_tot[i, :, :D] for i in range(3)], axis=1)[None],
+        a_tot[3, None, :, :D],
         grad_up[None],
-        jnp.concatenate(down_t, axis=0)[None],
+        m_tot[0][None],
         vectors[None, :2],
         vectors[None, 2:],
-        qkv_full[:, 3 * D + 8 : 3 * D + 8 + per_row].reshape(1, ff_here),
+        a_tot[3, :, D + 8 : D + 8 + per_row].reshape(1, ff_here),
     )
 
 

time: 1080 us -> 1040 us (0.963)
  waiting for transfers between devices: 366 us -> 159 us
  Pallas kernels: 187 us -> 367 us
  local copies, waits for them, and re-layouts: 129 us -> 99.3 us
  matrix products: 241 us -> 262 us
    psum x1 -> x2, waiting for transfers between devices: 250 us -> 85.5 us  [the longest x1 85.5 us: reduce_plain(): m = lax.psum(m, 'ctx')]
    pallas_call x0 -> x1, Pallas kernels: none -> 161 us  [reduce_layer(): pl.pallas_call(reduce_kernel, out_shape=(jax.ShapeDtypeStruct((2, 2, shar...]
    all_to_all x2, waiting for transfers between devices: 44.1 us -> 0.01 us  [on_device(): lax.all_to_all(up_g.astype(BF).reshape(nf, shard, ff_here), 'fsdp', split...]
    concatenate x2 -> x3, local copies, waits for them, and re-layouts: 25.5 us -> 6.47 us  [the longest x1 4.38 us: on_device(): jnp.concatenate([a_tot[i, :, :D] for i in range(3)], axis=1)[None]]
    pallas_call x4, Pallas kernels: 76 us -> 88.7 us  [plane_scatter(): pl.pallas_call(scatter_kernel, out_shape=jax.ShapeDtypeStruct((rows, widt...]
    unnamed x186 -> x165, local copies, waits for them, and re-layouts: 26.8 us -> 16 us
  transfers between devices with their start and end apart: 34 -> 30, of which waited for: 13 -> 9; matrix products, arithmetic and copies ran while one was open for 32% -> 33% of each run, Pallas kernels for 12% -> 30%
where the time goes in v2:
time: 1040 us; the launch traced here: 1030 us
  Pallas kernels  367 us (35%)
  matrix products  262 us (25%)
  waiting for transfers between devices  159 us (15%)
  local copies, waits for them, and re-layouts  99.3 us (10%)
  other arithmetic  87.8 us (8%)
  starting transfers between devices  38 us (4%)
  between operations  16.1 us (2%)
    pallas_call x1, Pallas kernels, reduce_layer(): pl.pallas_call(reduce_kernel, out_shape=(jax.ShapeDtypeStruct((2, 2, shar...  161 us
    pallas_call x4, Pallas kernels, plane_gather(): pl.pallas_call(gather_kernel, out_shape=jax.ShapeDtypeStruct((4, rows, wi...  117 us
    pallas_call x4, Pallas kernels, plane_scatter(): pl.pallas_call(scatter_kernel, out_shape=jax.ShapeDtypeStruct((rows, widt...  88.7 us
    psum x1, waiting for transfers between devices, reduce_plain(): m = lax.psum(m, 'ctx')  85.5 us
    dot_general x12, matrix products, mm_nt(): lax.dot_general(a, b, (((1,), (1,)), ((), ())), preferred_element_type=F32)  60.3 us
    dot_general x12, matrix products, mm_tn(): lax.dot_general(a, b, (((0,), (0,)), ((), ())), preferred_element_type=F32)  55.7 us
    dot_general x12, matrix products, mm(): return jnp.dot(a, b, preferred_element_type=F32)  55 us
    ppermute x8, waiting for transfers between devices, shift(): return lax.ppermute(value, 'ctx', pairs)  34.5 us
  transfers between devices with their start and end apart: 30, of which 9 were waited for; matrix products, arithmetic and copies ran while one was open for 33% of the time, Pallas kernels for 30%

profile of v2, /device:TPU:0, one launch (start us, length us, event | category | flops | bytes accessed | tf_op | source)
XLA Modules:
  0.0 1029.1 jit_solution(1021433157208899685)
XLA Ops:
  25.4 5.6 collective-permute-start
  38.5 4.7 all-to-all-start
  49.3 9.5 collective-permute-done.1
  60.1 32.0 %all-to-all-done = bf16[272,4,1088]{2,0,1:T(8,128)(2,1)} async-done(((bf16[272,4,1088]{2,0,1:T(8,128)(2,1)}), bf16[272,4,1088]{2,0,1:T(8,128)(2,1)}, u32[]{:S(2)}, u32[]{:S(2)}) %all-to-all-start) | async-done | bytes 2367520 | tf_op jit(solution)/shard_map/all_to_all | solution.py:584
  110.6 12.5 %fusion.5 = f32[17,256,768]{2,1,0:T(8,128)} fusion(pred[256,768]{1,0:T(8,128)(4,1)S(1)} %fusion.108, bf16[256,17,64]{0,2,1:T(8,128)(2,1)S(1)} %bitcast.294, bf16[768,17,64]{0,2,1:T(8,128)(2,1)} %bitcast.279), kind=kOutput, calls=%fused_computation.7 | convolution fusion | flops 872354816 | bytes 15794176 | tf_op jit(solution)/shard_map/reduce_sum | solution.py:524
  123.1 7.5 fusion.92
  135.1 39.1 %plane_gather.4 = bf16[4,256,1088]{2,1,0:T(8,128)(2,1)} custom-call(bf16[256,1088]{1,0:T(8,128)(2,1)} %add_convert_fusion.5.b_ref), custom_call_target="tpu_custom_call" | custom-call | tf_op jit(solution)/shard_map/plane_gather/pallas_call | solution.py:433
  175.8 8.4 multiply_convert_fusion.3
  194.1 24.5 %plane_scatter.4 = f32[256,1088]{1,0:T(8,128)} custom-call(bf16[4,256,1088]{2,1,0:T(8,128)(2,1)} %bitcast.249), custom_call_target="tpu_custom_call" | custom-call | tf_op jit(solution)/shard_map/plane_scatter/pallas_call | solution.py:450
  224.9 23.5 %plane_gather.6 = bf16[4,256,1088]{2,1,0:T(8,128)(2,1)} custom-call(bf16[256,1088]{1,0:T(8,128)(2,1)} %bitcast.257), custom_call_target="tpu_custom_call" | custom-call | tf_op jit(solution)/shard_map/plane_gather/pallas_call | solution.py:433
  278.0 12.3 %fusion.3 = f32[17,256,768]{2,1,0:T(8,128)} fusion(pred[256,768]{1,0:T(8,128)(4,1)S(1)} %copy-done.54, bf16[256,17,64]{0,2,1:T(8,128)(2,1)S(1)} %bitcast.296, bf16[768,17,64]{0,2,1:T(8,128)(2,1)} %bitcast.281), kind=kOutput, calls=%fused_computation.4 | convolution fusion | flops 872354816 | bytes 15794176 | tf_op jit(solution)/shard_map/reduce_sum | solution.py:524
  290.3 7.5 fusion.95
  302.3 24.4 %plane_gather.5 = bf16[4,256,1088]{2,1,0:T(8,128)(2,1)} custom-call(bf16[256,1088]{1,0:T(8,128)(2,1)} %add_convert_fusion.3.b_ref), custom_call_target="tpu_custom_call" | custom-call | tf_op jit(solution)/shard_map/plane_gather/pallas_call | solution.py:433
  326.7 7.8 multiply_convert_fusion.2
  334.5 7.2 fusion.147
  343.0 6.1 convolution_convert_fusion.11
  353.5 17.7 %plane_scatter.6 = f32[256,1088]{1,0:T(8,128)} custom-call(bf16[4,256,1088]{2,1,0:T(8,128)(2,1)} %bitcast.250), custom_call_target="tpu_custom_call" | custom-call | tf_op jit(solution)/shard_map/plane_scatter/pallas_call | solution.py:450
  373.0 7.6 convolution_convert_fusion.12
  384.8 18.1 %plane_scatter.5 = f32[256,1088]{1,0:T(8,128)} custom-call(bf16[4,256,1088]{2,1,0:T(8,128)(2,1)} %bitcast.251), custom_call_target="tpu_custom_call" | custom-call | tf_op jit(solution)/shard_map/plane_scatter/pallas_call | solution.py:450
  407.9 11.8 %multiply_reduce_fusion.1 = (f32[17,256]{1,0:T(8,128)S(1)}, f32[17,256,768]{2,1,0:T(8,128)}) fusion(f32[17,256,768]{2,1,0:T(8,128)} %fusion.3, bf16[256,17,64]{0,2,1:T(8,128)(2,1)S(1)} %bitcast.274, bf16[768,17,64]{0,2,1:T(8,128)(2,1)S(1)} %bitcast.256), kind=kOutput, calls=%fused_computation.11 | convolution fusion | flops 434499328 | bytes 28984320 | tf_op jit(solution)/shard_map/qhd,khd->hqk/dot_general | solution.py:535
  419.7 6.4 multiply_convert_fusion.1
  443.2 7.3 convolution_convert_fusion.2
  455.3 6.2 convert_reduce_fusion.2
  461.5 5.2 fusion.65
  466.7 5.3 convolution_add_fusion.7
  489.4 6.2 convolution_convert_fusion.3
  502.2 14.4 %collective-permute-done.10 = bf16[256,1088]{0,1:T(8,128)(2,1)S(1)} collective-permute-done((bf16[256,1088]{0,1:T(8,128)(2,1)S(1)}, bf16[256,1088]{0,1:T(8,128)(2,1)S(1)}, u32[]{:S(2)}, u32[]{:S(2)}) %collective-permute-start.10) | collective-permute-done | bytes 557088 | tf_op jit(solution)/shard_map/ppermute | solution.py:473
  517.0 4.7 multiply_reduce_fusion.3
  526.1 30.1 %plane_gather.7 = bf16[4,256,1088]{2,1,0:T(8,128)(2,1)} custom-call(bf16[256,1088]{1,0:T(8,128)(2,1)} %get-tuple-element.89.b_ref), custom_call_target="tpu_custom_call" | custom-call | tf_op jit(solution)/shard_map/plane_gather/pallas_call | solution.py:433
  556.3 7.6 fusion.146
  565.2 5.0 convolution_convert_fusion.10
  572.7 28.3 %plane_scatter.7 = f32[256,1088]{1,0:T(8,128)} custom-call(bf16[4,256,1088]{2,1,0:T(8,128)(2,1)} %bitcast.252), custom_call_target="tpu_custom_call" | custom-call | tf_op jit(solution)/shard_map/plane_scatter/pallas_call | solution.py:450
  609.4 7.4 convert_reduce_fusion.3
  616.8 11.6 %multiply_reduce_fusion = (f32[17,256]{1,0:T(8,128)S(1)}, f32[17,256,768]{2,1,0:T(8,128)}) fusion(f32[17,256,768]{2,1,0:T(8,128)} %fusion.5, bf16[256,17,64]{0,2,1:T(8,128)(2,1)S(1)} %bitcast.277, bf16[768,17,64]{0,2,1:T(8,128)(2,1)S(1)} %bitcast.254), kind=kOutput, calls=%fused_computation.9 | convolution fusion | flops 434499328 | bytes 28984320 | tf_op jit(solution)/shard_map/qhd,khd->hqk/dot_general | solution.py:535
  628.4 10.1 multiply_convert_fusion
  641.5 5.1 fusion.73
  646.6 7.1 convolution_add_fusion.6
  664.9 7.1 convolution_convert_fusion.6
  675.9 4.5 all-to-all-start.1
  680.5 6.4 convert_reduce_fusion.7
  695.1 6.0 convolution_convert_fusion.8.av
  701.1 6.1 collective-permute-done.12
  715.9 85.5 %all-reduce.18.cloned.1.call-done = bf16[2,544,1088]{2,1,0:T(8,128)(2,1)} async-done(((bf16[2,544,1088]{2,1,0:T(8,128)(2,1)}), bf16[2,544,1088]{2,1,0:T(8,128)(2,1)}) %all-reduce.18.cloned.1.call-update) | async-done | bytes 2367504 | tf_op jit(solution)/shard_map/psum | solution.py:415
  815.9 161.3 %reduce_layer.1 = (bf16[2,2,272,1152]{3,2,1,0:T(8,128)(2,1)}, bf16[2,1088,1088]{2,1,0:T(8,128)(2,1)}) custom-call(bf16[1088,1152]{1,0:T(8,128)(2,1)} %convolution_convert_fusion.1.aq, bf16[1088,1152]{1,0:T(8,128)(2,1)} %convolution_convert_fusion.9.ak, bf16[1088,1152]{1,0:T(8,128)(2,1)} %convolution_convert_fusion.8.av, bf16[1088,1152]{1,0:T(8,128)(2,1)} %fusion.16.ao, ...), custom_call_target="tpu_custom_call" | custom-call | tf_op jit(solution)/shard_map/reduce_layer/pallas_call | solution.py:383
  979.2 5.2 broadcast_select_fusion.1
  984.4 4.9 fusion.24
  993.9 6.6 copy.165
  1000.5 6.6 broadcast_in_dim_reshape.3
  (403 shorter events, 257.2 us)
Async XLA Ops:
  7.2 17.3 %copy-start = (bf16[2,1,256,1088]{2,3,1,0:T(8,128)(2,1)S(1)}, bf16[2,1,256,1088]{2,3,1,0:T(8,128)(2,1)}, u32[]{:S(2)}) copy-start(bf16[2,1,256,1088]{2,3,1,0:T(8,128)(2,1)} %param.10) | copy-start | bytes 3342340
  7.2 87.2 %all-gather.5.cloned.1.call-start = ((), (), s32[]{:S(2)}) async-start(), calls=%async_computation.7 | async-start | bytes 8146944 | tf_op jit(solution)/shard_map/all_gather | solution.py:592
  13.5 2.9 collective-permute-start.2
  18.9 12.0 %copy-start.22 = (bf16[1,272,4352]{2,1,0:T(8,128)(2,1)S(1)}, bf16[1,272,4352]{2,1,0:T(8,128)(2,1)}, u32[]{:S(2)}) copy-start(bf16[1,272,4352]{2,1,0:T(8,128)(2,1)} %param.15) | copy-start | bytes 7102468
  19.0 111.7 %all-gather.7.cloned.1.call-start = ((), (), s32[]{:S(2)}) async-start(), calls=%async_computation.8 | async-start | bytes 2820096 | tf_op jit(solution)/shard_map/all_gather | solution.py:594
  20.2 1.7 collective-permute-start.3
  23.8 224.7 %all-gather.9.cloned.1.call-start = ((), (), s32[]{:S(2)}) async-start(), calls=%async_computation.9 | async-start | bytes 8146944 | tf_op jit(solution)/shard_map/all_gather | solution.py:592
  25.4 17.9 %collective-permute-start = (bf16[256,1088]{0,1:T(8,128)(2,1)}, bf16[256,1088]{0,1:T(8,128)(2,1)}, u32[]{:S(2)}, u32[]{:S(2)}) collective-permute-start(bf16[256,1088]{0,1:T(8,128)(2,1)} %fusion.212), channel_id=1, source_target_pairs={{0,1},{1,2},{2,3},{4,5},{5,6},{6,7},{8,9},{9,10},{10,11},{12,13},{... | collective-permute-start | bytes 1671176 | tf_op jit(solution)/shard_map/ppermute | solution.py:473
  38.5 53.7 %all-to-all-start = ((bf16[272,4,1088]{2,0,1:T(8,128)(2,1)}), bf16[272,4,1088]{2,0,1:T(8,128)(2,1)}, u32[]{:S(2)}, u32[]{:S(2)}) async-start(bf16[272,4,1088]{2,0,1:T(8,128)(2,1)} %copy.133), calls=%async_computation | async-start | bytes 5013504 | tf_op jit(solution)/shard_map/all_to_all | solution.py:584
  43.2 254.7 %all-gather.11.cloned.1.call-start = ((), (), s32[]{:S(2)}) async-start(), calls=%async_computation.10 | async-start | bytes 2820096 | tf_op jit(solution)/shard_map/all_gather | solution.py:594
  43.2 140.9 %collective-permute-start.5 = (bf16[1088,1088]{1,0:T(8,128)(2,1)}, bf16[1088,1088]{1,0:T(8,128)(2,1)}, u32[]{:S(2)}, u32[]{:S(2)}) collective-permute-start(bf16[1088,1088]{1,0:T(8,128)(2,1)} %bitcast.317), channel_id=1, source_target_pairs={{0,16},{16,0},{1,17},{17,1},{2,18},{18,2},{3,19},{19,3},{4,20},{20... | collective-permute-start | bytes 7102472 | tf_op jit(solution)/shard_map/ppermute | solution.py:497
  43.3 15.6 %collective-permute-start.1 = (bf16[256,1088]{0,1:T(8,128)(2,1)}, bf16[256,1088]{0,1:T(8,128)(2,1)S(1)}, u32[]{:S(2)}, u32[]{:S(2)}) collective-permute-start(bf16[256,1088]{0,1:T(8,128)(2,1)} %collective-permute-done), channel_id=1, source_target_pairs={{0,1},{1,2},{2,3},{4,5},{5,6},{6,7},{8,9},{9,10},{10,11},{12,13},{... | collective-permute-start | bytes 1671176 | tf_op jit(solution)/shard_map/ppermute | solution.py:473
  47.8 62.9 %copy-start.53 = (pred[256,768]{1,0:T(8,128)(4,1)}, pred[256,768]{1,0:T(8,128)(4,1)S(1)}, u32[]{:S(2)}) copy-start(pred[256,768]{1,0:T(8,128)(4,1)S(1)} %fusion.108) | copy-start | bytes 589828
  92.2 83.6 %collective-permute-start.4 = (bf16[1088,1088]{1,0:T(8,128)(2,1)}, bf16[1088,1088]{1,0:T(8,128)(2,1)}, u32[]{:S(2)}, u32[]{:S(2)}) collective-permute-start(bf16[1088,1088]{1,0:T(8,128)(2,1)} %bitcast.24), channel_id=1, source_target_pairs={{0,16},{16,0},{1,17},{17,1},{2,18},{18,2},{3,19},{19,3},{4,20},{20... | collective-permute-start | bytes 7102472 | tf_op jit(solution)/shard_map/ppermute | solution.py:497
  97.8 36.2 %copy-start.55 = (f32[1088]{0:T(1024)}, f32[1088]{0:T(1024)S(1)}, u32[]{:S(2)}) copy-start(f32[1088]{0:T(1024)S(1)} %get-tuple-element.80) | copy-start | bytes 13060
  133.7 84.8 %copy-start.4 = (f32[256,1088]{1,0:T(8,128)}, f32[256,1088]{1,0:T(8,128)S(1)}, u32[]{:S(2)}) copy-start(f32[256,1088]{1,0:T(8,128)S(1)} %get-tuple-element.124) | copy-start | bytes 3342340
  133.7 40.6 %copy-start.60 = (f32[256]{0:T(256)}, f32[256]{0:T(256)S(1)}, u32[]{:S(2)}) copy-start(f32[256]{0:T(256)S(1)} %broadcast_multiply_fusion.11) | copy-start | bytes 3076
  134.0 41.4 %copy-start.64 = (f32[256]{0:T(256)}, f32[256]{0:T(256)S(1)}, u32[]{:S(2)}) copy-start(f32[256]{0:T(256)S(1)} %add_rsqrt_fusion.3) | copy-start | bytes 3076
  220.2 29.8 %collective-permute-start.6 = (bf16[256,1088]{0,1:T(8,128)(2,1)S(1)}, bf16[256,1088]{0,1:T(8,128)(2,1)S(1)}, u32[]{:S(2)}, u32[]{:S(2)}) collective-permute-start(bf16[256,1088]{0,1:T(8,128)(2,1)S(1)} %copy.135), channel_id=1, source_target_pairs={{0,1},{1,2},{2,3},{4,5},{5,6},{6,7},{8,9},{9,10},{10,11},{12,13},{... | collective-permute-start | bytes 1671176 | tf_op jit(solution)/shard_map/ppermute | solution.py:473
  248.4 467.4 %reduce-scatter.13.cloned.1.call-start = ((), (), s32[]{:S(2)}) async-start(), calls=%async_computation.13 | async-start | bytes 2820096
  249.9 11.6 %collective-permute-start.7 = (bf16[256,1088]{0,1:T(8,128)(2,1)S(1)}, bf16[256,1088]{0,1:T(8,128)(2,1)S(1)}, u32[]{:S(2)}, u32[]{:S(2)}) collective-permute-start(bf16[256,1088]{0,1:T(8,128)(2,1)S(1)} %collective-permute-done.6), channel_id=1, source_target_pairs={{0,1},{1,2},{2,3},{4,5},{5,6},{6,7},{8,9},{9,10},{10,11},{12,13},{... | collective-permute-start | bytes 1671176 | tf_op jit(solution)/shard_map/ppermute | solution.py:473
  384.8 18.2 %copy-start.13 = (bf16[1,1,256,1088]{3,2,1,0:T(8,128)(2,1)S(1)}, bf16[1,1,256,1088]{3,2,1,0:T(8,128)(2,1)}, u32[]{:S(2)}) copy-start(bf16[1,1,256,1088]{3,2,1,0:T(8,128)(2,1)} %copy.142) | copy-start | bytes 1671172
  407.4 12.3 %slice-start = ((s8[13369344]{0:T(1024)(128)(4,1)}), s8[4194304]{0:T(1024)(128)(4,1)S(1)}, s32[]{:S(2)}) async-start(s8[13369344]{0:T(1024)(128)(4,1)} %bitcast.239), calls=%async_computation.17 | async-start | bytes 8388608
  432.6 283.3 %reduce-scatter.15.cloned.1.call-start = ((), (), s32[]{:S(2)}) async-start(), calls=%async_computation.14 | async-start | bytes 2820096
  450.5 203.1 %all-to-all-start.2 = ((bf16[4,272,1088]{2,1,0:T(8,128)(2,1)}), bf16[4,272,1088]{2,1,0:T(8,128)(2,1)}, u32[]{:S(2)}, u32[]{:S(2)}) async-start(bf16[4,272,1088]{2,1,0:T(8,128)(2,1)} %bitcast.260), calls=%async_computation.2 | async-start | bytes 5013504 | tf_op jit(solution)/shard_map/all_to_all | solution.py:681
  455.0 260.8 %reduce-scatter.17.cloned.1.call-start = ((), (), s32[]{:S(2)}) async-start(), calls=%async_computation.15 | async-start | bytes 2820096
  474.8 20.8 %collective-permute-start.9 = (bf16[256,1088]{0,1:T(8,128)(2,1)}, bf16[256,1088]{0,1:T(8,128)(2,1)}, u32[]{:S(2)}, u32[]{:S(2)}) collective-permute-start(bf16[256,1088]{0,1:T(8,128)(2,1)} %copy.147), channel_id=1, source_target_pairs={{1,0},{2,1},{3,2},{5,4},{6,5},{7,6},{9,8},{10,9},{11,10},{13,12},{... | collective-permute-start | bytes 1671176 | tf_op jit(solution)/shard_map/ppermute | solution.py:473
  479.3 20.7 %collective-permute-start.8 = (bf16[256,1088]{0,1:T(8,128)(2,1)}, bf16[256,1088]{0,1:T(8,128)(2,1)}, u32[]{:S(2)}, u32[]{:S(2)}) collective-permute-start(bf16[256,1088]{0,1:T(8,128)(2,1)} %bitcast.40), channel_id=1, source_target_pairs={{0,16},{16,0},{1,17},{17,1},{2,18},{18,2},{3,19},{19,3},{4,20},{20... | collective-permute-start | bytes 1671176 | tf_op jit(solution)/shard_map/ppermute | solution.py:497
  487.8 228.1 %reduce-scatter.19.cloned.1.call-start = ((), (), s32[]{:S(2)}) async-start(), calls=%async_computation.16 | async-start | bytes 2820096
  498.5 18.4 %copy-start.27 = (bf16[17,64,256]{2,1,0:T(8,128)(2,1)S(1)}, bf16[17,64,256]{2,1,0:T(8,128)(2,1)}, u32[]{:S(2)}) copy-start(bf16[17,64,256]{2,1,0:T(8,128)(2,1)} %copy-done.26) | copy-start | bytes 1671172
  498.6 18.1 %collective-permute-start.10 = (bf16[256,1088]{0,1:T(8,128)(2,1)S(1)}, bf16[256,1088]{0,1:T(8,128)(2,1)S(1)}, u32[]{:S(2)}, u32[]{:S(2)}) collective-permute-start(bf16[256,1088]{0,1:T(8,128)(2,1)S(1)} %copy.149), channel_id=1, source_target_pairs={{1,0},{2,1},{3,2},{5,4},{6,5},{7,6},{9,8},{10,9},{11,10},{13,12},{... | collective-permute-start | bytes 1671176 | tf_op jit(solution)/shard_map/ppermute | solution.py:473
  572.7 28.4 %copy-start.5 = (f32[256,1088]{1,0:T(8,128)S(1)}, f32[256,1088]{1,0:T(8,128)}, u32[]{:S(2)}) copy-start(f32[256,1088]{1,0:T(8,128)} %copy-done.4) | copy-start | bytes 3342340
  572.7 28.4 %copy-start.56 = (f32[1088]{0:T(1024)S(1)}, f32[1088]{0:T(1024)}, u32[]{:S(2)}) copy-start(f32[1088]{0:T(1024)} %copy-done.55) | copy-start | bytes 13060
  572.7 28.4 %copy-start.61 = (f32[256]{0:T(256)S(1)}, f32[256]{0:T(256)}, u32[]{:S(2)}) copy-start(f32[256]{0:T(256)} %copy-done.60) | copy-start | bytes 3076
  572.7 28.4 %copy-start.65 = (f32[256]{0:T(256)S(1)}, f32[256]{0:T(256)}, u32[]{:S(2)}) copy-start(f32[256]{0:T(256)} %copy-done.64) | copy-start | bytes 3076
  572.7 30.3 %copy-start.12 = (bf16[256,1088]{1,0:T(8,128)(2,1)S(1)}, bf16[256,1088]{1,0:T(8,128)(2,1)}, u32[]{:S(2)}) copy-start(bf16[256,1088]{1,0:T(8,128)(2,1)} %get-tuple-element.89.b_ref) | copy-start | bytes 1671172
  657.2 32.8 %collective-permute-start.14 = (bf16[2,544,1088]{2,1,0:T(8,128)(2,1)}, bf16[2,544,1088]{2,1,0:T(8,128)(2,1)}, u32[]{:S(2)}, u32[]{:S(2)}) collective-permute-start(bf16[2,544,1088]{2,1,0:T(8,128)(2,1)} %fusion.55), channel_id=1, source_target_pairs={{0,16},{16,0},{1,17},{17,1},{2,18},{18,2},{3,19},{19,3},{4,20},{20... | collective-permute-start | bytes 7102472 | tf_op jit(solution)/shard_map/ppermute | solution.py:497
  663.1 23.8 %collective-permute-start.11 = (bf16[256,1088]{0,1:T(8,128)(2,1)S(1)}, bf16[256,1088]{0,1:T(8,128)(2,1)S(1)}, u32[]{:S(2)}, u32[]{:S(2)}) collective-permute-start(bf16[256,1088]{0,1:T(8,128)(2,1)S(1)} %copy.155), channel_id=1, source_target_pairs={{1,0},{2,1},{3,2},{5,4},{6,5},{7,6},{9,8},{10,9},{11,10},{13,12},{... | collective-permute-start | bytes 1671176 | tf_op jit(solution)/shard_map/ppermute | solution.py:473
  675.9 140.0 %all-to-all-start.1 = ((bf16[4,272,1088]{2,1,0:T(8,128)(2,1)}), bf16[4,272,1088]{2,1,0:T(8,128)(2,1)}, u32[]{:S(2)}, u32[]{:S(2)}) async-start(bf16[4,272,1088]{2,1,0:T(8,128)(2,1)} %bitcast.261), calls=%async_computation.1 | async-start | bytes 5013504 | tf_op jit(solution)/shard_map/all_to_all | solution.py:681
  680.5 120.9 %all-reduce.18.cloned.1.call-start = ((), (), s32[]{:S(2)}) async-start(), calls=%async_computation.11 | async-start | bytes 5013504 | tf_op jit(solution)/shard_map/psum | solution.py:415
  688.7 18.4 %collective-permute-start.12 = (bf16[256,1088]{0,1:T(8,128)(2,1)S(1)}, bf16[256,1088]{0,1:T(8,128)(2,1)}, u32[]{:S(2)}, u32[]{:S(2)}) collective-permute-start(bf16[256,1088]{0,1:T(8,128)(2,1)S(1)} %copy.157), channel_id=1, source_target_pairs={{1,0},{2,1},{3,2},{5,4},{6,5},{7,6},{9,8},{10,9},{11,10},{13,12},{... | collective-permute-start | bytes 1671176 | tf_op jit(solution)/shard_map/ppermute | solution.py:473
  694.6 13.9 %copy-start.28 = (bf16[17,64,256]{2,1,0:T(8,128)(2,1)S(1)}, bf16[17,64,256]{2,1,0:T(8,128)(2,1)}, u32[]{:S(2)}) copy-start(bf16[17,64,256]{2,1,0:T(8,128)(2,1)} %get-tuple-element.138) | copy-start | bytes 1671172
  694.6 13.9 %copy-start.58 = (f32[1088]{0:T(1024)S(1)}, f32[1088]{0:T(1024)}, u32[]{:S(2)}) copy-start(f32[1088]{0:T(1024)} %copy-done.57) | copy-start | bytes 13060
  694.6 284.3 %all-reduce.20.cloned.1.call-start = ((), (), s32[]{:S(2)}) async-start(), calls=%async_computation.12 | async-start | bytes 2506752 | tf_op jit(solution)/shard_map/psum | solution.py:419
  715.8 89.0 %copy-start.29 = (bf16[17,64,256]{2,1,0:T(8,128)(2,1)S(1)}, bf16[17,64,256]{2,1,0:T(8,128)(2,1)}, u32[]{:S(2)}) copy-start(bf16[17,64,256]{2,1,0:T(8,128)(2,1)} %get-tuple-element.138) | copy-start | bytes 1671172
  715.8 261.4 %collective-permute-start.13 = (f32[256,1088]{0,1:T(8,128)}, f32[256,1088]{0,1:T(8,128)S(1)}, u32[]{:S(2)}, u32[]{:S(2)}) collective-permute-start(f32[256,1088]{0,1:T(8,128)} %bitcast.291), channel_id=1, source_target_pairs={{0,16},{16,0},{1,17},{17,1},{2,18},{18,2},{3,19},{19,3},{4,20},{20... | collective-permute-start | bytes 3342344 | tf_op jit(solution)/shard_map/ppermute | solution.py:497
  801.4 177.8 %collective-permute-start.16 = (bf16[2,544,1088]{2,1,0:T(8,128)(2,1)}, bf16[2,544,1088]{2,1,0:T(8,128)(2,1)}, u32[]{:S(2)}, u32[]{:S(2)}) collective-permute-start(bf16[2,544,1088]{2,1,0:T(8,128)(2,1)} %all-reduce.18.cloned.1.call-done), channel_id=1, source_target_pairs={{0,16},{16,0},{1,17},{17,1},{2,18},{18,2},{3,19},{19,3},{4,20},{20... | collective-permute-start | bytes 7102472 | tf_op jit(solution)/shard_map/ppermute | solution.py:497
  978.9 28.3 %collective-permute-start.15 = (bf16[4,136,1152]{2,1,0:T(8,128)(2,1)}, bf16[4,136,1152]{2,1,0:T(8,128)(2,1)}, u32[]{:S(2)}, u32[]{:S(2)}) collective-permute-start(bf16[4,136,1152]{2,1,0:T(8,128)(2,1)} %all-reduce.20.cloned.1.call-done), channel_id=1, source_target_pairs={{0,16},{16,0},{1,17},{17,1},{2,18},{18,2},{3,19},{19,3},{4,20},{20... | collective-permute-start | bytes 3760136 | tf_op jit(solution)/shard_map/ppermute | solution.py:497
  (64 other events, 310.5 us)
Sparse Core Ops, SparseCore 0:
  19.1 75.2 all-gather.4
  96.9 27.9 all-gather.6
  127.4 62.5 all-gather.8
  248.5 27.6 all-gather.10
  432.7 58.7 reduce-scatter.12
  494.7 45.7 reduce-scatter.14
  543.9 45.7 reduce-scatter.16
  628.5 42.7 reduce-scatter.18
  694.7 106.6 all-reduce.17
  812.6 93.7 all-reduce.19

commit v3 on v1

v3 whole, which is shorter than its diff:
```python
import functools
import math

import jax
import jax.numpy as jnp
from jax import lax
from jax.experimental import pallas as pl
from jax.experimental.pallas import tpu as pltpu
from jax.sharding import PartitionSpec as P

D = 1088
HD = 64
F32 = jnp.float32
BF = jnp.bfloat16
SCALE = 1.0 / math.sqrt(HD)
WIDE = 1152
MESH = pl.DeviceIdType.MESH
SWAP = [(0, 1), (1, 0)]


def mm(a, b):
    return jnp.dot(a, b, preferred_element_type=F32)


def mm_nt(a, b):
    return lax.dot_general(a, b, (((1,), (1,)), ((), ())), preferred_element_type=F32)


def mm_tn(a, b):
    return lax.dot_general(a, b, (((0,), (0,)), ((), ())), preferred_element_type=F32)


def norm_parts(values):
    center = jnp.mean(values, axis=-1, keepdims=True)
    offset = values - center
    spread = jnp.mean(offset * offset, axis=-1, keepdims=True)
    inv = lax.rsqrt(spread + 1e-05)
    return offset * inv, inv


def norm_back(grad, gain, unit, inv):
    dn = grad * gain
    return inv * (
        dn
        - jnp.mean(dn, axis=-1, keepdims=True)
        - unit * jnp.mean(dn * unit, axis=-1, keepdims=True)
    )


def phi_parts(z):
    cdf = 0.5 * (1.0 + lax.erf(z * (1.0 / math.sqrt(2.0))))
    pdf = jnp.exp(-0.5 * z * z) * (1.0 / math.sqrt(2.0 * math.pi))
    return cdf, pdf


def plane_neighbours():
    f = lax.axis_index("fsdp")
    x = lax.rem(f, 2)
    y = f // 2
    return y * 2 + (1 - x), (1 - y) * 2 + x


def plane_barrier(xn, yn):
    barrier = pltpu.get_barrier_semaphore()
    for nb in (xn, yn):
        pl.semaphore_signal(barrier, inc=1, device_id={"fsdp": nb}, device_id_type=MESH)
    pl.semaphore_wait(barrier, 2)


def remote(src, dst, send, recv, nb):
    return pltpu.make_async_remote_copy(
        src_ref=src, dst_ref=dst, send_sem=send, recv_sem=recv,
        device_id={"fsdp": nb}, device_id_type=MESH,
    )


def exchange_rows(own_ref, all_ref, parts, compute, total_ref, bufs, send, recv):
    x1, y1, x2, y2, sum_x, sum_y = bufs
    xn, yn = plane_neighbours()
    half = own_ref.shape[0] // 2
    top, low = pl.ds(0, half), pl.ds(half, half)
    plane_barrier(xn, yn)

    to_x = remote(own_ref, all_ref.at[1], send.at[0], recv.at[0], xn)
    to_y = remote(own_ref, all_ref.at[2], send.at[1], recv.at[1], yn)
    far_x = remote(all_ref.at[2, top], all_ref.at[3, top], send.at[2], recv.at[2], xn)
    far_y = remote(all_ref.at[1, low], all_ref.at[3, low], send.at[3], recv.at[3], yn)
    first_x = remote(parts.at[3, top], x1, send.at[4], recv.at[4], xn)
    first_y = remote(parts.at[3, low], y1, send.at[5], recv.at[5], yn)
    own_x = remote(parts.at[1, top], x2.at[top], send.at[6], recv.at[6], xn)
    own_y = remote(parts.at[2, low], y2.at[low], send.at[7], recv.at[7], yn)
    rest_x = remote(sum_x, x2.at[low], send.at[8], recv.at[8], xn)
    rest_y = remote(sum_y, y2.at[top], send.at[9], recv.at[9], yn)

    to_x.start()
    to_y.start()
    all_ref[0] = own_ref[...]
    compute(0)
    to_x.wait_recv()
    far_y.start()
    to_y.wait_recv()
    far_x.start()
    compute(1)
    own_x.start()
    far_x.wait_recv()
    far_y.wait_recv()
    compute(3)
    first_x.start()
    first_y.start()
    compute(2)
    own_y.start()
    first_x.wait_recv()
    sum_y[...] = (parts[2, top, :].astype(F32) + x1[...].astype(F32)).astype(BF)
    rest_y.start()
    first_y.wait_recv()
    sum_x[...] = (parts[1, low, :].astype(F32) + y1[...].astype(F32)).astype(BF)
    rest_x.start()
    own_x.wait_recv()
    rest_y.wait_recv()
    total_ref[top, :] = (
        parts[0, top, :].astype(F32) + x2[top, :].astype(F32) + y2[top, :].astype(F32)
    )
    own_y.wait_recv()
    rest_x.wait_recv()
    total_ref[low, :] = (
        parts[0, low, :].astype(F32) + x2[low, :].astype(F32) + y2[low, :].astype(F32)
    )
    for copy in (to_x, to_y, far_x, far_y, first_x, first_y, own_x, own_y, rest_x, rest_y):
        copy.wait_send()


def forward_kernel(
    own, up, down, bias, total, all_ref, active, slope, parts, x1, y1, x2, y2, sx, sy, send, recv
):
    def compute(r):
        z = mm(all_ref[r], up[...]) + bias[...]
        cdf, pdf = phi_parts(z)
        active[r] = (z * cdf).astype(BF)
        slope[r] = cdf + z * pdf
        parts[r] = mm(active[r], down[...]).astype(BF)

    exchange_rows(own, all_ref, parts, compute, total, (x1, y1, x2, y2, sx, sy), send, recv)


def backward_kernel(
    own, up, down, slope, total, all_ref, dz_all, bias_g, parts, x1, y1, x2, y2, sx, sy, send, recv
):
    bias_g[...] = jnp.zeros_like(bias_g)

    def compute(r):
        dz = mm_nt(all_ref[r], down[...]) * slope[r]
        bias_g[...] += jnp.sum(dz, axis=0, keepdims=True)
        dz_all[r] = dz.astype(BF)
        parts[r] = mm_nt(dz_all[r], up[...]).astype(BF)

    exchange_rows(own, all_ref, parts, compute, total, (x1, y1, x2, y2, sx, sy), send, recv)


VSPEC = pl.BlockSpec(memory_space=pltpu.VMEM)


def lasting(micros):
    return pl.CostEstimate(flops=0, transcendentals=0, bytes_accessed=int(micros * 3.5e6))


def plane_call(kernel, ident, outs, rows, *operands):
    half = rows // 2
    return pl.pallas_call(
        kernel,
        out_shape=outs,
        in_specs=[VSPEC] * len(operands),
        out_specs=(VSPEC,) * len(outs),
        scratch_shapes=[
            pltpu.VMEM((4, rows, D), BF),
            pltpu.VMEM((half, D), BF),
            pltpu.VMEM((half, D), BF),
            pltpu.VMEM((rows, D), BF),
            pltpu.VMEM((rows, D), BF),
            pltpu.VMEM((half, D), BF),
            pltpu.VMEM((half, D), BF),
            pltpu.SemaphoreType.DMA((10,)),
            pltpu.SemaphoreType.DMA((10,)),
        ],
        compiler_params=pltpu.CompilerParams(
            collective_id=ident, has_side_effects=True, vmem_limit_bytes=40 * 1024 * 1024
        ),
        cost_estimate=lasting(40),
    )(*operands)


def mlp_forward(own, up, down, bias):
    rows = own.shape[0]
    if lax.axis_size("fsdp") != 4:
        every = lax.all_gather(own, "fsdp", axis=0, tiled=True)
        z = mm(every, up) + bias
        cdf, pdf = phi_parts(z)
        active = (z * cdf).astype(BF)
        part = mm(active, down).astype(BF)
        total = lax.psum_scatter(part, "fsdp", scatter_dimension=0, tiled=True).astype(F32)
        return total, every, active, cdf + z * pdf
    shape = (4, rows, D)
    return plane_call(
        forward_kernel, 1,
        (
            jax.ShapeDtypeStruct((rows, D), F32),
            jax.ShapeDtypeStruct(shape, BF),
            jax.ShapeDtypeStruct(shape, BF),
            jax.ShapeDtypeStruct(shape, F32),
        ),
        rows, own, up, down, bias,
    )


def mlp_backward(own, up, down, slope):
    rows = own.shape[0]
    if lax.axis_size("fsdp") != 4:
        every = lax.all_gather(own, "fsdp", axis=0, tiled=True)
        dz = mm_nt(every, down) * slope
        dz_b = dz.astype(BF)
        part = mm_nt(dz_b, up).astype(BF)
        total = lax.psum_scatter(part, "fsdp", scatter_dimension=0, tiled=True).astype(F32)
        return total, every, dz_b, jnp.sum(dz, axis=0, keepdims=True)
    shape = (4, rows, D)
    return plane_call(
        backward_kernel, 2,
        (
            jax.ShapeDtypeStruct((rows, D), F32),
            jax.ShapeDtypeStruct(shape, BF),
            jax.ShapeDtypeStruct(shape, BF),
            jax.ShapeDtypeStruct((1, D), F32),
        ),
        rows, own, up, down, slope,
    )


def weights_kernel(
    own, rows_in, full, rows_out, load, core_s, core_r, p_send, p_recv, f_send, f_recv, z_send, z_recv
):
    s = lax.axis_index("section")
    f = lax.axis_index("fsdp")
    xn, yn = plane_neighbours()
    dn = 3 - f
    shard, wide = own.shape[1], own.shape[2]
    cut = 640
    left = pl.ds(0, cut)
    right = pl.ds(cut, wide - cut)

    def to(src, dst, send, recv, **where):
        return pltpu.make_async_remote_copy(
            src_ref=src, dst_ref=dst, send_sem=send, recv_sem=recv,
            device_id=where, device_id_type=MESH,
        )

    barrier = pltpu.get_barrier_semaphore()
    z = lax.axis_index("ctx")
    above = {"ctx": lax.rem(z + 1, 4)}
    below = {"ctx": lax.rem(z + 3, 4)}
    for where in ({"section": 1 - s}, {"fsdp": xn}, {"fsdp": yn}, above, below):
        pl.semaphore_signal(barrier, inc=1, device_id=where, device_id_type=MESH)
    pl.semaphore_wait(barrier, 5)
    rows = rows_in.shape[0]
    near_rows, far_rows = pl.ds(rows, rows), pl.ds(0, rows)
    step_one = to(rows_in, rows_out.at[near_rows], z_send.at[0], z_recv.at[0], **above)
    step_two = to(
        rows_out.at[near_rows], rows_out.at[far_rows], z_send.at[1], z_recv.at[1], **above
    )

    @pl.when(z < 3)
    def _():
        step_one.start()

    rows_out[pl.ds(2 * rows, rows), :] = rows_in[...]

    @pl.when(z == 0)
    def _():
        rows_out[near_rows, :] = jnp.zeros(rows_in.shape, BF)

    @pl.when(z < 2)
    def _():
        rows_out[far_rows, :] = jnp.zeros(rows_in.shape, BF)

    def blk(owner):
        return pl.ds(pl.multiple_of(owner * shard, 16), shard)

    def give(p):
        return to(own.at[p], full.at[p, blk(f)], core_s.at[p], core_r.at[p], section=1)

    def keep(p):
        return pltpu.make_async_copy(own.at[p], full.at[p, blk(f)], load.at[p])

    @pl.when(s == 0)
    def _():
        for p in (2, 3, 0, 1):
            give(p).start()
        for p in range(4):
            keep(p).start()
        keep(0).wait()
        keep(1).wait()

    @pl.when(s == 1)
    def _():
        give(2).wait_recv()
        give(3).wait_recv()

    def same(piece, rows, send, recv, cols=slice(None), **where):
        ref = full.at[piece, rows, cols]
        return to(ref, ref, send, recv, **where)

    def hops(k):
        p = 2 * s + k
        return (
            same(p, blk(f), p_send.at[k, 0], p_recv.at[k, 0], fsdp=xn),
            same(p, blk(f), p_send.at[k, 1], p_recv.at[k, 1], fsdp=yn),
            same(p, blk(yn), p_send.at[k, 2], p_recv.at[k, 2], left, fsdp=xn),
            same(p, blk(xn), p_send.at[k, 3], p_recv.at[k, 3], right, fsdp=yn),
        )

    def here(k):
        p = 2 * s + k
        return [
            same(p, blk(owner), f_send.at[k, i], f_recv.at[k, i], section=1 - s)
            for i, owner in enumerate((xn, yn, dn))
        ]

    for k in range(2):
        copies = hops(k)
        copies[0].start()
        copies[1].start()
    for k in range(2):
        copies, across = hops(k), here(k)
        copies[0].wait_recv()
        copies[3].start()
        across[0].start()
        copies[1].wait_recv()
        copies[2].start()
        across[1].start()

    @pl.when(z > 0)
    def _():
        step_one.wait_recv()

    @pl.when((z == 1) | (z == 2))
    def _():
        step_two.start()

    for k in range(2):
        copies, across = hops(k), here(k)
        copies[2].wait_recv()
        copies[3].wait_recv()
        across[2].start()
    for k in range(2):
        for copy in here(k):
            copy.wait()
        for copy in hops(k):
            copy.wait_send()

    @pl.when(s == 0)
    def _():
        for p in range(4):
            give(p).wait_send()
        keep(2).wait()
        keep(3).wait()

    @pl.when(s == 1)
    def _():
        give(0).wait_recv()
        give(1).wait_recv()

    @pl.when(z < 3)
    def _():
        step_one.wait_send()

    @pl.when((z == 1) | (z == 2))
    def _():
        step_two.wait_send()

    @pl.when(z > 1)
    def _():
        step_two.wait_recv()


def first_weights(own, rows_in):
    dma = pltpu.SemaphoreType.DMA
    return pl.pallas_call(
        weights_kernel,
        out_shape=(
            jax.ShapeDtypeStruct((4, D, WIDE), BF),
            jax.ShapeDtypeStruct((3 * rows_in.shape[0], D), BF),
        ),
        in_specs=[pl.BlockSpec(memory_space=pl.ANY), VSPEC],
        out_specs=(VSPEC, VSPEC),
        scratch_shapes=[
            dma((4,)), dma((4,)), dma((4,)), dma((2, 4)), dma((2, 4)), dma((2, 3)), dma((2, 3)),
            dma((2,)), dma((2,)),
        ],
        compiler_params=pltpu.CompilerParams(
            collective_id=4, has_side_effects=True, vmem_limit_bytes=16 * 1024 * 1024
        ),
        cost_estimate=lasting(50),
        name="first_weights",
    )(own, rows_in)


def z_partners():
    z = lax.axis_index("ctx")
    return z + 1 - 2 * lax.rem(z, 2), 3 - z, (z == 1) | (z == 2)


def add_rows(dst, one, two, rows, step):
    @pl.loop(0, rows // step)
    def _(i):
        at = pl.ds(pl.multiple_of(i * step, 16), step)
        dst[at, :] = (one[at, :].astype(F32) + two[at, :].astype(F32)).astype(dst.dtype)


CUTS = ((0, 640, 384), (640, 512, 256))


def reduce_kernel(
    q0, k0, v0, o0, q1, k1, v1, o1, mlp, halo,
    qkv_out, out_out, down_out, up_out, rows_out,
    own_in, held, up_own, up_far, sent, caught,
    x1a, y1a, x2a, y2a, sxa, sya, ta, zaa, zba,
    x1b, y1b, x2b, y2b, sxb, syb, tb, zab, zbb,
    load, core_s, core_r, p_send, p_recv, z_send, z_recv, h_send, h_recv,
):
    s = lax.axis_index("section")
    f = lax.axis_index("fsdp")
    xn, yn = plane_neighbours()
    dn = 3 - f
    side, across, inner = z_partners()
    pieces = ((q0, k0, v0, o0), (q1, k1, v1, o1))
    sets = (
        (x1a, y1a, x2a, y2a, sxa, sya, ta, zaa, zba),
        (x1b, y1b, x2b, y2b, sxb, syb, tb, zab, zbb),
    )
    shard = out_out.shape[0]
    rows = rows_out.shape[0]
    z = lax.axis_index("ctx")
    above, below = {"ctx": lax.rem(z + 1, 4)}, {"ctx": lax.rem(z + 3, 4)}

    def to(src, dst, send, recv, **where):
        return pltpu.make_async_remote_copy(
            src_ref=src, dst_ref=dst, send_sem=send, recv_sem=recv,
            device_id=where, device_id_type=MESH,
        )

    barrier = pltpu.get_barrier_semaphore()
    partners = ({"section": 1 - s}, {"fsdp": xn}, {"fsdp": yn}, above, below)
    for where in partners:
        pl.semaphore_signal(barrier, inc=1, device_id=where, device_id_type=MESH)
    pl.semaphore_wait(barrier, 5)

    def blk(owner):
        return pl.ds(pl.multiple_of(owner * shard, 16), shard)

    def by_core(act):
        for core in range(2):
            pl.when(s == core)(functools.partial(act, core))

    def far(j, src):
        return to(src, held.at[j], core_s.at[j], core_r.at[j], section=1 - s)

    def near(j, src):
        return pltpu.make_async_copy(src, own_in.at[j % 2], load.at[j])

    def bufs(c):
        return tuple(ref.at[c // 2] for ref in sets[c % 2])

    def plane(c):
        x1, y1, x2, y2, sx, sy = bufs(c)[:6]
        own = held.at[c // 2]
        at, width, cut = CUTS[c % 2]
        left, right = pl.ds(at, cut), pl.ds(at + cut, width - cut)
        to_left, to_right = pl.ds(0, cut), pl.ds(cut, width - cut)
        sems = [(p_send.at[c, i], p_recv.at[c, i]) for i in range(6)]
        return (
            to(own.at[blk(dn), left], x1, *sems[0], fsdp=xn),
            to(own.at[blk(dn), right], y1, *sems[1], fsdp=yn),
            to(own.at[blk(xn), left], x2.at[:, to_left], *sems[2], fsdp=xn),
            to(own.at[blk(yn), right], y2.at[:, to_right], *sems[3], fsdp=yn),
            to(sx, x2.at[:, to_right], *sems[4], fsdp=xn),
            to(sy, y2.at[:, to_left], *sems[5], fsdp=yn),
        )

    def along(c):
        t, za, zb = bufs(c)[6:]
        sems = [(z_send.at[c, i], z_recv.at[c, i]) for i in range(3)]
        return (
            to(t, za, *sems[0], ctx=side),
            to(za, zb, *sems[1], ctx=across),
            to(zb, zb, *sems[2], ctx=side),
        )

    def join(j):
        far(j, q0).wait_recv()
        near(j, q0).wait()
        add_rows(held.at[j], own_in.at[j % 2], held.at[j], 4 * shard, shard)
        for c in (2 * j, 2 * j + 1):
            for copy in plane(c)[:4]:
                copy.start()
        if j < 2:
            by_core(lambda core: near(j + 2, pieces[core][j + 2]).start())

    def second(c):
        copies = plane(c)
        x1, y1, _, _, sx, sy = bufs(c)[:6]
        at, width, cut = CUTS[c % 2]
        own = held.at[c // 2]
        copies[0].wait_recv()
        add_rows(sy, own.at[blk(yn), pl.ds(at, cut)], x1, shard, shard)
        copies[5].start()
        copies[1].wait_recv()
        add_rows(sx, own.at[blk(xn), pl.ds(at + cut, width - cut)], y1, shard, shard)
        copies[4].start()

    def third(c):
        copies = plane(c)
        _, _, x2, y2, _, _, t, _, _ = bufs(c)
        at, width, _ = CUTS[c % 2]
        for copy in copies[2:]:
            copy.wait_recv()
        t[...] = (
            held[c // 2, blk(f), pl.ds(at, width)].astype(F32)
            + x2[...].astype(F32)
            + y2[...].astype(F32)
        ).astype(BF)

        @pl.when(jnp.logical_not(inner))
        def _():
            along(c)[0].start()

    def inward(c):
        @pl.when(inner)
        def _():
            t, za, _ = bufs(c)[6:]
            copies = along(c)
            copies[0].wait_recv()
            add_rows(za, t, za, shard, shard)
            copies[1].start()

    def crossed(c):
        @pl.when(inner)
        def _():
            _, za, zb = bufs(c)[6:]
            copies = along(c)
            copies[1].wait_recv()
            add_rows(zb, za, zb, shard, shard)
            copies[2].start()

    def last(c):
        at, width, _ = CUTS[c % 2]
        j = c // 2

        @pl.when(jnp.logical_not(inner))
        def _():
            along(c)[2].wait_recv()

        if j < 3:
            width = min(width, D - at)
            qkv_out[:, pl.ds(j * D + at, width)] = bufs(c)[8][:, pl.ds(0, width)]
        else:
            out_out[:, pl.ds(at, width)] = bufs(c)[8][...]

    half = down_out.shape[0] // 2
    mine = pl.ds(pl.multiple_of(s * half, 16), half)
    down_far = to(mlp.at[0], down_out.at[mine], core_s.at[4], core_r.at[4], section=1 - s)
    down_near = pltpu.make_async_copy(mlp.at[0], down_out.at[mine], load.at[4])
    far_up = to(mlp.at[1], up_far, core_s.at[5], core_r.at[5], section=1 - s)
    near_up = pltpu.make_async_copy(mlp.at[1], up_own, load.at[5])

    def lay_up():
        far_up.wait_recv()
        near_up.wait()

        @pl.when(s == 1)
        def _():
            for k in range(2):
                up_out[:, pl.ds(k * D, D)] = up_far[pl.ds(k * shard, shard), :]
                up_out[:, pl.ds((2 + k) * D, D)] = up_own[pl.ds(k * shard, shard), :]

    back_one = to(halo.at[pl.ds(0, rows)], caught.at[0], h_send.at[0], h_recv.at[0], **below)
    back_two = to(sent, caught.at[1], h_send.at[1], h_recv.at[1], **below)

    def back():
        @pl.when(z < 3)
        def _():
            back_one.wait_recv()

        @pl.when(z == 3)
        def _():
            caught[0] = jnp.zeros_like(caught[0])

        @pl.when(z > 0)
        def _():
            add_rows(sent, halo.at[pl.ds(rows, rows)], caught.at[0], rows, rows)
            back_two.start()

    def back_end():
        @pl.when(z < 3)
        def _():
            back_two.wait_recv()
            rows_out[...] = caught[1]

        @pl.when(z == 3)
        def _():
            rows_out[...] = jnp.zeros_like(rows_out)

    @pl.when(z > 0)
    def _():
        back_one.start()

    for j in range(4):
        by_core(lambda core: far(j, pieces[1 - core][j]).start())
        if j < 2:
            by_core(lambda core: near(j, pieces[core][j]).start())
    for copy in (down_far, down_near, far_up, near_up):
        copy.start()

    join(0)
    for c in range(12):
        if c in (1, 3, 5):
            join((c + 1) // 2)
        if c < 8:
            second(c)
        if 1 <= c <= 8:
            third(c - 1)
        if 2 <= c <= 9:
            inward(c - 2)
        if 3 <= c <= 10:
            crossed(c - 3)
        if c >= 4:
            last(c - 4)
        if c == 2:
            back()
        if c == 4:
            lay_up()
        if c == 6:
            back_end()

    down_near.wait()
    down_far.wait()
    far_up.wait_send()

    @pl.when(z > 0)
    def _():
        back_one.wait_send()
        back_two.wait_send()

    for j in range(4):
        far(j, q0).wait_send()
    for c in range(8):
        for copy in plane(c):
            copy.wait_send()

    @pl.when(inner)
    def _():
        for c in range(8):
            for copy in along(c)[1:]:
                copy.wait_send()

    @pl.when(jnp.logical_not(inner))
    def _():
        for c in range(8):
            along(c)[0].wait_send()


def reduce_both(zero, one, mlp, halo):
    shard = D // 4
    rows = halo.shape[0] // 2
    dma = pltpu.SemaphoreType.DMA
    any_spec = pl.BlockSpec(memory_space=pl.ANY)

    def buf(*shape):
        return pltpu.VMEM(shape, BF)

    def part(_, width, cut):
        wide = buf(4, shard, width)
        return [
            buf(4, shard, cut), buf(4, shard, width - cut), wide, wide,
            buf(4, shard, width - cut), buf(4, shard, cut), wide, wide, wide,
        ]

    return pl.pallas_call(
        reduce_kernel,
        out_shape=tuple(
            jax.ShapeDtypeStruct(shape, BF)
            for shape in ((shard, 3 * D), (shard, WIDE), (D, D), (shard, 4 * D), (rows, D))
        ),
        in_specs=[any_spec] * 9 + [VSPEC],
        out_specs=(VSPEC,) * 5,
        scratch_shapes=[
            buf(2, D, WIDE), buf(4, D, WIDE), buf(D // 2, D), buf(D // 2, D), buf(rows, D),
            buf(2, rows, D), *part(*CUTS[0]), *part(*CUTS[1]),
            dma((6,)), dma((6,)), dma((6,)), dma((8, 6)), dma((8, 6)), dma((8, 3)), dma((8, 3)),
            dma((2,)), dma((2,)),
        ],
        compiler_params=pltpu.CompilerParams(
            collective_id=3, has_side_effects=True, vmem_limit_bytes=58 * 1024 * 1024
        ),
        cost_estimate=lasting(120),
        name="reduce_both",
    )(*zero, *one, mlp, halo)


def halves_pair(down, up):
    s = lax.axis_index("section")
    both = jnp.stack([down, up])
    both = both.reshape(2, 2, both.shape[1] // 2, D)
    keep = lax.dynamic_index_in_dim(both, s, 1, keepdims=False)
    give = lax.dynamic_index_in_dim(both, 1 - s, 1, keepdims=False)
    return (keep.astype(F32) + on_chip(give).astype(F32)).astype(BF)


def halves_settle(zero, one):
    s = lax.axis_index("section")
    mine, far = pick(s, zero, one), on_chip(pick(s, one, zero))
    return jnp.concatenate([pick(s, mine, far), pick(s, far, mine)], axis=1).astype(F32)


def reduce_plain(pieces):
    s = lax.axis_index("section")
    pair = ("fsdp", "section")
    a = jnp.stack([lax.psum_scatter(p, pair, scatter_dimension=0, tiled=True) for p in pieces])
    a = lax.psum(a, "ctx")
    far = on_chip(a)
    return jnp.concatenate([pick(s, a, far), pick(s, far, a)], axis=1)


def shift(value, steps):
    count = lax.axis_size("ctx")
    pairs = [(i, i + steps) for i in range(count) if 0 <= i + steps < count]
    return lax.ppermute(value, "ctx", pairs)


def with_halo(own, chunks):
    parts = [own]
    for _ in range(chunks):
        parts.append(shift(parts[-1], 1))
    return jnp.concatenate(parts[::-1], axis=0)


def return_halo(halo, chunks, rows):
    carried = None
    for far in range(chunks):
        mine = halo[far * rows : (far + 1) * rows]
        carried = mine if carried is None else mine + carried
        carried = shift(carried.astype(BF), -1).astype(F32)
    return carried


def pick(s, first, second):
    return jnp.where(s == 0, first, second)


def on_chip(value):
    return lax.ppermute(value, "section", SWAP)


def both_layers(own, s):
    other = on_chip(own)
    return pick(s, own, other), pick(s, other, own)


def flat(values):
    return values.reshape(-1, values.shape[-1])


def widen(values):
    return jnp.pad(values, ((0, 0), (0, WIDE - D)))


def attend_kernel(q_ref, k_ref, v_ref, bias_ref, out_ref):
    lanes = lax.broadcasted_iota(jnp.int32, q_ref.shape, 1)
    q = q_ref[...] * jnp.asarray(SCALE, BF)
    outs = []
    for low in (True, False):
        mine = (lanes < HD) if low else (lanes >= HD)
        one = jnp.where(mine, q, jnp.zeros_like(q))
        weight = jnp.exp(mm_nt(one, k_ref[...]) + bias_ref[...])
        prob = weight * (1.0 / jnp.sum(weight, axis=-1, keepdims=True))
        outs.append(mm(prob.astype(BF), v_ref[...]))
    out_ref[...] = jnp.where(lanes < HD, outs[0], outs[1]).astype(BF)


def attend(q, k, v, bias):
    rows, keys = q.shape[0], k.shape[0]
    return pl.pallas_call(
        attend_kernel,
        out_shape=jax.ShapeDtypeStruct((rows, D), BF),
        grid=(WIDE // 128,),
        in_specs=[
            pl.BlockSpec((rows, 128), lambda i: (0, i)),
            pl.BlockSpec((keys, 128), lambda i: (0, i)),
            pl.BlockSpec((keys, 128), lambda i: (0, i)),
            pl.BlockSpec((rows, keys), lambda i: (0, 0)),
        ],
        out_specs=pl.BlockSpec((rows, 128), lambda i: (0, i)),
        compiler_params=pltpu.CompilerParams(vmem_limit_bytes=24 * 1024 * 1024),
        cost_estimate=lasting(12),
        name="attend",
    )(q, k, v, bias)


def attend_back_kernel(q_ref, k_ref, v_ref, g_ref, bias_ref, dq_ref, dk_ref, dv_ref):
    lanes = lax.broadcasted_iota(jnp.int32, q_ref.shape, 1)
    q = q_ref[...] * jnp.asarray(SCALE, BF)
    dqs, dk, dv = [], 0.0, 0.0
    for low in (True, False):
        mine = (lanes < HD) if low else (lanes >= HD)
        one = jnp.where(mine, q, jnp.zeros_like(q))
        grad = jnp.where(mine, g_ref[...], jnp.zeros_like(q))
        weight = jnp.exp(mm_nt(k_ref[...], one) + bias_ref[...])
        prob = weight * (1.0 / jnp.sum(weight, axis=0, keepdims=True))
        d_prob = mm_nt(v_ref[...], grad)
        row = jnp.sum(prob * d_prob, axis=0, keepdims=True)
        d_score = (prob * (d_prob - row)).astype(BF)
        dqs.append(mm_tn(d_score, k_ref[...]))
        dk = dk + mm(d_score, one)
        dv = dv + mm(prob.astype(BF), grad)
    dq_ref[...] = (jnp.where(lanes < HD, dqs[0], dqs[1]) * SCALE).astype(BF)
    dk_ref[...] = dk.astype(BF)
    dv_ref[...] = dv.astype(BF)


def attend_back(q, k, v, grad, bias):
    rows, keys = q.shape[0], k.shape[0]
    few = pl.BlockSpec((rows, 128), lambda i: (0, i))
    many = pl.BlockSpec((keys, 128), lambda i: (0, i))
    return pl.pallas_call(
        attend_back_kernel,
        out_shape=(
            jax.ShapeDtypeStruct((rows, WIDE), BF),
            jax.ShapeDtypeStruct((keys, WIDE), BF),
            jax.ShapeDtypeStruct((keys, WIDE), BF),
        ),
        grid=(WIDE // 128,),
        in_specs=[few, many, many, few, pl.BlockSpec((keys, rows), lambda i: (0, 0))],
        out_specs=(few, many, many),
        compiler_params=pltpu.CompilerParams(vmem_limit_bytes=24 * 1024 * 1024),
        cost_estimate=lasting(22),
        name="attend_back",
    )(q, k, v, grad, bias)


def on_device(
    inputs, segments, cotangent, qkv_weight, out_weight, up_weight, down_weight,
    norm_gains, biases, ff_bias,
):
    rows = inputs.shape[2]
    length = segments.shape[2]
    chunks = min((length // 2 - 1 + rows - 1) // rows, lax.axis_size("ctx") - 1)
    reach = chunks * rows
    s = lax.axis_index("section")
    f = lax.axis_index("fsdp")
    nf = lax.axis_size("fsdp")
    shard = D // nf
    ff_here = ff_bias.shape[1]
    per_row = ff_here // shard
    pair = ("fsdp", "section")
    fits = nf == 4 and lax.axis_size("ctx") == 4 and chunks == 2

    own_in = lax.dynamic_index_in_dim(inputs, s, 0, keepdims=False)[0]
    own_cot = lax.dynamic_index_in_dim(cotangent, s, 0, keepdims=False)[0]
    seg = lax.dynamic_index_in_dim(segments, s, 0, keepdims=False)[0]
    start = lax.axis_index("ctx") * rows
    key_seg = lax.dynamic_slice_in_dim(
        jnp.pad(seg, (reach, 0), constant_values=-1), start, reach + rows, 0
    )
    allowed = (key_seg[reach:, None] == key_seg[None, :]) & (
        jnp.arange(reach + rows, dtype=jnp.int32)[None, :] - reach
        <= jnp.arange(rows, dtype=jnp.int32)[:, None]
    )

    bias = jnp.where(allowed, 0.0, -1e30).astype(F32)
    bias_t = bias.T

    small = jnp.concatenate(
        [norm_gains[0].T, biases[0].T, ff_bias[0].reshape(shard, per_row)], axis=1
    )
    packed = jnp.stack(
        [
            widen(qkv_weight[0][:, :D]),
            widen(qkv_weight[0][:, D : 2 * D]),
            widen(qkv_weight[0][:, 2 * D :]),
            jnp.concatenate(
                [out_weight[0], small, jnp.zeros((shard, WIDE - D - 8 - per_row), BF)], axis=1
            ),
        ]
    )
    if fits:
        zero, wide_in = first_weights(packed, own_in)
        packed, up_shard, down_shard, zero = lax.optimization_barrier(
            (packed, up_weight[0], down_weight[0], zero)
        )
    else:
        up_shard, down_shard = up_weight[0], down_weight[0]
        wide_in = with_halo(own_in, chunks)
    half = shard // 2
    halves = packed.reshape(4, 2, half, WIDE)
    keep = lax.dynamic_index_in_dim(halves, s, 1, keepdims=False)
    give = lax.dynamic_index_in_dim(halves, 1 - s, 1, keepdims=False)

    def gathered(part):
        rows_first = part.transpose(1, 0, 2).reshape(half, 4 * WIDE)
        every = lax.all_gather(rows_first, pair, axis=0, tiled=True)
        return [every[:, i * WIDE : (i + 1) * WIDE] for i in range(4)]

    recv = on_chip(give)
    one = gathered(pick(s, recv, keep))
    zero = [zero[i] for i in range(4)] if fits else gathered(pick(s, keep, recv))
    up_own = lax.all_to_all(
        up_shard.reshape(shard, nf, ff_here), "fsdp", split_axis=1, concat_axis=0, tiled=True
    ).reshape(D, ff_here)
    up_w = both_layers(up_own, s)
    down_w = both_layers(down_shard, s)

    weights = (zero, one)
    gains, shifts, ffb = [], [], []
    for layer in range(2):
        beside = weights[layer][3]
        vectors = beside[:, D : D + 8].T.astype(F32)
        gains.append(vectors[:2])
        shifts.append(vectors[2:])
        hidden = beside[:, D + 8 : D + 8 + per_row].reshape(-1).astype(F32)
        ffb.append(lax.dynamic_slice_in_dim(hidden, f * ff_here, ff_here, 0))

    kept = []
    current = own_in
    produced = []
    for layer in range(2):
        gain, shift_rows = gains[layer], shifts[layer]
        wide = (with_halo(current, chunks) if layer else wide_in).astype(F32)
        n1, inv1 = norm_parts(wide)
        normed = (n1 * gain[0] + shift_rows[0]).astype(BF)
        wq, wk, wv, wo = weights[layer]
        q = (mm(normed[reach:], wq) + widen(shift_rows[1:2])).astype(BF)
        k = mm(normed, wk).astype(BF)
        v = (mm(normed, wv) + widen(shift_rows[2:3])).astype(BF)
        att = attend(q, k, v, bias)
        resid = current.astype(F32) + mm(att, wo[:, :D]) + shift_rows[3]
        n2, inv2 = norm_parts(resid)
        second = (n2 * gain[1] + shift_rows[4]).astype(BF)
        total, second_all, active, slope = mlp_forward(
            second, up_w[layer], down_w[layer], ffb[layer][None]
        )
        out = resid + total + shift_rows[5]
        low = out.astype(BF)
        produced.append(low)
        kept.append((wide, normed, q, k, v, att, resid, second_all, slope, active))
        current = low

    upstream = own_cot.astype(F32)
    derived = [None, None]
    parts = [None, None]
    mlp_sums = [None, None]
    for layer in (1, 0):
        wide, normed, q, k, v, att, resid, second_all, slope, active = kept[layer]
        gain = gains[layer]
        up_b = upstream.astype(BF)
        d_second, up_all, dz_b, ffb_g = mlp_backward(up_b, up_w[layer], down_w[layer], slope)
        down_g = mm_tn(flat(active), flat(up_all))
        up_g = mm_tn(flat(second_all), flat(dz_b))
        n2, inv2 = norm_parts(resid)
        d_resid = upstream + norm_back(d_second, gain[1], n2, inv2)
        c = d_resid.astype(BF)
        wq, wk, wv, wo = weights[layer]
        d_att = widen(mm_nt(c, wo[:, :D]).astype(BF))
        dq, dk, dv = attend_back(q, k, v, d_att, bias_t)
        da_wide = mm_nt(dk, wk) + mm_nt(dv, wv)
        da_own = da_wide[reach:] + mm_nt(dq, wq)
        da_halo = da_wide[:reach]
        n1, inv1 = norm_parts(wide)
        if layer == 1 or not fits:
            da = da_own + return_halo(da_halo, chunks, rows)
            derived[layer] = d_resid + norm_back(da, gain[0], n1[reach:], inv1[reach:])
            upstream_next = derived[layer].astype(BF).astype(F32)
        vectors = jnp.stack(
            [
                jnp.sum(da_halo * n1[:reach], axis=0) + jnp.sum(da_own * n1[reach:], axis=0),
                jnp.sum(d_second * n2, axis=0),
                jnp.sum(da_halo, axis=0) + jnp.sum(da_own, axis=0),
                jnp.sum(dq.astype(F32), axis=0)[:D],
                jnp.sum(dv.astype(F32), axis=0)[:D],
                jnp.sum(d_resid, axis=0),
                jnp.sum(d_second, axis=0),
                jnp.sum(upstream, axis=0),
            ]
        )
        ffb_block = lax.dynamic_update_slice(
            jnp.zeros((D, per_row), F32), ffb_g.reshape(shard, per_row), (f * shard, 0)
        )
        extra = jnp.pad(
            jnp.concatenate([vectors.T, ffb_block], axis=1),
            ((0, 0), (D, WIDE - D - 8 - per_row)),
        )
        pieces = (
            mm_tn(normed[reach:], dq).astype(BF),
            mm_tn(normed, dk).astype(BF),
            mm_tn(normed, dv).astype(BF),
            (mm_tn(att, widen(c)) + extra).astype(BF),
        )
        parts[layer] = pieces
        up_g = lax.all_to_all(
            up_g.astype(BF).reshape(nf, shard, ff_here), "fsdp",
            split_axis=0, concat_axis=0, tiled=True,
        ).reshape(nf * shard * ff_here // D, D)
        down_g = down_g.astype(BF)
        if layer == 0:
            down_g, up_g, _ = lax.optimization_barrier((down_g, up_g, dq))
        halves = halves_pair(down_g, up_g)
        if layer == 1:
            _, upstream_next = lax.optimization_barrier((halves, upstream_next))
        else:
            halves, mlp_sums[1] = lax.optimization_barrier((halves, mlp_sums[1]))
        mlp_sums[layer] = lax.psum(halves, "ctx")
        if layer == 1:
            upstream = upstream_next

    if fits:
        qkv_g, out_g, down_one, up_one, late = reduce_both(
            parts[0], parts[1], mlp_sums[1], da_halo.astype(BF)
        )
        da = da_own + late.astype(F32)
        derived[0] = d_resid + norm_back(da, gain[0], n1[reach:], inv1[reach:])
        far = lax.ppermute(mlp_sums[0], "section", [(1, 0)])
        down_zero, up_zero = split_up(jnp.concatenate([mlp_sums[0], far], axis=1), nf, shard)
        grad_down = pick(s, down_zero, down_one).astype(F32)
        grad_up = pick(s, up_zero, up_one).astype(F32)
        qkv_g, out_g = qkv_g.astype(F32), out_g.astype(F32)
    else:
        a_tot = pick(s, reduce_plain(parts[0]), reduce_plain(parts[1])).astype(F32)
        qkv_g = jnp.concatenate([a_tot[i, :, :D] for i in range(3)], axis=1)
        out_g = a_tot[3]
        grad_down, grad_up = split_up(halves_settle(*mlp_sums), nf, shard)
    vectors = out_g[:, D : D + 8].T
    return (
        both_micros(produced, s),
        both_micros(derived, s),
        qkv_g[None],
        out_g[None, :, :D],
        grad_up[None],
        grad_down[None],
        vectors[None, :2],
        vectors[None, 2:],
        out_g[:, D + 8 : D + 8 + per_row].reshape(1, ff_here),
    )


def split_up(both, nf, shard):
    up = both[1].reshape(nf, shard, -1)
    return both[0], up.transpose(1, 0, 2).reshape(shard, -1)


def both_micros(layers, s):
    to_zero = lax.ppermute(layers[0], "section", [(1, 0)])
    to_one = lax.ppermute(layers[1], "section", [(0, 1)])
    out = jnp.stack([pick(s, layers[0], to_one), pick(s, to_zero, layers[1])])
    return out[None, :, None]


def solution(mesh):
    return jax.shard_map(
        on_device,
        mesh=mesh,
        in_specs=(
            P(None, "fsdp", "ctx", None),
            P(None, "fsdp", None),
            P(None, "fsdp", "ctx", None),
            P("section", "fsdp", None),
            P("section", "fsdp", None),
            P("section", "fsdp", None),
            P("section", "fsdp", None),
            P("section", None, "fsdp"),
            P("section", None, "fsdp"),
            P("section", "fsdp"),
        ),
        out_specs=(
            P("section", None, "fsdp", "ctx", None),
            P("section", None, "fsdp", "ctx", None),
            P("section", "fsdp", None),
            P("section", "fsdp", None),
            P("section", "fsdp", None),
            P("section", "fsdp", None),
            P("section", None, "fsdp"),
            P("section", None, "fsdp"),
            P("section", "fsdp"),
        ),
        check_vma=False,
    )
```

time: 1080 us -> 915 us (0.85)
  waiting for transfers between devices: 366 us -> 30.5 us
  Pallas kernels: 187 us -> 493 us
  matrix products: 241 us -> 100 us
  local copies, waits for them, and re-layouts: 129 us -> 143 us
    pallas_call x8 -> x10, Pallas kernels: 187 us -> 493 us  [the longest x4 195 us: plane_call(): pl.pallas_call(kernel, out_shape=outs, in_specs=[VSPEC] * len(operands),...]
    psum x1 -> x2, waiting for transfers between devices: 250 us -> 0.01 us  [on_device(): mlp_sums[layer] = lax.psum(halves, 'ctx')]
    all_to_all x3, waiting for transfers between devices: 76.1 us -> 13.8 us  [the longest x1 10.9 us: on_device(): lax.all_to_all(up_shard.reshape(shard, nf, ff_here), 'fsdp', split_axis=1...]
    dot_general x10 -> x0, matrix products: 55.7 us -> none  [the longest x2 19.5 us: attention_back(): d_prob = jnp.einsum('qhd,khd->hqk', gh, vh, preferred_element_type=F32)]
    dot_general x12 -> x8, matrix products: 53.2 us -> 14.7 us  [mm(): return jnp.dot(a, b, preferred_element_type=F32)]
    unnamed x186 -> x248, local copies, waits for them, and re-layouts: 26.8 us -> 54.7 us
    dot_general x12 -> x8, matrix products: 58.4 us -> 32.5 us  [mm_nt(): lax.dot_general(a, b, (((1,), (1,)), ((), ())), preferred_element_type=F32)]
    reduce_sum x2 -> x0, matrix products: 24.9 us -> none  [attention(): jnp.sum(jnp.where(allowed, jnp.exp(scores), 0.0), axis=-1, keepdims=True)]
  transfers between devices with their start and end apart: 34 -> 20, of which waited for: 13 -> 6; matrix products, arithmetic and copies ran while one was open for 32% -> 25% of each run, Pallas kernels for 12% -> 43%
where the time goes in v3:
time: 915 us; the launch traced here: 904 us
  Pallas kernels  493 us (54%)
  local copies, waits for them, and re-layouts  143 us (16%)
  matrix products  100 us (11%)
  other arithmetic  84.4 us (9%)
  starting transfers between devices  36.9 us (4%)
  waiting for transfers between devices  30.5 us (3%)
  between operations  15.9 us (2%)
    pallas_call x4, Pallas kernels, plane_call(): pl.pallas_call(kernel, out_shape=outs, in_specs=[VSPEC] * len(operands),...  195 us
    pallas_call x1, Pallas kernels, reduce_both(): pl.pallas_call(reduce_kernel, out_shape=tuple((jax.ShapeDtypeStruct(shape...  188 us
    unnamed x248, local copies, waits for them, and re-layouts  54.7 us
    dot_general x12, matrix products, mm_tn(): lax.dot_general(a, b, (((0,), (0,)), ((), ())), preferred_element_type=F32)  52.8 us
    pallas_call x1, Pallas kernels, first_weights(): pl.pallas_call(weights_kernel, out_shape=(jax.ShapeDtypeStruct((4, D, WID...  52.6 us
    pallas_call x2, Pallas kernels, attend_back(): pl.pallas_call(attend_back_kernel, out_shape=(jax.ShapeDtypeStruct((rows,...  36.5 us
    dot_general x8, matrix products, mm_nt(): lax.dot_general(a, b, (((1,), (1,)), ((), ())), preferred_element_type=F32)  32.5 us
    pallas_call x2, Pallas kernels, attend(): pl.pallas_call(attend_kernel, out_shape=jax.ShapeDtypeStruct((rows, D), B...  20.2 us
  transfers between devices with their start and end apart: 20, of which 6 were waited for; matrix products, arithmetic and copies ran while one was open for 25% of the time, Pallas kernels for 43%

profile of v3, /device:TPU:0, one launch (start us, length us, event | category | flops | bytes accessed | tf_op | source)
XLA Modules:
  0.0 903.8 jit_solution(6187296839726548515)
XLA Ops:
  19.9 52.6 %first_weights.1 = (bf16[4,1088,1152]{2,1,0:T(8,128)(2,1)S(1)}, bf16[768,1088]{1,0:T(8,128)(2,1)S(1)}) custom-call(bf16[4,272,1152]{2,1,0:T(8,128)(2,1)S(1)} %pad_maximum_fusion.own, bf16[256,1088]{1,0:T(8,128)(2,1)S(1)} %bitcast.187), custom_call_target="tpu_custom_call" | custom-call | bytes 175000000 | tf_op jit(solution)/shard_map/first_weights/pallas_call | solution.py:384
  73.7 3.8 copy-done.25
  79.5 3.1 collective-permute-done.4
  85.8 5.4 reshape.248
  92.9 5.0 all-to-all-start
  113.0 10.2 %attend.2 = bf16[256,1088]{1,0:T(8,128)(2,1)S(1)} custom-call(bf16[256,1152]{1,0:T(8,128)(2,1)S(1)} %fusion.18.q_ref, bf16[768,1152]{1,0:T(8,128)(2,1)S(1)} %convolution_convert_fusion.7.k_ref, bf16[768,1152]{1,0:T(8,128)(2,1)S(1)} %fusion.14.v_ref, f32[256,768]{1,0:T(8,128)S(1)} %fusion.59.bias_ref), custom_call_target="tpu_custom_call" | custom-call | bytes 42000000 | tf_op jit(solution)/shard_map/attend/pallas_call | solution.py:788
  124.7 10.9 %all-to-all-done = bf16[272,4,1088]{2,0,1:T(8,128)(2,1)} async-done(((bf16[272,4,1088]{2,0,1:T(8,128)(2,1)}), bf16[272,4,1088]{2,0,1:T(8,128)(2,1)}, u32[]{:S(2)}, u32[]{:S(2)}) %all-to-all-start) | async-done | bytes 2367520 | tf_op jit(solution)/shard_map/all_to_all | solution.py:912
  136.3 5.3 broadcast_select_fusion
  143.4 4.4 broadcast_select_fusion.1
  147.8 63.4 %shard_map.169 = (f32[256,1088]{1,0:T(8,128)S(1)}, bf16[4,256,1088]{2,1,0:T(8,128)(2,1)S(1)}, bf16[4,256,1088]{2,1,0:T(8,128)(2,1)S(1)}, f32[4,256,1088]{2,1,0:T(8,128)}) custom-call(bf16[256,1088]{1,0:T(8,128)(2,1)S(1)} %add_convert_fusion.5.own, bf16[1088,1088]{1,0:T(8,128)(2,1)S(1)} %get-tuple-element.164.up, ...), custom_call_target="tpu_custom_call" | custom-call | bytes 140000000 | tf_op jit(solution)/shard_map/pallas_call | solution.py:168
  215.2 4.2 collective-permute-start.2
  220.7 9.1 %collective-permute-done.2 = bf16[256,1088]{0,1:T(8,128)(2,1)} collective-permute-done((bf16[256,1088]{0,1:T(8,128)(2,1)}, bf16[256,1088]{0,1:T(8,128)(2,1)}, u32[]{:S(2)}, u32[]{:S(2)}) %collective-permute-start.2) | collective-permute-done | bytes 557088 | tf_op jit(solution)/shard_map/ppermute | solution.py:733
  229.8 5.3 collective-permute-start.3
  254.2 3.1 fusion.10
  263.6 10.0 %attend.3 = bf16[256,1088]{1,0:T(8,128)(2,1)S(1)} custom-call(bf16[256,1152]{1,0:T(8,128)(2,1)S(1)} %fusion.19.q_ref, bf16[768,1152]{1,0:T(8,128)(2,1)S(1)} %convolution_convert_fusion.6.k_ref, bf16[768,1152]{1,0:T(8,128)(2,1)S(1)} %fusion.15.v_ref, f32[256,768]{1,0:T(8,128)S(1)} %copy-done.21), custom_call_target="tpu_custom_call" | custom-call | bytes 42000000 | tf_op jit(solution)/shard_map/attend/pallas_call | solution.py:788
  283.4 42.9 %shard_map.170 = (f32[256,1088]{1,0:T(8,128)S(1)}, bf16[4,256,1088]{2,1,0:T(8,128)(2,1)S(1)}, bf16[4,256,1088]{2,1,0:T(8,128)(2,1)S(1)}, f32[4,256,1088]{2,1,0:T(8,128)}) custom-call(bf16[256,1088]{1,0:T(8,128)(2,1)S(1)} %add_convert_fusion.3.own, bf16[1088,1088]{1,0:T(8,128)(2,1)S(1)} %copy-done.6, bf16[1088,1088]{1,0:T(8,128)(2,1)S(1)} %copy-done.4, ...), custom_call_target="tpu_custom_call" | custom-call | bytes 140000000 | tf_op jit(solution)/shard_map/pallas_call | solution.py:168
  337.9 42.3 %shard_map.171 = (f32[256,1088]{1,0:T(8,128)S(1)}, bf16[4,256,1088]{2,1,0:T(8,128)(2,1)S(1)}, bf16[4,256,1088]{2,1,0:T(8,128)(2,1)S(1)}, f32[1,1088]{1,0:T(1,128)S(1)}) custom-call(bf16[256,1088]{1,0:T(8,128)(2,1)S(1)} %bitcast.184, bf16[1088,1088]{1,0:T(8,128)(2,1)S(1)} %copy-done.7, bf16[1088,1088]{1,0:T(8,128)(2,1)S(1)} %copy-done.5, ...), custom_call_target="tpu_custom_call" | custom-call | bytes 140000000 | tf_op jit(solution)/shard_map/pallas_call | solution.py:168
  384.2 3.5 convolution_convert_fusion.9
  395.0 18.3 %attend_back.2 = (bf16[256,1152]{1,0:T(8,128)(2,1)S(1)}, bf16[768,1152]{1,0:T(8,128)(2,1)S(1)}, bf16[768,1152]{1,0:T(8,128)(2,1)S(1)}) custom-call(bf16[256,1152]{1,0:T(8,128)(2,1)S(1)} %copy-done.31, bf16[768,1152]{1,0:T(8,128)(2,1)S(1)} %copy-done.15, bf16[768,1152]{1,0:T(8,128)(2,1)S(1)} %copy-done.17, bf16[256,1152]{1,0:T(8,128)(2,1)S(1)} %pad.55.g_ref, ...), custom_call_target="tpu_custom_call" | custom-call | bytes 77000000 | tf_op jit(solution)/shard_map/attend_back/pallas_call | solution.py:830
  413.3 3.9 convolution_convert_fusion.3.k1
  426.9 7.0 fusion.1
  433.9 4.6 all-to-all-start.1
  438.7 7.1 fusion
  459.2 5.9 convolution_convert_fusion.2.v1
  472.0 4.7 multiply_reduce_fusion.2
  476.7 3.6 fusion.25
  480.3 3.1 convert_convert_fusion
  486.1 3.8 collective-permute-start.11
  495.7 3.6 fusion.5.o1
  502.0 4.5 fusion.7
  509.6 46.7 %shard_map.172 = (f32[256,1088]{1,0:T(8,128)S(1)}, bf16[4,256,1088]{2,1,0:T(8,128)(2,1)S(1)}, bf16[4,256,1088]{2,1,0:T(8,128)(2,1)S(1)}, f32[1,1088]{1,0:T(1,128)S(1)}) custom-call(bf16[256,1088]{1,0:T(8,128)(2,1)S(1)} %convert_element_type.246.own, bf16[1088,1088]{1,0:T(8,128)(2,1)S(1)} %copy-done.3, bf16[1088,1088]{1,0:T(8,128)(2,1)S(1)} %get-tuple-element.162.down, ...), custom_call_target="tpu_custom_call" | custom-call | bytes 140000000 | tf_op jit(solution)/shard_map/pallas_call | solution.py:168
  568.8 18.3 %attend_back.3 = (bf16[256,1152]{1,0:T(8,128)(2,1)S(1)}, bf16[768,1152]{1,0:T(8,128)(2,1)S(1)}, bf16[768,1152]{1,0:T(8,128)(2,1)S(1)}) custom-call(bf16[256,1152]{1,0:T(8,128)(2,1)S(1)} %copy-done.29, bf16[768,1152]{1,0:T(8,128)(2,1)S(1)} %copy-done.11, bf16[768,1152]{1,0:T(8,128)(2,1)S(1)} %copy-done.13, bf16[256,1152]{1,0:T(8,128)(2,1)S(1)} %pad.56.g_ref, ...), custom_call_target="tpu_custom_call" | custom-call | bytes 77000000 | tf_op jit(solution)/shard_map/attend_back/pallas_call | solution.py:830
  587.1 7.3 fusion.33
  594.5 4.6 fusion.3
  599.1 4.7 all-to-all-start.2
  603.8 5.1 convolution_add_fusion.2
  613.3 3.2 slice_reduce_fusion.13
  616.4 3.1 copy.206
  619.5 4.8 fusion.73
  624.4 4.6 fusion.2
  631.9 3.6 fusion.21
  655.6 3.6 fusion.4.o0
  661.6 3.9 convolution_convert_fusion.5.k0
  665.4 3.9 convolution_convert_fusion.4.v0
  669.4 4.2 fusion.6
  673.6 188.1 %reduce_both.1 = (bf16[272,3264]{1,0:T(8,128)(2,1)}, bf16[272,1152]{1,0:T(8,128)(2,1)}, bf16[1088,1088]{1,0:T(8,128)(2,1)}, bf16[272,4352]{1,0:T(8,128)(2,1)}, bf16[256,1088]{1,0:T(8,128)(2,1)}) custom-call(bf16[1088,1152]{1,0:T(8,128)(2,1)} %convolution_convert_fusion.1.q0, bf16[1088,1152]{1,0:T(8,128)(2,1)} %convolution_convert_fusion.5.k0, ...), custom_call_target="tpu_custom_call" | custom-call | bytes 420000000 | tf_op jit(solution)/shard_map/reduce_both/pallas_call | solution.py:684
  887.0 2.9 reshape.257
  889.9 4.5 fusion.30
  (450 shorter events, 216.6 us)
Async XLA Ops:
  7.2 243.3 %all-gather.2.cloned.1.call-start = ((), (), s32[]{:S(2)}) async-start(), calls=%async_computation.3 | async-start | bytes 11280384 | tf_op jit(solution)/shard_map/all_gather | solution.py:906
  79.4 3.1 collective-permute-start.4
  92.9 13.3 %slice-start = ((s8[10027008]{0:T(1024)(128)(4,1)}), s8[1638400]{0:T(1024)(128)(4,1)S(1)}, s32[]{:S(2)}) async-start(s8[10027008]{0:T(1024)(128)(4,1)} %bitcast.185), calls=%async_computation.6 | async-start | bytes 3276800
  92.9 42.7 %all-to-all-start = ((bf16[272,4,1088]{2,0,1:T(8,128)(2,1)}), bf16[272,4,1088]{2,0,1:T(8,128)(2,1)}, u32[]{:S(2)}, u32[]{:S(2)}) async-start(bf16[272,4,1088]{2,0,1:T(8,128)(2,1)} %copy.146), calls=%async_computation | async-start | bytes 5013504 | tf_op jit(solution)/shard_map/all_to_all | solution.py:912
  97.9 38.4 %collective-permute-start.1 = (bf16[1088,1088]{1,0:T(8,128)(2,1)}, bf16[1088,1088]{1,0:T(8,128)(2,1)}, u32[]{:S(2)}, u32[]{:S(2)}) collective-permute-start(bf16[1088,1088]{1,0:T(8,128)(2,1)} %bitcast.196), channel_id=1, source_target_pairs={{0,16},{16,0},{1,17},{17,1},{2,18},{18,2},{3,19},{19,3},{4,20},{20... | collective-permute-start | bytes 7102472 | tf_op jit(solution)/shard_map/ppermute | solution.py:757
  98.1 8.0 slice-start.1
  100.2 24.4 %copy-start.89 = (bf16[1088,1152]{1,0:T(8,128)(2,1)}, bf16[1088,1152]{1,0:T(8,128)(2,1)S(1)}, u32[]{:S(2)}) copy-start(bf16[1088,1152]{1,0:T(8,128)(2,1)S(1)} %slice_bitcast_fusion.1) | copy-start | bytes 7520260
  113.0 10.2 %copy-start.28 = (bf16[256,1152]{1,0:T(8,128)(2,1)}, bf16[256,1152]{1,0:T(8,128)(2,1)S(1)}, u32[]{:S(2)}) copy-start(bf16[256,1152]{1,0:T(8,128)(2,1)S(1)} %fusion.18.q_ref) | copy-start | bytes 1769476
  124.3 12.0 %copy-start.54 = (f32[256,1088]{1,0:T(8,128)}, f32[256,1088]{1,0:T(8,128)S(1)}, u32[]{:S(2)}) copy-start(f32[256,1088]{1,0:T(8,128)S(1)} %get-tuple-element.196) | copy-start | bytes 3342340
  135.6 7.8 collective-permute-start
  147.8 63.4 %copy-start.2 = (bf16[1088,1088]{1,0:T(8,128)(2,1)}, bf16[1088,1088]{1,0:T(8,128)(2,1)S(1)}, u32[]{:S(2)}) copy-start(bf16[1088,1088]{1,0:T(8,128)(2,1)S(1)} %get-tuple-element.164.up) | copy-start | bytes 7102468
  147.8 66.2 %copy-start.55 = (f32[256,1088]{1,0:T(8,128)S(1)}, f32[256,1088]{1,0:T(8,128)}, u32[]{:S(2)}) copy-start(f32[256,1088]{1,0:T(8,128)} %copy-done.54) | copy-start | bytes 3342340
  214.2 25.5 %copy-start.62 = (bf16[256,1088]{1,0:T(8,128)(2,1)}, bf16[256,1088]{1,0:T(8,128)(2,1)S(1)}, u32[]{:S(2)}) copy-start(bf16[256,1088]{1,0:T(8,128)(2,1)S(1)} %add_convert_fusion.4) | copy-start | bytes 1671172
  215.2 14.6 %collective-permute-start.2 = (bf16[256,1088]{0,1:T(8,128)(2,1)}, bf16[256,1088]{0,1:T(8,128)(2,1)}, u32[]{:S(2)}, u32[]{:S(2)}) collective-permute-start(bf16[256,1088]{0,1:T(8,128)(2,1)} %copy.147), channel_id=1, source_target_pairs={{0,1},{1,2},{2,3},{4,5},{5,6},{6,7},{8,9},{9,10},{10,11},{12,13},{... | collective-permute-start | bytes 1671176 | tf_op jit(solution)/shard_map/ppermute | solution.py:733
  219.4 23.0 %collective-permute-start.6 = (bf16[256,1088]{0,1:T(8,128)(2,1)}, bf16[256,1088]{0,1:T(8,128)(2,1)}, u32[]{:S(2)}, u32[]{:S(2)}) collective-permute-start(bf16[256,1088]{0,1:T(8,128)(2,1)} %copy.147), channel_id=1, source_target_pairs={{16,0},{17,1},{18,2},{19,3},{20,4},{21,5},{22,6},{23,7},{24,8},{25... | collective-permute-start | bytes 1671176 | tf_op jit(solution)/shard_map/ppermute | solution.py:1056
  229.8 14.7 %collective-permute-start.3 = (bf16[256,1088]{0,1:T(8,128)(2,1)}, bf16[256,1088]{0,1:T(8,128)(2,1)}, u32[]{:S(2)}, u32[]{:S(2)}) collective-permute-start(bf16[256,1088]{0,1:T(8,128)(2,1)} %collective-permute-done.2), channel_id=1, source_target_pairs={{0,1},{1,2},{2,3},{4,5},{5,6},{6,7},{8,9},{9,10},{10,11},{12,13},{... | collective-permute-start | bytes 1671176 | tf_op jit(solution)/shard_map/ppermute | solution.py:733
  240.0 151.0 %copy-start.18 = (f32[768,256]{1,0:T(8,128)}, f32[768,256]{1,0:T(8,128)S(1)}, u32[]{:S(2)}) copy-start(f32[768,256]{1,0:T(8,128)S(1)} %fusion.61.bias_ref) | copy-start | bytes 2359300
  263.6 10.0 %copy-start.16 = (bf16[768,1152]{1,0:T(8,128)(2,1)}, bf16[768,1152]{1,0:T(8,128)(2,1)S(1)}, u32[]{:S(2)}) copy-start(bf16[768,1152]{1,0:T(8,128)(2,1)S(1)} %fusion.15.v_ref) | copy-start | bytes 5308420
  283.4 42.9 %copy-start.58 = (f32[256,1088]{1,0:T(8,128)S(1)}, f32[256,1088]{1,0:T(8,128)}, u32[]{:S(2)}) copy-start(f32[256,1088]{1,0:T(8,128)} %copy-done.57) | copy-start | bytes 3342340
  283.4 42.9 %copy-start.93 = (bf16[256,1088]{1,0:T(8,128)(2,1)S(1)}, bf16[256,1088]{1,0:T(8,128)(2,1)}, u32[]{:S(2)}) copy-start(bf16[256,1088]{1,0:T(8,128)(2,1)} %copy.156) | copy-start | bytes 1671172
  330.9 134.2 %collective-permute-start.5 = (bf16[256,1088]{0,1:T(8,128)(2,1)}, bf16[256,1088]{0,1:T(8,128)(2,1)}, u32[]{:S(2)}, u32[]{:S(2)}) collective-permute-start(bf16[256,1088]{0,1:T(8,128)(2,1)} %copy.153), channel_id=1, source_target_pairs={{0,16},{1,17},{2,18},{3,19},{4,20},{5,21},{6,22},{7,23},{8,24},{9,... | collective-permute-start | bytes 1671176 | tf_op jit(solution)/shard_map/ppermute | solution.py:1057
  337.9 42.4 %copy-start.59 = (f32[256,1088]{1,0:T(8,128)S(1)}, f32[256,1088]{1,0:T(8,128)}, u32[]{:S(2)}) copy-start(f32[256,1088]{1,0:T(8,128)} %copy-done.57) | copy-start | bytes 3342340
  395.0 18.3 %copy-start.87 = (bf16[768,1088]{1,0:T(8,128)(2,1)S(1)}, bf16[768,1088]{1,0:T(8,128)(2,1)}, u32[]{:S(2)}) copy-start(bf16[768,1088]{1,0:T(8,128)(2,1)} %copy-done.86) | copy-start | bytes 5013508
  395.0 22.2 %slice-start.3 = ((s8[10027008]{0:T(1024)(128)(4,1)}), s8[4194304]{0:T(1024)(128)(4,1)S(1)}, s32[]{:S(2)}) async-start(s8[10027008]{0:T(1024)(128)(4,1)} %bitcast.214), calls=%async_computation.9 | async-start | bytes 8388608
  425.6 24.6 %collective-permute-start.8 = (bf16[256,1088]{0,1:T(8,128)(2,1)}, bf16[256,1088]{0,1:T(8,128)(2,1)}, u32[]{:S(2)}, u32[]{:S(2)}) collective-permute-start(bf16[256,1088]{0,1:T(8,128)(2,1)} %copy.166), channel_id=1, source_target_pairs={{1,0},{2,1},{3,2},{5,4},{6,5},{7,6},{9,8},{10,9},{11,10},{13,12},{... | collective-permute-start | bytes 1671176 | tf_op jit(solution)/shard_map/ppermute | solution.py:733
  433.9 42.8 %all-to-all-start.1 = ((bf16[4,272,1088]{2,1,0:T(8,128)(2,1)}), bf16[4,272,1088]{2,1,0:T(8,128)(2,1)}, u32[]{:S(2)}, u32[]{:S(2)}) async-start(bf16[4,272,1088]{2,1,0:T(8,128)(2,1)} %bitcast.198), calls=%async_computation.1 | async-start | bytes 5013504 | tf_op jit(solution)/shard_map/all_to_all | solution.py:1004
  438.4 235.1 %all-reduce.16.cloned.1.call-start = ((), (), s32[]{:S(2)}) async-start(), calls=%async_computation.4 | async-start | bytes 5013504 | tf_op jit(solution)/shard_map/psum | solution.py:1016
  438.7 7.1 copy-start.65
  457.2 12.7 %collective-permute-start.9 = (bf16[256,1088]{0,1:T(8,128)(2,1)}, bf16[256,1088]{0,1:T(8,128)(2,1)}, u32[]{:S(2)}, u32[]{:S(2)}) collective-permute-start(bf16[256,1088]{0,1:T(8,128)(2,1)} %copy.168), channel_id=1, source_target_pairs={{1,0},{2,1},{3,2},{5,4},{6,5},{7,6},{9,8},{10,9},{11,10},{13,12},{... | collective-permute-start | bytes 1671176 | tf_op jit(solution)/shard_map/ppermute | solution.py:733
  480.3 21.7 %collective-permute-start.7 = (bf16[2,544,1088]{2,1,0:T(8,128)(2,1)}, bf16[2,544,1088]{2,1,0:T(8,128)(2,1)}, u32[]{:S(2)}, u32[]{:S(2)}) collective-permute-start(bf16[2,544,1088]{2,1,0:T(8,128)(2,1)} %fusion.25), channel_id=1, source_target_pairs={{0,16},{16,0},{1,17},{17,1},{2,18},{18,2},{3,19},{19,3},{4,20},{20... | collective-permute-start | bytes 7102472 | tf_op jit(solution)/shard_map/ppermute | solution.py:757
  486.1 13.3 %collective-permute-start.11 = (f32[256,1088]{0,1:T(8,128)}, f32[256,1088]{0,1:T(8,128)}, u32[]{:S(2)}, u32[]{:S(2)}) collective-permute-start(f32[256,1088]{0,1:T(8,128)} %copy.182), channel_id=1, source_target_pairs={{0,16},{1,17},{2,18},{3,19},{4,20},{5,21},{6,22},{7,23},{8,24},{9,... | collective-permute-start | bytes 3342344 | tf_op jit(solution)/shard_map/ppermute | solution.py:1057
  509.6 46.8 %copy-start.56 = (f32[256,1088]{1,0:T(8,128)S(1)}, f32[256,1088]{1,0:T(8,128)}, u32[]{:S(2)}) copy-start(f32[256,1088]{1,0:T(8,128)} %copy-done.54) | copy-start | bytes 3342340
  587.1 7.4 copy-start.23
  587.1 7.4 copy-start.32
  587.1 7.4 copy-start.52
  587.1 7.4 copy-start.43
  587.1 7.4 copy-start.51
  599.1 32.8 %all-to-all-start.2 = ((bf16[4,272,1088]{2,1,0:T(8,128)(2,1)}), bf16[4,272,1088]{2,1,0:T(8,128)(2,1)}, u32[]{:S(2)}, u32[]{:S(2)}) async-start(bf16[4,272,1088]{2,1,0:T(8,128)(2,1)} %bitcast.199), calls=%async_computation.2 | async-start | bytes 5013504 | tf_op jit(solution)/shard_map/all_to_all | solution.py:1004
  603.7 265.5 %all-reduce.18.cloned.1.call-start = ((), (), s32[]{:S(2)}) async-start(), calls=%async_computation.5 | async-start | bytes 5013504 | tf_op jit(solution)/shard_map/psum | solution.py:1016
  635.5 33.9 %collective-permute-start.10 = (bf16[2,544,1088]{2,1,0:T(8,128)(2,1)}, bf16[2,544,1088]{2,1,0:T(8,128)(2,1)}, u32[]{:S(2)}, u32[]{:S(2)}) collective-permute-start(bf16[2,544,1088]{2,1,0:T(8,128)(2,1)} %fusion.21), channel_id=1, source_target_pairs={{0,16},{16,0},{1,17},{17,1},{2,18},{18,2},{3,19},{19,3},{4,20},{20... | collective-permute-start | bytes 7102472 | tf_op jit(solution)/shard_map/ppermute | solution.py:757
  638.2 17.4 %copy-start.37 = (bf16[256,1088]{1,0:T(8,128)(2,1)S(1)}, bf16[256,1088]{1,0:T(8,128)(2,1)}, u32[]{:S(2)}) copy-start(bf16[256,1088]{1,0:T(8,128)(2,1)} %copy-done.36) | copy-start | bytes 1671172
  638.2 17.4 %copy-start.102 = (bf16[256,1088]{1,0:T(8,128)(2,1)S(1)}, bf16[256,1088]{1,0:T(8,128)(2,1)}, u32[]{:S(2)}) copy-start(bf16[256,1088]{1,0:T(8,128)(2,1)} %copy-done.101) | copy-start | bytes 1671172
  638.8 9.2 %copy-start.105 = (f32[1088]{0:T(1024)S(1)}, f32[1088]{0:T(1024)}, u32[]{:S(2)}) copy-start(f32[1088]{0:T(1024)} %get-tuple-element.136) | copy-start | bytes 13060
  673.6 188.2 %copy-start.61 = (f32[768,1088]{1,0:T(8,128)S(1)}, f32[768,1088]{1,0:T(8,128)}, u32[]{:S(2)}) copy-start(f32[768,1088]{1,0:T(8,128)} %get-tuple-element.173) | copy-start | bytes 10027012
  673.6 188.2 %copy-start.70 = (f32[256,1088]{1,0:T(8,128)S(1)}, f32[256,1088]{1,0:T(8,128)}, u32[]{:S(2)}) copy-start(f32[256,1088]{1,0:T(8,128)} %get-tuple-element.200) | copy-start | bytes 3342340
  673.6 188.2 %copy-start.104 = (f32[1088]{0:T(1024)S(1)}, f32[1088]{0:T(1024)}, u32[]{:S(2)}) copy-start(f32[1088]{0:T(1024)} %copy-done.103) | copy-start | bytes 13060
  866.6 9.2 %collective-permute-start.12 = (f32[256,1088]{0,1:T(8,128)}, f32[256,1088]{0,1:T(8,128)}, u32[]{:S(2)}, u32[]{:S(2)}) collective-permute-start(f32[256,1088]{0,1:T(8,128)} %copy.184), channel_id=1, source_target_pairs={{16,0},{17,1},{18,2},{19,3},{20,4},{21,5},{22,6},{23,7},{24,8},{25... | collective-permute-start | bytes 3342344 | tf_op jit(solution)/shard_map/ppermute | solution.py:1056
  869.2 12.5 %collective-permute-start.13 = (bf16[2,544,1088]{2,1,0:T(8,128)(2,1)}, bf16[2,544,1088]{2,1,0:T(8,128)(2,1)}, u32[]{:S(2)}, u32[]{:S(2)}) collective-permute-start(bf16[2,544,1088]{2,1,0:T(8,128)(2,1)} %all-reduce.18.cloned.1.call-done), channel_id=1, source_target_pairs={{16,0},{17,1},{18,2},{19,3},{20,4},{21,5},{22,6},{23,7},{24,8},{25... | collective-permute-start | bytes 7102472 | tf_op jit(solution)/shard_map/ppermute | solution.py:1026
  (91 other events, 270.7 us)
Sparse Core Ops, SparseCore 0:
  85.9 96.4 all-gather.1
  506.6 103.2 all-reduce.15
  673.7 150.1 all-reduce.17

commit v4 on v3

--- a/solution.py
+++ b/solution.py
@@ -74,7 +74,7 @@
     )
 
 
-def exchange_rows(own_ref, all_ref, parts, compute, total_ref, bufs, send, recv):
+def exchange_rows(own_ref, all_ref, parts, compute, finish, bufs, send, recv):
     x1, y1, x2, y2, sum_x, sum_y = bufs
     xn, yn = plane_neighbours()
     half = own_ref.shape[0] // 2
@@ -117,21 +117,21 @@
     rest_x.start()
     own_x.wait_recv()
     rest_y.wait_recv()
-    total_ref[top, :] = (
-        parts[0, top, :].astype(F32) + x2[top, :].astype(F32) + y2[top, :].astype(F32)
-    )
+    finish(top, parts[0, top, :].astype(F32) + x2[top, :].astype(F32) + y2[top, :].astype(F32))
     own_y.wait_recv()
     rest_x.wait_recv()
-    total_ref[low, :] = (
-        parts[0, low, :].astype(F32) + x2[low, :].astype(F32) + y2[low, :].astype(F32)
-    )
+    finish(low, parts[0, low, :].astype(F32) + x2[low, :].astype(F32) + y2[low, :].astype(F32))
     for copy in (to_x, to_y, far_x, far_y, first_x, first_y, own_x, own_y, rest_x, rest_y):
         copy.wait_send()
 
 
 def forward_kernel(
-    own, up, down, bias, total, all_ref, active, slope, parts, x1, y1, x2, y2, sx, sy, send, recv
+    own, up, down, bias, resid, par, out, all_ref, active, slope,
+    parts, x1, y1, x2, y2, sx, sy, send, recv,
 ):
+    def finish(at, value):
+        out[at, :] = (resid[at, :] + value + par[7:8, :]).astype(BF)
+
     def compute(r):
         z = mm(all_ref[r], up[...]) + bias[...]
         cdf, pdf = phi_parts(z)
@@ -139,13 +139,16 @@
         slope[r] = cdf + z * pdf
         parts[r] = mm(active[r], down[...]).astype(BF)
 
-    exchange_rows(own, all_ref, parts, compute, total, (x1, y1, x2, y2, sx, sy), send, recv)
+    exchange_rows(own, all_ref, parts, compute, finish, (x1, y1, x2, y2, sx, sy), send, recv)
 
 
 def backward_kernel(
     own, up, down, slope, total, all_ref, dz_all, bias_g, parts, x1, y1, x2, y2, sx, sy, send, recv
 ):
     bias_g[...] = jnp.zeros_like(bias_g)
+
+    def finish(at, value):
+        total[at, :] = value
 
     def compute(r):
         dz = mm_nt(all_ref[r], down[...]) * slope[r]
@@ -153,7 +156,7 @@
         dz_all[r] = dz.astype(BF)
         parts[r] = mm_nt(dz_all[r], up[...]).astype(BF)
 
-    exchange_rows(own, all_ref, parts, compute, total, (x1, y1, x2, y2, sx, sy), send, recv)
+    exchange_rows(own, all_ref, parts, compute, finish, (x1, y1, x2, y2, sx, sy), send, recv)
 
 
 VSPEC = pl.BlockSpec(memory_space=pltpu.VMEM)
@@ -188,7 +191,7 @@
     )(*operands)
 
 
-def mlp_forward(own, up, down, bias):
+def mlp_forward(own, up, down, bias, resid, par):
     rows = own.shape[0]
     if lax.axis_size("fsdp") != 4:
         every = lax.all_gather(own, "fsdp", axis=0, tiled=True)
@@ -197,17 +200,18 @@
         active = (z * cdf).astype(BF)
         part = mm(active, down).astype(BF)
         total = lax.psum_scatter(part, "fsdp", scatter_dimension=0, tiled=True).astype(F32)
-        return total, every, active, cdf + z * pdf
+        out = (resid + total + par[7]).astype(BF)
+        return out, every, active, cdf + z * pdf
     shape = (4, rows, D)
     return plane_call(
         forward_kernel, 1,
         (
-            jax.ShapeDtypeStruct((rows, D), F32),
+            jax.ShapeDtypeStruct((rows, D), BF),
             jax.ShapeDtypeStruct(shape, BF),
             jax.ShapeDtypeStruct(shape, BF),
             jax.ShapeDtypeStruct(shape, F32),
         ),
-        rows, own, up, down, bias,
+        rows, own, up, down, bias, resid, par,
     )
 
 
@@ -770,77 +774,201 @@
     return jnp.pad(values, ((0, 0), (0, WIDE - D)))
 
 
-def attend_kernel(q_ref, k_ref, v_ref, bias_ref, out_ref):
-    lanes = lax.broadcasted_iota(jnp.int32, q_ref.shape, 1)
-    q = q_ref[...] * jnp.asarray(SCALE, BF)
+TAIL = 1024
+
+
+def scores_forward(q, k, v, bias, lanes):
     outs = []
     for low in (True, False):
-        mine = (lanes < HD) if low else (lanes >= HD)
-        one = jnp.where(mine, q, jnp.zeros_like(q))
-        weight = jnp.exp(mm_nt(one, k_ref[...]) + bias_ref[...])
+        one = jnp.where((lanes < HD) if low else (lanes >= HD), q, jnp.zeros_like(q))
+        weight = jnp.exp(mm_nt(one, k) + bias)
         prob = weight * (1.0 / jnp.sum(weight, axis=-1, keepdims=True))
-        outs.append(mm(prob.astype(BF), v_ref[...]))
-    out_ref[...] = jnp.where(lanes < HD, outs[0], outs[1]).astype(BF)
-
-
-def attend(q, k, v, bias):
-    rows, keys = q.shape[0], k.shape[0]
-    return pl.pallas_call(
-        attend_kernel,
-        out_shape=jax.ShapeDtypeStruct((rows, D), BF),
-        grid=(WIDE // 128,),
-        in_specs=[
-            pl.BlockSpec((rows, 128), lambda i: (0, i)),
-            pl.BlockSpec((keys, 128), lambda i: (0, i)),
-            pl.BlockSpec((keys, 128), lambda i: (0, i)),
-            pl.BlockSpec((rows, keys), lambda i: (0, 0)),
-        ],
-        out_specs=pl.BlockSpec((rows, 128), lambda i: (0, i)),
-        compiler_params=pltpu.CompilerParams(vmem_limit_bytes=24 * 1024 * 1024),
-        cost_estimate=lasting(12),
-        name="attend",
-    )(q, k, v, bias)
-
-
-def attend_back_kernel(q_ref, k_ref, v_ref, g_ref, bias_ref, dq_ref, dk_ref, dv_ref):
-    lanes = lax.broadcasted_iota(jnp.int32, q_ref.shape, 1)
-    q = q_ref[...] * jnp.asarray(SCALE, BF)
+        outs.append(mm(prob.astype(BF), v))
+    return jnp.where(lanes < HD, outs[0], outs[1]).astype(BF)
+
+
+def scores_backward(q, k, v, grad, bias_t, lanes):
     dqs, dk, dv = [], 0.0, 0.0
     for low in (True, False):
         mine = (lanes < HD) if low else (lanes >= HD)
         one = jnp.where(mine, q, jnp.zeros_like(q))
-        grad = jnp.where(mine, g_ref[...], jnp.zeros_like(q))
-        weight = jnp.exp(mm_nt(k_ref[...], one) + bias_ref[...])
+        g = jnp.where(mine, grad, jnp.zeros_like(grad))
+        weight = jnp.exp(mm_nt(k, one) + bias_t)
         prob = weight * (1.0 / jnp.sum(weight, axis=0, keepdims=True))
-        d_prob = mm_nt(v_ref[...], grad)
+        d_prob = mm_nt(v, g)
         row = jnp.sum(prob * d_prob, axis=0, keepdims=True)
         d_score = (prob * (d_prob - row)).astype(BF)
-        dqs.append(mm_tn(d_score, k_ref[...]))
+        dqs.append(mm_tn(d_score, k))
         dk = dk + mm(d_score, one)
-        dv = dv + mm(prob.astype(BF), grad)
-    dq_ref[...] = (jnp.where(lanes < HD, dqs[0], dqs[1]) * SCALE).astype(BF)
-    dk_ref[...] = dk.astype(BF)
-    dv_ref[...] = dv.astype(BF)
-
-
-def attend_back(q, k, v, grad, bias):
-    rows, keys = q.shape[0], k.shape[0]
-    few = pl.BlockSpec((rows, 128), lambda i: (0, i))
-    many = pl.BlockSpec((keys, 128), lambda i: (0, i))
+        dv = dv + mm(prob.astype(BF), g)
+    dq = jnp.where(lanes < HD, dqs[0], dqs[1]) * SCALE
+    return dq.astype(BF), dk.astype(BF), dv.astype(BF)
+
+
+def lane_tile(i):
+    return pl.ds(pl.multiple_of(i * 128, 128), 128)
+
+
+def widened(row):
+    return jnp.concatenate([row, jnp.zeros((row.shape[0], WIDE - D), row.dtype)], axis=1)
+
+
+def block_kernel(
+    wide, wq, wk, wv, wo, bias, normed, q_ref, k_ref, v_ref, att, resid, second, par, held
+):
+    rows = resid.shape[0]
+    total = wide.shape[0]
+    pick_row = (
+        lax.broadcasted_iota(jnp.int32, (16, 128), 1)
+        == lax.broadcasted_iota(jnp.int32, (16, 128), 0) + (D - TAIL)
+    )
+    par[...] = mm_nt(pick_row.astype(F32).astype(BF), wo[:, pl.ds(TAIL, 128)])
+
+    @pl.loop(0, total // rows)
+    def _(i):
+        at = pl.ds(pl.multiple_of(i * rows, 16), rows)
+        unit, _ = norm_parts(wide[at, :].astype(F32))
+        low = (unit * par[0:1, :] + par[2:3, :]).astype(BF)
+        normed[at, :] = low
+        k_ref[at, :] = mm(low, wk[...]).astype(BF)
+        v_ref[at, :] = (mm(low, wv[...]) + widened(par[4:5, :])).astype(BF)
+
+    own = pl.ds(total - rows, rows)
+    q_ref[...] = (mm(normed[own, :], wq[...]) + widened(par[3:4, :])).astype(BF)
+    lanes = lax.broadcasted_iota(jnp.int32, (rows, 128), 1)
+
+    @pl.loop(0, WIDE // 128)
+    def _(i):
+        at = lane_tile(i)
+        held[:, at] = scores_forward(
+            q_ref[:, at] * jnp.asarray(SCALE, BF), k_ref[:, at], v_ref[:, at], bias[...], lanes
+        )
+
+    att[...] = held[:, pl.ds(0, D)]
+    res = wide[own, :].astype(F32) + mm(att[...], wo[:, pl.ds(0, D)]) + par[5:6, :]
+    resid[...] = res
+    unit, _ = norm_parts(res)
+    second[...] = (unit * par[1:2, :] + par[6:7, :]).astype(BF)
+
+
+def weight_specs(weights):
+    if weights.ndim == 3:
+        return [pl.BlockSpec((None, D, WIDE), lambda i, p=p: (p, 0, 0)) for p in range(4)]
+    return [pl.BlockSpec((D, WIDE), lambda i, p=p: (0, p)) for p in range(4)]
+
+
+def whole(shape):
+    return pl.BlockSpec(shape, lambda i: (0,) * len(shape))
+
+
+def block_forward(wide, weights, bias):
+    total, rows = wide.shape[0], bias.shape[0]
+    outs = (
+        ((total, D), BF), ((rows, WIDE), BF), ((total, WIDE), BF), ((total, WIDE), BF),
+        ((rows, D), BF), ((rows, D), F32), ((rows, D), BF), ((16, D), F32),
+    )
     return pl.pallas_call(
-        attend_back_kernel,
-        out_shape=(
-            jax.ShapeDtypeStruct((rows, WIDE), BF),
-            jax.ShapeDtypeStruct((keys, WIDE), BF),
-            jax.ShapeDtypeStruct((keys, WIDE), BF),
-        ),
-        grid=(WIDE // 128,),
-        in_specs=[few, many, many, few, pl.BlockSpec((keys, rows), lambda i: (0, 0))],
-        out_specs=(few, many, many),
-        compiler_params=pltpu.CompilerParams(vmem_limit_bytes=24 * 1024 * 1024),
+        block_kernel,
+        out_shape=tuple(jax.ShapeDtypeStruct(*out) for out in outs),
+        grid=(1,),
+        in_specs=[whole(wide.shape), *weight_specs(weights), whole(bias.shape)],
+        out_specs=tuple(whole(shape) for shape, _ in outs),
+        scratch_shapes=[pltpu.VMEM((rows, WIDE), BF)],
+        compiler_params=pltpu.CompilerParams(vmem_limit_bytes=56 * 1024 * 1024),
         cost_estimate=lasting(22),
-        name="attend_back",
-    )(q, k, v, grad, bias)
+        name="block_forward",
+    )(wide, weights, weights, weights, weights, bias)
+
+
+def block_back_kernel(
+    d_second, up, resid, wide, q_ref, k_ref, v_ref, att, ffb_rows, wq, wk, wv, wo, par, bias_t,
+    d_resid, dq_ref, dk_ref, dv_ref, da_own, da_halo, left, right, held, sums,
+):
+    rows = resid.shape[0]
+    total = wide.shape[0]
+    own = total - rows
+
+    def total_of(values):
+        return jnp.sum(values, axis=0, keepdims=True)
+
+    upstream = up[...].astype(F32)
+    unit, inv = norm_parts(resid[...])
+    grad = upstream + norm_back(d_second[...], par[1:2, :], unit, inv)
+    d_resid[...] = grad
+    sums[1:2, :] = total_of(d_second[...] * unit)
+    sums[5:6, :] = total_of(grad)
+    sums[6:7, :] = total_of(d_second[...])
+    sums[7:8, :] = total_of(upstream)
+    sums[8:16, :] = ffb_rows[...]
+    low = grad.astype(BF)
+    right[pl.ds(0, rows), :] = jnp.zeros((rows, WIDE), BF)
+    right[pl.ds(0, rows), pl.ds(0, D)] = low
+    right[pl.ds(rows, 16), :] = (
+        lax.broadcasted_iota(jnp.int32, (16, WIDE), 1)
+        == lax.broadcasted_iota(jnp.int32, (16, WIDE), 0) + D
+    ).astype(F32).astype(BF)
+    held[...] = jnp.zeros((rows, WIDE), BF)
+    held[:, pl.ds(0, D)] = mm_nt(low, wo[:, pl.ds(0, D)]).astype(BF)
+    lanes = lax.broadcasted_iota(jnp.int32, (rows, 128), 1)
+
+    @pl.loop(0, WIDE // 128)
+    def _(i):
+        at = lane_tile(i)
+        dq_ref[:, at], dk_ref[:, at], dv_ref[:, at] = scores_backward(
+            q_ref[:, at] * jnp.asarray(SCALE, BF), k_ref[:, at], v_ref[:, at], held[:, at],
+            bias_t[...], lanes,
+        )
+
+    sums[3:4, :] = total_of(dq_ref[...].astype(F32))[:, :D]
+    sums[4:5, :] = total_of(dv_ref[...].astype(F32))[:, :D]
+    sums[0:1, :] = jnp.zeros((1, D), F32)
+    sums[2:3, :] = jnp.zeros((1, D), F32)
+
+    def back(at):
+        da = mm_nt(dk_ref[at, :], wk[...]) + mm_nt(dv_ref[at, :], wv[...])
+        return da
+
+    def count(da, at):
+        unit, _ = norm_parts(wide[at, :].astype(F32))
+        sums[0:1, :] += total_of(da * unit)
+        sums[2:3, :] += total_of(da)
+
+    @pl.loop(0, own // rows)
+    def _(i):
+        at = pl.ds(pl.multiple_of(i * rows, 16), rows)
+        da = back(at)
+        da_halo[at, :] = da.astype(BF)
+        count(da, at)
+
+    at = pl.ds(own, rows)
+    da = back(at) + mm_nt(dq_ref[...], wq[...])
+    da_own[...] = da
+    count(da, at)
+    left[pl.ds(0, rows), :] = att[...]
+    left[pl.ds(rows, 16), :] = sums[...].astype(BF)
+
+
+def block_backward(d_second, up, resid, wide, q, k, v, att, ffb_rows, weights, par, bias_t):
+    total, rows = wide.shape[0], resid.shape[0]
+    outs = (
+        ((rows, D), F32), ((rows, WIDE), BF), ((total, WIDE), BF), ((total, WIDE), BF),
+        ((rows, D), F32), ((total - rows, D), BF), ((rows + 16, D), BF), ((rows + 16, WIDE), BF),
+    )
+    before = (d_second, up, resid, wide, q, k, v, att, ffb_rows)
+    return pl.pallas_call(
+        block_back_kernel,
+        out_shape=tuple(jax.ShapeDtypeStruct(*out) for out in outs),
+        grid=(1,),
+        in_specs=[
+            *(whole(value.shape) for value in before), *weight_specs(weights),
+            whole(par.shape), whole(bias_t.shape),
+        ],
+        out_specs=tuple(whole(shape) for shape, _ in outs),
+        scratch_shapes=[pltpu.VMEM((rows, WIDE), BF), pltpu.VMEM((16, D), F32)],
+        compiler_params=pltpu.CompilerParams(vmem_limit_bytes=60 * 1024 * 1024),
+        cost_estimate=lasting(38),
+        name="block_backward",
+    )(*before, weights, weights, weights, weights, par, bias_t)
 
 
 def on_device(
@@ -876,7 +1004,7 @@
     bias_t = bias.T
 
     small = jnp.concatenate(
-        [norm_gains[0].T, biases[0].T, ff_bias[0].reshape(shard, per_row)], axis=1
+        [norm_gains[0].T, biases[0].T, ff_bias[0].reshape(per_row, shard).T], axis=1
     )
     packed = jnp.stack(
         [
@@ -903,12 +1031,12 @@
 
     def gathered(part):
         rows_first = part.transpose(1, 0, 2).reshape(half, 4 * WIDE)
-        every = lax.all_gather(rows_first, pair, axis=0, tiled=True)
-        return [every[:, i * WIDE : (i + 1) * WIDE] for i in range(4)]
+        return lax.all_gather(rows_first, pair, axis=0, tiled=True)
 
     recv = on_chip(give)
     one = gathered(pick(s, recv, keep))
-    zero = [zero[i] for i in range(4)] if fits else gathered(pick(s, keep, recv))
+    if not fits:
+        zero = gathered(pick(s, keep, recv))
     up_own = lax.all_to_all(
         up_shard.reshape(shard, nf, ff_here), "fsdp", split_axis=1, concat_axis=0, tiled=True
     ).reshape(D, ff_here)
@@ -916,89 +1044,48 @@
     down_w = both_layers(down_shard, s)
 
     weights = (zero, one)
-    gains, shifts, ffb = [], [], []
-    for layer in range(2):
-        beside = weights[layer][3]
-        vectors = beside[:, D : D + 8].T.astype(F32)
-        gains.append(vectors[:2])
-        shifts.append(vectors[2:])
-        hidden = beside[:, D + 8 : D + 8 + per_row].reshape(-1).astype(F32)
-        ffb.append(lax.dynamic_slice_in_dim(hidden, f * ff_here, ff_here, 0))
 
     kept = []
     current = own_in
     produced = []
     for layer in range(2):
-        gain, shift_rows = gains[layer], shifts[layer]
-        wide = (with_halo(current, chunks) if layer else wide_in).astype(F32)
-        n1, inv1 = norm_parts(wide)
-        normed = (n1 * gain[0] + shift_rows[0]).astype(BF)
-        wq, wk, wv, wo = weights[layer]
-        q = (mm(normed[reach:], wq) + widen(shift_rows[1:2])).astype(BF)
-        k = mm(normed, wk).astype(BF)
-        v = (mm(normed, wv) + widen(shift_rows[2:3])).astype(BF)
-        att = attend(q, k, v, bias)
-        resid = current.astype(F32) + mm(att, wo[:, :D]) + shift_rows[3]
-        n2, inv2 = norm_parts(resid)
-        second = (n2 * gain[1] + shift_rows[4]).astype(BF)
-        total, second_all, active, slope = mlp_forward(
-            second, up_w[layer], down_w[layer], ffb[layer][None]
-        )
-        out = resid + total + shift_rows[5]
-        low = out.astype(BF)
-        produced.append(low)
-        kept.append((wide, normed, q, k, v, att, resid, second_all, slope, active))
-        current = low
-
-    upstream = own_cot.astype(F32)
+        wide = with_halo(current, chunks) if layer else wide_in
+        normed, q, k, v, att, resid, second, par = block_forward(wide, weights[layer], bias)
+        ffb = lax.dynamic_slice(par, (8, f * shard), (per_row, shard)).reshape(1, ff_here)
+        current, second_all, active, slope = mlp_forward(
+            second, up_w[layer], down_w[layer], ffb, resid, par
+        )
+        produced.append(current)
+        kept.append((wide, normed, q, k, v, att, resid, second_all, slope, active, par))
+
+    upstream = own_cot
     derived = [None, None]
     parts = [None, None]
     mlp_sums = [None, None]
     for layer in (1, 0):
-        wide, normed, q, k, v, att, resid, second_all, slope, active = kept[layer]
-        gain = gains[layer]
-        up_b = upstream.astype(BF)
-        d_second, up_all, dz_b, ffb_g = mlp_backward(up_b, up_w[layer], down_w[layer], slope)
+        wide, normed, q, k, v, att, resid, second_all, slope, active, par = kept[layer]
+        d_second, up_all, dz_b, ffb_g = mlp_backward(upstream, up_w[layer], down_w[layer], slope)
         down_g = mm_tn(flat(active), flat(up_all))
         up_g = mm_tn(flat(second_all), flat(dz_b))
-        n2, inv2 = norm_parts(resid)
-        d_resid = upstream + norm_back(d_second, gain[1], n2, inv2)
-        c = d_resid.astype(BF)
-        wq, wk, wv, wo = weights[layer]
-        d_att = widen(mm_nt(c, wo[:, :D]).astype(BF))
-        dq, dk, dv = attend_back(q, k, v, d_att, bias_t)
-        da_wide = mm_nt(dk, wk) + mm_nt(dv, wv)
-        da_own = da_wide[reach:] + mm_nt(dq, wq)
-        da_halo = da_wide[:reach]
-        n1, inv1 = norm_parts(wide)
+        ffb_rows = lax.dynamic_update_slice(
+            jnp.zeros((8, D), F32), ffb_g.reshape(per_row, shard), (0, f * shard)
+        )
+        d_resid, dq, dk, dv, da_own, da_halo, left, right = block_backward(
+            d_second, upstream, resid, wide, q, k, v, att, ffb_rows, weights[layer], par, bias_t
+        )
+
+        def through_norm(late):
+            unit, inv = norm_parts(wide[reach:].astype(F32))
+            return d_resid + norm_back(da_own + late, par[0], unit, inv)
+
         if layer == 1 or not fits:
-            da = da_own + return_halo(da_halo, chunks, rows)
-            derived[layer] = d_resid + norm_back(da, gain[0], n1[reach:], inv1[reach:])
-            upstream_next = derived[layer].astype(BF).astype(F32)
-        vectors = jnp.stack(
-            [
-                jnp.sum(da_halo * n1[:reach], axis=0) + jnp.sum(da_own * n1[reach:], axis=0),
-                jnp.sum(d_second * n2, axis=0),
-                jnp.sum(da_halo, axis=0) + jnp.sum(da_own, axis=0),
-                jnp.sum(dq.astype(F32), axis=0)[:D],
-                jnp.sum(dv.astype(F32), axis=0)[:D],
-                jnp.sum(d_resid, axis=0),
-                jnp.sum(d_second, axis=0),
-                jnp.sum(upstream, axis=0),
-            ]
-        )
-        ffb_block = lax.dynamic_update_slice(
-            jnp.zeros((D, per_row), F32), ffb_g.reshape(shard, per_row), (f * shard, 0)
-        )
-        extra = jnp.pad(
-            jnp.concatenate([vectors.T, ffb_block], axis=1),
-            ((0, 0), (D, WIDE - D - 8 - per_row)),
-        )
+            derived[layer] = through_norm(return_halo(da_halo, chunks, rows))
+            upstream_next = derived[layer].astype(BF)
         pieces = (
             mm_tn(normed[reach:], dq).astype(BF),
             mm_tn(normed, dk).astype(BF),
             mm_tn(normed, dv).astype(BF),
-            (mm_tn(att, widen(c)) + extra).astype(BF),
+            mm_tn(left, right).astype(BF),
         )
         parts[layer] = pieces
         up_g = lax.all_to_all(
@@ -1019,10 +1106,9 @@
 
     if fits:
         qkv_g, out_g, down_one, up_one, late = reduce_both(
-            parts[0], parts[1], mlp_sums[1], da_halo.astype(BF)
-        )
-        da = da_own + late.astype(F32)
-        derived[0] = d_resid + norm_back(da, gain[0], n1[reach:], inv1[reach:])
+            parts[0], parts[1], mlp_sums[1], da_halo
+        )
+        derived[0] = through_norm(late.astype(F32))
         far = lax.ppermute(mlp_sums[0], "section", [(1, 0)])
         down_zero, up_zero = split_up(jnp.concatenate([mlp_sums[0], far], axis=1), nf, shard)
         grad_down = pick(s, down_zero, down_one).astype(F32)
@@ -1043,7 +1129,7 @@
         grad_down[None],
         vectors[None, :2],
         vectors[None, 2:],
-        out_g[:, D + 8 : D + 8 + per_row].reshape(1, ff_here),
+        out_g[:, D + 8 : D + 8 + per_row].T.reshape(1, ff_here),
     )
 
 

time: 915 us -> 951 us (1.039)
  waiting for transfers between devices: 30.5 us -> 136 us
  local copies, waits for them, and re-layouts: 143 us -> 87.6 us
  Pallas kernels: 493 us -> 541 us
  matrix products: 100 us -> 63.6 us
  other arithmetic: 84.4 us -> 59.7 us
    psum x2, waiting for transfers between devices: 0.01 us -> 76.9 us  [on_device(): mlp_sums[layer] = lax.psum(halves, 'ctx')]
    pallas_call x4, Pallas kernels: 56.7 us -> 118 us  [the longest x2 67.7 us: block_backward(): pl.pallas_call(block_back_kernel, out_shape=tuple((jax.ShapeDtypeStruct(*...]
    dot_general x16 -> x0, matrix products: 47.3 us -> none  [the longest x8 32.5 us: mm_nt(): lax.dot_general(a, b, (((1,), (1,)), ((), ())), preferred_element_type=F32)]
    all_to_all x1, waiting for transfers between devices: 10.9 us -> 37.8 us  [on_device(): lax.all_to_all(up_shard.reshape(shard, nf, ff_here), 'fsdp', split_axis=1...]
    unnamed x248 -> x144, local copies, waits for them, and re-layouts: 54.7 us -> 30.7 us
    pallas_call x4, Pallas kernels: 195 us -> 184 us  [plane_call(): pl.pallas_call(kernel, out_shape=outs, in_specs=[VSPEC] * len(operands),...]
    dot_general x12, matrix products: 52.8 us -> 63.6 us  [mm_tn(): lax.dot_general(a, b, (((0,), (0,)), ((), ())), preferred_element_type=F32)]
  transfers between devices with their start and end apart: 20 -> 20, of which waited for: 6 -> 6; matrix products, arithmetic and copies ran while one was open for 25% -> 17% of each run, Pallas kernels for 43% -> 52%
where the time goes in v4:
time: 951 us; the launch traced here: 938 us
  Pallas kernels  541 us (57%)
  waiting for transfers between devices  136 us (14%)
  local copies, waits for them, and re-layouts  87.6 us (9%)
  matrix products  63.6 us (7%)
  other arithmetic  59.7 us (6%)
  starting transfers between devices  35.3 us (4%)
  between operations  14.8 us (2%)
    pallas_call x1, Pallas kernels, reduce_both(): pl.pallas_call(reduce_kernel, out_shape=tuple((jax.ShapeDtypeStruct(shape...  187 us
    pallas_call x4, Pallas kernels, plane_call(): pl.pallas_call(kernel, out_shape=outs, in_specs=[VSPEC] * len(operands),...  184 us
    psum x2, waiting for transfers between devices, on_device(): mlp_sums[layer] = lax.psum(halves, 'ctx')  76.9 us
    pallas_call x2, Pallas kernels, block_backward(): pl.pallas_call(block_back_kernel, out_shape=tuple((jax.ShapeDtypeStruct(*...  67.7 us
    dot_general x12, matrix products, mm_tn(): lax.dot_general(a, b, (((0,), (0,)), ((), ())), preferred_element_type=F32)  63.6 us
    pallas_call x1, Pallas kernels, first_weights(): pl.pallas_call(weights_kernel, out_shape=(jax.ShapeDtypeStruct((4, D, WID...  52.6 us
    pallas_call x2, Pallas kernels, block_forward(): pl.pallas_call(block_kernel, out_shape=tuple((jax.ShapeDtypeStruct(*out)...  49.9 us
    all_to_all x1, waiting for transfers between devices, on_device(): lax.all_to_all(up_shard.reshape(shard, nf, ff_here), 'fsdp', split_axis=1...  37.8 us
  transfers between devices with their start and end apart: 20, of which 6 were waited for; matrix products, arithmetic and copies ran while one was open for 17% of the time, Pallas kernels for 52%

profile of v4, /device:TPU:0, one launch (start us, length us, event | category | flops | bytes accessed | tf_op | source)
XLA Modules:
  0.0 938.4 jit_solution(16283264624498900208)
XLA Ops:
  20.1 52.6 %first_weights.1 = (bf16[4,1088,1152]{2,1,0:T(8,128)(2,1)S(1)}, bf16[768,1088]{1,0:T(8,128)(2,1)S(1)}) custom-call(bf16[4,272,1152]{2,1,0:T(8,128)(2,1)S(1)} %pad_maximum_fusion.own, bf16[256,1088]{1,0:T(8,128)(2,1)S(1)} %bitcast.144), custom_call_target="tpu_custom_call" | custom-call | bytes 175000000 | tf_op jit(solution)/shard_map/first_weights/pallas_call | solution.py:388
  72.7 3.9 copy-done.2
  79.7 3.1 collective-permute-done.4
  86.0 5.4 reshape.130
  93.1 4.8 all-to-all-start
  98.0 37.8 %all-to-all-done = bf16[272,4,1088]{2,0,1:T(8,128)(2,1)} async-done(((bf16[272,4,1088]{2,0,1:T(8,128)(2,1)}), bf16[272,4,1088]{2,0,1:T(8,128)(2,1)}, u32[]{:S(2)}, u32[]{:S(2)}) %all-to-all-start) | async-done | bytes 2367520 | tf_op jit(solution)/shard_map/all_to_all | solution.py:1040
  137.0 25.8 %block_forward.2 = (bf16[768,1088]{1,0:T(8,128)(2,1)}, bf16[256,1152]{1,0:T(8,128)(2,1)}, bf16[768,1152]{1,0:T(8,128)(2,1)}, bf16[768,1152]{1,0:T(8,128)(2,1)}, ...) custom-call(bf16[768,1088]{1,0:T(8,128)(2,1)} %copy-done.8, ...), custom_call_target="tpu_custom_call" | custom-call | bytes 77000000 | tf_op jit(solution)/shard_map/block_forward/pallas_call | solution.py:870
  163.6 4.4 broadcast_select_fusion
  168.1 4.5 broadcast_select_fusion.1
  172.6 48.2 %shard_map.169 = (bf16[256,1088]{1,0:T(8,128)(2,1)S(1)}, bf16[4,256,1088]{2,1,0:T(8,128)(2,1)S(1)}, bf16[4,256,1088]{2,1,0:T(8,128)(2,1)S(1)}, f32[4,256,1088]{2,1,0:T(8,128)}) custom-call(bf16[256,1088]{1,0:T(8,128)(2,1)S(1)} %copy-done.18, bf16[1088,1088]{1,0:T(8,128)(2,1)S(1)} %get-tuple-element.184.up, bf16[1088,1088]{1,0:T(8,128)(2,1)S(1)} %get-tuple-element.182.down, ...), custom_call_target="tpu_custom_call" | custom-call | bytes 140000000 | tf_op jit(solution)/shard_map/pallas_call | solution.py:171
  224.6 4.1 collective-permute-start.2
  233.4 4.9 collective-permute-done.2
  238.3 5.2 collective-permute-start.3
  246.5 2.1 copy.105
  248.7 3.6 collective-permute-done.3
  254.3 2.6 pad_maximum_fusion.1.wide
  256.9 24.1 %block_forward.3 = (bf16[768,1088]{1,0:T(8,128)(2,1)}, bf16[256,1152]{1,0:T(8,128)(2,1)}, bf16[768,1152]{1,0:T(8,128)(2,1)}, bf16[768,1152]{1,0:T(8,128)(2,1)}, ...) custom-call(bf16[768,1088]{1,0:T(8,128)(2,1)} %pad_maximum_fusion.1.wide, ...), custom_call_target="tpu_custom_call" | custom-call | bytes 77000000 | tf_op jit(solution)/shard_map/block_forward/pallas_call | solution.py:870
  288.6 44.1 %shard_map.170 = (bf16[256,1088]{1,0:T(8,128)(2,1)S(1)}, bf16[4,256,1088]{2,1,0:T(8,128)(2,1)S(1)}, bf16[4,256,1088]{2,1,0:T(8,128)(2,1)S(1)}, f32[4,256,1088]{2,1,0:T(8,128)}) custom-call(bf16[256,1088]{1,0:T(8,128)(2,1)S(1)} %copy-done.19, bf16[1088,1088]{1,0:T(8,128)(2,1)S(1)} %copy-done.7, bf16[1088,1088]{1,0:T(8,128)(2,1)S(1)} %copy-done.5, ...), custom_call_target="tpu_custom_call" | custom-call | bytes 140000000 | tf_op jit(solution)/shard_map/pallas_call | solution.py:171
  332.8 43.6 %shard_map.171 = (f32[256,1088]{1,0:T(8,128)S(1)}, bf16[4,256,1088]{2,1,0:T(8,128)(2,1)S(1)}, bf16[4,256,1088]{2,1,0:T(8,128)(2,1)S(1)}, f32[1,1088]{1,0:T(1,128)S(1)}) custom-call(bf16[256,1088]{1,0:T(8,128)(2,1)S(1)} %bitcast.143, bf16[1088,1088]{1,0:T(8,128)(2,1)S(1)} %copy-done.7, bf16[1088,1088]{1,0:T(8,128)(2,1)S(1)} %copy-done.6, ...), custom_call_target="tpu_custom_call" | custom-call | bytes 140000000 | tf_op jit(solution)/shard_map/pallas_call | solution.py:171
  376.4 4.6 fusion.1
  381.0 4.5 all-to-all-start.1
  393.8 33.8 %block_backward.2 = (f32[256,1088]{1,0:T(8,128)}, bf16[256,1152]{1,0:T(8,128)(2,1)}, bf16[768,1152]{1,0:T(8,128)(2,1)}, bf16[768,1152]{1,0:T(8,128)(2,1)}, f32[2...) custom-call(f32[256,1088]{1,0:T(8,128)} %copy-done.17, ...), custom_call_target="tpu_custom_call" | custom-call | bytes 133000000 | tf_op jit(solution)/shard_map/block_backward/pallas_call | solution.py:958
  433.1 7.1 fusion
  440.2 4.0 convolution_convert_fusion.3.k1
  446.3 3.6 fusion.11
  455.3 5.8 convolution_convert_fusion.2.v1
  461.1 9.9 %collective-permute-done.9 = bf16[256,1088]{0,1:T(8,128)(2,1)} collective-permute-done((bf16[256,1088]{0,1:T(8,128)(2,1)}, bf16[256,1088]{0,1:T(8,128)(2,1)}, u32[]{:S(2)}, u32[]{:S(2)}) %collective-permute-start.9) | collective-permute-done | bytes 557088 | tf_op jit(solution)/shard_map/ppermute | solution.py:737
  475.2 3.2 fusion.45
  478.4 4.2 fusion.5
  485.3 48.2 %shard_map.172 = (f32[256,1088]{1,0:T(8,128)S(1)}, bf16[4,256,1088]{2,1,0:T(8,128)(2,1)S(1)}, bf16[4,256,1088]{2,1,0:T(8,128)(2,1)S(1)}, f32[1,1088]{1,0:T(1,128)S(1)}) custom-call(bf16[256,1088]{1,0:T(8,128)(2,1)S(1)} %copy-done.10, bf16[1088,1088]{1,0:T(8,128)(2,1)S(1)} %copy-done.4, bf16[1088,1088]{1,0:T(8,128)(2,1)S(1)} %get-tuple-element.182.down, ...), custom_call_target="tpu_custom_call" | custom-call | bytes 140000000 | tf_op jit(solution)/shard_map/pallas_call | solution.py:171
  533.6 15.9 %fusion.3 = bf16[1088,1088]{1,0:T(8,128)(2,1)} fusion(bf16[4,256,1088]{2,1,0:T(8,128)(2,1)S(1)} %copy-done.25, bf16[4,256,1088]{2,1,0:T(8,128)(2,1)S(1)} %get-tuple-element.126), kind=kOutput, calls=%fused_computation.9 | convolution fusion | flops 2425491456 | bytes 6823936 | tf_op jit(solution)/shard_map/dot_general | solution.py:30
  549.5 4.7 all-to-all-start.2
  554.2 3.0 convolution_convert_fusion.6.o1
  557.3 2.4 convolution_convert_fusion.q1
  563.3 2.3 collective-permute-start.11
  566.8 33.9 %block_backward.3 = (f32[256,1088]{1,0:T(8,128)}, bf16[256,1152]{1,0:T(8,128)(2,1)}, bf16[768,1152]{1,0:T(8,128)(2,1)}, bf16[768,1152]{1,0:T(8,128)(2,1)}, f32[2...) custom-call(f32[256,1088]{1,0:T(8,128)} %copy-done.16, ...), custom_call_target="tpu_custom_call" | custom-call | bytes 133000000 | tf_op jit(solution)/shard_map/block_backward/pallas_call | solution.py:958
  600.7 6.3 fusion.2
  607.0 3.5 fusion.7
  614.7 3.7 convolution_convert_fusion.1.q0
  618.4 3.2 convolution_convert_fusion.7.o0
  621.6 3.9 convolution_convert_fusion.5.k0
  625.5 3.9 convolution_convert_fusion.4.v0
  629.3 4.3 fusion.4
  633.7 76.9 %all-reduce.6.cloned.1.call-done.mlp = bf16[2,544,1088]{2,1,0:T(8,128)(2,1)} async-done(((bf16[2,544,1088]{2,1,0:T(8,128)(2,1)}), bf16[2,544,1088]{2,1,0:T(8,128)(2,1)}) %all-reduce.6.cloned.1.call-update) | async-done | bytes 2367504 | tf_op jit(solution)/shard_map/psum | solution.py:1103
  710.7 186.7 %reduce_both.1 = (bf16[272,3264]{1,0:T(8,128)(2,1)}, bf16[272,1152]{1,0:T(8,128)(2,1)}, bf16[1088,1088]{1,0:T(8,128)(2,1)}, bf16[272,4352]{1,0:T(8,128)(2,1)}, bf16[256,1088]{1,0:T(8,128)(2,1)}) custom-call(bf16[1088,1152]{1,0:T(8,128)(2,1)} %convolution_convert_fusion.1.q0, bf16[1088,1152]{1,0:T(8,128)(2,1)} %convolution_convert_fusion.5.k0, ...), custom_call_target="tpu_custom_call" | custom-call | bytes 420000000 | tf_op jit(solution)/shard_map/reduce_both/pallas_call | solution.py:688
  921.8 2.9 reshape.141
  924.7 4.5 fusion.16
  929.2 2.5 bitcast_convert_fusion
  (256 shorter events, 105.6 us)
Async XLA Ops:
  7.2 128.7 %copy-start = (s32[2,1,1024]{2,1,0:T(1,128)S(1)}, s32[2,1,1024]{2,1,0:T(1,128)}, u32[]{:S(2)}) copy-start(s32[2,1,1024]{2,1,0:T(1,128)} %param.11) | copy-start | bytes 24580
  7.2 249.7 %all-gather.2.cloned.1.call-start = ((), (), s32[]{:S(2)}) async-start(), calls=%async_computation.3 | async-start | bytes 11280384 | tf_op jit(solution)/shard_map/all_gather | solution.py:1034
  79.6 3.1 collective-permute-start.4
  93.1 4.8 copy-start.40
  93.1 42.7 %all-to-all-start = ((bf16[272,4,1088]{2,0,1:T(8,128)(2,1)}), bf16[272,4,1088]{2,0,1:T(8,128)(2,1)}, u32[]{:S(2)}, u32[]{:S(2)}) async-start(bf16[272,4,1088]{2,0,1:T(8,128)(2,1)} %copy.102), calls=%async_computation | async-start | bytes 5013504 | tf_op jit(solution)/shard_map/all_to_all | solution.py:1040
  97.9 65.7 %collective-permute-start.1 = (bf16[1088,1088]{1,0:T(8,128)(2,1)S(1)}, bf16[1088,1088]{1,0:T(8,128)(2,1)}, u32[]{:S(2)}, u32[]{:S(2)}) collective-permute-start(bf16[1088,1088]{1,0:T(8,128)(2,1)S(1)} %bitcast.154), channel_id=1, source_target_pairs={{0,16},{16,0},{1,17},{17,1},{2,18},{18,2},{3,19},{19,3},{4,20},{20... | collective-permute-start | bytes 7102472 | tf_op jit(solution)/shard_map/ppermute | solution.py:761
  135.9 32.2 %collective-permute-start = (bf16[1088,1088]{1,0:T(8,128)(2,1)}, bf16[1088,1088]{1,0:T(8,128)(2,1)}, u32[]{:S(2)}, u32[]{:S(2)}) collective-permute-start(bf16[1088,1088]{1,0:T(8,128)(2,1)} %bitcast.17), channel_id=1, source_target_pairs={{0,16},{16,0},{1,17},{17,1},{2,18},{18,2},{3,19},{19,3},{4,20},{20... | collective-permute-start | bytes 7102472 | tf_op jit(solution)/shard_map/ppermute | solution.py:761
  168.1 4.5 copy-start.12
  168.1 4.5 copy-start.18
  168.1 4.5 copy-start.20
  172.6 48.2 %copy-start.3 = (bf16[1088,1088]{1,0:T(8,128)(2,1)}, bf16[1088,1088]{1,0:T(8,128)(2,1)S(1)}, u32[]{:S(2)}) copy-start(bf16[1088,1088]{1,0:T(8,128)(2,1)S(1)} %get-tuple-element.184.up) | copy-start | bytes 7102468
  224.6 13.7 %collective-permute-start.2 = (bf16[256,1088]{0,1:T(8,128)(2,1)}, bf16[256,1088]{0,1:T(8,128)(2,1)}, u32[]{:S(2)}, u32[]{:S(2)}) collective-permute-start(bf16[256,1088]{0,1:T(8,128)(2,1)} %copy.103), channel_id=1, source_target_pairs={{0,1},{1,2},{2,3},{4,5},{5,6},{6,7},{8,9},{9,10},{10,11},{12,13},{... | collective-permute-start | bytes 1671176 | tf_op jit(solution)/shard_map/ppermute | solution.py:737
  232.1 24.9 %copy-start.57 = (f32[256]{0:T(256)}, f32[256]{0:T(256)S(1)}, u32[]{:S(2)}) copy-start(f32[256]{0:T(256)S(1)} %broadcast_multiply_fusion.2) | copy-start | bytes 3076
  238.3 13.9 %collective-permute-start.3 = (bf16[256,1088]{0,1:T(8,128)(2,1)}, bf16[256,1088]{0,1:T(8,128)(2,1)}, u32[]{:S(2)}, u32[]{:S(2)}) collective-permute-start(bf16[256,1088]{0,1:T(8,128)(2,1)} %collective-permute-done.2), channel_id=1, source_target_pairs={{0,1},{1,2},{2,3},{4,5},{5,6},{6,7},{8,9},{9,10},{10,11},{12,13},{... | collective-permute-start | bytes 1671176 | tf_op jit(solution)/shard_map/ppermute | solution.py:737
  245.2 140.8 %collective-permute-start.6 = (bf16[256,1088]{0,1:T(8,128)(2,1)}, bf16[256,1088]{0,1:T(8,128)(2,1)}, u32[]{:S(2)}, u32[]{:S(2)}) collective-permute-start(bf16[256,1088]{0,1:T(8,128)(2,1)} %copy.103), channel_id=1, source_target_pairs={{16,0},{17,1},{18,2},{19,3},{20,4},{21,5},{22,6},{23,7},{24,8},{25... | collective-permute-start | bytes 1671176 | tf_op jit(solution)/shard_map/ppermute | solution.py:1142
  288.6 44.2 %copy-start.6 = (bf16[1088,1088]{1,0:T(8,128)(2,1)S(1)}, bf16[1088,1088]{1,0:T(8,128)(2,1)}, u32[]{:S(2)}) copy-start(bf16[1088,1088]{1,0:T(8,128)(2,1)} %get-tuple-element.181.down) | copy-start | bytes 7102468
  288.6 44.2 %copy-start.11 = (bf16[1,1,256,1088]{3,2,1,0:T(8,128)(2,1)S(1)}, bf16[1,1,256,1088]{3,2,1,0:T(8,128)(2,1)}, u32[]{:S(2)}) copy-start(bf16[1,1,256,1088]{3,2,1,0:T(8,128)(2,1)} %copy.112) | copy-start | bytes 1671172
  332.8 43.6 %copy-start.14 = (bf16[256,1088]{1,0:T(8,128)(2,1)}, bf16[256,1088]{1,0:T(8,128)(2,1)S(1)}, u32[]{:S(2)}) copy-start(bf16[256,1088]{1,0:T(8,128)(2,1)S(1)} %get-tuple-element.86) | copy-start | bytes 1671172
  332.8 43.6 %copy-start.26 = (bf16[4,256,1088]{2,1,0:T(8,128)(2,1)}, bf16[4,256,1088]{2,1,0:T(8,128)(2,1)S(1)}, u32[]{:S(2)}) copy-start(bf16[4,256,1088]{2,1,0:T(8,128)(2,1)S(1)} %get-tuple-element.87) | copy-start | bytes 6684676
  376.4 4.6 copy-start.17
  376.4 4.6 copy-start.28
  381.0 65.2 %all-to-all-start.1 = ((bf16[4,272,1088]{2,1,0:T(8,128)(2,1)}), bf16[4,272,1088]{2,1,0:T(8,128)(2,1)}, u32[]{:S(2)}, u32[]{:S(2)}) async-start(bf16[4,272,1088]{2,1,0:T(8,128)(2,1)} %bitcast.155), calls=%async_computation.1 | async-start | bytes 5013504 | tf_op jit(solution)/shard_map/all_to_all | solution.py:1091
  390.3 170.3 %collective-permute-start.5 = (bf16[256,1088]{0,1:T(8,128)(2,1)}, bf16[256,1088]{0,1:T(8,128)(2,1)}, u32[]{:S(2)}, u32[]{:S(2)}) collective-permute-start(bf16[256,1088]{0,1:T(8,128)(2,1)} %copy.108), channel_id=1, source_target_pairs={{0,16},{1,17},{2,18},{3,19},{4,20},{5,21},{6,22},{7,23},{8,24},{9,... | collective-permute-start | bytes 1671176 | tf_op jit(solution)/shard_map/ppermute | solution.py:1143
  431.6 12.6 %collective-permute-start.8 = (bf16[256,1088]{0,1:T(8,128)(2,1)}, bf16[256,1088]{0,1:T(8,128)(2,1)}, u32[]{:S(2)}, u32[]{:S(2)}) collective-permute-start(bf16[256,1088]{0,1:T(8,128)(2,1)} %copy.117), channel_id=1, source_target_pairs={{1,0},{2,1},{3,2},{5,4},{6,5},{7,6},{9,8},{10,9},{11,10},{13,12},{... | collective-permute-start | bytes 1671176 | tf_op jit(solution)/shard_map/ppermute | solution.py:737
  433.1 7.1 copy-start.52
  433.1 7.1 copy-start.63
  449.8 28.6 %collective-permute-start.7 = (bf16[2,544,1088]{2,1,0:T(8,128)(2,1)}, bf16[2,544,1088]{2,1,0:T(8,128)(2,1)}, u32[]{:S(2)}, u32[]{:S(2)}) collective-permute-start(bf16[2,544,1088]{2,1,0:T(8,128)(2,1)} %fusion.11), channel_id=1, source_target_pairs={{0,16},{16,0},{1,17},{17,1},{2,18},{18,2},{3,19},{19,3},{4,20},{20... | collective-permute-start | bytes 7102472 | tf_op jit(solution)/shard_map/ppermute | solution.py:761
  452.9 18.1 %collective-permute-start.9 = (bf16[256,1088]{0,1:T(8,128)(2,1)}, bf16[256,1088]{0,1:T(8,128)(2,1)}, u32[]{:S(2)}, u32[]{:S(2)}) collective-permute-start(bf16[256,1088]{0,1:T(8,128)(2,1)} %copy.119), channel_id=1, source_target_pairs={{1,0},{2,1},{3,2},{5,4},{6,5},{7,6},{9,8},{10,9},{11,10},{13,12},{... | collective-permute-start | bytes 1671176 | tf_op jit(solution)/shard_map/ppermute | solution.py:737
  485.3 48.2 %copy-start.25 = (bf16[4,256,1088]{2,1,0:T(8,128)(2,1)S(1)}, bf16[4,256,1088]{2,1,0:T(8,128)(2,1)}, u32[]{:S(2)}) copy-start(bf16[4,256,1088]{2,1,0:T(8,128)(2,1)} %copy-done.24) | copy-start | bytes 6684676
  533.5 15.9 %copy-start.16 = (f32[256,1088]{1,0:T(8,128)}, f32[256,1088]{1,0:T(8,128)S(1)}, u32[]{:S(2)}) copy-start(f32[256,1088]{1,0:T(8,128)S(1)} %get-tuple-element.103.d_second) | copy-start | bytes 3342340
  533.5 15.9 %copy-start.27 = (bf16[4,256,1088]{2,1,0:T(8,128)(2,1)}, bf16[4,256,1088]{2,1,0:T(8,128)(2,1)S(1)}, u32[]{:S(2)}) copy-start(bf16[4,256,1088]{2,1,0:T(8,128)(2,1)S(1)} %get-tuple-element.124) | copy-start | bytes 6684676
  549.5 4.7 copy-start.64
  549.5 4.8 copy-start.65
  549.5 57.5 %all-to-all-start.2 = ((bf16[4,272,1088]{2,1,0:T(8,128)(2,1)}), bf16[4,272,1088]{2,1,0:T(8,128)(2,1)}, u32[]{:S(2)}, u32[]{:S(2)}) async-start(bf16[4,272,1088]{2,1,0:T(8,128)(2,1)} %bitcast.37), calls=%async_computation.2 | async-start | bytes 5013504 | tf_op jit(solution)/shard_map/all_to_all | solution.py:1091
  554.1 156.5 %all-reduce.6.cloned.1.call-start = ((), (), s32[]{:S(2)}) async-start(), calls=%async_computation.4 | async-start | bytes 5013504 | tf_op jit(solution)/shard_map/psum | solution.py:1103
  563.3 49.8 %collective-permute-start.11 = (f32[256,1088]{0,1:T(8,128)}, f32[256,1088]{0,1:T(8,128)}, u32[]{:S(2)}, u32[]{:S(2)}) collective-permute-start(f32[256,1088]{0,1:T(8,128)} %copy.125), channel_id=1, source_target_pairs={{0,16},{1,17},{2,18},{3,19},{4,20},{5,21},{6,22},{7,23},{8,24},{9,... | collective-permute-start | bytes 3342344 | tf_op jit(solution)/shard_map/ppermute | solution.py:1143
  566.8 33.9 %copy-start.23 = (bf16[4,256,1088]{2,1,0:T(8,128)(2,1)S(1)}, bf16[4,256,1088]{2,1,0:T(8,128)(2,1)}, u32[]{:S(2)}) copy-start(bf16[4,256,1088]{2,1,0:T(8,128)(2,1)} %copy-done.22) | copy-start | bytes 6684676
  610.5 18.8 %collective-permute-start.10 = (bf16[2,544,1088]{2,1,0:T(8,128)(2,1)}, bf16[2,544,1088]{2,1,0:T(8,128)(2,1)}, u32[]{:S(2)}, u32[]{:S(2)}) collective-permute-start(bf16[2,544,1088]{2,1,0:T(8,128)(2,1)} %fusion.7), channel_id=1, source_target_pairs={{0,16},{16,0},{1,17},{17,1},{2,18},{18,2},{3,19},{19,3},{4,20},{20... | collective-permute-start | bytes 7102472 | tf_op jit(solution)/shard_map/ppermute | solution.py:761
  610.6 294.3 %all-reduce.8.cloned.1.call-start = ((), (), s32[]{:S(2)}) async-start(), calls=%async_computation.5 | async-start | bytes 5013504 | tf_op jit(solution)/shard_map/psum | solution.py:1103
  710.6 186.8 %copy-start.9 = (bf16[768,1088]{1,0:T(8,128)(2,1)S(1)}, bf16[768,1088]{1,0:T(8,128)(2,1)}, u32[]{:S(2)}) copy-start(bf16[768,1088]{1,0:T(8,128)(2,1)} %copy-done.8) | copy-start | bytes 5013508
  710.6 186.8 %copy-start.37 = (f32[256,1088]{1,0:T(8,128)S(1)}, f32[256,1088]{1,0:T(8,128)}, u32[]{:S(2)}) copy-start(f32[256,1088]{1,0:T(8,128)} %get-tuple-element.110) | copy-start | bytes 3342340
  710.6 186.8 %copy-start.58 = (f32[256]{0:T(256)S(1)}, f32[256]{0:T(256)}, u32[]{:S(2)}) copy-start(f32[256]{0:T(256)} %copy-done.57) | copy-start | bytes 3076
  710.7 186.8 %copy-start.59 = (f32[256]{0:T(256)S(1)}, f32[256]{0:T(256)}, u32[]{:S(2)}) copy-start(f32[256]{0:T(256)} %add_rsqrt_fusion) | copy-start | bytes 3076
  902.1 8.4 collective-permute-start.12
  903.5 4.9 copy-start.46
  904.9 11.6 %collective-permute-start.13 = (bf16[2,544,1088]{2,1,0:T(8,128)(2,1)}, bf16[2,544,1088]{2,1,0:T(8,128)(2,1)}, u32[]{:S(2)}, u32[]{:S(2)}) collective-permute-start(bf16[2,544,1088]{2,1,0:T(8,128)(2,1)} %all-reduce.8.cloned.1.call-done), channel_id=1, source_target_pairs={{16,0},{17,1},{18,2},{19,3},{20,4},{21,5},{22,6},{23,7},{24,8},{25... | collective-permute-start | bytes 7102472 | tf_op jit(solution)/shard_map/ppermute | solution.py:1112
  924.7 4.5 copy-start.34
  924.7 4.5 copy-start.41
  (40 other events, 92.4 us)
Sparse Core Ops, SparseCore 0:
  86.1 82.8 all-gather.1
  610.7 99.8 all-reduce.5
  713.0 147.5 all-reduce.7

commit v5 on v4

--- a/solution.py
+++ b/solution.py
@@ -238,7 +238,8 @@
 
 
 def weights_kernel(
-    own, rows_in, full, rows_out, load, core_s, core_r, p_send, p_recv, f_send, f_recv, z_send, z_recv
+    own, rows_in, up_in, down_in, full, rows_out, up_out, down_out,
+    load, core_s, core_r, p_send, p_recv, f_send, f_recv, z_send, z_recv,
 ):
     s = lax.axis_index("section")
     f = lax.axis_index("fsdp")
@@ -330,6 +331,12 @@
         copies = hops(k)
         copies[0].start()
         copies[1].start()
+    down_far = to(down_in, down_out.at[s], core_s.at[4], core_r.at[4], section=1 - s)
+    down_near = pltpu.make_async_copy(down_in, down_out.at[s], load.at[4])
+    down_far.start()
+    down_near.start()
+    for j in range(4):
+        up_out[j] = up_in[:, pl.ds(j * D, D)]
     for k in range(2):
         copies, across = hops(k), here(k)
         copies[0].wait_recv()
@@ -370,6 +377,9 @@
         give(0).wait_recv()
         give(1).wait_recv()
 
+    down_near.wait()
+    down_far.wait()
+
     @pl.when(z < 3)
     def _():
         step_one.wait_send()
@@ -383,26 +393,28 @@
         step_two.wait_recv()
 
 
-def first_weights(own, rows_in):
+def first_weights(own, rows_in, up, down):
     dma = pltpu.SemaphoreType.DMA
     return pl.pallas_call(
         weights_kernel,
         out_shape=(
             jax.ShapeDtypeStruct((4, D, WIDE), BF),
             jax.ShapeDtypeStruct((3 * rows_in.shape[0], D), BF),
+            jax.ShapeDtypeStruct((4, up.shape[0], D), BF),
+            jax.ShapeDtypeStruct((2, D, D), BF),
         ),
-        in_specs=[pl.BlockSpec(memory_space=pl.ANY), VSPEC],
-        out_specs=(VSPEC, VSPEC),
+        in_specs=[pl.BlockSpec(memory_space=pl.ANY), VSPEC, VSPEC, pl.BlockSpec(memory_space=pl.ANY)],
+        out_specs=(VSPEC,) * 4,
         scratch_shapes=[
-            dma((4,)), dma((4,)), dma((4,)), dma((2, 4)), dma((2, 4)), dma((2, 3)), dma((2, 3)),
+            dma((5,)), dma((5,)), dma((5,)), dma((2, 4)), dma((2, 4)), dma((2, 3)), dma((2, 3)),
             dma((2,)), dma((2,)),
         ],
         compiler_params=pltpu.CompilerParams(
-            collective_id=4, has_side_effects=True, vmem_limit_bytes=16 * 1024 * 1024
+            collective_id=4, has_side_effects=True, vmem_limit_bytes=32 * 1024 * 1024
         ),
         cost_estimate=lasting(50),
         name="first_weights",
-    )(own, rows_in)
+    )(own, rows_in, up, down)
 
 
 def z_partners():
@@ -421,12 +433,12 @@
 
 
 def reduce_kernel(
-    q0, k0, v0, o0, q1, k1, v1, o1, mlp, halo,
-    qkv_out, out_out, down_out, up_out, rows_out,
-    own_in, held, up_own, up_far, sent, caught,
+    q0, k0, v0, o0, q1, k1, v1, o1, mlp, made0, made1, grad1, halo, d_resid, da_own, wide, par,
+    qkv_out, out_out, down_out, up_out, made_out, grad_out,
+    own_in, held, up_own, up_far, sent, caught, grad0,
     x1a, y1a, x2a, y2a, sxa, sya, ta, zaa, zba,
     x1b, y1b, x2b, y2b, sxb, syb, tb, zab, zbb,
-    load, core_s, core_r, p_send, p_recv, z_send, z_recv, h_send, h_recv,
+    load, core_s, core_r, p_send, p_recv, z_send, z_recv, h_send, h_recv, x_send, x_recv,
 ):
     s = lax.axis_index("section")
     f = lax.axis_index("fsdp")
@@ -439,7 +451,7 @@
         (x1b, y1b, x2b, y2b, sxb, syb, tb, zab, zbb),
     )
     shard = out_out.shape[0]
-    rows = rows_out.shape[0]
+    rows = da_own.shape[0]
     z = lax.axis_index("ctx")
     above, below = {"ctx": lax.rem(z + 1, 4)}, {"ctx": lax.rem(z + 3, 4)}
 
@@ -600,15 +612,52 @@
             add_rows(sent, halo.at[pl.ds(rows, rows)], caught.at[0], rows, rows)
             back_two.start()
 
+    made_far = (
+        to(made1, made_out.at[0], x_send.at[0], x_recv.at[0], section=1),
+        to(made0, made_out.at[1], x_send.at[0], x_recv.at[0], section=0),
+    )
+    grad_far = (
+        to(grad1, grad_out.at[0], x_send.at[1], x_recv.at[1], section=1),
+        to(grad0, grad_out.at[1], x_send.at[1], x_recv.at[1], section=0),
+    )
+    made_near = (
+        pltpu.make_async_copy(made0, made_out.at[0], load.at[6]),
+        pltpu.make_async_copy(made1, made_out.at[1], load.at[6]),
+    )
+    grad_near = pltpu.make_async_copy(grad1, grad_out.at[1], load.at[7])
+
     def back_end():
         @pl.when(z < 3)
         def _():
             back_two.wait_recv()
-            rows_out[...] = caught[1]
 
         @pl.when(z == 3)
         def _():
-            rows_out[...] = jnp.zeros_like(rows_out)
+            caught[1] = jnp.zeros_like(caught[1])
+
+        unit, inv = norm_parts(wide[...].astype(F32))
+        da = da_own[...] + caught[1].astype(F32)
+        grad0[...] = d_resid[...] + norm_back(da, par[0:1, :], unit, inv)
+
+        @pl.when(s == 0)
+        def _():
+            grad_out[0] = grad0[...]
+
+        @pl.when(s == 1)
+        def _():
+            grad_far[1].start()
+
+    @pl.when(s == 0)
+    def _():
+        made_far[0].start()
+        grad_far[0].start()
+        made_near[0].start()
+
+    @pl.when(s == 1)
+    def _():
+        made_far[1].start()
+        made_near[1].start()
+        grad_near.start()
 
     @pl.when(z > 0)
     def _():
@@ -646,6 +695,23 @@
     down_far.wait()
     far_up.wait_send()
 
+    @pl.when(s == 0)
+    def _():
+        made_near[0].wait()
+        made_far[0].wait_send()
+        grad_far[0].wait_send()
+        made_far[1].wait_recv()
+        grad_far[1].wait_recv()
+
+    @pl.when(s == 1)
+    def _():
+        made_near[1].wait()
+        grad_near.wait()
+        made_far[1].wait_send()
+        grad_far[1].wait_send()
+        made_far[0].wait_recv()
+        grad_far[0].wait_recv()
+
     @pl.when(z > 0)
     def _():
         back_one.wait_send()
@@ -669,9 +735,9 @@
             along(c)[0].wait_send()
 
 
-def reduce_both(zero, one, mlp, halo):
+def reduce_both(zero, one, mlp, made, grad1, halo, d_resid, da_own, wide, par):
     shard = D // 4
-    rows = halo.shape[0] // 2
+    rows = da_own.shape[0]
     dma = pltpu.SemaphoreType.DMA
     any_spec = pl.BlockSpec(memory_space=pl.ANY)
 
@@ -679,32 +745,74 @@
         return pltpu.VMEM(shape, BF)
 
     def part(_, width, cut):
-        wide = buf(4, shard, width)
+        wide_buf = buf(4, shard, width)
         return [
-            buf(4, shard, cut), buf(4, shard, width - cut), wide, wide,
-            buf(4, shard, width - cut), buf(4, shard, cut), wide, wide, wide,
+            buf(4, shard, cut), buf(4, shard, width - cut), wide_buf, wide_buf,
+            buf(4, shard, width - cut), buf(4, shard, cut), wide_buf, wide_buf, wide_buf,
         ]
 
+    shapes = ((shard, 3 * D), (shard, WIDE), (D, D), (shard, 4 * D), (2, rows, D))
     return pl.pallas_call(
         reduce_kernel,
-        out_shape=tuple(
-            jax.ShapeDtypeStruct(shape, BF)
-            for shape in ((shard, 3 * D), (shard, WIDE), (D, D), (shard, 4 * D), (rows, D))
+        out_shape=(
+            *(jax.ShapeDtypeStruct(shape, BF) for shape in shapes),
+            jax.ShapeDtypeStruct((2, rows, D), F32),
         ),
-        in_specs=[any_spec] * 9 + [VSPEC],
-        out_specs=(VSPEC,) * 5,
+        in_specs=[any_spec] * 12 + [VSPEC] * 5,
+        out_specs=(VSPEC,) * 6,
         scratch_shapes=[
             buf(2, D, WIDE), buf(4, D, WIDE), buf(D // 2, D), buf(D // 2, D), buf(rows, D),
-            buf(2, rows, D), *part(*CUTS[0]), *part(*CUTS[1]),
-            dma((6,)), dma((6,)), dma((6,)), dma((8, 6)), dma((8, 6)), dma((8, 3)), dma((8, 3)),
-            dma((2,)), dma((2,)),
+            buf(2, rows, D), pltpu.VMEM((rows, D), F32), *part(*CUTS[0]), *part(*CUTS[1]),
+            dma((8,)), dma((6,)), dma((6,)), dma((8, 6)), dma((8, 6)), dma((8, 3)), dma((8, 3)),
+            dma((2,)), dma((2,)), dma((2,)), dma((2,)),
         ],
         compiler_params=pltpu.CompilerParams(
-            collective_id=3, has_side_effects=True, vmem_limit_bytes=58 * 1024 * 1024
+            collective_id=3, has_side_effects=True, vmem_limit_bytes=60 * 1024 * 1024
         ),
         cost_estimate=lasting(120),
         name="reduce_both",
-    )(*zero, *one, mlp, halo)
+    )(*zero, *one, mlp, *made, grad1, halo, d_resid, da_own, wide, par)
+
+
+def final_kernel(qkv, out, mine, far, down_one, up_one, qkv_f, out_f, down_f, up_f, small):
+    s = lax.axis_index("section")
+    half = mine.shape[1]
+    shard = qkv.shape[0]
+    qkv_f[...] = qkv[...].astype(F32)
+    out_f[...] = out[:, pl.ds(0, D)].astype(F32)
+    pick_row = (
+        lax.broadcasted_iota(jnp.int32, (16, 128), 1)
+        == lax.broadcasted_iota(jnp.int32, (16, 128), 0) + (D - TAIL)
+    )
+    small[...] = mm_nt(pick_row.astype(F32).astype(BF), out[:, pl.ds(TAIL, 128)])
+
+    @pl.when(s == 0)
+    def _():
+        down_f[pl.ds(0, half), :] = mine[0].astype(F32)
+        down_f[pl.ds(half, half), :] = far[0].astype(F32)
+        for k in range(2):
+            at = pl.ds(k * shard, shard)
+            up_f[:, pl.ds(k * D, D)] = mine[1, at, :].astype(F32)
+            up_f[:, pl.ds((2 + k) * D, D)] = far[1, at, :].astype(F32)
+
+    @pl.when(s == 1)
+    def _():
+        down_f[...] = down_one[...].astype(F32)
+        up_f[...] = up_one[...].astype(F32)
+
+
+def final_layouts(qkv, out, mine, far, down_one, up_one):
+    shard = qkv.shape[0]
+    outs = (qkv.shape, (shard, D), down_one.shape, up_one.shape, (16, shard))
+    return pl.pallas_call(
+        final_kernel,
+        out_shape=tuple(jax.ShapeDtypeStruct(shape, F32) for shape in outs),
+        in_specs=[VSPEC] * 6,
+        out_specs=(VSPEC,) * 5,
+        compiler_params=pltpu.CompilerParams(vmem_limit_bytes=48 * 1024 * 1024),
+        cost_estimate=lasting(10),
+        name="final_layouts",
+    )(qkv, out, mine, far, down_one, up_one)
 
 
 def halves_pair(down, up):
@@ -1017,12 +1125,13 @@
         ]
     )
     if fits:
-        zero, wide_in = first_weights(packed, own_in)
-        packed, up_shard, down_shard, zero = lax.optimization_barrier(
-            (packed, up_weight[0], down_weight[0], zero)
-        )
+        zero, wide_in, up_blocks, down_w = first_weights(
+            packed, own_in, up_weight[0], down_weight[0]
+        )
+        packed, zero = lax.optimization_barrier((packed, zero))
     else:
-        up_shard, down_shard = up_weight[0], down_weight[0]
+        up_blocks = up_weight[0].reshape(shard, nf, ff_here).transpose(1, 0, 2)
+        down_w = both_layers(down_weight[0], s)
         wide_in = with_halo(own_in, chunks)
     half = shard // 2
     halves = packed.reshape(4, 2, half, WIDE)
@@ -1038,10 +1147,8 @@
     if not fits:
         zero = gathered(pick(s, keep, recv))
     up_own = lax.all_to_all(
-        up_shard.reshape(shard, nf, ff_here), "fsdp", split_axis=1, concat_axis=0, tiled=True
+        up_blocks, "fsdp", split_axis=0, concat_axis=0, tiled=True
     ).reshape(D, ff_here)
-    up_w = both_layers(up_own, s)
-    down_w = both_layers(down_shard, s)
 
     weights = (zero, one)
 
@@ -1051,6 +1158,9 @@
     for layer in range(2):
         wide = with_halo(current, chunks) if layer else wide_in
         normed, q, k, v, att, resid, second, par = block_forward(wide, weights[layer], bias)
+        if layer == 0:
+            up_own, second = lax.optimization_barrier((up_own, second))
+            up_w = both_layers(up_own, s)
         ffb = lax.dynamic_slice(par, (8, f * shard), (per_row, shard)).reshape(1, ff_here)
         current, second_all, active, slope = mlp_forward(
             second, up_w[layer], down_w[layer], ffb, resid, par
@@ -1105,31 +1215,33 @@
             upstream = upstream_next
 
     if fits:
-        qkv_g, out_g, down_one, up_one, late = reduce_both(
-            parts[0], parts[1], mlp_sums[1], da_halo
-        )
-        derived[0] = through_norm(late.astype(F32))
-        far = lax.ppermute(mlp_sums[0], "section", [(1, 0)])
-        down_zero, up_zero = split_up(jnp.concatenate([mlp_sums[0], far], axis=1), nf, shard)
-        grad_down = pick(s, down_zero, down_one).astype(F32)
-        grad_up = pick(s, up_zero, up_one).astype(F32)
-        qkv_g, out_g = qkv_g.astype(F32), out_g.astype(F32)
+        qkv_g, out_g, down_one, up_one, made, grads = reduce_both(
+            parts[0], parts[1], mlp_sums[1], produced, derived[1], da_halo, d_resid, da_own,
+            wide[reach:], par,
+        )
+        late_sum, qkv_g = lax.optimization_barrier((mlp_sums[0], qkv_g))
+        far = lax.ppermute(late_sum, "section", [(1, 0)])
+        qkv_g, out_g, grad_down, grad_up, small = final_layouts(
+            qkv_g, out_g, late_sum, far, down_one, up_one
+        )
+        made, grads = made[None, :, None], grads[None, :, None]
     else:
         a_tot = pick(s, reduce_plain(parts[0]), reduce_plain(parts[1])).astype(F32)
         qkv_g = jnp.concatenate([a_tot[i, :, :D] for i in range(3)], axis=1)
-        out_g = a_tot[3]
+        out_g = a_tot[3, :, :D]
+        small = a_tot[3, :, D : D + 16].T
         grad_down, grad_up = split_up(halves_settle(*mlp_sums), nf, shard)
-    vectors = out_g[:, D : D + 8].T
+        made, grads = both_micros(produced, s), both_micros(derived, s)
     return (
-        both_micros(produced, s),
-        both_micros(derived, s),
+        made,
+        grads,
         qkv_g[None],
-        out_g[None, :, :D],
+        out_g[None],
         grad_up[None],
         grad_down[None],
-        vectors[None, :2],
-        vectors[None, 2:],
-        out_g[:, D + 8 : D + 8 + per_row].T.reshape(1, ff_here),
+        small[None, :2],
+        small[None, 2:8],
+        small[8 : 8 + per_row].reshape(1, ff_here),
     )
 
 

time: 951 us -> 901 us (0.947)
  local copies, waits for them, and re-layouts: 87.6 us -> 63.5 us
  other arithmetic: 59.7 us -> 37.7 us
  Pallas kernels: 541 us -> 555 us
  matrix products: 63.6 us -> 50.2 us
    all_to_all x1, waiting for transfers between devices: 37.8 us -> 15.6 us  [on_device(): lax.all_to_all(up_blocks, 'fsdp', split_axis=0, concat_axis=0, tiled=True)]
    ppermute x4, waiting for transfers between devices: 18.3 us -> 35 us  [shift(): return lax.ppermute(value, 'ctx', pairs)]
    pallas_call x4, Pallas kernels: 184 us -> 200 us  [plane_call(): pl.pallas_call(kernel, out_shape=outs, in_specs=[VSPEC] * len(operands),...]
    dot_general x12, matrix products: 63.6 us -> 50.2 us  [mm_tn(): lax.dot_general(a, b, (((0,), (0,)), ((), ())), preferred_element_type=F32)]
    psum x2, waiting for transfers between devices: 76.9 us -> 87.9 us  [on_device(): mlp_sums[layer] = lax.psum(halves, 'ctx')]
    reshape x4 -> x1, local copies, waits for them, and re-layouts: 10.8 us -> 0.68 us  [on_device(): small[8:8 + per_row].reshape(1, ff_here)]
    pallas_call x1 -> x2, Pallas kernels: 187 us -> 181 us  [the longest x1 171 us: reduce_both(): pl.pallas_call(reduce_kernel, out_shape=(*(jax.ShapeDtypeStruct(shape, BF...]
    unnamed x144 -> x128, local copies, waits for them, and re-layouts: 30.7 us -> 26.1 us
  transfers between devices with their start and end apart: 20 -> 15, of which waited for: 6 -> 9; matrix products, arithmetic and copies ran while one was open for 17% -> 11% of each run, Pallas kernels for 52% -> 37%
where the time goes in v5:
time: 901 us; the launch traced here: 891 us
  Pallas kernels  555 us (62%)
  waiting for transfers between devices  142 us (16%)
  local copies, waits for them, and re-layouts  63.5 us (7%)
  matrix products  50.2 us (6%)
  other arithmetic  37.7 us (4%)
  starting transfers between devices  27 us (3%)
  between operations  14.8 us (2%)
    pallas_call x4, Pallas kernels, plane_call(): pl.pallas_call(kernel, out_shape=outs, in_specs=[VSPEC] * len(operands),...  200 us
    pallas_call x1, Pallas kernels, reduce_both(): pl.pallas_call(reduce_kernel, out_shape=(*(jax.ShapeDtypeStruct(shape, BF...  171 us
    psum x2, waiting for transfers between devices, on_device(): mlp_sums[layer] = lax.psum(halves, 'ctx')  87.9 us
    pallas_call x2, Pallas kernels, block_backward(): pl.pallas_call(block_back_kernel, out_shape=tuple((jax.ShapeDtypeStruct(*...  67.6 us
    pallas_call x1, Pallas kernels, first_weights(): pl.pallas_call(weights_kernel, out_shape=(jax.ShapeDtypeStruct((4, D, WID...  57 us
    dot_general x12, matrix products, mm_tn(): lax.dot_general(a, b, (((0,), (0,)), ((), ())), preferred_element_type=F32)  50.2 us
    pallas_call x2, Pallas kernels, block_forward(): pl.pallas_call(block_kernel, out_shape=tuple((jax.ShapeDtypeStruct(*out)...  49.5 us
    ppermute x4, waiting for transfers between devices, shift(): return lax.ppermute(value, 'ctx', pairs)  35 us
  transfers between devices with their start and end apart: 15, of which 9 were waited for; matrix products, arithmetic and copies ran while one was open for 11% of the time, Pallas kernels for 37%

profile of v5, /device:TPU:0, one launch (start us, length us, event | category | flops | bytes accessed | tf_op | source)
XLA Modules:
  0.0 890.9 jit_solution(5382977391660843907)
XLA Ops:
  16.1 2.2 pad_maximum_fusion.own
  19.2 57.0 %first_weights.1 = (bf16[4,1088,1152]{2,1,0:T(8,128)(2,1)}, bf16[768,1088]{1,0:T(8,128)(2,1)S(1)}, bf16[4,272,1088]{2,1,0:T(8,128)(2,1)}, bf16[2,1088,1088]{2,1,0:T(8,128)(2,1)S(1)}) custom-call(bf16[4,272,1152]{2,1,0:T(8,128)(2,1)S(1)} %pad_maximum_fusion.own, bf16[256,1088]{1,0:T(8,128)(2,1)S(1)} %bitcast.109, bf16[272,4352]{1,0:T(8,128)(2,1)S(1)} %bitcast.108, ...), custom_call_target="tpu_custom_call" | custom-call | bytes 175000000 | tf_op jit(solution)/shard_map/first_weights/pallas_call | solution.py:398
  77.5 2.3 copy-done.12
  81.7 3.1 collective-permute-done.3
  88.0 3.7 all-to-all-start
  92.8 25.2 %block_forward.2 = (bf16[768,1088]{1,0:T(8,128)(2,1)}, bf16[256,1152]{1,0:T(8,128)(2,1)}, bf16[768,1152]{1,0:T(8,128)(2,1)}, bf16[768,1152]{1,0:T(8,128)(2,1)}, ...) custom-call(bf16[768,1088]{1,0:T(8,128)(2,1)} %copy-done.9, ...), custom_call_target="tpu_custom_call" | custom-call | bytes 77000000 | tf_op jit(solution)/shard_map/block_forward/pallas_call | solution.py:978
  118.0 15.6 %all-to-all-done = bf16[4,272,1088]{2,1,0:T(8,128)(2,1)S(1)} async-done(((bf16[4,272,1088]{2,1,0:T(8,128)(2,1)}), bf16[4,272,1088]{2,1,0:T(8,128)(2,1)S(1)}, u32[]{:S(2)}, u32[]{:S(2)}) %all-to-all-start) | async-done | bytes 2367520 | tf_op jit(solution)/shard_map/all_to_all | solution.py:1149
  134.5 4.4 slice_bitcast_fusion
  139.5 5.2 broadcast_select_fusion
  144.8 66.3 %shard_map.169 = (bf16[256,1088]{1,0:T(8,128)(2,1)S(1)}, bf16[4,256,1088]{2,1,0:T(8,128)(2,1)S(1)}, bf16[4,256,1088]{2,1,0:T(8,128)(2,1)S(1)}, f32[4,256,1088]{2,1,0:T(8,128)}) custom-call(bf16[256,1088]{1,0:T(8,128)(2,1)S(1)} %copy-done.23, bf16[1088,1088]{1,0:T(8,128)(2,1)S(1)} %get-tuple-element.200.up, bf16[1088,1088]{1,0:T(8,128)(2,1)S(1)} %get-tuple-element.198.down, ...), custom_call_target="tpu_custom_call" | custom-call | bytes 140000000 | tf_op jit(solution)/shard_map/pallas_call | solution.py:171
  215.0 4.2 collective-permute-start.1
  219.3 10.6 %collective-permute-done.1 = bf16[256,1088]{0,1:T(8,128)(2,1)} collective-permute-done((bf16[256,1088]{0,1:T(8,128)(2,1)}, bf16[256,1088]{0,1:T(8,128)(2,1)}, u32[]{:S(2)}, u32[]{:S(2)}) %collective-permute-start.1) | collective-permute-done | bytes 557088 | tf_op jit(solution)/shard_map/ppermute | solution.py:845
  229.9 5.2 collective-permute-start.2
  235.1 2.2 copy.88
  239.4 5.5 collective-permute-done.2
  247.0 2.6 pad_maximum_fusion.1.wide
  249.6 24.4 %block_forward.3 = (bf16[768,1088]{1,0:T(8,128)(2,1)}, bf16[256,1152]{1,0:T(8,128)(2,1)}, bf16[768,1152]{1,0:T(8,128)(2,1)}, bf16[768,1152]{1,0:T(8,128)(2,1)}, ...) custom-call(bf16[768,1088]{1,0:T(8,128)(2,1)} %pad_maximum_fusion.1.wide, ...), custom_call_target="tpu_custom_call" | custom-call | bytes 77000000 | tf_op jit(solution)/shard_map/block_forward/pallas_call | solution.py:978
  281.4 42.8 %shard_map.170 = (bf16[256,1088]{1,0:T(8,128)(2,1)S(1)}, bf16[4,256,1088]{2,1,0:T(8,128)(2,1)S(1)}, bf16[4,256,1088]{2,1,0:T(8,128)(2,1)S(1)}, f32[4,256,1088]{2,1,0:T(8,128)}) custom-call(bf16[256,1088]{1,0:T(8,128)(2,1)S(1)} %copy-done.24, bf16[1088,1088]{1,0:T(8,128)(2,1)S(1)} %copy-done.3, bf16[1088,1088]{1,0:T(8,128)(2,1)S(1)} %copy-done.7, ...), custom_call_target="tpu_custom_call" | custom-call | bytes 140000000 | tf_op jit(solution)/shard_map/pallas_call | solution.py:171
  324.3 44.1 %shard_map.171 = (f32[256,1088]{1,0:T(8,128)S(1)}, bf16[4,256,1088]{2,1,0:T(8,128)(2,1)S(1)}, bf16[4,256,1088]{2,1,0:T(8,128)(2,1)S(1)}, f32[1,1088]{1,0:T(1,128)S(1)}) custom-call(bf16[256,1088]{1,0:T(8,128)(2,1)S(1)} %bitcast.106, bf16[1088,1088]{1,0:T(8,128)(2,1)S(1)} %copy-done.4, bf16[1088,1088]{1,0:T(8,128)(2,1)S(1)} %copy-done.8, ...), custom_call_target="tpu_custom_call" | custom-call | bytes 140000000 | tf_op jit(solution)/shard_map/pallas_call | solution.py:171
  368.5 4.6 fusion.1
  373.1 4.5 all-to-all-start.1
  380.1 33.8 %block_backward.2 = (f32[256,1088]{1,0:T(8,128)}, bf16[256,1152]{1,0:T(8,128)(2,1)}, bf16[768,1152]{1,0:T(8,128)(2,1)}, bf16[768,1152]{1,0:T(8,128)(2,1)}, f32[2...) custom-call(f32[256,1088]{1,0:T(8,128)} %copy-done.20, ...), custom_call_target="tpu_custom_call" | custom-call | bytes 133000000 | tf_op jit(solution)/shard_map/block_backward/pallas_call | solution.py:1066
  419.3 6.9 fusion
  426.2 4.5 collective-permute-done.5
  432.8 3.6 fusion.11
  442.2 14.4 %collective-permute-done.6 = bf16[256,1088]{0,1:T(8,128)(2,1)} collective-permute-done((bf16[256,1088]{0,1:T(8,128)(2,1)}, bf16[256,1088]{0,1:T(8,128)(2,1)}, u32[]{:S(2)}, u32[]{:S(2)}) %collective-permute-start.6) | collective-permute-done | bytes 557088 | tf_op jit(solution)/shard_map/ppermute | solution.py:845
  460.9 3.2 fusion.31
  464.1 4.3 fusion.5
  470.0 47.3 %shard_map.172 = (f32[256,1088]{1,0:T(8,128)S(1)}, bf16[4,256,1088]{2,1,0:T(8,128)(2,1)S(1)}, bf16[4,256,1088]{2,1,0:T(8,128)(2,1)S(1)}, f32[1,1088]{1,0:T(1,128)S(1)}) custom-call(bf16[256,1088]{1,0:T(8,128)(2,1)S(1)} %copy-done.10, bf16[1088,1088]{1,0:T(8,128)(2,1)S(1)} %get-tuple-element.200.up, bf16[1088,1088]{1,0:T(8,128)(2,1)S(1)} %copy-done.6, ...), custom_call_target="tpu_custom_call" | custom-call | bytes 140000000 | tf_op jit(solution)/shard_map/pallas_call | solution.py:171
  517.3 4.6 fusion.3
  521.9 4.5 all-to-all-start.2
  527.9 33.9 %block_backward.3 = (f32[256,1088]{1,0:T(8,128)}, bf16[256,1152]{1,0:T(8,128)(2,1)}, bf16[768,1152]{1,0:T(8,128)(2,1)}, bf16[768,1152]{1,0:T(8,128)(2,1)}, f32[2...) custom-call(f32[256,1088]{1,0:T(8,128)} %copy-done.19, ...), custom_call_target="tpu_custom_call" | custom-call | bytes 133000000 | tf_op jit(solution)/shard_map/block_backward/pallas_call | solution.py:1066
  561.8 6.3 fusion.2
  568.1 3.4 fusion.7
  573.7 4.3 convolution_convert_fusion.6.o1
  578.0 3.8 convolution_convert_fusion.2.v1
  581.8 3.4 fusion.4
  585.2 87.9 %all-reduce.6.cloned.1.call-done.mlp = bf16[2,544,1088]{2,1,0:T(8,128)(2,1)} async-done(((bf16[2,544,1088]{2,1,0:T(8,128)(2,1)}), bf16[2,544,1088]{2,1,0:T(8,128)(2,1)}) %all-reduce.6.cloned.1.call-update) | async-done | bytes 2367504 | tf_op jit(solution)/shard_map/psum | solution.py:1213
  673.2 2.4 convolution_convert_fusion.q1
  675.6 3.9 convolution_convert_fusion.3.k1
  679.5 2.4 convolution_convert_fusion.1.q0
  681.8 3.1 convolution_convert_fusion.7.o0
  684.9 4.1 convolution_convert_fusion.4.v0
  689.0 3.8 convolution_convert_fusion.5.k0
  692.9 170.9 %reduce_both.1 = (bf16[272,3264]{1,0:T(8,128)(2,1)}, bf16[272,1152]{1,0:T(8,128)(2,1)}, bf16[1088,1088]{1,0:T(8,128)(2,1)}, bf16[272,4352]{1,0:T(8,128)(2,1)}, b...) custom-call(bf16[1088,1152]{1,0:T(8,128)(2,1)} %convolution_convert_fusion.1.q0, ...), custom_call_target="tpu_custom_call" | custom-call | bytes 420000000 | tf_op jit(solution)/shard_map/reduce_both/pallas_call | solution.py:755
  865.1 3.1 copy.102
  868.3 2.3 copy.101
  872.3 9.8 %final_layouts.1 = (f32[272,3264]{1,0:T(8,128)}, f32[272,1088]{1,0:T(8,128)}, f32[1088,1088]{1,0:T(8,128)}, f32[272,4352]{1,0:T(8,128)}, f32[16,272]{1,0:T(8,128)S(1)}) custom-call(bf16[272,3264]{1,0:T(8,128)(2,1)S(1)} %copy-done.18, bf16[272,1152]{1,0:T(8,128)(2,1)S(1)} %copy-done.22, bf16[2,544,1088]{2,1,0:T(8,128)(2,1)} %all-reduce.8.cloned.1.call-done.mine, ...), custom_call_target="tpu_custom_call" | custom-call | bytes 35000000 | tf_op jit(solution)/shard_map/final_layouts/pallas_call | solution.py:807
  (198 shorter events, 64.8 us)
Async XLA Ops:
  7.2 84.5 %copy-start = (s32[2,1,1024]{2,1,0:T(1,128)S(1)}, s32[2,1,1024]{2,1,0:T(1,128)}, u32[]{:S(2)}) copy-start(s32[2,1,1024]{2,1,0:T(1,128)} %param.11) | copy-start | bytes 24580
  7.2 242.4 %all-gather.2.cloned.1.call-start = ((), (), s32[]{:S(2)}) async-start(), calls=%async_computation.3 | async-start | bytes 11280384 | tf_op jit(solution)/shard_map/all_gather | solution.py:1143
  9.3 3.9 copy-start.51
  9.3 4.2 copy-start.53
  9.3 4.3 copy-start.50
  81.6 3.1 collective-permute-start.3
  88.0 45.6 %all-to-all-start = ((bf16[4,272,1088]{2,1,0:T(8,128)(2,1)}), bf16[4,272,1088]{2,1,0:T(8,128)(2,1)S(1)}, u32[]{:S(2)}, u32[]{:S(2)}) async-start(bf16[4,272,1088]{2,1,0:T(8,128)(2,1)} %get-tuple-element.87), calls=%async_computation | async-start | bytes 5013504 | tf_op jit(solution)/shard_map/all_to_all | solution.py:1149
  133.6 5.3 copy-start.34
  133.6 5.9 collective-permute-start
  138.9 5.8 copy-start.5
  138.9 5.8 copy-start.13
  138.9 5.8 copy-start.21
  138.9 5.8 copy-start.23
  214.0 246.8 %copy-start.2 = (bf16[256,1088]{1,0:T(8,128)(2,1)}, bf16[256,1088]{1,0:T(8,128)(2,1)S(1)}, u32[]{:S(2)}) copy-start(bf16[256,1088]{1,0:T(8,128)(2,1)S(1)} %get-tuple-element.94.made0) | copy-start | bytes 1671172
  215.0 14.9 %collective-permute-start.1 = (bf16[256,1088]{0,1:T(8,128)(2,1)}, bf16[256,1088]{0,1:T(8,128)(2,1)}, u32[]{:S(2)}, u32[]{:S(2)}) collective-permute-start(bf16[256,1088]{0,1:T(8,128)(2,1)} %copy.83), channel_id=1, source_target_pairs={{0,1},{1,2},{2,3},{4,5},{5,6},{6,7},{8,9},{9,10},{10,11},{12,13},{... | collective-permute-start | bytes 1671176 | tf_op jit(solution)/shard_map/ppermute | solution.py:845
  229.9 14.9 %collective-permute-start.2 = (bf16[256,1088]{0,1:T(8,128)(2,1)}, bf16[256,1088]{0,1:T(8,128)(2,1)}, u32[]{:S(2)}, u32[]{:S(2)}) collective-permute-start(bf16[256,1088]{0,1:T(8,128)(2,1)} %collective-permute-done.1), channel_id=1, source_target_pairs={{0,1},{1,2},{2,3},{4,5},{5,6},{6,7},{8,9},{9,10},{10,11},{12,13},{... | collective-permute-start | bytes 1671176 | tf_op jit(solution)/shard_map/ppermute | solution.py:845
  281.4 42.9 %copy-start.4 = (bf16[1088,1088]{1,0:T(8,128)(2,1)S(1)}, bf16[1088,1088]{1,0:T(8,128)(2,1)}, u32[]{:S(2)}) copy-start(bf16[1088,1088]{1,0:T(8,128)(2,1)} %get-tuple-element.199.up) | copy-start | bytes 7102468
  281.4 42.9 %copy-start.8 = (bf16[1088,1088]{1,0:T(8,128)(2,1)S(1)}, bf16[1088,1088]{1,0:T(8,128)(2,1)}, u32[]{:S(2)}) copy-start(bf16[1088,1088]{1,0:T(8,128)(2,1)} %get-tuple-element.197.down) | copy-start | bytes 7102468
  281.4 42.9 %copy-start.11 = (bf16[1,1,256,1088]{3,2,1,0:T(8,128)(2,1)S(1)}, bf16[1,1,256,1088]{3,2,1,0:T(8,128)(2,1)}, u32[]{:S(2)}) copy-start(bf16[1,1,256,1088]{3,2,1,0:T(8,128)(2,1)} %copy.88) | copy-start | bytes 1671172
  324.3 44.2 %copy-start.25 = (bf16[256,1088]{1,0:T(8,128)(2,1)}, bf16[256,1088]{1,0:T(8,128)(2,1)S(1)}, u32[]{:S(2)}) copy-start(bf16[256,1088]{1,0:T(8,128)(2,1)S(1)} %get-tuple-element.139.made1) | copy-start | bytes 1671172
  324.3 44.2 %copy-start.31 = (bf16[4,256,1088]{2,1,0:T(8,128)(2,1)}, bf16[4,256,1088]{2,1,0:T(8,128)(2,1)S(1)}, u32[]{:S(2)}) copy-start(bf16[4,256,1088]{2,1,0:T(8,128)(2,1)S(1)} %get-tuple-element.99) | copy-start | bytes 6684676
  368.5 4.6 copy-start.20
  368.5 4.6 copy-start.32
  373.1 59.7 %all-to-all-start.1 = ((bf16[4,272,1088]{2,1,0:T(8,128)(2,1)}), bf16[4,272,1088]{2,1,0:T(8,128)(2,1)}, u32[]{:S(2)}, u32[]{:S(2)}) async-start(bf16[4,272,1088]{2,1,0:T(8,128)(2,1)} %bitcast.118), calls=%async_computation.1 | async-start | bytes 5013504 | tf_op jit(solution)/shard_map/all_to_all | solution.py:1201
  418.0 12.7 %collective-permute-start.5 = (bf16[256,1088]{0,1:T(8,128)(2,1)}, bf16[256,1088]{0,1:T(8,128)(2,1)}, u32[]{:S(2)}, u32[]{:S(2)}) collective-permute-start(bf16[256,1088]{0,1:T(8,128)(2,1)} %copy.93), channel_id=1, source_target_pairs={{1,0},{2,1},{3,2},{5,4},{6,5},{7,6},{9,8},{10,9},{11,10},{13,12},{... | collective-permute-start | bytes 1671176 | tf_op jit(solution)/shard_map/ppermute | solution.py:845
  436.3 27.7 %collective-permute-start.4 = (bf16[2,544,1088]{2,1,0:T(8,128)(2,1)}, bf16[2,544,1088]{2,1,0:T(8,128)(2,1)}, u32[]{:S(2)}, u32[]{:S(2)}) collective-permute-start(bf16[2,544,1088]{2,1,0:T(8,128)(2,1)} %fusion.11), channel_id=1, source_target_pairs={{0,16},{16,0},{1,17},{17,1},{2,18},{18,2},{3,19},{19,3},{4,20},{20... | collective-permute-start | bytes 7102472 | tf_op jit(solution)/shard_map/ppermute | solution.py:869
  439.4 17.2 %collective-permute-start.6 = (bf16[256,1088]{0,1:T(8,128)(2,1)}, bf16[256,1088]{0,1:T(8,128)(2,1)}, u32[]{:S(2)}, u32[]{:S(2)}) collective-permute-start(bf16[256,1088]{0,1:T(8,128)(2,1)} %copy.95), channel_id=1, source_target_pairs={{1,0},{2,1},{3,2},{5,4},{6,5},{7,6},{9,8},{10,9},{11,10},{13,12},{... | collective-permute-start | bytes 1671176 | tf_op jit(solution)/shard_map/ppermute | solution.py:845
  464.1 4.3 copy-start.10
  470.0 47.3 %copy-start.30 = (bf16[4,256,1088]{2,1,0:T(8,128)(2,1)S(1)}, bf16[4,256,1088]{2,1,0:T(8,128)(2,1)}, u32[]{:S(2)}) copy-start(bf16[4,256,1088]{2,1,0:T(8,128)(2,1)} %copy-done.29) | copy-start | bytes 6684676
  517.3 4.6 copy-start.19
  517.3 4.6 copy-start.33
  521.9 46.1 %all-to-all-start.2 = ((bf16[4,272,1088]{2,1,0:T(8,128)(2,1)}), bf16[4,272,1088]{2,1,0:T(8,128)(2,1)}, u32[]{:S(2)}, u32[]{:S(2)}) async-start(bf16[4,272,1088]{2,1,0:T(8,128)(2,1)} %bitcast.32), calls=%async_computation.2 | async-start | bytes 5013504 | tf_op jit(solution)/shard_map/all_to_all | solution.py:1201
  526.5 146.6 %all-reduce.6.cloned.1.call-start = ((), (), s32[]{:S(2)}) async-start(), calls=%async_computation.4 | async-start | bytes 5013504 | tf_op jit(solution)/shard_map/psum | solution.py:1213
  527.9 33.9 %copy-start.28 = (bf16[4,256,1088]{2,1,0:T(8,128)(2,1)S(1)}, bf16[4,256,1088]{2,1,0:T(8,128)(2,1)}, u32[]{:S(2)}) copy-start(bf16[4,256,1088]{2,1,0:T(8,128)(2,1)} %copy-done.27) | copy-start | bytes 6684676
  571.5 10.3 %collective-permute-start.7 = (bf16[2,544,1088]{2,1,0:T(8,128)(2,1)}, bf16[2,544,1088]{2,1,0:T(8,128)(2,1)S(1)}, u32[]{:S(2)}, u32[]{:S(2)}) collective-permute-start(bf16[2,544,1088]{2,1,0:T(8,128)(2,1)} %fusion.7), channel_id=1, source_target_pairs={{0,16},{16,0},{1,17},{17,1},{2,18},{18,2},{3,19},{19,3},{4,20},{20... | collective-permute-start | bytes 7102472 | tf_op jit(solution)/shard_map/ppermute | solution.py:869
  571.5 292.3 %all-reduce.8.cloned.1.call-start = ((), (), s32[]{:S(2)}) async-start(), calls=%async_computation.5 | async-start | bytes 5013504 | tf_op jit(solution)/shard_map/psum | solution.py:1213
  573.7 4.3 copy-start.44
  573.7 4.3 copy-start.55
  578.0 3.8 copy-start.36
  585.2 87.9 %copy-start.45 = (bf16[768,1088]{1,0:T(8,128)(2,1)S(1)}, bf16[768,1088]{1,0:T(8,128)(2,1)}, u32[]{:S(2)}) copy-start(bf16[768,1088]{1,0:T(8,128)(2,1)} %get-tuple-element.126) | copy-start | bytes 5013508
  585.2 87.9 %copy-start.46 = (bf16[256,1152]{1,0:T(8,128)(2,1)S(1)}, bf16[256,1152]{1,0:T(8,128)(2,1)}, u32[]{:S(2)}) copy-start(bf16[256,1152]{1,0:T(8,128)(2,1)} %get-tuple-element.127) | copy-start | bytes 1769476
  675.6 3.9 copy-start.43
  675.6 3.9 copy-start.47
  684.9 4.1 copy-start.56
  863.8 7.0 collective-permute-start.8
  865.1 5.7 copy-start.17
  865.1 5.7 copy-start.22
  872.3 11.7 %copy-start.1 = (s32[2,1,1024]{2,1,0:T(1,128)S(1)}, s32[2,1,1024]{2,1,0:T(1,128)}, u32[]{:S(2)}) copy-start(s32[2,1,1024]{2,1,0:T(1,128)} %param.11) | copy-start | bytes 24580
  (28 other events, 59.4 us)
Sparse Core Ops, SparseCore 0:
  88.1 96.0 all-gather.1
  571.6 101.4 all-reduce.5
  675.5 141.0 all-reduce.7

commit v6 on v5

--- a/solution.py
+++ b/solution.py
@@ -95,19 +95,29 @@
     to_x.start()
     to_y.start()
     all_ref[0] = own_ref[...]
-    compute(0)
-    to_x.wait_recv()
-    far_y.start()
-    to_y.wait_recv()
-    far_x.start()
-    compute(1)
-    own_x.start()
-    far_x.wait_recv()
-    far_y.wait_recv()
-    compute(3)
-    first_x.start()
-    first_y.start()
-    compute(2)
+
+    @pl.loop(0, 4)
+    def _(i):
+        @pl.when(i == 1)
+        def _():
+            to_x.wait_recv()
+            far_y.start()
+            to_y.wait_recv()
+            far_x.start()
+
+        @pl.when(i == 2)
+        def _():
+            own_x.start()
+            far_x.wait_recv()
+            far_y.wait_recv()
+
+        @pl.when(i == 3)
+        def _():
+            first_x.start()
+            first_y.start()
+
+        compute(i + (i // 2) * (1 - 2 * lax.rem(i, 2)))
+
     own_y.start()
     first_x.wait_recv()
     sum_y[...] = (parts[2, top, :].astype(F32) + x1[...].astype(F32)).astype(BF)
@@ -133,10 +143,16 @@
         out[at, :] = (resid[at, :] + value + par[7:8, :]).astype(BF)
 
     def compute(r):
-        z = mm(all_ref[r], up[...]) + bias[...]
-        cdf, pdf = phi_parts(z)
-        active[r] = (z * cdf).astype(BF)
-        slope[r] = cdf + z * pdf
+        slope[r] = mm(all_ref[r], up[...]) + bias[...]
+
+        @pl.loop(0, own.shape[0] // 64)
+        def _(j):
+            at = pl.ds(pl.multiple_of(j * 64, 64), 64)
+            z = slope[r, at, :]
+            cdf, pdf = phi_parts(z)
+            active[r, at, :] = (z * cdf).astype(BF)
+            slope[r, at, :] = cdf + z * pdf
+
         parts[r] = mm(active[r], down[...]).astype(BF)
 
     exchange_rows(own, all_ref, parts, compute, finish, (x1, y1, x2, y2, sx, sy), send, recv)
@@ -511,7 +527,7 @@
     def join(j):
         far(j, q0).wait_recv()
         near(j, q0).wait()
-        add_rows(held.at[j], own_in.at[j % 2], held.at[j], 4 * shard, shard)
+        add_rows(held.at[j], own_in.at[j % 2], held.at[j], 4 * shard, 64)
         for c in (2 * j, 2 * j + 1):
             for copy in plane(c)[:4]:
                 copy.start()
@@ -524,10 +540,10 @@
         at, width, cut = CUTS[c % 2]
         own = held.at[c // 2]
         copies[0].wait_recv()
-        add_rows(sy, own.at[blk(yn), pl.ds(at, cut)], x1, shard, shard)
+        add_rows(sy, own.at[blk(yn), pl.ds(at, cut)], x1, shard, 16)
         copies[5].start()
         copies[1].wait_recv()
-        add_rows(sx, own.at[blk(xn), pl.ds(at + cut, width - cut)], y1, shard, shard)
+        add_rows(sx, own.at[blk(xn), pl.ds(at + cut, width - cut)], y1, shard, 16)
         copies[4].start()
 
     def third(c):
@@ -536,11 +552,14 @@
         at, width, _ = CUTS[c % 2]
         for copy in copies[2:]:
             copy.wait_recv()
-        t[...] = (
-            held[c // 2, blk(f), pl.ds(at, width)].astype(F32)
-            + x2[...].astype(F32)
-            + y2[...].astype(F32)
-        ).astype(BF)
+        own = held.at[c // 2, blk(f), pl.ds(at, width)]
+
+        @pl.loop(0, shard // 16)
+        def _(i):
+            part = pl.ds(pl.multiple_of(i * 16, 16), 16)
+            t[part, :] = (
+                own[part, :].astype(F32) + x2[part, :].astype(F32) + y2[part, :].astype(F32)
+            ).astype(BF)
 
         @pl.when(jnp.logical_not(inner))
         def _():
@@ -552,7 +571,7 @@
             t, za, _ = bufs(c)[6:]
             copies = along(c)
             copies[0].wait_recv()
-            add_rows(za, t, za, shard, shard)
+            add_rows(za, t, za, shard, 16)
             copies[1].start()
 
     def crossed(c):
@@ -561,7 +580,7 @@
             _, za, zb = bufs(c)[6:]
             copies = along(c)
             copies[1].wait_recv()
-            add_rows(zb, za, zb, shard, shard)
+            add_rows(zb, za, zb, shard, 16)
             copies[2].start()
 
     def last(c):
@@ -572,11 +591,16 @@
         def _():
             along(c)[2].wait_recv()
 
-        if j < 3:
-            width = min(width, D - at)
-            qkv_out[:, pl.ds(j * D + at, width)] = bufs(c)[8][:, pl.ds(0, width)]
-        else:
-            out_out[:, pl.ds(at, width)] = bufs(c)[8][...]
+        done = bufs(c)[8]
+        keep = min(width, D - at) if j < 3 else width
+
+        @pl.loop(0, shard // 16)
+        def _(i):
+            part = pl.ds(pl.multiple_of(i * 16, 16), 16)
+            if j < 3:
+                qkv_out[part, pl.ds(j * D + at, keep)] = done[part, pl.ds(0, keep)]
+            else:
+                out_out[part, pl.ds(at, keep)] = done[part, :]
 
     half = down_out.shape[0] // 2
     mine = pl.ds(pl.multiple_of(s * half, 16), half)
@@ -609,7 +633,7 @@
 
         @pl.when(z > 0)
         def _():
-            add_rows(sent, halo.at[pl.ds(rows, rows)], caught.at[0], rows, rows)
+            add_rows(sent, halo.at[pl.ds(rows, rows)], caught.at[0], rows, 64)
             back_two.start()
 
     made_far = (
@@ -778,27 +802,43 @@
     s = lax.axis_index("section")
     half = mine.shape[1]
     shard = qkv.shape[0]
-    qkv_f[...] = qkv[...].astype(F32)
-    out_f[...] = out[:, pl.ds(0, D)].astype(F32)
     pick_row = (
         lax.broadcasted_iota(jnp.int32, (16, 128), 1)
         == lax.broadcasted_iota(jnp.int32, (16, 128), 0) + (D - TAIL)
     )
     small[...] = mm_nt(pick_row.astype(F32).astype(BF), out[:, pl.ds(TAIL, 128)])
 
-    @pl.when(s == 0)
-    def _():
-        down_f[pl.ds(0, half), :] = mine[0].astype(F32)
-        down_f[pl.ds(half, half), :] = far[0].astype(F32)
-        for k in range(2):
-            at = pl.ds(k * shard, shard)
-            up_f[:, pl.ds(k * D, D)] = mine[1, at, :].astype(F32)
-            up_f[:, pl.ds((2 + k) * D, D)] = far[1, at, :].astype(F32)
-
-    @pl.when(s == 1)
-    def _():
-        down_f[...] = down_one[...].astype(F32)
-        up_f[...] = up_one[...].astype(F32)
+    @pl.loop(0, shard // 16)
+    def _(i):
+        at = pl.ds(pl.multiple_of(i * 16, 16), 16)
+        qkv_f[at, :] = qkv[at, :].astype(F32)
+        out_f[at, :] = out[at, pl.ds(0, D)].astype(F32)
+
+        @pl.when(s == 0)
+        def _():
+            for k in range(2):
+                from_k = pl.ds(pl.multiple_of(k * shard + i * 16, 16), 16)
+                up_f[at, pl.ds(k * D, D)] = mine[1, from_k, :].astype(F32)
+                up_f[at, pl.ds((2 + k) * D, D)] = far[1, from_k, :].astype(F32)
+
+        @pl.when(s == 1)
+        def _():
+            up_f[at, :] = up_one[at, :].astype(F32)
+
+    @pl.loop(0, half // 16)
+    def _(i):
+        at = pl.ds(pl.multiple_of(i * 16, 16), 16)
+        after = pl.ds(pl.multiple_of(half + i * 16, 16), 16)
+
+        @pl.when(s == 0)
+        def _():
+            down_f[at, :] = mine[0, at, :].astype(F32)
+            down_f[after, :] = far[0, at, :].astype(F32)
+
+        @pl.when(s == 1)
+        def _():
+            down_f[at, :] = down_one[at, :].astype(F32)
+            down_f[after, :] = down_one[after, :].astype(F32)
 
 
 def final_layouts(qkv, out, mine, far, down_one, up_one):
@@ -921,28 +961,102 @@
     return jnp.concatenate([row, jnp.zeros((row.shape[0], WIDE - D), row.dtype)], axis=1)
 
 
+def ctx_ring(rows_in, landing, send, recv):
+    z = lax.axis_index("ctx")
+    above = {"ctx": lax.rem(z + 1, 4)}
+    below = {"ctx": lax.rem(z + 3, 4)}
+    rows = rows_in.shape[0]
+    near, far = pl.ds(rows, rows), pl.ds(0, rows)
+    barrier = pltpu.get_barrier_semaphore()
+
+    def on(src, dst, i):
+        return pltpu.make_async_remote_copy(
+            src_ref=src, dst_ref=dst, send_sem=send.at[i], recv_sem=recv.at[i],
+            device_id=above, device_id_type=MESH,
+        )
+
+    one = on(rows_in, landing.at[near], 0)
+    two = on(landing.at[near], landing.at[far], 1)
+
+    def begin():
+        for where in (above, below):
+            pl.semaphore_signal(barrier, inc=1, device_id=where, device_id_type=MESH)
+        pl.semaphore_wait(barrier, 2)
+
+        @pl.when(z < 3)
+        def _():
+            one.start()
+
+        landing[pl.ds(2 * rows, rows), :] = rows_in[...]
+
+        @pl.when(z == 0)
+        def _():
+            landing[near, :] = jnp.zeros(rows_in.shape, BF)
+
+        @pl.when(z < 2)
+        def _():
+            landing[far, :] = jnp.zeros(rows_in.shape, BF)
+
+    def middle():
+        @pl.when(z > 0)
+        def _():
+            one.wait_recv()
+
+        @pl.when((z == 1) | (z == 2))
+        def _():
+            two.start()
+
+    def end():
+        @pl.when(z > 1)
+        def _():
+            two.wait_recv()
+
+        @pl.when(z < 3)
+        def _():
+            one.wait_send()
+
+        @pl.when((z == 1) | (z == 2))
+        def _():
+            two.wait_send()
+
+    return begin, middle, end
+
+
 def block_kernel(
-    wide, wq, wk, wv, wo, bias, normed, q_ref, k_ref, v_ref, att, resid, second, par, held
+    ring, first, wq, wk, wv, wo, bias, normed, q_ref, k_ref, v_ref, att, resid, second, par, *rest
 ):
     rows = resid.shape[0]
-    total = wide.shape[0]
+    total = normed.shape[0]
+    if ring:
+        wide_out, held, wide, send, recv = rest
+        begin, middle, end = ctx_ring(first, wide, send, recv)
+        begin()
+    else:
+        (held,), wide = rest, first
     pick_row = (
         lax.broadcasted_iota(jnp.int32, (16, 128), 1)
         == lax.broadcasted_iota(jnp.int32, (16, 128), 0) + (D - TAIL)
     )
     par[...] = mm_nt(pick_row.astype(F32).astype(BF), wo[:, pl.ds(TAIL, 128)])
-
-    @pl.loop(0, total // rows)
+    last = total // rows - 1
+
+    @pl.loop(0, last + 1)
     def _(i):
-        at = pl.ds(pl.multiple_of(i * rows, 16), rows)
+        if ring:
+            pl.when(i == 1)(middle)
+            pl.when(i == 2)(end)
+        at = pl.ds(pl.multiple_of((last - i) * rows, 16), rows)
         unit, _ = norm_parts(wide[at, :].astype(F32))
         low = (unit * par[0:1, :] + par[2:3, :]).astype(BF)
         normed[at, :] = low
         k_ref[at, :] = mm(low, wk[...]).astype(BF)
         v_ref[at, :] = (mm(low, wv[...]) + widened(par[4:5, :])).astype(BF)
 
+        @pl.when(i == 0)
+        def _():
+            q_ref[...] = (mm(normed[at, :], wq[...]) + widened(par[3:4, :])).astype(BF)
+
     own = pl.ds(total - rows, rows)
-    q_ref[...] = (mm(normed[own, :], wq[...]) + widened(par[3:4, :])).astype(BF)
     lanes = lax.broadcasted_iota(jnp.int32, (rows, 128), 1)
 
     @pl.loop(0, WIDE // 128)
@@ -957,6 +1071,8 @@
     resid[...] = res
     unit, _ = norm_parts(res)
     second[...] = (unit * par[1:2, :] + par[6:7, :]).astype(BF)
+    if ring:
+        wide_out[...] = wide[...]
 
 
 def weight_specs(weights):
@@ -969,32 +1085,60 @@
     return pl.BlockSpec(shape, lambda i: (0,) * len(shape))
 
 
-def block_forward(wide, weights, bias):
-    total, rows = wide.shape[0], bias.shape[0]
+def block_forward(first, weights, bias, ring):
+    rows, total = bias.shape
     outs = (
         ((total, D), BF), ((rows, WIDE), BF), ((total, WIDE), BF), ((total, WIDE), BF),
         ((rows, D), BF), ((rows, D), F32), ((rows, D), BF), ((16, D), F32),
     )
+    scratch = [pltpu.VMEM((rows, WIDE), BF)]
+    params = {}
+    if ring:
+        outs += (((total, D), BF),)
+        scratch += [pltpu.VMEM((total, D), BF)] + [pltpu.SemaphoreType.DMA((2,))] * 2
+        params = {"collective_id": 5, "has_side_effects": True}
     return pl.pallas_call(
-        block_kernel,
+        functools.partial(block_kernel, ring),
         out_shape=tuple(jax.ShapeDtypeStruct(*out) for out in outs),
         grid=(1,),
-        in_specs=[whole(wide.shape), *weight_specs(weights), whole(bias.shape)],
+        in_specs=[whole(first.shape), *weight_specs(weights), whole(bias.shape)],
         out_specs=tuple(whole(shape) for shape, _ in outs),
-        scratch_shapes=[pltpu.VMEM((rows, WIDE), BF)],
-        compiler_params=pltpu.CompilerParams(vmem_limit_bytes=56 * 1024 * 1024),
-        cost_estimate=lasting(22),
+        scratch_shapes=scratch,
+        compiler_params=pltpu.CompilerParams(vmem_limit_bytes=56 * 1024 * 1024, **params),
+        cost_estimate=lasting(45 if ring else 22),
         name="block_forward",
-    )(wide, weights, weights, weights, weights, bias)
+    )(first, weights, weights, weights, weights, bias)
 
 
 def block_back_kernel(
-    d_second, up, resid, wide, q_ref, k_ref, v_ref, att, ffb_rows, wq, wk, wv, wo, par, bias_t,
-    d_resid, dq_ref, dk_ref, dv_ref, da_own, da_halo, left, right, held, sums,
+    ring, d_second, up, resid, wide, q_ref, k_ref, v_ref, att, ffb_rows, wq, wk, wv, wo, par, bias_t,
+    *rest,
 ):
+    if ring:
+        (d_in, d_low, dq_ref, dk_ref, dv_ref, left, right,
+         held, sums, d_resid, da_own, da_halo, sent, caught, send, recv) = rest
+    else:
+        d_resid, dq_ref, dk_ref, dv_ref, da_own, da_halo, left, right, held, sums = rest
     rows = resid.shape[0]
     total = wide.shape[0]
     own = total - rows
+    z = lax.axis_index("ctx")
+
+    def back_to(src, dst, i):
+        return pltpu.make_async_remote_copy(
+            src_ref=src, dst_ref=dst, send_sem=send.at[i], recv_sem=recv.at[i],
+            device_id={"ctx": lax.rem(z + 3, 4)}, device_id_type=MESH,
+        )
+
+    if ring:
+        one = back_to(da_halo.at[pl.ds(0, rows)], caught.at[0], 0)
+        two = back_to(sent, caught.at[1], 1)
+        barrier = pltpu.get_barrier_semaphore()
+        for step in (1, 3):
+            pl.semaphore_signal(
+                barrier, inc=1, device_id={"ctx": lax.rem(z + step, 4)}, device_id_type=MESH
+            )
+        pl.semaphore_wait(barrier, 2)
 
     def total_of(values):
         return jnp.sum(values, axis=0, keepdims=True)
@@ -1046,25 +1190,79 @@
         at = pl.ds(pl.multiple_of(i * rows, 16), rows)
         da = back(at)
         da_halo[at, :] = da.astype(BF)
+        if ring:
+
+            @pl.when((i == 0) & (z > 0))
+            def _():
+                one.start()
+
         count(da, at)
 
     at = pl.ds(own, rows)
     da = back(at) + mm_nt(dq_ref[...], wq[...])
     da_own[...] = da
     count(da, at)
+    if ring:
+
+        @pl.when(z < 3)
+        def _():
+            one.wait_recv()
+
+        @pl.when(z == 3)
+        def _():
+            caught[0] = jnp.zeros_like(caught[0])
+
+        @pl.when(z > 0)
+        def _():
+            add_rows(sent, da_halo.at[pl.ds(rows, rows)], caught.at[0], rows, 64)
+            two.start()
+
     left[pl.ds(0, rows), :] = att[...]
     left[pl.ds(rows, 16), :] = sums[...].astype(BF)
-
-
-def block_backward(d_second, up, resid, wide, q, k, v, att, ffb_rows, weights, par, bias_t):
+    if ring:
+
+        @pl.when(z < 3)
+        def _():
+            two.wait_recv()
+
+        @pl.when(z == 3)
+        def _():
+            caught[1] = jnp.zeros_like(caught[1])
+
+        @pl.loop(0, rows // 64)
+        def _(i):
+            part = pl.ds(pl.multiple_of(i * 64, 64), 64)
+            behind = pl.ds(pl.multiple_of(own + i * 64, 64), 64)
+            unit, inv = norm_parts(wide[behind, :].astype(F32))
+            da = da_own[part, :] + caught[1, part, :].astype(F32)
+            grad = d_resid[part, :] + norm_back(da, par[0:1, :], unit, inv)
+            d_in[part, :] = grad
+            d_low[part, :] = grad.astype(BF)
+
+        @pl.when(z > 0)
+        def _():
+            one.wait_send()
+            two.wait_send()
+
+
+def block_backward(d_second, up, resid, wide, q, k, v, att, ffb_rows, weights, par, bias_t, ring):
     total, rows = wide.shape[0], resid.shape[0]
-    outs = (
-        ((rows, D), F32), ((rows, WIDE), BF), ((total, WIDE), BF), ((total, WIDE), BF),
-        ((rows, D), F32), ((total - rows, D), BF), ((rows + 16, D), BF), ((rows + 16, WIDE), BF),
-    )
+    f32_rows, low_rows = ((rows, D), F32), ((rows, D), BF)
+    heads = (((rows, WIDE), BF), ((total, WIDE), BF), ((total, WIDE), BF))
+    factors = (((rows + 16, D), BF), ((rows + 16, WIDE), BF))
+    halo = ((total - rows, D), BF)
+    held = [pltpu.VMEM((rows, WIDE), BF), pltpu.VMEM((16, D), F32)]
+    params = {}
+    if ring:
+        outs = (f32_rows, low_rows, *heads, *factors)
+        held += [pltpu.VMEM(*f32_rows), pltpu.VMEM(*f32_rows), pltpu.VMEM(*halo), pltpu.VMEM(*low_rows)]
+        held += [pltpu.VMEM((2, rows, D), BF)] + [pltpu.SemaphoreType.DMA((2,))] * 2
+        params = {"collective_id": 6, "has_side_effects": True}
+    else:
+        outs = (f32_rows, *heads, f32_rows, halo, *factors)
     before = (d_second, up, resid, wide, q, k, v, att, ffb_rows)
     return pl.pallas_call(
-        block_back_kernel,
+        functools.partial(block_back_kernel, ring),
         out_shape=tuple(jax.ShapeDtypeStruct(*out) for out in outs),
         grid=(1,),
         in_specs=[
@@ -1072,9 +1270,9 @@
             whole(par.shape), whole(bias_t.shape),
         ],
         out_specs=tuple(whole(shape) for shape, _ in outs),
-        scratch_shapes=[pltpu.VMEM((rows, WIDE), BF), pltpu.VMEM((16, D), F32)],
-        compiler_params=pltpu.CompilerParams(vmem_limit_bytes=60 * 1024 * 1024),
-        cost_estimate=lasting(38),
+        scratch_shapes=held,
+        compiler_params=pltpu.CompilerParams(vmem_limit_bytes=60 * 1024 * 1024, **params),
+        cost_estimate=lasting(58 if ring else 38),
         name="block_backward",
     )(*before, weights, weights, weights, weights, par, bias_t)
 
@@ -1156,8 +1354,12 @@
     current = own_in
     produced = []
     for layer in range(2):
-        wide = with_halo(current, chunks) if layer else wide_in
-        normed, q, k, v, att, resid, second, par = block_forward(wide, weights[layer], bias)
+        if layer == 1 and fits:
+            *made, wide = block_forward(current, weights[layer], bias, True)
+        else:
+            wide = with_halo(current, chunks) if layer else wide_in
+            made = block_forward(wide, weights[layer], bias, False)
+        normed, q, k, v, att, resid, second, par = made
         if layer == 0:
             up_own, second = lax.optimization_barrier((up_own, second))
             up_w = both_layers(up_own, s)
@@ -1180,16 +1382,17 @@
         ffb_rows = lax.dynamic_update_slice(
             jnp.zeros((8, D), F32), ffb_g.reshape(per_row, shard), (0, f * shard)
         )
-        d_resid, dq, dk, dv, da_own, da_halo, left, right = block_backward(
+        block = (
             d_second, upstream, resid, wide, q, k, v, att, ffb_rows, weights[layer], par, bias_t
         )
-
-        def through_norm(late):
+        if layer == 1 and fits:
+            derived[1], upstream_next, dq, dk, dv, left, right = block_backward(*block, True)
+        else:
+            d_resid, dq, dk, dv, da_own, da_halo, left, right = block_backward(*block, False)
+        if not fits:
             unit, inv = norm_parts(wide[reach:].astype(F32))
-            return d_resid + norm_back(da_own + late, par[0], unit, inv)
-
-        if layer == 1 or not fits:
-            derived[layer] = through_norm(return_halo(da_halo, chunks, rows))
+            late = return_halo(da_halo, chunks, rows)
+            derived[layer] = d_resid + norm_back(da_own + late, par[0], unit, inv)
             upstream_next = derived[layer].astype(BF)
         pieces = (
             mm_tn(normed[reach:], dq).astype(BF),

time: 901 us -> 894 us (level)
  Pallas kernels: 555 us -> 606 us
  waiting for transfers between devices: 142 us -> 124 us
  local copies, waits for them, and re-layouts: 63.5 us -> 48.2 us
  starting transfers between devices: 27 us -> 15.6 us
    pallas_call x4, Pallas kernels: 117 us -> 168 us  [the longest x2 109 us: block_backward(): pl.pallas_call(functools.partial(block_back_kernel, ring), out_shape=tupl...]
    ppermute x4 -> x0, waiting for transfers between devices: 35 us -> none  [shift(): return lax.ppermute(value, 'ctx', pairs)]
    all_to_all x2, waiting for transfers between devices: 0.01 us -> 18.9 us  [on_device(): lax.all_to_all(up_g.astype(BF).reshape(nf, shard, ff_here), 'fsdp', split...]
    ppermute x4 -> x0, starting transfers between devices: 12.4 us -> none  [shift(): return lax.ppermute(value, 'ctx', pairs)]
    unnamed x128 -> x118, local copies, waits for them, and re-layouts: 26.1 us -> 26.8 us
  transfers between devices with their start and end apart: 15 -> 11, of which waited for: 9 -> 5; matrix products, arithmetic and copies ran while one was open for 11% -> 8% of each run, Pallas kernels for 37% -> 42%
where the time goes in v6:
time: 894 us; the launch traced here: 888 us
  Pallas kernels  606 us (68%)
  waiting for transfers between devices  124 us (14%)
  matrix products  50.2 us (6%)
  local copies, waits for them, and re-layouts  48.2 us (5%)
  other arithmetic  28.9 us (3%)
  starting transfers between devices  15.6 us (2%)
  between operations  14.5 us (2%)
    pallas_call x4, Pallas kernels, plane_call(): pl.pallas_call(kernel, out_shape=outs, in_specs=[VSPEC] * len(operands),...  199 us
    pallas_call x1, Pallas kernels, reduce_both(): pl.pallas_call(reduce_kernel, out_shape=(*(jax.ShapeDtypeStruct(shape, BF...  171 us
    pallas_call x2, Pallas kernels, block_backward(): pl.pallas_call(functools.partial(block_back_kernel, ring), out_shape=tupl...  109 us
    psum x2, waiting for transfers between devices, on_device(): mlp_sums[layer] = lax.psum(halves, 'ctx')  85.7 us
    pallas_call x2, Pallas kernels, block_forward(): pl.pallas_call(functools.partial(block_kernel, ring), out_shape=tuple((ja...  59.1 us
    pallas_call x1, Pallas kernels, first_weights(): pl.pallas_call(weights_kernel, out_shape=(jax.ShapeDtypeStruct((4, D, WID...  57.3 us
    dot_general x12, matrix products, mm_tn(): lax.dot_general(a, b, (((0,), (0,)), ((), ())), preferred_element_type=F32)  50.2 us
    unnamed x118, local copies, waits for them, and re-layouts  26.8 us
  transfers between devices with their start and end apart: 11, of which 5 were waited for; matrix products, arithmetic and copies ran while one was open for 8% of the time, Pallas kernels for 42%

profile of v6, /device:TPU:0, one launch (start us, length us, event | category | flops | bytes accessed | tf_op | source)
XLA Modules:
  0.0 887.9 jit_solution(12574303088954079528)
XLA Ops:
  7.3 2.1 constant_dynamic-slice_fusion
  9.7 1.6 fusion.21
  11.2 2.0 fusion.18
  16.1 2.2 pad_maximum_fusion.own
  19.3 57.3 %first_weights.1 = (bf16[4,1088,1152]{2,1,0:T(8,128)(2,1)}, bf16[768,1088]{1,0:T(8,128)(2,1)S(1)}, bf16[4,272,1088]{2,1,0:T(8,128)(2,1)}, bf16[2,1088,1088]{2,1,0:T(8,128)(2,1)S(1)}) custom-call(bf16[4,272,1152]{2,1,0:T(8,128)(2,1)S(1)} %pad_maximum_fusion.own, bf16[256,1088]{1,0:T(8,128)(2,1)S(1)} %bitcast.109, bf16[272,4352]{1,0:T(8,128)(2,1)S(1)} %bitcast.108, ...), custom_call_target="tpu_custom_call" | custom-call | bytes 175000000 | tf_op jit(solution)/shard_map/first_weights/pallas_call | solution.py:414
  77.7 2.3 copy-done.10
  81.9 3.1 collective-permute-done.1
  85.0 2.1 bitcast_select_fusion
  88.3 4.2 all-to-all-start
  93.6 24.7 %block_forward.2 = (bf16[768,1088]{1,0:T(8,128)(2,1)}, bf16[256,1152]{1,0:T(8,128)(2,1)}, bf16[768,1152]{1,0:T(8,128)(2,1)}, bf16[768,1152]{1,0:T(8,128)(2,1)}, ...) custom-call(bf16[768,1088]{1,0:T(8,128)(2,1)} %copy-done.8, ...), custom_call_target="tpu_custom_call" | custom-call | bytes 77000000 | tf_op jit(solution)/shard_map/block_forward/pallas_call | solution.py:1100
  118.3 16.1 %all-to-all-done = bf16[4,272,1088]{2,1,0:T(8,128)(2,1)S(1)} async-done(((bf16[4,272,1088]{2,1,0:T(8,128)(2,1)}), bf16[4,272,1088]{2,1,0:T(8,128)(2,1)S(1)}, u32[]{:S(2)}, u32[]{:S(2)}) %all-to-all-start) | async-done | bytes 2367520 | tf_op jit(solution)/shard_map/all_to_all | solution.py:1347
  136.7 5.7 slice_bitcast_fusion
  142.4 5.4 broadcast_select_fusion
  147.8 64.6 %shard_map.169 = (bf16[256,1088]{1,0:T(8,128)(2,1)S(1)}, bf16[4,256,1088]{2,1,0:T(8,128)(2,1)S(1)}, bf16[4,256,1088]{2,1,0:T(8,128)(2,1)S(1)}, f32[4,256,1088]{2,1,0:T(8,128)}) custom-call(bf16[256,1088]{1,0:T(8,128)(2,1)S(1)} %copy-done.23, bf16[1088,1088]{1,0:T(8,128)(2,1)S(1)} %get-tuple-element.178.up, bf16[1088,1088]{1,0:T(8,128)(2,1)S(1)} %get-tuple-element.176.down, ...), custom_call_target="tpu_custom_call" | custom-call | bytes 140000000 | tf_op jit(solution)/shard_map/pallas_call | solution.py:187
  216.1 34.3 %block_forward.3 = (bf16[768,1088]{1,0:T(8,128)(2,1)}, bf16[256,1152]{1,0:T(8,128)(2,1)}, bf16[768,1152]{1,0:T(8,128)(2,1)}, bf16[768,1152]{1,0:T(8,128)(2,1)}, ...) custom-call(bf16[256,1088]{1,0:T(8,128)(2,1)} %copy-done.17, ...), custom_call_target="tpu_custom_call" | custom-call | bytes 157500000 | tf_op jit(solution)/shard_map/block_forward/pallas_call | solution.py:1100
  251.3 1.7 copy-done.2
  253.0 1.7 copy-done.6
  257.9 43.5 %shard_map.170 = (bf16[256,1088]{1,0:T(8,128)(2,1)S(1)}, bf16[4,256,1088]{2,1,0:T(8,128)(2,1)S(1)}, bf16[4,256,1088]{2,1,0:T(8,128)(2,1)S(1)}, f32[4,256,1088]{2,1,0:T(8,128)}) custom-call(bf16[256,1088]{1,0:T(8,128)(2,1)S(1)} %copy-done.24, bf16[1088,1088]{1,0:T(8,128)(2,1)S(1)} %copy-done.2, bf16[1088,1088]{1,0:T(8,128)(2,1)S(1)} %copy-done.6, ...), custom_call_target="tpu_custom_call" | custom-call | bytes 140000000 | tf_op jit(solution)/shard_map/pallas_call | solution.py:187
  301.5 45.2 %shard_map.171 = (f32[256,1088]{1,0:T(8,128)S(1)}, bf16[4,256,1088]{2,1,0:T(8,128)(2,1)S(1)}, bf16[4,256,1088]{2,1,0:T(8,128)(2,1)S(1)}, f32[1,1088]{1,0:T(1,128)S(1)}) custom-call(bf16[256,1088]{1,0:T(8,128)(2,1)S(1)} %bitcast.105, bf16[1088,1088]{1,0:T(8,128)(2,1)S(1)} %copy-done.3, bf16[1088,1088]{1,0:T(8,128)(2,1)S(1)} %copy-done.7, ...), custom_call_target="tpu_custom_call" | custom-call | bytes 140000000 | tf_op jit(solution)/shard_map/pallas_call | solution.py:187
  346.7 4.6 fusion.1
  351.3 4.9 all-to-all-start.1
  356.2 6.9 fusion
  363.1 18.9 %all-to-all-done.1 = bf16[4,272,1088]{2,1,0:T(8,128)(2,1)} async-done(((bf16[4,272,1088]{2,1,0:T(8,128)(2,1)}), bf16[4,272,1088]{2,1,0:T(8,128)(2,1)}, u32[]{:S(2)}, u32[]{:S(2)}) %all-to-all-start.1) | async-done | bytes 2367520 | tf_op jit(solution)/shard_map/all_to_all | solution.py:1404
  382.0 3.4 fusion.11
  387.8 75.0 %block_backward.2 = (f32[256,1088]{1,0:T(8,128)}, bf16[256,1088]{1,0:T(8,128)(2,1)}, bf16[256,1152]{1,0:T(8,128)(2,1)}, bf16[768,1152]{1,0:T(8,128)(2,1)}, bf16[...) custom-call(f32[256,1088]{1,0:T(8,128)} %copy-done.19, bf16[256,1088]{1,0:T(8,128)(2,1)} %bitcast.106, ...), custom_call_target="tpu_custom_call" | custom-call | bytes 203000000 | tf_op jit(solution)/shard_map/block_backward/pallas_call | solution.py:1264
  462.8 4.6 fusion.5
  467.4 1.7 copy-done.5
  469.1 45.4 %shard_map.172 = (f32[256,1088]{1,0:T(8,128)S(1)}, bf16[4,256,1088]{2,1,0:T(8,128)(2,1)S(1)}, bf16[4,256,1088]{2,1,0:T(8,128)(2,1)S(1)}, f32[1,1088]{1,0:T(1,128)S(1)}) custom-call(bf16[256,1088]{1,0:T(8,128)(2,1)S(1)} %copy-done.16, bf16[1088,1088]{1,0:T(8,128)(2,1)S(1)} %get-tuple-element.178.up, bf16[1088,1088]{1,0:T(8,128)(2,1)S(1)} %copy-done.5, ...), custom_call_target="tpu_custom_call" | custom-call | bytes 140000000 | tf_op jit(solution)/shard_map/pallas_call | solution.py:187
  514.5 4.6 fusion.3
  519.1 4.6 all-to-all-start.2
  525.0 33.8 %block_backward.3 = (f32[256,1088]{1,0:T(8,128)}, bf16[256,1152]{1,0:T(8,128)(2,1)}, bf16[768,1152]{1,0:T(8,128)(2,1)}, bf16[768,1152]{1,0:T(8,128)(2,1)}, f32[2...) custom-call(f32[256,1088]{1,0:T(8,128)} %copy-done.20, ...), custom_call_target="tpu_custom_call" | custom-call | bytes 133000000 | tf_op jit(solution)/shard_map/block_backward/pallas_call | solution.py:1264
  558.8 6.3 fusion.2
  565.1 3.4 fusion.7
  569.0 1.9 slice.47.wide
  570.9 4.4 convolution_convert_fusion.6.o1
  575.3 3.9 convolution_convert_fusion.2.v1
  579.3 3.5 fusion.4
  582.8 85.7 %all-reduce.6.cloned.1.call-done.mlp = bf16[2,544,1088]{2,1,0:T(8,128)(2,1)} async-done(((bf16[2,544,1088]{2,1,0:T(8,128)(2,1)}), bf16[2,544,1088]{2,1,0:T(8,128)(2,1)}) %all-reduce.6.cloned.1.call-update) | async-done | bytes 2367504 | tf_op jit(solution)/shard_map/psum | solution.py:1416
  668.5 2.4 convolution_convert_fusion.q1
  670.9 3.9 convolution_convert_fusion.3.k1
  674.8 2.4 convolution_convert_fusion.1.q0
  677.2 3.1 convolution_convert_fusion.7.o0
  680.3 4.0 convolution_convert_fusion.4.v0
  684.3 3.8 convolution_convert_fusion.5.k0
  688.1 171.2 %reduce_both.1 = (bf16[272,3264]{1,0:T(8,128)(2,1)}, bf16[272,1152]{1,0:T(8,128)(2,1)}, bf16[1088,1088]{1,0:T(8,128)(2,1)}, bf16[272,4352]{1,0:T(8,128)(2,1)}, b...) custom-call(bf16[1088,1152]{1,0:T(8,128)(2,1)} %convolution_convert_fusion.1.q0, ...), custom_call_target="tpu_custom_call" | custom-call | bytes 420000000 | tf_op jit(solution)/shard_map/reduce_both/pallas_call | solution.py:779
  860.7 3.1 copy.52
  863.8 2.3 copy.51
  867.9 11.4 %final_layouts.1 = (f32[272,3264]{1,0:T(8,128)}, f32[272,1088]{1,0:T(8,128)}, f32[1088,1088]{1,0:T(8,128)}, f32[272,4352]{1,0:T(8,128)}, f32[16,272]{1,0:T(8,128)S(1)}) custom-call(bf16[272,3264]{1,0:T(8,128)(2,1)S(1)} %copy-done.18, bf16[272,1152]{1,0:T(8,128)(2,1)S(1)} %copy-done.22, bf16[2,544,1088]{2,1,0:T(8,128)(2,1)} %all-reduce.8.cloned.1.call-done.mine, ...), custom_call_target="tpu_custom_call" | custom-call | bytes 35000000 | tf_op jit(solution)/shard_map/final_layouts/pallas_call | solution.py:847
  (161 shorter events, 28.6 us)
Async XLA Ops:
  7.2 85.3 %copy-start = (s32[2,1,1024]{2,1,0:T(1,128)S(1)}, s32[2,1,1024]{2,1,0:T(1,128)}, u32[]{:S(2)}) copy-start(s32[2,1,1024]{2,1,0:T(1,128)} %param.11) | copy-start | bytes 24580
  7.2 208.9 %all-gather.2.cloned.1.call-start = ((), (), s32[]{:S(2)}) async-start(), calls=%async_computation.3 | async-start | bytes 11280384 | tf_op jit(solution)/shard_map/all_gather | solution.py:1341
  7.2 4.0 copy-start.47
  9.4 3.9 copy-start.46
  9.4 4.2 copy-start.48
  9.4 4.3 copy-start.45
  11.2 3.8 copy-start.37
  16.1 3.2 copy-start.14
  81.4 3.6 copy-start.36
  81.9 3.1 collective-permute-start.1
  88.3 46.1 %all-to-all-start = ((bf16[4,272,1088]{2,1,0:T(8,128)(2,1)}), bf16[4,272,1088]{2,1,0:T(8,128)(2,1)S(1)}, u32[]{:S(2)}, u32[]{:S(2)}) async-start(bf16[4,272,1088]{2,1,0:T(8,128)(2,1)} %get-tuple-element.87), calls=%async_computation | async-start | bytes 5013504 | tf_op jit(solution)/shard_map/all_to_all | solution.py:1347
  134.4 8.0 copy-start.34
  134.4 8.0 collective-permute-start
  136.7 164.8 %copy-start.9 = (bf16[1,1,256,1088]{3,2,1,0:T(8,128)(2,1)}, bf16[1,1,256,1088]{3,2,1,0:T(8,128)(2,1)S(1)}, u32[]{:S(2)}) copy-start(bf16[1,1,256,1088]{3,2,1,0:T(8,128)(2,1)S(1)} %copy.42) | copy-start | bytes 1671172
  142.4 5.4 copy-start.4
  142.4 5.4 copy-start.11
  142.4 5.4 copy-start.21
  142.4 5.4 copy-start.23
  257.9 43.5 %copy-start.3 = (bf16[1088,1088]{1,0:T(8,128)(2,1)S(1)}, bf16[1088,1088]{1,0:T(8,128)(2,1)}, u32[]{:S(2)}) copy-start(bf16[1088,1088]{1,0:T(8,128)(2,1)} %get-tuple-element.177.up) | copy-start | bytes 7102468
  257.9 43.5 %copy-start.7 = (bf16[1088,1088]{1,0:T(8,128)(2,1)S(1)}, bf16[1088,1088]{1,0:T(8,128)(2,1)}, u32[]{:S(2)}) copy-start(bf16[1088,1088]{1,0:T(8,128)(2,1)} %get-tuple-element.175.down) | copy-start | bytes 7102468
  301.4 45.2 %copy-start.25 = (bf16[256,1088]{1,0:T(8,128)(2,1)}, bf16[256,1088]{1,0:T(8,128)(2,1)S(1)}, u32[]{:S(2)}) copy-start(bf16[256,1088]{1,0:T(8,128)(2,1)S(1)} %get-tuple-element.138.made1) | copy-start | bytes 1671172
  301.4 45.2 %copy-start.32 = (bf16[4,256,1088]{2,1,0:T(8,128)(2,1)}, bf16[4,256,1088]{2,1,0:T(8,128)(2,1)S(1)}, u32[]{:S(2)}) copy-start(bf16[4,256,1088]{2,1,0:T(8,128)(2,1)S(1)} %get-tuple-element.99) | copy-start | bytes 6684676
  346.7 4.6 copy-start.19
  346.7 4.6 copy-start.33
  351.3 30.7 %all-to-all-start.1 = ((bf16[4,272,1088]{2,1,0:T(8,128)(2,1)}), bf16[4,272,1088]{2,1,0:T(8,128)(2,1)}, u32[]{:S(2)}, u32[]{:S(2)}) async-start(bf16[4,272,1088]{2,1,0:T(8,128)(2,1)} %bitcast.118), calls=%async_computation.1 | async-start | bytes 5013504 | tf_op jit(solution)/shard_map/all_to_all | solution.py:1404
  385.4 77.4 %collective-permute-start.2 = (bf16[2,544,1088]{2,1,0:T(8,128)(2,1)}, bf16[2,544,1088]{2,1,0:T(8,128)(2,1)}, u32[]{:S(2)}, u32[]{:S(2)}) collective-permute-start(bf16[2,544,1088]{2,1,0:T(8,128)(2,1)} %fusion.11), channel_id=1, source_target_pairs={{0,16},{16,0},{1,17},{17,1},{2,18},{18,2},{3,19},{19,3},{4,20},{20... | collective-permute-start | bytes 7102472 | tf_op jit(solution)/shard_map/ppermute | solution.py:909
  462.8 4.6 copy-start.16
  469.1 45.4 %copy-start.30 = (bf16[4,256,1088]{2,1,0:T(8,128)(2,1)S(1)}, bf16[4,256,1088]{2,1,0:T(8,128)(2,1)}, u32[]{:S(2)}) copy-start(bf16[4,256,1088]{2,1,0:T(8,128)(2,1)} %copy-done.29) | copy-start | bytes 6684676
  514.5 4.6 copy-start.20
  514.5 4.6 copy-start.31
  519.1 46.0 %all-to-all-start.2 = ((bf16[4,272,1088]{2,1,0:T(8,128)(2,1)}), bf16[4,272,1088]{2,1,0:T(8,128)(2,1)}, u32[]{:S(2)}, u32[]{:S(2)}) async-start(bf16[4,272,1088]{2,1,0:T(8,128)(2,1)} %bitcast.32), calls=%async_computation.2 | async-start | bytes 5013504 | tf_op jit(solution)/shard_map/all_to_all | solution.py:1404
  523.7 144.8 %all-reduce.6.cloned.1.call-start = ((), (), s32[]{:S(2)}) async-start(), calls=%async_computation.4 | async-start | bytes 5013504 | tf_op jit(solution)/shard_map/psum | solution.py:1416
  525.0 33.9 %copy-start.28 = (bf16[4,256,1088]{2,1,0:T(8,128)(2,1)S(1)}, bf16[4,256,1088]{2,1,0:T(8,128)(2,1)}, u32[]{:S(2)}) copy-start(bf16[4,256,1088]{2,1,0:T(8,128)(2,1)} %copy-done.27) | copy-start | bytes 6684676
  568.5 10.7 %collective-permute-start.3 = (bf16[2,544,1088]{2,1,0:T(8,128)(2,1)}, bf16[2,544,1088]{2,1,0:T(8,128)(2,1)S(1)}, u32[]{:S(2)}, u32[]{:S(2)}) collective-permute-start(bf16[2,544,1088]{2,1,0:T(8,128)(2,1)} %fusion.7), channel_id=1, source_target_pairs={{0,16},{16,0},{1,17},{17,1},{2,18},{18,2},{3,19},{19,3},{4,20},{20... | collective-permute-start | bytes 7102472 | tf_op jit(solution)/shard_map/ppermute | solution.py:909
  568.5 290.8 %all-reduce.8.cloned.1.call-start = ((), (), s32[]{:S(2)}) async-start(), calls=%async_computation.5 | async-start | bytes 5013504 | tf_op jit(solution)/shard_map/psum | solution.py:1416
  570.9 4.4 copy-start.39
  570.9 4.4 copy-start.50
  575.3 4.0 copy-start.35
  582.8 85.8 %copy-start.40 = (bf16[768,1088]{1,0:T(8,128)(2,1)S(1)}, bf16[768,1088]{1,0:T(8,128)(2,1)}, u32[]{:S(2)}) copy-start(bf16[768,1088]{1,0:T(8,128)(2,1)} %get-tuple-element.125) | copy-start | bytes 5013508
  582.8 85.8 %copy-start.41 = (bf16[256,1152]{1,0:T(8,128)(2,1)S(1)}, bf16[256,1152]{1,0:T(8,128)(2,1)}, u32[]{:S(2)}) copy-start(bf16[256,1152]{1,0:T(8,128)(2,1)} %get-tuple-element.126) | copy-start | bytes 1769476
  670.9 3.9 copy-start.38
  670.9 3.9 copy-start.42
  677.2 3.1 copy-start.52
  680.3 4.0 copy-start.51
  859.4 7.0 collective-permute-start.4
  860.7 5.7 copy-start.15
  860.7 5.7 copy-start.22
  867.9 13.3 %copy-start.1 = (s32[2,1,1024]{2,1,0:T(1,128)S(1)}, s32[2,1,1024]{2,1,0:T(1,128)}, u32[]{:S(2)}) copy-start(s32[2,1,1024]{2,1,0:T(1,128)} %param.11) | copy-start | bytes 24580
  (19 other events, 30.2 us)
Sparse Core Ops, SparseCore 0:
  88.4 94.0 all-gather.1
  568.7 99.7 all-reduce.5
  670.9 140.9 all-reduce.7

commit v7 on v6

--- a/solution.py
+++ b/solution.py
@@ -74,7 +74,17 @@
     )
 
 
-def exchange_rows(own_ref, all_ref, parts, compute, finish, bufs, send, recv):
+def load_layer(layer, sources, targets, sems):
+    copies = [
+        pltpu.make_async_copy(source.at[layer], target, sems.at[i])
+        for i, (source, target) in enumerate(zip(sources, targets))
+    ]
+    for copy in copies:
+        copy.start()
+    return copies
+
+
+def exchange_rows(own_ref, all_ref, parts, compute, finish, bufs, send, recv, loads):
     x1, y1, x2, y2, sum_x, sum_y = bufs
     xn, yn = plane_neighbours()
     half = own_ref.shape[0] // 2
@@ -95,6 +105,8 @@
     to_x.start()
     to_y.start()
     all_ref[0] = own_ref[...]
+    for copy in loads:
+        copy.wait()
 
     @pl.loop(0, 4)
     def _(i):
@@ -136,9 +148,11 @@
 
 
 def forward_kernel(
-    own, up, down, bias, resid, par, out, all_ref, active, slope,
-    parts, x1, y1, x2, y2, sx, sy, send, recv,
+    layer, own, up_both, down_both, bias, resid, par, out, all_ref, active, slope,
+    up, down, load, parts, x1, y1, x2, y2, sx, sy, send, recv,
 ):
+    loads = load_layer(layer, (up_both, down_both), (up, down), load)
+
     def finish(at, value):
         out[at, :] = (resid[at, :] + value + par[7:8, :]).astype(BF)
 
@@ -155,12 +169,14 @@
 
         parts[r] = mm(active[r], down[...]).astype(BF)
 
-    exchange_rows(own, all_ref, parts, compute, finish, (x1, y1, x2, y2, sx, sy), send, recv)
+    exchange_rows(own, all_ref, parts, compute, finish, (x1, y1, x2, y2, sx, sy), send, recv, loads)
 
 
 def backward_kernel(
-    own, up, down, slope, total, all_ref, dz_all, bias_g, parts, x1, y1, x2, y2, sx, sy, send, recv
+    layer, own, up_both, down_both, slope, total, all_ref, dz_all, bias_g,
+    up, down, load, parts, x1, y1, x2, y2, sx, sy, send, recv,
 ):
+    loads = load_layer(layer, (up_both, down_both), (up, down), load)
     bias_g[...] = jnp.zeros_like(bias_g)
 
     def finish(at, value):
@@ -172,7 +188,7 @@
         dz_all[r] = dz.astype(BF)
         parts[r] = mm_nt(dz_all[r], up[...]).astype(BF)
 
-    exchange_rows(own, all_ref, parts, compute, finish, (x1, y1, x2, y2, sx, sy), send, recv)
+    exchange_rows(own, all_ref, parts, compute, finish, (x1, y1, x2, y2, sx, sy), send, recv, loads)
 
 
 VSPEC = pl.BlockSpec(memory_space=pltpu.VMEM)
@@ -184,12 +200,16 @@
 
 def plane_call(kernel, ident, outs, rows, *operands):
     half = rows // 2
+    any_spec = pl.BlockSpec(memory_space=pl.ANY)
     return pl.pallas_call(
         kernel,
         out_shape=outs,
-        in_specs=[VSPEC] * len(operands),
+        in_specs=[VSPEC, any_spec, any_spec] + [VSPEC] * (len(operands) - 3),
         out_specs=(VSPEC,) * len(outs),
         scratch_shapes=[
+            pltpu.VMEM((D, D), BF),
+            pltpu.VMEM((D, D), BF),
+            pltpu.SemaphoreType.DMA((2,)),
             pltpu.VMEM((4, rows, D), BF),
             pltpu.VMEM((half, D), BF),
             pltpu.VMEM((half, D), BF),
@@ -207,10 +227,11 @@
     )(*operands)
 
 
-def mlp_forward(own, up, down, bias, resid, par):
+def mlp_forward(own, up, down, layer, bias, resid, par):
     rows = own.shape[0]
     if lax.axis_size("fsdp") != 4:
         every = lax.all_gather(own, "fsdp", axis=0, tiled=True)
+        up, down = up[layer], down[layer]
         z = mm(every, up) + bias
         cdf, pdf = phi_parts(z)
         active = (z * cdf).astype(BF)
@@ -220,7 +241,7 @@
         return out, every, active, cdf + z * pdf
     shape = (4, rows, D)
     return plane_call(
-        forward_kernel, 1,
+        functools.partial(forward_kernel, layer), 1 + 6 * layer,
         (
             jax.ShapeDtypeStruct((rows, D), BF),
             jax.ShapeDtypeStruct(shape, BF),
@@ -231,10 +252,11 @@
     )
 
 
-def mlp_backward(own, up, down, slope):
+def mlp_backward(own, up, down, layer, slope):
     rows = own.shape[0]
     if lax.axis_size("fsdp") != 4:
         every = lax.all_gather(own, "fsdp", axis=0, tiled=True)
+        up, down = up[layer], down[layer]
         dz = mm_nt(every, down) * slope
         dz_b = dz.astype(BF)
         part = mm_nt(dz_b, up).astype(BF)
@@ -242,7 +264,7 @@
         return total, every, dz_b, jnp.sum(dz, axis=0, keepdims=True)
     shape = (4, rows, D)
     return plane_call(
-        backward_kernel, 2,
+        functools.partial(backward_kernel, layer), 2 + 6 * layer,
         (
             jax.ShapeDtypeStruct((rows, D), F32),
             jax.ShapeDtypeStruct(shape, BF),
@@ -255,7 +277,8 @@
 
 def weights_kernel(
     own, rows_in, up_in, down_in, full, rows_out, up_out, down_out,
-    load, core_s, core_r, p_send, p_recv, f_send, f_recv, z_send, z_recv,
+    up_blocks, load, core_s, core_r, p_send, p_recv, f_send, f_recv, z_send, z_recv,
+    u_send, u_recv, v_send, v_recv,
 ):
     s = lax.axis_index("section")
     f = lax.axis_index("fsdp")
@@ -276,9 +299,10 @@
     z = lax.axis_index("ctx")
     above = {"ctx": lax.rem(z + 1, 4)}
     below = {"ctx": lax.rem(z + 3, 4)}
-    for where in ({"section": 1 - s}, {"fsdp": xn}, {"fsdp": yn}, above, below):
+    partners = ({"section": 1 - s}, {"fsdp": xn}, {"fsdp": yn}, {"fsdp": dn}, above, below)
+    for where in partners:
         pl.semaphore_signal(barrier, inc=1, device_id=where, device_id_type=MESH)
-    pl.semaphore_wait(barrier, 5)
+    pl.semaphore_wait(barrier, 6)
     rows = rows_in.shape[0]
     near_rows, far_rows = pl.ds(rows, rows), pl.ds(0, rows)
     step_one = to(rows_in, rows_out.at[near_rows], z_send.at[0], z_recv.at[0], **above)
@@ -352,7 +376,22 @@
     down_far.start()
     down_near.start()
     for j in range(4):
-        up_out[j] = up_in[:, pl.ds(j * D, D)]
+        up_blocks[j] = up_in[:, pl.ds(j * D, D)]
+
+    def up_to(i, owner, where):
+        return to(up_blocks.at[owner], up_out.at[s, blk(f)], u_send.at[i], u_recv.at[i], fsdp=where)
+
+    def up_over(i, owner):
+        rows_here = up_out.at[s, blk(owner)]
+        return to(rows_here, rows_here, v_send.at[i], v_recv.at[i], section=1 - s)
+
+    others = (xn, yn, dn)
+    up_near = pltpu.make_async_copy(up_blocks.at[f], up_out.at[s, blk(f)], load.at[5])
+    up_near.start()
+    for i, owner in enumerate(others):
+        up_to(i, owner, owner).start()
+    up_near.wait()
+    up_over(3, f).start()
     for k in range(2):
         copies, across = hops(k), here(k)
         copies[0].wait_recv()
@@ -375,11 +414,18 @@
         copies[2].wait_recv()
         copies[3].wait_recv()
         across[2].start()
+    for i, owner in enumerate(others):
+        up_to(i, owner, owner).wait_recv()
+        up_over(i, owner).start()
     for k in range(2):
         for copy in here(k):
             copy.wait()
         for copy in hops(k):
             copy.wait_send()
+    for i, owner in enumerate(others):
+        up_to(i, owner, owner).wait_send()
+        up_over(i, owner).wait()
+    up_over(3, f).wait()
 
     @pl.when(s == 0)
     def _():
@@ -416,19 +462,20 @@
         out_shape=(
             jax.ShapeDtypeStruct((4, D, WIDE), BF),
             jax.ShapeDtypeStruct((3 * rows_in.shape[0], D), BF),
-            jax.ShapeDtypeStruct((4, up.shape[0], D), BF),
+            jax.ShapeDtypeStruct((2, D, D), BF),
             jax.ShapeDtypeStruct((2, D, D), BF),
         ),
         in_specs=[pl.BlockSpec(memory_space=pl.ANY), VSPEC, VSPEC, pl.BlockSpec(memory_space=pl.ANY)],
         out_specs=(VSPEC,) * 4,
         scratch_shapes=[
-            dma((5,)), dma((5,)), dma((5,)), dma((2, 4)), dma((2, 4)), dma((2, 3)), dma((2, 3)),
-            dma((2,)), dma((2,)),
+            pltpu.VMEM((4, up.shape[0], D), BF),
+            dma((6,)), dma((5,)), dma((5,)), dma((2, 4)), dma((2, 4)), dma((2, 3)), dma((2, 3)),
+            dma((2,)), dma((2,)), dma((3,)), dma((3,)), dma((4,)), dma((4,)),
         ],
         compiler_params=pltpu.CompilerParams(
-            collective_id=4, has_side_effects=True, vmem_limit_bytes=32 * 1024 * 1024
+            collective_id=4, has_side_effects=True, vmem_limit_bytes=40 * 1024 * 1024
         ),
-        cost_estimate=lasting(50),
+        cost_estimate=lasting(75),
         name="first_weights",
     )(own, rows_in, up, down)
 
@@ -798,7 +845,10 @@
     )(*zero, *one, mlp, *made, grad1, halo, d_resid, da_own, wide, par)
 
 
-def final_kernel(qkv, out, mine, far, down_one, up_one, qkv_f, out_f, down_f, up_f, small):
+def final_kernel(
+    qkv, out, mine, far, down_one, up_one, made, grads,
+    qkv_f, out_f, down_f, up_f, small, made_out, grads_out,
+):
     s = lax.axis_index("section")
     half = mine.shape[1]
     shard = qkv.shape[0]
@@ -808,6 +858,13 @@
     )
     small[...] = mm_nt(pick_row.astype(F32).astype(BF), out[:, pl.ds(TAIL, 128)])
 
+    @pl.loop(0, made.shape[1] // 16)
+    def _(i):
+        at = pl.ds(pl.multiple_of(i * 16, 16), 16)
+        for m in range(2):
+            made_out[m, at, :] = made[m, at, :]
+            grads_out[m, at, :] = grads[m, at, :]
+
     @pl.loop(0, shard // 16)
     def _(i):
         at = pl.ds(pl.multiple_of(i * 16, 16), 16)
@@ -841,18 +898,20 @@
             down_f[after, :] = down_one[after, :].astype(F32)
 
 
-def final_layouts(qkv, out, mine, far, down_one, up_one):
+def final_layouts(*values):
+    qkv, _, _, _, down_one, up_one, made, grads = values
     shard = qkv.shape[0]
-    outs = (qkv.shape, (shard, D), down_one.shape, up_one.shape, (16, shard))
+    outs = [(shape, F32) for shape in (qkv.shape, (shard, D), down_one.shape, up_one.shape)]
+    outs += [((16, shard), F32), (made.shape, BF), (grads.shape, F32)]
     return pl.pallas_call(
         final_kernel,
-        out_shape=tuple(jax.ShapeDtypeStruct(shape, F32) for shape in outs),
-        in_specs=[VSPEC] * 6,
-        out_specs=(VSPEC,) * 5,
-        compiler_params=pltpu.CompilerParams(vmem_limit_bytes=48 * 1024 * 1024),
+        out_shape=tuple(jax.ShapeDtypeStruct(*out) for out in outs),
+        in_specs=[VSPEC] * 8,
+        out_specs=(VSPEC,) * 7,
+        compiler_params=pltpu.CompilerParams(vmem_limit_bytes=52 * 1024 * 1024),
         cost_estimate=lasting(10),
         name="final_layouts",
-    )(qkv, out, mine, far, down_one, up_one)
+    )(*values)
 
 
 def halves_pair(down, up):
@@ -1323,12 +1382,15 @@
         ]
     )
     if fits:
-        zero, wide_in, up_blocks, down_w = first_weights(
+        zero, wide_in, up_w, down_w = first_weights(
             packed, own_in, up_weight[0], down_weight[0]
         )
         packed, zero = lax.optimization_barrier((packed, zero))
     else:
-        up_blocks = up_weight[0].reshape(shard, nf, ff_here).transpose(1, 0, 2)
+        up_own = lax.all_to_all(
+            up_weight[0].reshape(shard, nf, ff_here), "fsdp", split_axis=1, concat_axis=0, tiled=True
+        ).reshape(D, ff_here)
+        up_w = both_layers(up_own, s)
         down_w = both_layers(down_weight[0], s)
         wide_in = with_halo(own_in, chunks)
     half = shard // 2
@@ -1344,10 +1406,6 @@
     one = gathered(pick(s, recv, keep))
     if not fits:
         zero = gathered(pick(s, keep, recv))
-    up_own = lax.all_to_all(
-        up_blocks, "fsdp", split_axis=0, concat_axis=0, tiled=True
-    ).reshape(D, ff_here)
-
     weights = (zero, one)
 
     kept = []
@@ -1360,12 +1418,9 @@
             wide = with_halo(current, chunks) if layer else wide_in
             made = block_forward(wide, weights[layer], bias, False)
         normed, q, k, v, att, resid, second, par = made
-        if layer == 0:
-            up_own, second = lax.optimization_barrier((up_own, second))
-            up_w = both_layers(up_own, s)
         ffb = lax.dynamic_slice(par, (8, f * shard), (per_row, shard)).reshape(1, ff_here)
         current, second_all, active, slope = mlp_forward(
-            second, up_w[layer], down_w[layer], ffb, resid, par
+            second, up_w, down_w, layer, ffb, resid, par
         )
         produced.append(current)
         kept.append((wide, normed, q, k, v, att, resid, second_all, slope, active, par))
@@ -1376,7 +1431,7 @@
     mlp_sums = [None, None]
     for layer in (1, 0):
         wide, normed, q, k, v, att, resid, second_all, slope, active, par = kept[layer]
-        d_second, up_all, dz_b, ffb_g = mlp_backward(upstream, up_w[layer], down_w[layer], slope)
+        d_second, up_all, dz_b, ffb_g = mlp_backward(upstream, up_w, down_w, layer, slope)
         down_g = mm_tn(flat(active), flat(up_all))
         up_g = mm_tn(flat(second_all), flat(dz_b))
         ffb_rows = lax.dynamic_update_slice(
@@ -1406,8 +1461,7 @@
             split_axis=0, concat_axis=0, tiled=True,
         ).reshape(nf * shard * ff_here // D, D)
         down_g = down_g.astype(BF)
-        if layer == 0:
-            down_g, up_g, _ = lax.optimization_barrier((down_g, up_g, dq))
+        down_g, up_g, _ = lax.optimization_barrier((down_g, up_g, dq))
         halves = halves_pair(down_g, up_g)
         if layer == 1:
             _, upstream_next = lax.optimization_barrier((halves, upstream_next))
@@ -1424,8 +1478,8 @@
         )
         late_sum, qkv_g = lax.optimization_barrier((mlp_sums[0], qkv_g))
         far = lax.ppermute(late_sum, "section", [(1, 0)])
-        qkv_g, out_g, grad_down, grad_up, small = final_layouts(
-            qkv_g, out_g, late_sum, far, down_one, up_one
+        qkv_g, out_g, grad_down, grad_up, small, made, grads = final_layouts(
+            qkv_g, out_g, late_sum, far, down_one, up_one, made, grads
         )
         made, grads = made[None, :, None], grads[None, :, None]
     else:

time: 894 us -> 881 us (0.985)
  Pallas kernels: 606 us -> 629 us
  waiting for transfers between devices: 124 us -> 101 us
    pallas_call x1, Pallas kernels: 57.3 us -> 89.1 us  [first_weights(): pl.pallas_call(weights_kernel, out_shape=(jax.ShapeDtypeStruct((4, D, WID...]
    all_to_all x2, waiting for transfers between devices: 18.9 us -> 0.01 us  [on_device(): lax.all_to_all(up_g.astype(BF).reshape(nf, shard, ff_here), 'fsdp', split...]
    all_to_all x1 -> x0, waiting for transfers between devices: 16.1 us -> none  [on_device(): lax.all_to_all(up_blocks, 'fsdp', split_axis=0, concat_axis=0, tiled=True)]
    unnamed x118 -> x98, local copies, waits for them, and re-layouts: 26.8 us -> 28.8 us
  transfers between devices with their start and end apart: 11 -> 9, of which waited for: 5 -> 4; matrix products, arithmetic and copies ran while one was open for 8% -> 6% of each run, Pallas kernels for 42% -> 42%
where the time goes in v7:
time: 881 us; the launch traced here: 871 us
  Pallas kernels  629 us (71%)
  waiting for transfers between devices  101 us (11%)
  matrix products  50.3 us (6%)
  local copies, waits for them, and re-layouts  43.4 us (5%)
  other arithmetic  21.7 us (2%)
  between operations  14.4 us (2%)
  starting transfers between devices  11.4 us (1%)
    pallas_call x4, Pallas kernels, plane_call(): pl.pallas_call(kernel, out_shape=outs, in_specs=[VSPEC, any_spec, any_spe...  194 us
    pallas_call x1, Pallas kernels, reduce_both(): pl.pallas_call(reduce_kernel, out_shape=(*(jax.ShapeDtypeStruct(shape, BF...  171 us
    pallas_call x2, Pallas kernels, block_backward(): pl.pallas_call(functools.partial(block_back_kernel, ring), out_shape=tupl...  104 us
    pallas_call x1, Pallas kernels, first_weights(): pl.pallas_call(weights_kernel, out_shape=(jax.ShapeDtypeStruct((4, D, WID...  89.1 us
    psum x2, waiting for transfers between devices, on_device(): mlp_sums[layer] = lax.psum(halves, 'ctx')  87.7 us
    pallas_call x2, Pallas kernels, block_forward(): pl.pallas_call(functools.partial(block_kernel, ring), out_shape=tuple((ja...  56.5 us
    dot_general x12, matrix products, mm_tn(): lax.dot_general(a, b, (((0,), (0,)), ((), ())), preferred_element_type=F32)  50.3 us
    unnamed x98, local copies, waits for them, and re-layouts  28.8 us
  transfers between devices with their start and end apart: 9, of which 4 were waited for; matrix products, arithmetic and copies ran while one was open for 6% of the time, Pallas kernels for 42%

profile of v7, /device:TPU:0, one launch (start us, length us, event | category | flops | bytes accessed | tf_op | source)
XLA Modules:
  0.0 871.0 jit_solution(1722423523110024158)
XLA Ops:
  9.9 1.6 fusion.21
  11.4 2.0 fusion.18
  13.4 2.1 constant_dynamic-slice_fusion
  18.0 2.2 pad_maximum_fusion.own
  21.2 89.1 %first_weights.1 = (bf16[4,1088,1152]{2,1,0:T(8,128)(2,1)}, bf16[768,1088]{1,0:T(8,128)(2,1)S(1)}, bf16[2,1088,1088]{2,1,0:T(8,128)(2,1)}, bf16[2,1088,1088]{2,1,0:T(8,128)(2,1)}) custom-call(bf16[4,272,1152]{2,1,0:T(8,128)(2,1)S(1)} %pad_maximum_fusion.own, bf16[256,1088]{1,0:T(8,128)(2,1)S(1)} %bitcast.105, bf16[272,4352]{1,0:T(8,128)(2,1)S(1)} %bitcast.104, ...), custom_call_target="tpu_custom_call" | custom-call | bytes 262500000 | tf_op jit(solution)/shard_map/first_weights/pallas_call | solution.py:460
  111.5 1.3 constant_dynamic-slice_fusion.1
  113.4 3.1 collective-permute-done
  116.5 2.1 bitcast_select_fusion
  120.9 24.5 %block_forward.2 = (bf16[768,1088]{1,0:T(8,128)(2,1)}, bf16[256,1152]{1,0:T(8,128)(2,1)}, bf16[768,1152]{1,0:T(8,128)(2,1)}, bf16[768,1152]{1,0:T(8,128)(2,1)}, ...) custom-call(bf16[768,1088]{1,0:T(8,128)(2,1)} %copy-done.2, ...), custom_call_target="tpu_custom_call" | custom-call | bytes 77000000 | tf_op jit(solution)/shard_map/block_forward/pallas_call | solution.py:1159
  146.6 1.5 copy-done.4
  150.2 66.9 %shard_map.169 = (bf16[256,1088]{1,0:T(8,128)(2,1)S(1)}, bf16[4,256,1088]{2,1,0:T(8,128)(2,1)S(1)}, bf16[4,256,1088]{2,1,0:T(8,128)(2,1)S(1)}, f32[4,256,1088]{2,1,0:T(8,128)S(1)}) custom-call(bf16[256,1088]{1,0:T(8,128)(2,1)S(1)} %copy-done.16, bf16[2,1088,1088]{2,1,0:T(8,128)(2,1)} %get-tuple-element.89.up_both, ...), custom_call_target="tpu_custom_call" | custom-call | bytes 140000000 | tf_op jit(solution)/shard_map/pallas_call | solution.py:204
  217.1 2.2 copy-done.6
  220.1 1.4 copy-done.20
  221.5 32.0 %block_forward.3 = (bf16[768,1088]{1,0:T(8,128)(2,1)}, bf16[256,1152]{1,0:T(8,128)(2,1)}, bf16[768,1152]{1,0:T(8,128)(2,1)}, bf16[768,1152]{1,0:T(8,128)(2,1)}, ...) custom-call(bf16[256,1088]{1,0:T(8,128)(2,1)} %copy-done.11, ...), custom_call_target="tpu_custom_call" | custom-call | bytes 157500000 | tf_op jit(solution)/shard_map/block_forward/pallas_call | solution.py:1159
  257.6 40.8 %shard_map.170 = (bf16[256,1088]{1,0:T(8,128)(2,1)S(1)}, bf16[4,256,1088]{2,1,0:T(8,128)(2,1)S(1)}, bf16[4,256,1088]{2,1,0:T(8,128)(2,1)S(1)}, f32[4,256,1088]{2,1,0:T(8,128)S(1)}) custom-call(bf16[256,1088]{1,0:T(8,128)(2,1)S(1)} %copy-done.17, bf16[2,1088,1088]{2,1,0:T(8,128)(2,1)} %get-tuple-element.89.up_both, ...), custom_call_target="tpu_custom_call" | custom-call | bytes 140000000 | tf_op jit(solution)/shard_map/pallas_call | solution.py:204
  298.4 1.4 copy-done.22
  299.8 39.9 %shard_map.171 = (f32[256,1088]{1,0:T(8,128)S(1)}, bf16[4,256,1088]{2,1,0:T(8,128)(2,1)S(1)}, bf16[4,256,1088]{2,1,0:T(8,128)(2,1)S(1)}, f32[1,1088]{1,0:T(1,128)S(1)}) custom-call(bf16[256,1088]{1,0:T(8,128)(2,1)S(1)} %bitcast.101, bf16[2,1088,1088]{2,1,0:T(8,128)(2,1)} %get-tuple-element.89.up_both, bf16[2,1088,1088]{2,1,0:T(8,128)(2,1)} %get-tuple-element.90.down_both, ...), custom_call_target="tpu_custom_call" | custom-call | bytes 140000000 | tf_op jit(solution)/shard_map/pallas_call | solution.py:204
  339.8 4.6 fusion.1
  344.4 4.7 all-to-all-start
  351.5 69.9 %block_backward.2 = (f32[256,1088]{1,0:T(8,128)}, bf16[256,1088]{1,0:T(8,128)(2,1)}, bf16[256,1152]{1,0:T(8,128)(2,1)}, bf16[768,1152]{1,0:T(8,128)(2,1)}, bf16[...) custom-call(f32[256,1088]{1,0:T(8,128)} %copy-done.13, bf16[256,1088]{1,0:T(8,128)(2,1)} %bitcast.102, ...), custom_call_target="tpu_custom_call" | custom-call | bytes 203000000 | tf_op jit(solution)/shard_map/block_backward/pallas_call | solution.py:1323
  421.4 6.9 fusion
  428.3 2.1 fusion.11
  430.5 4.7 collective-permute-done.1
  435.3 3.5 fusion.5
  438.7 2.3 copy-done.7
  441.1 46.1 %shard_map.172 = (f32[256,1088]{1,0:T(8,128)S(1)}, bf16[4,256,1088]{2,1,0:T(8,128)(2,1)S(1)}, bf16[4,256,1088]{2,1,0:T(8,128)(2,1)S(1)}, f32[1,1088]{1,0:T(1,128)S(1)}) custom-call(bf16[256,1088]{1,0:T(8,128)(2,1)S(1)} %copy-done.10, bf16[2,1088,1088]{2,1,0:T(8,128)(2,1)} %get-tuple-element.89.up_both, bf16[2,1088,1088]{2,1,0:T(8,128)(2,1)} %get-tuple-element.90.down_both, ...), custom_call_target="tpu_custom_call" | custom-call | bytes 140000000 | tf_op jit(solution)/shard_map/pallas_call | solution.py:204
  487.2 4.6 fusion.3
  491.9 4.5 all-to-all-start.1
  498.0 33.7 %block_backward.3 = (f32[256,1088]{1,0:T(8,128)}, bf16[256,1152]{1,0:T(8,128)(2,1)}, bf16[768,1152]{1,0:T(8,128)(2,1)}, bf16[768,1152]{1,0:T(8,128)(2,1)}, f32[2...) custom-call(f32[256,1088]{1,0:T(8,128)} %copy-done.12, ...), custom_call_target="tpu_custom_call" | custom-call | bytes 133000000 | tf_op jit(solution)/shard_map/block_backward/pallas_call | solution.py:1323
  531.8 6.3 fusion.2
  538.0 3.4 fusion.7
  541.7 1.9 slice.37.wide
  543.6 4.4 convolution_convert_fusion.6.o1
  548.0 3.9 convolution_convert_fusion.3.k1
  551.9 3.4 fusion.4
  555.4 87.7 %all-reduce.6.cloned.1.call-done.mlp = bf16[2,544,1088]{2,1,0:T(8,128)(2,1)} async-done(((bf16[2,544,1088]{2,1,0:T(8,128)(2,1)}), bf16[2,544,1088]{2,1,0:T(8,128)(2,1)}) %all-reduce.6.cloned.1.call-update) | async-done | bytes 2367504 | tf_op jit(solution)/shard_map/psum | solution.py:1470
  643.1 2.4 convolution_convert_fusion.q1
  645.5 3.9 convolution_convert_fusion.2.v1
  649.4 2.4 convolution_convert_fusion.1.q0
  651.8 3.1 convolution_convert_fusion.7.o0
  654.9 4.1 convolution_convert_fusion.5.k0
  658.9 3.8 convolution_convert_fusion.4.v0
  662.8 171.3 %reduce_both.1 = (bf16[272,3264]{1,0:T(8,128)(2,1)}, bf16[272,1152]{1,0:T(8,128)(2,1)}, bf16[1088,1088]{1,0:T(8,128)(2,1)}, bf16[272,4352]{1,0:T(8,128)(2,1)}, b...) custom-call(bf16[1088,1152]{1,0:T(8,128)(2,1)} %convolution_convert_fusion.1.q0, ...), custom_call_target="tpu_custom_call" | custom-call | bytes 420000000 | tf_op jit(solution)/shard_map/reduce_both/pallas_call | solution.py:826
  835.4 5.5 collective-permute-done.3.far
  840.9 1.5 copy-done.28
  843.5 14.6 %final_layouts.1 = (f32[272,3264]{1,0:T(8,128)}, f32[272,1088]{1,0:T(8,128)}, f32[1088,1088]{1,0:T(8,128)}, f32[272,4352]{1,0:T(8,128)}, f32[16,272]{1,0:T(8,128...) custom-call(bf16[272,3264]{1,0:T(8,128)(2,1)} %get-tuple-element.147.qkv, ...), custom_call_target="tpu_custom_call" | custom-call | bytes 35000000 | tf_op jit(solution)/shard_map/final_layouts/pallas_call | solution.py:906
  858.6 1.4 copy.51
  860.0 3.0 copy.52
  (135 shorter events, 27.1 us)
Async XLA Ops:
  7.2 112.6 %copy-start = (s32[2,1,1024]{2,1,0:T(1,128)S(1)}, s32[2,1,1024]{2,1,0:T(1,128)}, u32[]{:S(2)}) copy-start(s32[2,1,1024]{2,1,0:T(1,128)} %param.11) | copy-start | bytes 24580
  7.2 4.2 copy-start.38
  7.2 214.3 %all-gather.2.cloned.1.call-start = ((), (), s32[]{:S(2)}) async-start(), calls=%async_computation.2 | async-start | bytes 11280384 | tf_op jit(solution)/shard_map/all_gather | solution.py:1403
  15.5 1.4 copy-start.30
  18.0 2.5 copy-start.8
  18.0 3.2 copy-start.9
  110.3 1.2 copy-start.2
  112.8 3.6 copy-start.27
  113.3 3.1 collective-permute-start
  120.9 25.4 %copy-start.29 = (bf16[1,1,256,1088]{2,3,1,0:T(8,128)(2,1)S(1)}, bf16[1,1,256,1088]{2,3,1,0:T(8,128)(2,1)}, u32[]{:S(2)}) copy-start(bf16[1,1,256,1088]{2,3,1,0:T(8,128)(2,1)} %get-tuple-element.185) | copy-start | bytes 1671172
  146.6 153.3 %copy-start.3 = (bf16[1,1,256,1088]{3,2,1,0:T(8,128)(2,1)}, bf16[1,1,256,1088]{3,2,1,0:T(8,128)(2,1)S(1)}, u32[]{:S(2)}) copy-start(bf16[1,1,256,1088]{3,2,1,0:T(8,128)(2,1)S(1)} %copy.42) | copy-start | bytes 1671172
  146.6 1.5 copy-start.4
  149.0 1.2 copy-start.16
  217.1 2.2 copy-start.6
  220.1 1.4 copy-start.20
  254.4 1.3 copy-start.5
  298.4 1.4 copy-start.22
  299.8 40.0 %copy-start.18 = (bf16[256,1088]{1,0:T(8,128)(2,1)}, bf16[256,1088]{1,0:T(8,128)(2,1)S(1)}, u32[]{:S(2)}) copy-start(bf16[256,1088]{1,0:T(8,128)(2,1)S(1)} %get-tuple-element.141.made1) | copy-start | bytes 1671172
  339.8 4.6 copy-start.13
  339.8 4.6 copy-start.24
  344.4 83.9 %all-to-all-start = ((bf16[4,272,1088]{2,1,0:T(8,128)(2,1)}), bf16[4,272,1088]{2,1,0:T(8,128)(2,1)}, u32[]{:S(2)}, u32[]{:S(2)}) async-start(bf16[4,272,1088]{2,1,0:T(8,128)(2,1)} %bitcast.114), calls=%async_computation | async-start | bytes 5013504 | tf_op jit(solution)/shard_map/all_to_all | solution.py:1459
  428.3 6.9 copy-start.26
  430.4 8.3 copy-start.10
  430.4 4.8 collective-permute-start.1
  438.7 2.3 copy-start.7
  441.1 46.2 %copy-start.21 = (bf16[4,256,1088]{2,1,0:T(8,128)(2,1)S(1)}, bf16[4,256,1088]{2,1,0:T(8,128)(2,1)}, u32[]{:S(2)}) copy-start(bf16[4,256,1088]{2,1,0:T(8,128)(2,1)} %copy-done.20) | copy-start | bytes 6684676
  487.2 4.6 copy-start.12
  487.2 4.6 copy-start.23
  491.9 46.2 %all-to-all-start.1 = ((bf16[4,272,1088]{2,1,0:T(8,128)(2,1)}), bf16[4,272,1088]{2,1,0:T(8,128)(2,1)}, u32[]{:S(2)}, u32[]{:S(2)}) async-start(bf16[4,272,1088]{2,1,0:T(8,128)(2,1)} %bitcast.113), calls=%async_computation.1 | async-start | bytes 5013504 | tf_op jit(solution)/shard_map/all_to_all | solution.py:1459
  496.4 146.7 %all-reduce.6.cloned.1.call-start = ((), (), s32[]{:S(2)}) async-start(), calls=%async_computation.3 | async-start | bytes 5013504 | tf_op jit(solution)/shard_map/psum | solution.py:1470
  541.5 2.2 copy-start.43
  541.5 10.5 %collective-permute-start.2 = (bf16[2,544,1088]{2,1,0:T(8,128)(2,1)}, bf16[2,544,1088]{2,1,0:T(8,128)(2,1)S(1)}, u32[]{:S(2)}, u32[]{:S(2)}) collective-permute-start(bf16[2,544,1088]{2,1,0:T(8,128)(2,1)} %fusion.7), channel_id=1, source_target_pairs={{0,16},{16,0},{1,17},{17,1},{2,18},{18,2},{3,19},{19,3},{4,20},{20... | collective-permute-start | bytes 7102472 | tf_op jit(solution)/shard_map/ppermute | solution.py:968
  541.5 292.6 %all-reduce.8.cloned.1.call-start = ((), (), s32[]{:S(2)}) async-start(), calls=%async_computation.4 | async-start | bytes 5013504 | tf_op jit(solution)/shard_map/psum | solution.py:1470
  543.6 4.4 copy-start.32
  543.6 4.4 copy-start.40
  548.0 3.9 copy-start.25
  555.4 87.7 %copy-start.33 = (bf16[768,1088]{1,0:T(8,128)(2,1)S(1)}, bf16[768,1088]{1,0:T(8,128)(2,1)}, u32[]{:S(2)}) copy-start(bf16[768,1088]{1,0:T(8,128)(2,1)} %get-tuple-element.135) | copy-start | bytes 5013508
  555.4 87.8 %copy-start.34 = (bf16[256,1152]{1,0:T(8,128)(2,1)S(1)}, bf16[256,1152]{1,0:T(8,128)(2,1)}, u32[]{:S(2)}) copy-start(bf16[256,1152]{1,0:T(8,128)(2,1)} %get-tuple-element.111) | copy-start | bytes 1769476
  643.1 2.4 copy-start.39
  645.5 3.9 copy-start.31
  645.5 3.9 copy-start.35
  649.4 2.4 copy-start.44
  649.4 2.4 copy-start.45
  651.8 3.1 copy-start.42
  654.9 4.1 copy-start.41
  834.1 6.8 collective-permute-start.3
  840.9 1.5 copy-start.28
  858.6 5.7 copy-start.1
  (7 other events, 6.0 us)
Sparse Core Ops, SparseCore 0:
  119.9 82.2 all-gather.1
  541.6 101.4 all-reduce.5
  645.5 140.9 all-reduce.7

commit v8 on v7

--- a/solution.py
+++ b/solution.py
@@ -276,8 +276,9 @@
 
 
 def weights_kernel(
-    own, rows_in, up_in, down_in, full, rows_out, up_out, down_out,
-    up_blocks, load, core_s, core_r, p_send, p_recv, f_send, f_recv, z_send, z_recv,
+    qkv_in, out_in, gains, biases, hidden, rows_in, up_in, down_in,
+    full, rows_out, up_out, down_out, next_half,
+    own, other_half, up_blocks, load, core_s, core_r, p_send, p_recv, f_send, f_recv, z_send, z_recv,
     u_send, u_recv, v_send, v_recv,
 ):
     s = lax.axis_index("section")
@@ -294,6 +295,23 @@
             src_ref=src, dst_ref=dst, send_sem=send, recv_sem=recv,
             device_id=where, device_id_type=MESH,
         )
+
+    pad = jnp.zeros((shard, wide - D), BF)
+    for p in range(3):
+        own[p] = jnp.concatenate([qkv_in[:, pl.ds(p * D, D)], pad], axis=1)
+    unit_rows = (
+        lax.broadcasted_iota(jnp.int32, (16, 64), 0) == lax.broadcasted_iota(jnp.int32, (16, 64), 1)
+    ).astype(F32)
+    hidden_rows = [hidden[:, pl.ds(i * shard, shard)] for i in range(hidden.shape[1] // shard)]
+    small = jnp.concatenate(
+        [
+            value.astype(F32)
+            for value in (gains[...], biases[...], *hidden_rows, jnp.zeros((8 - len(hidden_rows), shard)))
+        ],
+        axis=0,
+    )
+    beside = mm_tn(small.astype(BF), unit_rows.astype(BF)).astype(BF)
+    own[3] = jnp.concatenate([out_in[...], beside], axis=1)
 
     barrier = pltpu.get_barrier_semaphore()
     z = lax.axis_index("ctx")
@@ -375,6 +393,16 @@
     down_near = pltpu.make_async_copy(down_in, down_out.at[s], load.at[4])
     down_far.start()
     down_near.start()
+    swap = to(other_half, next_half, core_s.at[5], core_r.at[5], section=0)
+
+    @pl.when(s == 1)
+    def _():
+        for p in range(4):
+            at = pl.ds(p * wide, wide)
+            other_half[:, at] = own[p, pl.ds(0, shard // 2), :]
+            next_half[:, at] = own[p, pl.ds(shard // 2, shard // 2), :]
+        swap.start()
+
     for j in range(4):
         up_blocks[j] = up_in[:, pl.ds(j * D, D)]
 
@@ -441,6 +469,8 @@
 
     down_near.wait()
     down_far.wait()
+    pl.when(s == 0)(swap.wait_recv)
+    pl.when(s == 1)(swap.wait_send)
 
     @pl.when(z < 3)
     def _():
@@ -455,29 +485,28 @@
         step_two.wait_recv()
 
 
-def first_weights(own, rows_in, up, down):
+def first_weights(qkv, out, gains, biases, hidden, rows_in, up, down):
     dma = pltpu.SemaphoreType.DMA
+    shard = qkv.shape[0]
+    shapes = ((4, D, WIDE), (3 * rows_in.shape[0], D), (2, D, D), (2, D, D), (shard // 2, 4 * WIDE))
     return pl.pallas_call(
         weights_kernel,
-        out_shape=(
-            jax.ShapeDtypeStruct((4, D, WIDE), BF),
-            jax.ShapeDtypeStruct((3 * rows_in.shape[0], D), BF),
-            jax.ShapeDtypeStruct((2, D, D), BF),
-            jax.ShapeDtypeStruct((2, D, D), BF),
-        ),
-        in_specs=[pl.BlockSpec(memory_space=pl.ANY), VSPEC, VSPEC, pl.BlockSpec(memory_space=pl.ANY)],
-        out_specs=(VSPEC,) * 4,
+        out_shape=tuple(jax.ShapeDtypeStruct(shape, BF) for shape in shapes),
+        in_specs=[VSPEC] * 7 + [pl.BlockSpec(memory_space=pl.ANY)],
+        out_specs=(VSPEC,) * 5,
         scratch_shapes=[
-            pltpu.VMEM((4, up.shape[0], D), BF),
-            dma((6,)), dma((5,)), dma((5,)), dma((2, 4)), dma((2, 4)), dma((2, 3)), dma((2, 3)),
+            pltpu.VMEM((4, shard, WIDE), BF),
+            pltpu.VMEM((shard // 2, 4 * WIDE), BF),
+            pltpu.VMEM((4, shard, D), BF),
+            dma((6,)), dma((6,)), dma((6,)), dma((2, 4)), dma((2, 4)), dma((2, 3)), dma((2, 3)),
             dma((2,)), dma((2,)), dma((3,)), dma((3,)), dma((4,)), dma((4,)),
         ],
         compiler_params=pltpu.CompilerParams(
-            collective_id=4, has_side_effects=True, vmem_limit_bytes=40 * 1024 * 1024
+            collective_id=4, has_side_effects=True, vmem_limit_bytes=48 * 1024 * 1024
         ),
         cost_estimate=lasting(75),
         name="first_weights",
-    )(own, rows_in, up, down)
+    )(qkv, out, gains, biases, hidden, rows_in, up, down)
 
 
 def z_partners():
@@ -1368,44 +1397,36 @@
     bias = jnp.where(allowed, 0.0, -1e30).astype(F32)
     bias_t = bias.T
 
-    small = jnp.concatenate(
-        [norm_gains[0].T, biases[0].T, ff_bias[0].reshape(per_row, shard).T], axis=1
-    )
-    packed = jnp.stack(
-        [
-            widen(qkv_weight[0][:, :D]),
-            widen(qkv_weight[0][:, D : 2 * D]),
-            widen(qkv_weight[0][:, 2 * D :]),
-            jnp.concatenate(
-                [out_weight[0], small, jnp.zeros((shard, WIDE - D - 8 - per_row), BF)], axis=1
-            ),
-        ]
-    )
+    def gathered(rows_first):
+        return lax.all_gather(rows_first, pair, axis=0, tiled=True)
+
     if fits:
-        zero, wide_in, up_w, down_w = first_weights(
-            packed, own_in, up_weight[0], down_weight[0]
-        )
-        packed, zero = lax.optimization_barrier((packed, zero))
+        zero, wide_in, up_w, down_w, one_half = first_weights(
+            qkv_weight[0], out_weight[0], norm_gains[0], biases[0], ff_bias,
+            own_in, up_weight[0], down_weight[0],
+        )
+        one = gathered(one_half)
     else:
+        small = jnp.concatenate(
+            [norm_gains[0].T, biases[0].T, ff_bias[0].reshape(per_row, shard).T], axis=1
+        )
+        beside = jnp.pad(small, ((0, 0), (0, WIDE - D - 8 - per_row)))
+        packed = jnp.concatenate(
+            [widen(qkv_weight[0][:, i * D : (i + 1) * D]) for i in range(3)]
+            + [out_weight[0], beside],
+            axis=1,
+        )
+        halves = packed.reshape(2, shard // 2, 4 * WIDE)
+        keep = lax.dynamic_index_in_dim(halves, s, 0, keepdims=False)
+        recv = on_chip(lax.dynamic_index_in_dim(halves, 1 - s, 0, keepdims=False))
+        zero, one = gathered(pick(s, keep, recv)), gathered(pick(s, recv, keep))
         up_own = lax.all_to_all(
             up_weight[0].reshape(shard, nf, ff_here), "fsdp", split_axis=1, concat_axis=0, tiled=True
         ).reshape(D, ff_here)
         up_w = both_layers(up_own, s)
         down_w = both_layers(down_weight[0], s)
         wide_in = with_halo(own_in, chunks)
-    half = shard // 2
-    halves = packed.reshape(4, 2, half, WIDE)
-    keep = lax.dynamic_index_in_dim(halves, s, 1, keepdims=False)
-    give = lax.dynamic_index_in_dim(halves, 1 - s, 1, keepdims=False)
-
-    def gathered(part):
-        rows_first = part.transpose(1, 0, 2).reshape(half, 4 * WIDE)
-        return lax.all_gather(rows_first, pair, axis=0, tiled=True)
-
-    recv = on_chip(give)
-    one = gathered(pick(s, recv, keep))
-    if not fits:
-        zero = gathered(pick(s, keep, recv))
+
     weights = (zero, one)
 
     kept = []

time: 881 us -> 869 us (0.986)
    unnamed x98 -> x97, local copies, waits for them, and re-layouts: 28.8 us -> 26 us
  transfers between devices with their start and end apart: 9 -> 8, of which waited for: 4 -> 3; matrix products, arithmetic and copies ran while one was open for 6% -> 6% of each run, Pallas kernels for 42% -> 43%
where the time goes in v8:
time: 869 us; the launch traced here: 860 us
  Pallas kernels  635 us (73%)
  waiting for transfers between devices  98.1 us (11%)
  matrix products  50.2 us (6%)
  local copies, waits for them, and re-layouts  36.2 us (4%)
  other arithmetic  14.8 us (2%)
  between operations  14.4 us (2%)
  starting transfers between devices  11.3 us (1%)
    pallas_call x4, Pallas kernels, plane_call(): pl.pallas_call(kernel, out_shape=outs, in_specs=[VSPEC, any_spec, any_spe...  196 us
    pallas_call x1, Pallas kernels, reduce_both(): pl.pallas_call(reduce_kernel, out_shape=(*(jax.ShapeDtypeStruct(shape, BF...  171 us
    pallas_call x2, Pallas kernels, block_backward(): pl.pallas_call(functools.partial(block_back_kernel, ring), out_shape=tupl...  103 us
    pallas_call x1, Pallas kernels, first_weights(): pl.pallas_call(weights_kernel, out_shape=tuple((jax.ShapeDtypeStruct(shap...  91.3 us
    psum x2, waiting for transfers between devices, on_device(): mlp_sums[layer] = lax.psum(halves, 'ctx')  87.8 us
    pallas_call x2, Pallas kernels, block_forward(): pl.pallas_call(functools.partial(block_kernel, ring), out_shape=tuple((ja...  59 us
    dot_general x12, matrix products, mm_tn(): lax.dot_general(a, b, (((0,), (0,)), ((), ())), preferred_element_type=F32)  50.2 us
    unnamed x97, local copies, waits for them, and re-layouts  26 us
  transfers between devices with their start and end apart: 8, of which 3 were waited for; matrix products, arithmetic and copies ran while one was open for 6% of the time, Pallas kernels for 43%

profile of v8, /device:TPU:0, one launch (start us, length us, event | category | flops | bytes accessed | tf_op | source)
XLA Modules:
  0.0 860.4 jit_solution(12125272231867600515)
XLA Ops:
  7.3 2.4 constant_dynamic-slice_fusion
  9.7 1.3 copy.19
  11.1 91.3 %first_weights.1 = (bf16[4,1088,1152]{2,1,0:T(8,128)(2,1)}, bf16[768,1088]{1,0:T(8,128)(2,1)S(1)}, bf16[2,1088,1088]{2,1,0:T(8,128)(2,1)}, bf16[2,1088,1088]{2,1,0:T(8,128)(2,1)}, bf16[136,4608]{1,0:T(8,128)(2,1)S(1)}) custom-call(bf16[272,3264]{1,0:T(8,128)(2,1)S(1)} %bitcast.82, bf16[272,1088]{1,0:T(8,128)(2,1)S(1)} %bitcast.84, ...), custom_call_target="tpu_custom_call" | custom-call | bytes 262500000 | tf_op jit(solution)/shard_map/first_weights/pallas_call | solution.py:492
  102.4 1.2 copy-done.2
  105.8 24.5 %block_forward.2 = (bf16[768,1088]{1,0:T(8,128)(2,1)}, bf16[256,1152]{1,0:T(8,128)(2,1)}, bf16[768,1152]{1,0:T(8,128)(2,1)}, bf16[768,1152]{1,0:T(8,128)(2,1)}, ...) custom-call(bf16[768,1088]{1,0:T(8,128)(2,1)} %copy-done.2, ...), custom_call_target="tpu_custom_call" | custom-call | bytes 77000000 | tf_op jit(solution)/shard_map/block_forward/pallas_call | solution.py:1188
  131.5 1.5 copy-done.4
  133.9 1.2 copy-done.17
  135.1 67.6 %shard_map.169 = (bf16[256,1088]{1,0:T(8,128)(2,1)S(1)}, bf16[4,256,1088]{2,1,0:T(8,128)(2,1)S(1)}, bf16[4,256,1088]{2,1,0:T(8,128)(2,1)S(1)}, f32[4,256,1088]{2,1,0:T(8,128)S(1)}) custom-call(bf16[256,1088]{1,0:T(8,128)(2,1)S(1)} %copy-done.17, bf16[2,1088,1088]{2,1,0:T(8,128)(2,1)} %get-tuple-element.87.up_both, ...), custom_call_target="tpu_custom_call" | custom-call | bytes 140000000 | tf_op jit(solution)/shard_map/pallas_call | solution.py:204
  202.7 2.2 copy-done.6
  205.7 1.4 copy-done.24
  207.1 34.5 %block_forward.3 = (bf16[768,1088]{1,0:T(8,128)(2,1)}, bf16[256,1152]{1,0:T(8,128)(2,1)}, bf16[768,1152]{1,0:T(8,128)(2,1)}, bf16[768,1152]{1,0:T(8,128)(2,1)}, ...) custom-call(bf16[256,1088]{1,0:T(8,128)(2,1)} %copy-done.9, ...), custom_call_target="tpu_custom_call" | custom-call | bytes 157500000 | tf_op jit(solution)/shard_map/block_forward/pallas_call | solution.py:1188
  242.5 1.3 copy-done.5
  245.7 40.8 %shard_map.170 = (bf16[256,1088]{1,0:T(8,128)(2,1)S(1)}, bf16[4,256,1088]{2,1,0:T(8,128)(2,1)S(1)}, bf16[4,256,1088]{2,1,0:T(8,128)(2,1)S(1)}, f32[4,256,1088]{2,1,0:T(8,128)S(1)}) custom-call(bf16[256,1088]{1,0:T(8,128)(2,1)S(1)} %copy-done.18, bf16[2,1088,1088]{2,1,0:T(8,128)(2,1)} %get-tuple-element.87.up_both, ...), custom_call_target="tpu_custom_call" | custom-call | bytes 140000000 | tf_op jit(solution)/shard_map/pallas_call | solution.py:204
  286.5 1.4 copy-done.26
  287.9 41.8 %shard_map.171 = (f32[256,1088]{1,0:T(8,128)S(1)}, bf16[4,256,1088]{2,1,0:T(8,128)(2,1)S(1)}, bf16[4,256,1088]{2,1,0:T(8,128)(2,1)S(1)}, f32[1,1088]{1,0:T(1,128)S(1)}) custom-call(bf16[256,1088]{1,0:T(8,128)(2,1)S(1)} %bitcast.79, bf16[2,1088,1088]{2,1,0:T(8,128)(2,1)} %get-tuple-element.87.up_both, bf16[2,1088,1088]{2,1,0:T(8,128)(2,1)} %get-tuple-element.88.down_both, ...), custom_call_target="tpu_custom_call" | custom-call | bytes 140000000 | tf_op jit(solution)/shard_map/pallas_call | solution.py:204
  329.8 4.6 fusion.1
  334.4 4.7 all-to-all-start
  339.1 1.2 fusion.17.bias_t
  341.5 69.3 %block_backward.2 = (f32[256,1088]{1,0:T(8,128)}, bf16[256,1088]{1,0:T(8,128)(2,1)}, bf16[256,1152]{1,0:T(8,128)(2,1)}, bf16[768,1152]{1,0:T(8,128)(2,1)}, bf16[...) custom-call(f32[256,1088]{1,0:T(8,128)} %copy-done.12, bf16[256,1088]{1,0:T(8,128)(2,1)} %bitcast.80, ...), custom_call_target="tpu_custom_call" | custom-call | bytes 203000000 | tf_op jit(solution)/shard_map/block_backward/pallas_call | solution.py:1352
  410.8 6.9 fusion
  417.7 2.1 fusion.11
  419.9 4.7 collective-permute-done
  424.6 3.5 fusion.5
  428.1 2.3 copy-done.7
  430.5 46.1 %shard_map.172 = (f32[256,1088]{1,0:T(8,128)S(1)}, bf16[4,256,1088]{2,1,0:T(8,128)(2,1)S(1)}, bf16[4,256,1088]{2,1,0:T(8,128)(2,1)S(1)}, f32[1,1088]{1,0:T(1,128)S(1)}) custom-call(bf16[256,1088]{1,0:T(8,128)(2,1)S(1)} %copy-done.8, bf16[2,1088,1088]{2,1,0:T(8,128)(2,1)} %get-tuple-element.87.up_both, bf16[2,1088,1088]{2,1,0:T(8,128)(2,1)} %get-tuple-element.88.down_both, ...), custom_call_target="tpu_custom_call" | custom-call | bytes 140000000 | tf_op jit(solution)/shard_map/pallas_call | solution.py:204
  476.6 4.6 fusion.3
  481.2 4.5 all-to-all-start.1
  487.4 33.7 %block_backward.3 = (f32[256,1088]{1,0:T(8,128)}, bf16[256,1152]{1,0:T(8,128)(2,1)}, bf16[768,1152]{1,0:T(8,128)(2,1)}, bf16[768,1152]{1,0:T(8,128)(2,1)}, f32[2...) custom-call(f32[256,1088]{1,0:T(8,128)} %copy-done.13, ...), custom_call_target="tpu_custom_call" | custom-call | bytes 133000000 | tf_op jit(solution)/shard_map/block_backward/pallas_call | solution.py:1352
  521.1 6.3 fusion.2
  527.4 3.4 fusion.7
  531.1 1.9 slice.24.wide
  533.0 4.4 convolution_convert_fusion.6.o1
  537.4 3.9 convolution_convert_fusion.3.k1
  541.3 3.4 fusion.4
  544.7 87.8 %all-reduce.4.cloned.1.call-done.mlp = bf16[2,544,1088]{2,1,0:T(8,128)(2,1)} async-done(((bf16[2,544,1088]{2,1,0:T(8,128)(2,1)}), bf16[2,544,1088]{2,1,0:T(8,128)(2,1)}) %all-reduce.4.cloned.1.call-update) | async-done | bytes 2367504 | tf_op jit(solution)/shard_map/psum | solution.py:1491
  632.6 2.4 convolution_convert_fusion.q1
  634.9 3.9 convolution_convert_fusion.2.v1
  638.8 2.4 convolution_convert_fusion.1.q0
  641.2 3.1 convolution_convert_fusion.7.o0
  644.3 4.1 convolution_convert_fusion.5.k0
  648.4 3.8 convolution_convert_fusion.4.v0
  652.2 171.2 %reduce_both.1 = (bf16[272,3264]{1,0:T(8,128)(2,1)}, bf16[272,1152]{1,0:T(8,128)(2,1)}, bf16[1088,1088]{1,0:T(8,128)(2,1)}, bf16[272,4352]{1,0:T(8,128)(2,1)}, b...) custom-call(bf16[1088,1152]{1,0:T(8,128)(2,1)} %convolution_convert_fusion.1.q0, ...), custom_call_target="tpu_custom_call" | custom-call | bytes 420000000 | tf_op jit(solution)/shard_map/reduce_both/pallas_call | solution.py:855
  823.4 1.3 collective-permute-start.2
  824.7 5.5 collective-permute-done.2.far
  830.3 1.5 copy-done.31
  832.8 14.6 %final_layouts.1 = (f32[272,3264]{1,0:T(8,128)}, f32[272,1088]{1,0:T(8,128)}, f32[1088,1088]{1,0:T(8,128)}, f32[272,4352]{1,0:T(8,128)}, f32[16,272]{1,0:T(8,128...) custom-call(bf16[272,3264]{1,0:T(8,128)(2,1)} %get-tuple-element.145.qkv, ...), custom_call_target="tpu_custom_call" | custom-call | bytes 35000000 | tf_op jit(solution)/shard_map/final_layouts/pallas_call | solution.py:935
  848.0 1.4 copy.29
  849.4 3.0 copy.30
  (120 shorter events, 14.2 us)
Async XLA Ops:
  7.2 97.5 %copy-start = (s32[2,1,1024]{2,1,0:T(1,128)S(1)}, s32[2,1,1024]{2,1,0:T(1,128)}, u32[]{:S(2)}) copy-start(s32[2,1,1024]{2,1,0:T(1,128)} %param.11) | copy-start | bytes 24580
  7.2 3.9 copy-start.10
  7.2 3.9 copy-start.16
  7.2 3.9 copy-start.23
  7.2 3.9 copy-start.21
  7.2 3.9 copy-start.22
  7.2 199.8 %all-gather.2.cloned.1.call-start = ((), (), s32[]{:S(2)}) async-start(), calls=%async_computation.2 | async-start | bytes 11280384 | tf_op jit(solution)/shard_map/all_gather | solution.py:1401
  102.4 1.2 copy-start.2
  105.8 25.4 %copy-start.32 = (bf16[1,1,256,1088]{2,3,1,0:T(8,128)(2,1)S(1)}, bf16[1,1,256,1088]{2,3,1,0:T(8,128)(2,1)}, u32[]{:S(2)}) copy-start(bf16[1,1,256,1088]{2,3,1,0:T(8,128)(2,1)} %get-tuple-element.168) | copy-start | bytes 1671172
  131.5 156.4 %copy-start.3 = (bf16[1,1,256,1088]{3,2,1,0:T(8,128)(2,1)}, bf16[1,1,256,1088]{3,2,1,0:T(8,128)(2,1)S(1)}, u32[]{:S(2)}) copy-start(bf16[1,1,256,1088]{3,2,1,0:T(8,128)(2,1)S(1)} %copy.20) | copy-start | bytes 1671172
  131.5 1.5 copy-start.4
  133.9 1.2 copy-start.17
  202.7 2.2 copy-start.6
  205.7 1.4 copy-start.24
  242.5 1.3 copy-start.5
  286.5 1.4 copy-start.26
  287.9 41.8 %copy-start.19 = (bf16[256,1088]{1,0:T(8,128)(2,1)}, bf16[256,1088]{1,0:T(8,128)(2,1)S(1)}, u32[]{:S(2)}) copy-start(bf16[256,1088]{1,0:T(8,128)(2,1)S(1)} %get-tuple-element.139.made1) | copy-start | bytes 1671172
  329.8 4.6 copy-start.12
  329.8 4.6 copy-start.27
  334.4 83.3 %all-to-all-start = ((bf16[4,272,1088]{2,1,0:T(8,128)(2,1)}), bf16[4,272,1088]{2,1,0:T(8,128)(2,1)}, u32[]{:S(2)}, u32[]{:S(2)}) async-start(bf16[4,272,1088]{2,1,0:T(8,128)(2,1)} %bitcast.91), calls=%async_computation | async-start | bytes 5013504 | tf_op jit(solution)/shard_map/all_to_all | solution.py:1480
  417.7 6.9 copy-start.30
  419.8 8.3 copy-start.8
  419.8 4.8 collective-permute-start
  428.1 2.3 copy-start.7
  430.5 46.1 %copy-start.25 = (bf16[4,256,1088]{2,1,0:T(8,128)(2,1)S(1)}, bf16[4,256,1088]{2,1,0:T(8,128)(2,1)}, u32[]{:S(2)}) copy-start(bf16[4,256,1088]{2,1,0:T(8,128)(2,1)} %copy-done.24) | copy-start | bytes 6684676
  476.6 4.6 copy-start.13
  476.6 4.6 copy-start.28
  481.2 46.2 %all-to-all-start.1 = ((bf16[4,272,1088]{2,1,0:T(8,128)(2,1)}), bf16[4,272,1088]{2,1,0:T(8,128)(2,1)}, u32[]{:S(2)}, u32[]{:S(2)}) async-start(bf16[4,272,1088]{2,1,0:T(8,128)(2,1)} %bitcast.92), calls=%async_computation.1 | async-start | bytes 5013504 | tf_op jit(solution)/shard_map/all_to_all | solution.py:1480
  485.7 146.8 %all-reduce.4.cloned.1.call-start = ((), (), s32[]{:S(2)}) async-start(), calls=%async_computation.3 | async-start | bytes 5013504 | tf_op jit(solution)/shard_map/psum | solution.py:1491
  530.8 2.2 copy-start.44
  530.8 10.5 %collective-permute-start.1 = (bf16[2,544,1088]{2,1,0:T(8,128)(2,1)}, bf16[2,544,1088]{2,1,0:T(8,128)(2,1)S(1)}, u32[]{:S(2)}, u32[]{:S(2)}) collective-permute-start(bf16[2,544,1088]{2,1,0:T(8,128)(2,1)} %fusion.7), channel_id=1, source_target_pairs={{0,16},{16,0},{1,17},{17,1},{2,18},{18,2},{3,19},{19,3},{4,20},{20... | collective-permute-start | bytes 7102472 | tf_op jit(solution)/shard_map/ppermute | solution.py:997
  530.8 292.6 %all-reduce.6.cloned.1.call-start = ((), (), s32[]{:S(2)}) async-start(), calls=%async_computation.4 | async-start | bytes 5013504 | tf_op jit(solution)/shard_map/psum | solution.py:1491
  533.0 4.4 copy-start.34
  533.0 4.4 copy-start.41
  537.4 3.9 copy-start.29
  544.7 87.8 %copy-start.35 = (bf16[768,1088]{1,0:T(8,128)(2,1)S(1)}, bf16[768,1088]{1,0:T(8,128)(2,1)}, u32[]{:S(2)}) copy-start(bf16[768,1088]{1,0:T(8,128)(2,1)} %get-tuple-element.133) | copy-start | bytes 5013508
  544.7 87.8 %copy-start.36 = (bf16[256,1152]{1,0:T(8,128)(2,1)S(1)}, bf16[256,1152]{1,0:T(8,128)(2,1)}, u32[]{:S(2)}) copy-start(bf16[256,1152]{1,0:T(8,128)(2,1)} %get-tuple-element.109) | copy-start | bytes 1769476
  632.5 2.4 copy-start.40
  634.9 3.9 copy-start.33
  634.9 3.9 copy-start.37
  638.8 2.4 copy-start.45
  638.8 2.4 copy-start.46
  641.2 3.1 copy-start.43
  644.3 4.1 copy-start.42
  823.4 6.8 collective-permute-start.2
  830.3 1.5 copy-start.31
  831.7 1.1 copy-start.15
  848.0 5.7 copy-start.1
  (7 other events, 6.0 us)
Sparse Core Ops, SparseCore 0:
  104.8 80.5 all-gather.1
  531.0 101.4 all-reduce.3
  634.9 140.9 all-reduce.5

commit v9 on v8

--- a/solution.py
+++ b/solution.py
@@ -691,9 +691,9 @@
 
         @pl.when(s == 1)
         def _():
-            for k in range(2):
-                up_out[:, pl.ds(k * D, D)] = up_far[pl.ds(k * shard, shard), :]
-                up_out[:, pl.ds((2 + k) * D, D)] = up_own[pl.ds(k * shard, shard), :]
+            for k in range(4):
+                at = pl.ds(k * (shard // 2), shard // 2)
+                up_out[:, pl.ds(k * D, D)] = jnp.concatenate([up_far[at, :], up_own[at, :]], axis=0)
 
     back_one = to(halo.at[pl.ds(0, rows)], caught.at[0], h_send.at[0], h_recv.at[0], **below)
     back_two = to(sent, caught.at[1], h_send.at[1], h_recv.at[1], **below)
@@ -900,16 +900,16 @@
         qkv_f[at, :] = qkv[at, :].astype(F32)
         out_f[at, :] = out[at, pl.ds(0, D)].astype(F32)
 
-        @pl.when(s == 0)
-        def _():
-            for k in range(2):
-                from_k = pl.ds(pl.multiple_of(k * shard + i * 16, 16), 16)
-                up_f[at, pl.ds(k * D, D)] = mine[1, from_k, :].astype(F32)
-                up_f[at, pl.ds((2 + k) * D, D)] = far[1, from_k, :].astype(F32)
-
         @pl.when(s == 1)
         def _():
             up_f[at, :] = up_one[at, :].astype(F32)
+
+    @pl.when(s == 0)
+    def _():
+        for k in range(4):
+            at = pl.ds(k * (shard // 2), shard // 2)
+            rows_k = jnp.concatenate([mine[1, at, :], far[1, at, :]], axis=0)
+            up_f[:, pl.ds(k * D, D)] = rows_k.astype(F32)
 
     @pl.loop(0, half // 16)
     def _(i):
@@ -943,19 +943,20 @@
     )(*values)
 
 
-def halves_pair(down, up):
+def core_half(values, axis):
     s = lax.axis_index("section")
-    both = jnp.stack([down, up])
-    both = both.reshape(2, 2, both.shape[1] // 2, D)
-    keep = lax.dynamic_index_in_dim(both, s, 1, keepdims=False)
-    give = lax.dynamic_index_in_dim(both, 1 - s, 1, keepdims=False)
+    keep = lax.dynamic_index_in_dim(values, s, axis, keepdims=False)
+    give = lax.dynamic_index_in_dim(values, 1 - s, axis, keepdims=False)
     return (keep.astype(F32) + on_chip(give).astype(F32)).astype(BF)
 
 
-def halves_settle(zero, one):
+def halves_settle(zero, one, nf, shard):
     s = lax.axis_index("section")
     mine, far = pick(s, zero, one), on_chip(pick(s, one, zero))
-    return jnp.concatenate([pick(s, mine, far), pick(s, far, mine)], axis=1).astype(F32)
+    first, second = pick(s, mine, far).astype(F32), pick(s, far, mine).astype(F32)
+    down = jnp.concatenate([first[0], second[0]], axis=0)
+    up = jnp.concatenate([half[1].reshape(nf, shard // 2, -1) for half in (first, second)], axis=1)
+    return down, up.transpose(1, 0, 2).reshape(shard, -1)
 
 
 def reduce_plain(pieces):
@@ -1453,8 +1454,12 @@
     for layer in (1, 0):
         wide, normed, q, k, v, att, resid, second_all, slope, active, par = kept[layer]
         d_second, up_all, dz_b, ffb_g = mlp_backward(upstream, up_w, down_w, layer, slope)
-        down_g = mm_tn(flat(active), flat(up_all))
-        up_g = mm_tn(flat(second_all), flat(dz_b))
+        up_g = mm_tn(flat(second_all), flat(dz_b)).astype(BF)
+        up_half = core_half(up_g.reshape(nf, 2, shard // 2, ff_here), 1)
+        down_g = mm_tn(flat(active), flat(up_all)).astype(BF)
+        down_half = core_half(down_g.reshape(2, ff_here // 2, D), 0)
+        d_second, up_half, down_half = lax.optimization_barrier((d_second, up_half, down_half))
+        up_half = lax.all_to_all(up_half, "fsdp", split_axis=0, concat_axis=0, tiled=True)
         ffb_rows = lax.dynamic_update_slice(
             jnp.zeros((8, D), F32), ffb_g.reshape(per_row, shard), (0, f * shard)
         )
@@ -1477,13 +1482,8 @@
             mm_tn(left, right).astype(BF),
         )
         parts[layer] = pieces
-        up_g = lax.all_to_all(
-            up_g.astype(BF).reshape(nf, shard, ff_here), "fsdp",
-            split_axis=0, concat_axis=0, tiled=True,
-        ).reshape(nf * shard * ff_here // D, D)
-        down_g = down_g.astype(BF)
-        down_g, up_g, _ = lax.optimization_barrier((down_g, up_g, dq))
-        halves = halves_pair(down_g, up_g)
+        up_half, down_half, _ = lax.optimization_barrier((up_half, down_half, dq))
+        halves = jnp.stack([down_half, up_half.reshape(ff_here // 2, D)])
         if layer == 1:
             _, upstream_next = lax.optimization_barrier((halves, upstream_next))
         else:
@@ -1508,7 +1508,7 @@
         qkv_g = jnp.concatenate([a_tot[i, :, :D] for i in range(3)], axis=1)
         out_g = a_tot[3, :, :D]
         small = a_tot[3, :, D : D + 16].T
-        grad_down, grad_up = split_up(halves_settle(*mlp_sums), nf, shard)
+        grad_down, grad_up = halves_settle(*mlp_sums, nf, shard)
         made, grads = both_micros(produced, s), both_micros(derived, s)
     return (
         made,
@@ -1521,11 +1521,6 @@
         small[None, 2:8],
         small[8 : 8 + per_row].reshape(1, ff_here),
     )
-
-
-def split_up(both, nf, shard):
-    up = both[1].reshape(nf, shard, -1)
-    return both[0], up.transpose(1, 0, 2).reshape(shard, -1)
 
 
 def both_micros(layers, s):

time: 869 us -> 813 us (0.936)
  waiting for transfers between devices: 98.1 us -> 49.8 us
  matrix products: 50.2 us -> 40.4 us
    psum x2, waiting for transfers between devices: 87.8 us -> 42.4 us  [on_device(): mlp_sums[layer] = lax.psum(halves, 'ctx')]
    dot_general x12, matrix products: 50.2 us -> 40.4 us  [mm_tn(): lax.dot_general(a, b, (((0,), (0,)), ((), ())), preferred_element_type=F32)]
    unnamed x97 -> x93, local copies, waits for them, and re-layouts: 26 us -> 26.1 us
  transfers between devices with their start and end apart: 8 -> 10, of which waited for: 3 -> 4; matrix products, arithmetic and copies ran while one was open for 6% -> 6% of each run, Pallas kernels for 43% -> 46%
where the time goes in v9:
time: 813 us; the launch traced here: 805 us
  Pallas kernels  636 us (78%)
  waiting for transfers between devices  49.8 us (6%)
  matrix products  40.4 us (5%)
  local copies, waits for them, and re-layouts  38 us (5%)
  other arithmetic  15.2 us (2%)
  between operations  14.6 us (2%)
  starting transfers between devices  11 us (1%)
    pallas_call x4, Pallas kernels, plane_call(): pl.pallas_call(kernel, out_shape=outs, in_specs=[VSPEC, any_spec, any_spe...  192 us
    pallas_call x1, Pallas kernels, reduce_both(): pl.pallas_call(reduce_kernel, out_shape=(*(jax.ShapeDtypeStruct(shape, BF...  171 us
    pallas_call x2, Pallas kernels, block_backward(): pl.pallas_call(functools.partial(block_back_kernel, ring), out_shape=tupl...  109 us
    pallas_call x1, Pallas kernels, first_weights(): pl.pallas_call(weights_kernel, out_shape=tuple((jax.ShapeDtypeStruct(shap...  91.3 us
    pallas_call x2, Pallas kernels, block_forward(): pl.pallas_call(functools.partial(block_kernel, ring), out_shape=tuple((ja...  58.9 us
    psum x2, waiting for transfers between devices, on_device(): mlp_sums[layer] = lax.psum(halves, 'ctx')  42.4 us
    dot_general x12, matrix products, mm_tn(): lax.dot_general(a, b, (((0,), (0,)), ((), ())), preferred_element_type=F32)  40.4 us
    unnamed x93, local copies, waits for them, and re-layouts  26.1 us
  transfers between devices with their start and end apart: 10, of which 4 were waited for; matrix products, arithmetic and copies ran while one was open for 6% of the time, Pallas kernels for 46%

profile of v9, /device:TPU:0, one launch (start us, length us, event | category | flops | bytes accessed | tf_op | source)
XLA Modules:
  0.0 804.5 jit_solution(9876500702882604828)
XLA Ops:
  7.3 2.4 constant_dynamic-slice_fusion.1
  9.7 1.3 copy.20
  11.1 91.3 %first_weights.1 = (bf16[4,1088,1152]{2,1,0:T(8,128)(2,1)}, bf16[768,1088]{1,0:T(8,128)(2,1)S(1)}, bf16[2,1088,1088]{2,1,0:T(8,128)(2,1)}, bf16[2,1088,1088]{2,1,0:T(8,128)(2,1)}, bf16[136,4608]{1,0:T(8,128)(2,1)S(1)}) custom-call(bf16[272,3264]{1,0:T(8,128)(2,1)S(1)} %bitcast.92, bf16[272,1088]{1,0:T(8,128)(2,1)S(1)} %bitcast.94, ...), custom_call_target="tpu_custom_call" | custom-call | bytes 262500000 | tf_op jit(solution)/shard_map/first_weights/pallas_call | solution.py:492
  105.8 24.5 %block_forward.2 = (bf16[768,1088]{1,0:T(8,128)(2,1)}, bf16[256,1152]{1,0:T(8,128)(2,1)}, bf16[768,1152]{1,0:T(8,128)(2,1)}, bf16[768,1152]{1,0:T(8,128)(2,1)}, ...) custom-call(bf16[768,1088]{1,0:T(8,128)(2,1)} %copy-done.2, ...), custom_call_target="tpu_custom_call" | custom-call | bytes 77000000 | tf_op jit(solution)/shard_map/block_forward/pallas_call | solution.py:1189
  131.5 1.5 copy-done.4
  135.1 67.6 %shard_map.169 = (bf16[256,1088]{1,0:T(8,128)(2,1)S(1)}, bf16[4,256,1088]{2,1,0:T(8,128)(2,1)S(1)}, bf16[4,256,1088]{2,1,0:T(8,128)(2,1)S(1)}, f32[4,256,1088]{2,1,0:T(8,128)S(1)}) custom-call(bf16[256,1088]{1,0:T(8,128)(2,1)S(1)} %copy-done.17, bf16[2,1088,1088]{2,1,0:T(8,128)(2,1)} %get-tuple-element.90.up_both, ...), custom_call_target="tpu_custom_call" | custom-call | bytes 140000000 | tf_op jit(solution)/shard_map/pallas_call | solution.py:204
  202.7 2.2 copy-done.6
  205.7 1.4 copy-done.24
  207.1 34.5 %block_forward.3 = (bf16[768,1088]{1,0:T(8,128)(2,1)}, bf16[256,1152]{1,0:T(8,128)(2,1)}, bf16[768,1152]{1,0:T(8,128)(2,1)}, bf16[768,1152]{1,0:T(8,128)(2,1)}, ...) custom-call(bf16[256,1088]{1,0:T(8,128)(2,1)} %copy-done.9, ...), custom_call_target="tpu_custom_call" | custom-call | bytes 157500000 | tf_op jit(solution)/shard_map/block_forward/pallas_call | solution.py:1189
  242.5 1.3 copy-done.5
  245.7 41.1 %shard_map.170 = (bf16[256,1088]{1,0:T(8,128)(2,1)S(1)}, bf16[4,256,1088]{2,1,0:T(8,128)(2,1)S(1)}, bf16[4,256,1088]{2,1,0:T(8,128)(2,1)S(1)}, f32[4,256,1088]{2,1,0:T(8,128)S(1)}) custom-call(bf16[256,1088]{1,0:T(8,128)(2,1)S(1)} %copy-done.18, bf16[2,1088,1088]{2,1,0:T(8,128)(2,1)} %get-tuple-element.90.up_both, ...), custom_call_target="tpu_custom_call" | custom-call | bytes 140000000 | tf_op jit(solution)/shard_map/pallas_call | solution.py:204
  286.8 41.2 %shard_map.171 = (f32[256,1088]{1,0:T(8,128)S(1)}, bf16[4,256,1088]{2,1,0:T(8,128)(2,1)S(1)}, bf16[4,256,1088]{2,1,0:T(8,128)(2,1)S(1)}, f32[1,1088]{1,0:T(1,128)S(1)}) custom-call(bf16[256,1088]{1,0:T(8,128)(2,1)S(1)} %bitcast.89, bf16[2,1088,1088]{2,1,0:T(8,128)(2,1)} %get-tuple-element.90.up_both, bf16[2,1088,1088]{2,1,0:T(8,128)(2,1)} %get-tuple-element.91.down_both, ...), custom_call_target="tpu_custom_call" | custom-call | bytes 140000000 | tf_op jit(solution)/shard_map/pallas_call | solution.py:204
  328.0 3.1 fusion.1
  331.4 3.1 fusion
  335.2 1.4 fusion.6
  336.6 1.2 collective-permute-done
  337.8 1.4 fusion.7
  339.2 4.3 all-to-all-start
  346.1 74.8 %block_backward.2 = (f32[256,1088]{1,0:T(8,128)}, bf16[256,1088]{1,0:T(8,128)(2,1)}, bf16[256,1152]{1,0:T(8,128)(2,1)}, bf16[768,1152]{1,0:T(8,128)(2,1)}, bf16[...) custom-call(f32[256,1088]{1,0:T(8,128)} %copy-done.13, bf16[256,1088]{1,0:T(8,128)(2,1)} %bitcast.90, ...), custom_call_target="tpu_custom_call" | custom-call | bytes 203000000 | tf_op jit(solution)/shard_map/block_backward/pallas_call | solution.py:1353
  420.9 3.5 pad_maximum_fusion
  424.4 2.3 copy-done.7
  426.7 42.1 %shard_map.172 = (f32[256,1088]{1,0:T(8,128)S(1)}, bf16[4,256,1088]{2,1,0:T(8,128)(2,1)S(1)}, bf16[4,256,1088]{2,1,0:T(8,128)(2,1)S(1)}, f32[1,1088]{1,0:T(1,128)S(1)}) custom-call(bf16[256,1088]{1,0:T(8,128)(2,1)S(1)} %copy-done.8, bf16[2,1088,1088]{2,1,0:T(8,128)(2,1)} %get-tuple-element.90.up_both, bf16[2,1088,1088]{2,1,0:T(8,128)(2,1)} %get-tuple-element.91.down_both, ...), custom_call_target="tpu_custom_call" | custom-call | bytes 140000000 | tf_op jit(solution)/shard_map/pallas_call | solution.py:204
  468.9 3.1 fusion.3
  472.0 1.2 dynamic-slice_bitcast_fusion
  473.3 3.1 fusion.2
  476.5 1.4 copy-done.28
  478.6 2.1 fusion.4
  481.3 2.7 fusion.5
  484.0 3.7 all-to-all-start.1
  488.2 1.9 slice.24.wide
  490.1 4.3 convolution_convert_fusion.6.o1
  494.4 3.8 convolution_convert_fusion.2.v1
  499.4 34.0 %block_backward.3 = (f32[256,1088]{1,0:T(8,128)}, bf16[256,1152]{1,0:T(8,128)(2,1)}, bf16[768,1152]{1,0:T(8,128)(2,1)}, bf16[768,1152]{1,0:T(8,128)(2,1)}, f32[2...) custom-call(f32[256,1088]{1,0:T(8,128)} %copy-done.12, ...), custom_call_target="tpu_custom_call" | custom-call | bytes 133000000 | tf_op jit(solution)/shard_map/block_backward/pallas_call | solution.py:1353
  533.4 1.8 pad_maximum_fusion.1
  535.2 42.4 %all-reduce.4.cloned.1.call-done.mlp = bf16[2,544,1088]{2,1,0:T(8,128)(2,1)} async-done(((bf16[2,544,1088]{2,1,0:T(8,128)(2,1)}), bf16[2,544,1088]{2,1,0:T(8,128)(2,1)}) %all-reduce.4.cloned.1.call-update) | async-done | bytes 2367504 | tf_op jit(solution)/shard_map/psum | solution.py:1491
  577.7 2.4 convolution_convert_fusion.q1
  580.1 3.9 convolution_convert_fusion.3.k1
  584.0 2.4 convolution_convert_fusion.1.q0
  586.4 3.1 convolution_convert_fusion.7.o0
  589.5 3.8 convolution_convert_fusion.4.v0
  593.3 4.1 convolution_convert_fusion.5.k0
  597.4 171.0 %reduce_both.1 = (bf16[272,3264]{1,0:T(8,128)(2,1)}, bf16[272,1152]{1,0:T(8,128)(2,1)}, bf16[1088,1088]{1,0:T(8,128)(2,1)}, bf16[272,4352]{1,0:T(8,128)(2,1)}, b...) custom-call(bf16[1088,1152]{1,0:T(8,128)(2,1)} %convolution_convert_fusion.1.q0, ...), custom_call_target="tpu_custom_call" | custom-call | bytes 420000000 | tf_op jit(solution)/shard_map/reduce_both/pallas_call | solution.py:855
  768.5 1.3 collective-permute-start.4
  769.8 5.5 collective-permute-done.4.far
  775.3 1.5 copy-done.26
  777.9 13.7 %final_layouts.1 = (f32[272,3264]{1,0:T(8,128)}, f32[272,1088]{1,0:T(8,128)}, f32[1088,1088]{1,0:T(8,128)}, f32[272,4352]{1,0:T(8,128)}, f32[16,272]{1,0:T(8,128...) custom-call(bf16[272,3264]{1,0:T(8,128)(2,1)} %get-tuple-element.157.qkv, ...), custom_call_target="tpu_custom_call" | custom-call | bytes 35000000 | tf_op jit(solution)/shard_map/final_layouts/pallas_call | solution.py:935
  792.1 3.0 copy.32
  795.1 1.4 copy.31
  (126 shorter events, 19.8 us)
Async XLA Ops:
  7.2 97.5 %copy-start = (s32[2,1,1024]{2,1,0:T(1,128)S(1)}, s32[2,1,1024]{2,1,0:T(1,128)}, u32[]{:S(2)}) copy-start(s32[2,1,1024]{2,1,0:T(1,128)} %param.11) | copy-start | bytes 24580
  7.2 3.9 copy-start.10
  7.2 3.9 copy-start.16
  7.2 3.9 copy-start.23
  7.2 3.9 copy-start.21
  7.2 3.9 copy-start.22
  7.2 199.9 %all-gather.2.cloned.1.call-start = ((), (), s32[]{:S(2)}) async-start(), calls=%async_computation.2 | async-start | bytes 11280384 | tf_op jit(solution)/shard_map/all_gather | solution.py:1402
  102.4 1.2 copy-start.2
  105.8 25.3 %copy-start.30 = (bf16[1,1,256,1088]{2,3,1,0:T(8,128)(2,1)S(1)}, bf16[1,1,256,1088]{2,3,1,0:T(8,128)(2,1)}, u32[]{:S(2)}) copy-start(bf16[1,1,256,1088]{2,3,1,0:T(8,128)(2,1)} %get-tuple-element.181) | copy-start | bytes 1671172
  131.5 155.3 %copy-start.3 = (bf16[1,1,256,1088]{3,2,1,0:T(8,128)(2,1)}, bf16[1,1,256,1088]{3,2,1,0:T(8,128)(2,1)S(1)}, u32[]{:S(2)}) copy-start(bf16[1,1,256,1088]{3,2,1,0:T(8,128)(2,1)S(1)} %copy.19) | copy-start | bytes 1671172
  131.5 1.5 copy-start.4
  133.9 1.2 copy-start.17
  202.7 2.2 copy-start.6
  205.7 1.4 copy-start.24
  242.5 1.3 copy-start.5
  286.8 41.2 %copy-start.19 = (bf16[256,1088]{1,0:T(8,128)(2,1)}, bf16[256,1088]{1,0:T(8,128)(2,1)S(1)}, u32[]{:S(2)}) copy-start(bf16[256,1088]{1,0:T(8,128)(2,1)S(1)} %get-tuple-element.151.made1) | copy-start | bytes 1671172
  328.0 3.2 copy-start.13
  331.3 3.9 collective-permute-start.1
  334.7 3.1 collective-permute-start
  339.2 81.7 %all-to-all-start = ((bf16[4,136,1088]{2,1,0:T(8,128)(2,1)}), bf16[4,136,1088]{2,1,0:T(8,128)(2,1)}, u32[]{:S(2)}, u32[]{:S(2)}) async-start(bf16[4,136,1088]{2,1,0:T(8,128)(2,1)} %fusion.7), calls=%async_computation | async-start | bytes 2506752 | tf_op jit(solution)/shard_map/all_to_all | solution.py:1462
  343.5 234.1 %all-reduce.4.cloned.1.call-start = ((), (), s32[]{:S(2)}) async-start(), calls=%async_computation.3 | async-start | bytes 5013504 | tf_op jit(solution)/shard_map/psum | solution.py:1491
  420.9 3.5 copy-start.8
  424.4 2.3 copy-start.7
  426.7 42.1 %copy-start.25 = (bf16[4,256,1088]{2,1,0:T(8,128)(2,1)S(1)}, bf16[4,256,1088]{2,1,0:T(8,128)(2,1)}, u32[]{:S(2)}) copy-start(bf16[4,256,1088]{2,1,0:T(8,128)(2,1)} %copy-done.24) | copy-start | bytes 6684676
  468.8 3.2 copy-start.12
  472.0 4.4 copy-start.27
  473.3 5.3 collective-permute-start.3
  476.4 1.5 copy-start.28
  478.0 3.3 collective-permute-start.2
  478.6 2.7 copy-start.29
  484.0 6.1 copy-start.42
  484.0 49.4 %all-to-all-start.1 = ((bf16[4,136,1088]{2,1,0:T(8,128)(2,1)}), bf16[4,136,1088]{2,1,0:T(8,128)(2,1)S(1)}, u32[]{:S(2)}, u32[]{:S(2)}) async-start(bf16[4,136,1088]{2,1,0:T(8,128)(2,1)} %fusion.5), calls=%async_computation.1 | async-start | bytes 2506752 | tf_op jit(solution)/shard_map/all_to_all | solution.py:1462
  487.7 280.7 %all-reduce.6.cloned.1.call-start = ((), (), s32[]{:S(2)}) async-start(), calls=%async_computation.4 | async-start | bytes 5013504 | tf_op jit(solution)/shard_map/psum | solution.py:1491
  490.1 4.3 copy-start.32
  490.1 4.3 copy-start.39
  535.2 42.4 %copy-start.33 = (bf16[768,1088]{1,0:T(8,128)(2,1)S(1)}, bf16[768,1088]{1,0:T(8,128)(2,1)}, u32[]{:S(2)}) copy-start(bf16[768,1088]{1,0:T(8,128)(2,1)} %get-tuple-element.145) | copy-start | bytes 5013508
  535.2 42.4 %copy-start.34 = (bf16[256,1152]{1,0:T(8,128)(2,1)S(1)}, bf16[256,1152]{1,0:T(8,128)(2,1)}, u32[]{:S(2)}) copy-start(bf16[256,1152]{1,0:T(8,128)(2,1)} %get-tuple-element.117) | copy-start | bytes 1769476
  577.7 2.4 copy-start.38
  580.1 4.0 copy-start.31
  580.1 4.0 copy-start.35
  584.0 2.4 copy-start.43
  584.0 2.4 copy-start.44
  586.4 3.1 copy-start.41
  589.5 3.8 copy-start.40
  768.5 6.8 collective-permute-start.4
  775.3 1.5 copy-start.26
  776.8 1.1 copy-start.15
  792.1 5.7 copy-start.1
  (7 other events, 6.0 us)
Sparse Core Ops, SparseCore 0:
  104.8 80.5 all-gather.1
  478.7 98.8 all-reduce.3
  580.0 140.8 all-reduce.5

commit v10 on v9

--- a/solution.py
+++ b/solution.py
@@ -74,9 +74,9 @@
     )
 
 
-def load_layer(layer, sources, targets, sems):
+def load_layer(sources, targets, sems):
     copies = [
-        pltpu.make_async_copy(source.at[layer], target, sems.at[i])
+        pltpu.make_async_copy(source, target, sems.at[i])
         for i, (source, target) in enumerate(zip(sources, targets))
     ]
     for copy in copies:
@@ -148,10 +148,10 @@
 
 
 def forward_kernel(
-    layer, own, up_both, down_both, bias, resid, par, out, all_ref, active, slope,
+    layer, own, up_here, down_both, bias, resid, par, out, all_ref, active, slope,
     up, down, load, parts, x1, y1, x2, y2, sx, sy, send, recv,
 ):
-    loads = load_layer(layer, (up_both, down_both), (up, down), load)
+    loads = load_layer((up_here, down_both.at[layer]), (up, down), load)
 
     def finish(at, value):
         out[at, :] = (resid[at, :] + value + par[7:8, :]).astype(BF)
@@ -173,10 +173,10 @@
 
 
 def backward_kernel(
-    layer, own, up_both, down_both, slope, total, all_ref, dz_all, bias_g,
+    layer, own, up_here, down_both, slope, total, all_ref, dz_all, bias_g,
     up, down, load, parts, x1, y1, x2, y2, sx, sy, send, recv,
 ):
-    loads = load_layer(layer, (up_both, down_both), (up, down), load)
+    loads = load_layer((up_here, down_both.at[layer]), (up, down), load)
     bias_g[...] = jnp.zeros_like(bias_g)
 
     def finish(at, value):
@@ -231,7 +231,7 @@
     rows = own.shape[0]
     if lax.axis_size("fsdp") != 4:
         every = lax.all_gather(own, "fsdp", axis=0, tiled=True)
-        up, down = up[layer], down[layer]
+        down = down[layer]
         z = mm(every, up) + bias
         cdf, pdf = phi_parts(z)
         active = (z * cdf).astype(BF)
@@ -256,7 +256,7 @@
     rows = own.shape[0]
     if lax.axis_size("fsdp") != 4:
         every = lax.all_gather(own, "fsdp", axis=0, tiled=True)
-        up, down = up[layer], down[layer]
+        down = down[layer]
         dz = mm_nt(every, down) * slope
         dz_b = dz.astype(BF)
         part = mm_nt(dz_b, up).astype(BF)
@@ -275,10 +275,71 @@
     )
 
 
+def spread_up(core, blocks, full, load, u_send, u_recv, v_send, v_recv):
+    s = lax.axis_index("section")
+    f = lax.axis_index("fsdp")
+    xn, yn = plane_neighbours()
+    others = (xn, yn, 3 - f)
+    shard = blocks.shape[1]
+
+    def rows_of(owner):
+        return full.at[pl.ds(pl.multiple_of(owner * shard, 16), shard)]
+
+    def to(src, dst, send, recv, **where):
+        return pltpu.make_async_remote_copy(
+            src_ref=src, dst_ref=dst, send_sem=send, recv_sem=recv,
+            device_id=where, device_id_type=MESH,
+        )
+
+    def chip(i):
+        return to(blocks.at[others[i]], rows_of(f), u_send.at[i], u_recv.at[i], fsdp=others[i])
+
+    def over(i):
+        rows = rows_of((*others, f)[i])
+        return to(rows, rows, v_send.at[i], v_recv.at[i], section=1 - core)
+
+    near = pltpu.make_async_copy(blocks.at[f], rows_of(f), load)
+
+    def first():
+        @pl.when(s == core)
+        def _():
+            near.start()
+            for i in range(3):
+                chip(i).start()
+            near.wait()
+            over(3).start()
+
+    def then():
+        @pl.when(s == core)
+        def _():
+            for i in range(3):
+                chip(i).wait_recv()
+                over(i).start()
+
+    def last():
+        @pl.when(s == core)
+        def _():
+            for i in range(3):
+                chip(i).wait_send()
+            for i in range(4):
+                over(i).wait_send()
+
+        @pl.when(s == 1 - core)
+        def _():
+            for i in range(4):
+                over(i).wait_recv()
+
+    return first, then, last
+
+
+def spread_sems():
+    return [pltpu.SemaphoreType.DMA((n,)) for n in (3, 3, 4, 4)]
+
+
 def weights_kernel(
     qkv_in, out_in, gains, biases, hidden, rows_in, up_in, down_in,
-    full, rows_out, up_out, down_out, next_half,
-    own, other_half, up_blocks, load, core_s, core_r, p_send, p_recv, f_send, f_recv, z_send, z_recv,
+    full, rows_out, up_out, up_blocks, down_out, next_half,
+    own, other_half, load, core_s, core_r, p_send, p_recv, f_send, f_recv, z_send, z_recv,
     u_send, u_recv, v_send, v_recv,
 ):
     s = lax.axis_index("section")
@@ -406,20 +467,10 @@
     for j in range(4):
         up_blocks[j] = up_in[:, pl.ds(j * D, D)]
 
-    def up_to(i, owner, where):
-        return to(up_blocks.at[owner], up_out.at[s, blk(f)], u_send.at[i], u_recv.at[i], fsdp=where)
-
-    def up_over(i, owner):
-        rows_here = up_out.at[s, blk(owner)]
-        return to(rows_here, rows_here, v_send.at[i], v_recv.at[i], section=1 - s)
-
-    others = (xn, yn, dn)
-    up_near = pltpu.make_async_copy(up_blocks.at[f], up_out.at[s, blk(f)], load.at[5])
-    up_near.start()
-    for i, owner in enumerate(others):
-        up_to(i, owner, owner).start()
-    up_near.wait()
-    up_over(3, f).start()
+    up_first, up_then, up_last = spread_up(
+        0, up_blocks, up_out, load.at[5], u_send, u_recv, v_send, v_recv
+    )
+    up_first()
     for k in range(2):
         copies, across = hops(k), here(k)
         copies[0].wait_recv()
@@ -442,18 +493,13 @@
         copies[2].wait_recv()
         copies[3].wait_recv()
         across[2].start()
-    for i, owner in enumerate(others):
-        up_to(i, owner, owner).wait_recv()
-        up_over(i, owner).start()
+    up_then()
     for k in range(2):
         for copy in here(k):
             copy.wait()
         for copy in hops(k):
             copy.wait_send()
-    for i, owner in enumerate(others):
-        up_to(i, owner, owner).wait_send()
-        up_over(i, owner).wait()
-    up_over(3, f).wait()
+    up_last()
 
     @pl.when(s == 0)
     def _():
@@ -488,18 +534,19 @@
 def first_weights(qkv, out, gains, biases, hidden, rows_in, up, down):
     dma = pltpu.SemaphoreType.DMA
     shard = qkv.shape[0]
-    shapes = ((4, D, WIDE), (3 * rows_in.shape[0], D), (2, D, D), (2, D, D), (shard // 2, 4 * WIDE))
+    shapes = (
+        (4, D, WIDE), (3 * rows_in.shape[0], D), (D, D), (4, shard, D), (2, D, D), (shard // 2, 4 * WIDE)
+    )
     return pl.pallas_call(
         weights_kernel,
         out_shape=tuple(jax.ShapeDtypeStruct(shape, BF) for shape in shapes),
         in_specs=[VSPEC] * 7 + [pl.BlockSpec(memory_space=pl.ANY)],
-        out_specs=(VSPEC,) * 5,
+        out_specs=(VSPEC,) * 6,
         scratch_shapes=[
             pltpu.VMEM((4, shard, WIDE), BF),
             pltpu.VMEM((shard // 2, 4 * WIDE), BF),
-            pltpu.VMEM((4, shard, D), BF),
             dma((6,)), dma((6,)), dma((6,)), dma((2, 4)), dma((2, 4)), dma((2, 3)), dma((2, 3)),
-            dma((2,)), dma((2,)), dma((3,)), dma((3,)), dma((4,)), dma((4,)),
+            dma((2,)), dma((2,)), *spread_sems(),
         ],
         compiler_params=pltpu.CompilerParams(
             collective_id=4, has_side_effects=True, vmem_limit_bytes=48 * 1024 * 1024
@@ -1050,7 +1097,7 @@
     return jnp.concatenate([row, jnp.zeros((row.shape[0], WIDE - D), row.dtype)], axis=1)
 
 
-def ctx_ring(rows_in, landing, send, recv):
+def ctx_ring(rows_in, landing, send, recv, partners=()):
     z = lax.axis_index("ctx")
     above = {"ctx": lax.rem(z + 1, 4)}
     below = {"ctx": lax.rem(z + 3, 4)}
@@ -1068,9 +1115,9 @@
     two = on(landing.at[near], landing.at[far], 1)
 
     def begin():
-        for where in (above, below):
+        for where in (above, below, *partners):
             pl.semaphore_signal(barrier, inc=1, device_id=where, device_id_type=MESH)
-        pl.semaphore_wait(barrier, 2)
+        pl.semaphore_wait(barrier, 2 + len(partners))
 
         @pl.when(z < 3)
         def _():
@@ -1111,15 +1158,22 @@
     return begin, middle, end
 
 
-def block_kernel(
-    ring, first, wq, wk, wv, wo, bias, normed, q_ref, k_ref, v_ref, att, resid, second, par, *rest
-):
+def block_kernel(ring, first, wq, wk, wv, wo, bias, *rest):
+    if ring:
+        up_blocks, *rest = rest
+    normed, q_ref, k_ref, v_ref, att, resid, second, par, *rest = rest
     rows = resid.shape[0]
     total = normed.shape[0]
     if ring:
-        wide_out, held, wide, send, recv = rest
-        begin, middle, end = ctx_ring(first, wide, send, recv)
+        wide_out, up_out, held, wide, up_full, send, recv, load, *sems = rest
+        s = lax.axis_index("section")
+        f = lax.axis_index("fsdp")
+        xn, yn = plane_neighbours()
+        partners = ({"section": 1 - s}, {"fsdp": xn}, {"fsdp": yn}, {"fsdp": 3 - f})
+        begin, middle, end = ctx_ring(first, wide, send, recv, partners)
+        up_first, up_then, up_last = spread_up(1, up_blocks, up_full, load.at[0], *sems)
         begin()
+        up_first()
     else:
         (held,), wide = rest, first
     pick_row = (
@@ -1133,6 +1187,7 @@
     def _(i):
         if ring:
             pl.when(i == 1)(middle)
+            pl.when(i == 2)(up_then)
             pl.when(i == 2)(end)
         at = pl.ds(pl.multiple_of((last - i) * rows, 16), rows)
         unit, _ = norm_parts(wide[at, :].astype(F32))
@@ -1162,6 +1217,8 @@
     second[...] = (unit * par[1:2, :] + par[6:7, :]).astype(BF)
     if ring:
         wide_out[...] = wide[...]
+        up_last()
+        up_out[...] = up_full[...]
 
 
 def weight_specs(weights):
@@ -1174,29 +1231,33 @@
     return pl.BlockSpec(shape, lambda i: (0,) * len(shape))
 
 
-def block_forward(first, weights, bias, ring):
+def block_forward(first, weights, bias, up_blocks=None):
     rows, total = bias.shape
     outs = (
         ((total, D), BF), ((rows, WIDE), BF), ((total, WIDE), BF), ((total, WIDE), BF),
         ((rows, D), BF), ((rows, D), F32), ((rows, D), BF), ((16, D), F32),
     )
     scratch = [pltpu.VMEM((rows, WIDE), BF)]
-    params = {}
-    if ring:
-        outs += (((total, D), BF),)
-        scratch += [pltpu.VMEM((total, D), BF)] + [pltpu.SemaphoreType.DMA((2,))] * 2
-        params = {"collective_id": 5, "has_side_effects": True}
+    params, more = {}, ()
+    if up_blocks is not None:
+        outs += (((total, D), BF), ((D, D), BF))
+        scratch += [pltpu.VMEM((total, D), BF), pltpu.VMEM((D, D), BF)]
+        scratch += [pltpu.SemaphoreType.DMA((n,)) for n in (2, 2, 1)] + spread_sems()
+        params, more = {"collective_id": 5, "has_side_effects": True}, (up_blocks,)
     return pl.pallas_call(
-        functools.partial(block_kernel, ring),
+        functools.partial(block_kernel, bool(more)),
         out_shape=tuple(jax.ShapeDtypeStruct(*out) for out in outs),
         grid=(1,),
-        in_specs=[whole(first.shape), *weight_specs(weights), whole(bias.shape)],
+        in_specs=[
+            whole(first.shape), *weight_specs(weights), whole(bias.shape),
+            *(whole(value.shape) for value in more),
+        ],
         out_specs=tuple(whole(shape) for shape, _ in outs),
         scratch_shapes=scratch,
-        compiler_params=pltpu.CompilerParams(vmem_limit_bytes=56 * 1024 * 1024, **params),
-        cost_estimate=lasting(45 if ring else 22),
+        compiler_params=pltpu.CompilerParams(vmem_limit_bytes=60 * 1024 * 1024, **params),
+        cost_estimate=lasting(45 if more else 22),
         name="block_forward",
-    )(first, weights, weights, weights, weights, bias)
+    )(first, weights, weights, weights, weights, bias, *more)
 
 
 def block_back_kernel(
@@ -1402,11 +1463,12 @@
         return lax.all_gather(rows_first, pair, axis=0, tiled=True)
 
     if fits:
-        zero, wide_in, up_w, down_w, one_half = first_weights(
+        zero, wide_in, up_zero, up_blocks, down_w, one_half = first_weights(
             qkv_weight[0], out_weight[0], norm_gains[0], biases[0], ff_bias,
             own_in, up_weight[0], down_weight[0],
         )
         one = gathered(one_half)
+        up_w = (up_zero, None)
     else:
         small = jnp.concatenate(
             [norm_gains[0].T, biases[0].T, ff_bias[0].reshape(per_row, shard).T], axis=1
@@ -1435,14 +1497,15 @@
     produced = []
     for layer in range(2):
         if layer == 1 and fits:
-            *made, wide = block_forward(current, weights[layer], bias, True)
+            *made, wide, up_one = block_forward(current, weights[layer], bias, up_blocks)
+            up_w = (up_w[0], up_one)
         else:
             wide = with_halo(current, chunks) if layer else wide_in
-            made = block_forward(wide, weights[layer], bias, False)
+            made = block_forward(wide, weights[layer], bias)
         normed, q, k, v, att, resid, second, par = made
         ffb = lax.dynamic_slice(par, (8, f * shard), (per_row, shard)).reshape(1, ff_here)
         current, second_all, active, slope = mlp_forward(
-            second, up_w, down_w, layer, ffb, resid, par
+            second, up_w[layer], down_w, layer, ffb, resid, par
         )
         produced.append(current)
         kept.append((wide, normed, q, k, v, att, resid, second_all, slope, active, par))
@@ -1453,7 +1516,7 @@
     mlp_sums = [None, None]
     for layer in (1, 0):
         wide, normed, q, k, v, att, resid, second_all, slope, active, par = kept[layer]
-        d_second, up_all, dz_b, ffb_g = mlp_backward(upstream, up_w, down_w, layer, slope)
+        d_second, up_all, dz_b, ffb_g = mlp_backward(upstream, up_w[layer], down_w, layer, slope)
         up_g = mm_tn(flat(second_all), flat(dz_b)).astype(BF)
         up_half = core_half(up_g.reshape(nf, 2, shard // 2, ff_here), 1)
         down_g = mm_tn(flat(active), flat(up_all)).astype(BF)

time: 813 us -> 815 us (level)
  local copies, waits for them, and re-layouts: 38 us -> 48.8 us
  Pallas kernels: 636 us -> 627 us
    pallas_call x1, Pallas kernels: 91.3 us -> 78.4 us  [first_weights(): pl.pallas_call(weights_kernel, out_shape=tuple((jax.ShapeDtypeStruct(shap...]
    pallas_call x4, Pallas kernels: 192 us -> 203 us  [plane_call(): pl.pallas_call(kernel, out_shape=outs, in_specs=[VSPEC, any_spec, any_spe...]
    unnamed x93 -> x105, local copies, waits for them, and re-layouts: 26.1 us -> 37 us
    pallas_call x2, Pallas kernels: 109 us -> 99.6 us  [block_backward(): pl.pallas_call(functools.partial(block_back_kernel, ring), out_shape=tupl...]
  transfers between devices with their start and end apart: 10 -> 10, of which waited for: 4 -> 4; matrix products, arithmetic and copies ran while one was open for 6% -> 6% of each run, Pallas kernels for 46% -> 45%
where the time goes in v10:
time: 815 us; the launch traced here: 806 us
  Pallas kernels  627 us (77%)
  waiting for transfers between devices  49.5 us (6%)
  local copies, waits for them, and re-layouts  48.8 us (6%)
  matrix products  40.4 us (5%)
  other arithmetic  15.3 us (2%)
  between operations  14.6 us (2%)
  starting transfers between devices  10.6 us (1%)
    pallas_call x4, Pallas kernels, plane_call(): pl.pallas_call(kernel, out_shape=outs, in_specs=[VSPEC, any_spec, any_spe...  203 us
    pallas_call x1, Pallas kernels, reduce_both(): pl.pallas_call(reduce_kernel, out_shape=(*(jax.ShapeDtypeStruct(shape, BF...  171 us
    pallas_call x2, Pallas kernels, block_backward(): pl.pallas_call(functools.partial(block_back_kernel, ring), out_shape=tupl...  99.6 us
    pallas_call x1, Pallas kernels, first_weights(): pl.pallas_call(weights_kernel, out_shape=tuple((jax.ShapeDtypeStruct(shap...  78.4 us
    pallas_call x2, Pallas kernels, block_forward(): pl.pallas_call(functools.partial(block_kernel, bool(more)), out_shape=tup...  61.3 us
    psum x2, waiting for transfers between devices, on_device(): mlp_sums[layer] = lax.psum(halves, 'ctx')  41.8 us
    dot_general x12, matrix products, mm_tn(): lax.dot_general(a, b, (((0,), (0,)), ((), ())), preferred_element_type=F32)  40.4 us
    unnamed x105, local copies, waits for them, and re-layouts  37 us
  transfers between devices with their start and end apart: 10, of which 4 were waited for; matrix products, arithmetic and copies ran while one was open for 6% of the time, Pallas kernels for 45%

profile of v10, /device:TPU:0, one launch (start us, length us, event | category | flops | bytes accessed | tf_op | source)
XLA Modules:
  0.0 806.5 jit_solution(14656715470383582450)
XLA Ops:
  7.3 2.4 constant_dynamic-slice_fusion.1
  11.1 78.4 %first_weights.1 = (bf16[4,1088,1152]{2,1,0:T(8,128)(2,1)}, bf16[768,1088]{1,0:T(8,128)(2,1)S(1)}, bf16[1088,1088]{1,0:T(8,128)(2,1)}, bf16[4,272,1088]{2,1,0:T(...) custom-call(bf16[272,3264]{1,0:T(8,128)(2,1)S(1)} %bitcast.92, ...), custom_call_target="tpu_custom_call" | custom-call | bytes 262500000 | tf_op jit(solution)/shard_map/first_weights/pallas_call | solution.py:540
  93.0 24.6 %block_forward.2 = (bf16[768,1088]{1,0:T(8,128)(2,1)}, bf16[256,1152]{1,0:T(8,128)(2,1)}, bf16[768,1152]{1,0:T(8,128)(2,1)}, bf16[768,1152]{1,0:T(8,128)(2,1)}, ...) custom-call(bf16[768,1088]{1,0:T(8,128)(2,1)} %copy-done.5, ...), custom_call_target="tpu_custom_call" | custom-call | bytes 77000000 | tf_op jit(solution)/shard_map/block_forward/pallas_call | solution.py:1247
  118.5 1.3 copy.19
  119.8 1.8 copy-done.7
  123.6 67.5 %shard_map.169 = (bf16[256,1088]{1,0:T(8,128)(2,1)S(1)}, bf16[4,256,1088]{2,1,0:T(8,128)(2,1)S(1)}, bf16[4,256,1088]{2,1,0:T(8,128)(2,1)S(1)}, f32[4,256,1088]{2,1,0:T(8,128)S(1)}) custom-call(bf16[256,1088]{1,0:T(8,128)(2,1)S(1)} %copy-done.22, bf16[1088,1088]{1,0:T(8,128)(2,1)S(1)} %copy-done.2, bf16[2,1088,1088]{2,1,0:T(8,128)(2,1)} %get-tuple-element.96.down_both, ...), custom_call_target="tpu_custom_call" | custom-call | bytes 140000000 | tf_op jit(solution)/shard_map/pallas_call | solution.py:204
  191.0 2.2 copy-done.9
  194.0 1.4 copy-done.29
  195.4 1.4 copy-done.31
  196.8 36.7 %block_forward.3 = (bf16[768,1088]{1,0:T(8,128)(2,1)}, bf16[256,1152]{1,0:T(8,128)(2,1)}, bf16[768,1152]{1,0:T(8,128)(2,1)}, bf16[768,1152]{1,0:T(8,128)(2,1)}, ...) custom-call(bf16[256,1088]{1,0:T(8,128)(2,1)} %copy-done.14, ...), custom_call_target="tpu_custom_call" | custom-call | bytes 157500000 | tf_op jit(solution)/shard_map/block_forward/pallas_call | solution.py:1247
  234.5 1.7 copy-done.3
  239.4 45.9 %shard_map.170 = (bf16[256,1088]{1,0:T(8,128)(2,1)S(1)}, bf16[4,256,1088]{2,1,0:T(8,128)(2,1)S(1)}, bf16[4,256,1088]{2,1,0:T(8,128)(2,1)S(1)}, f32[4,256,1088]{2,1,0:T(8,128)S(1)}) custom-call(bf16[256,1088]{1,0:T(8,128)(2,1)S(1)} %copy-done.23, bf16[1088,1088]{1,0:T(8,128)(2,1)S(1)} %copy-done.3, bf16[2,1088,1088]{2,1,0:T(8,128)(2,1)} %get-tuple-element.96.down_both, ...), custom_call_target="tpu_custom_call" | custom-call | bytes 140000000 | tf_op jit(solution)/shard_map/pallas_call | solution.py:204
  285.3 2.2 copy-done.11
  288.3 2.3 copy-done.12
  290.7 47.4 %shard_map.171 = (f32[256,1088]{1,0:T(8,128)S(1)}, bf16[4,256,1088]{2,1,0:T(8,128)(2,1)S(1)}, bf16[4,256,1088]{2,1,0:T(8,128)(2,1)S(1)}, f32[1,1088]{1,0:T(1,128)S(1)}) custom-call(bf16[256,1088]{1,0:T(8,128)(2,1)S(1)} %bitcast.89, bf16[1088,1088]{1,0:T(8,128)(2,1)S(1)} %copy-done.4, bf16[2,1088,1088]{2,1,0:T(8,128)(2,1)} %get-tuple-element.96.down_both, ...), custom_call_target="tpu_custom_call" | custom-call | bytes 140000000 | tf_op jit(solution)/shard_map/pallas_call | solution.py:204
  338.1 3.1 fusion.1
  341.4 3.1 fusion
  347.8 1.4 fusion.7
  349.2 4.3 all-to-all-start
  356.1 65.5 %block_backward.2 = (f32[256,1088]{1,0:T(8,128)}, bf16[256,1088]{1,0:T(8,128)(2,1)}, bf16[256,1152]{1,0:T(8,128)(2,1)}, bf16[768,1152]{1,0:T(8,128)(2,1)}, bf16[...) custom-call(f32[256,1088]{1,0:T(8,128)} %copy-done.18, bf16[256,1088]{1,0:T(8,128)(2,1)} %bitcast.90, ...), custom_call_target="tpu_custom_call" | custom-call | bytes 203000000 | tf_op jit(solution)/shard_map/block_backward/pallas_call | solution.py:1414
  421.7 3.5 pad_maximum_fusion
  425.2 2.3 copy-done.10
  427.5 42.5 %shard_map.172 = (f32[256,1088]{1,0:T(8,128)S(1)}, bf16[4,256,1088]{2,1,0:T(8,128)(2,1)S(1)}, bf16[4,256,1088]{2,1,0:T(8,128)(2,1)S(1)}, f32[1,1088]{1,0:T(1,128)S(1)}) custom-call(bf16[256,1088]{1,0:T(8,128)(2,1)S(1)} %copy-done.13, bf16[1088,1088]{1,0:T(8,128)(2,1)S(1)} %copy-done.2, bf16[2,1088,1088]{2,1,0:T(8,128)(2,1)} %get-tuple-element.96.down_both, ...), custom_call_target="tpu_custom_call" | custom-call | bytes 140000000 | tf_op jit(solution)/shard_map/pallas_call | solution.py:204
  470.0 3.1 fusion.3
  473.4 2.4 copy-done.30
  475.7 3.1 fusion.2
  478.9 1.4 copy-done.35
  480.6 2.1 fusion.4
  483.6 2.9 fusion.5
  486.5 3.7 all-to-all-start.1
  490.7 1.9 slice.24.wide
  492.6 4.3 convolution_convert_fusion.6.o1
  496.9 3.8 convolution_convert_fusion.2.v1
  501.9 34.0 %block_backward.3 = (f32[256,1088]{1,0:T(8,128)}, bf16[256,1152]{1,0:T(8,128)(2,1)}, bf16[768,1152]{1,0:T(8,128)(2,1)}, bf16[768,1152]{1,0:T(8,128)(2,1)}, f32[2...) custom-call(f32[256,1088]{1,0:T(8,128)} %copy-done.17, ...), custom_call_target="tpu_custom_call" | custom-call | bytes 133000000 | tf_op jit(solution)/shard_map/block_backward/pallas_call | solution.py:1414
  536.0 1.8 pad_maximum_fusion.1
  537.7 41.8 %all-reduce.4.cloned.1.call-done.mlp = bf16[2,544,1088]{2,1,0:T(8,128)(2,1)} async-done(((bf16[2,544,1088]{2,1,0:T(8,128)(2,1)}), bf16[2,544,1088]{2,1,0:T(8,128)(2,1)}) %all-reduce.4.cloned.1.call-update) | async-done | bytes 2367504 | tf_op jit(solution)/shard_map/psum | solution.py:1554
  579.6 2.4 convolution_convert_fusion.q1
  582.0 4.0 convolution_convert_fusion.3.k1
  586.0 2.4 convolution_convert_fusion.1.q0
  588.3 3.1 convolution_convert_fusion.7.o0
  591.4 3.8 convolution_convert_fusion.4.v0
  595.3 4.1 convolution_convert_fusion.5.k0
  599.3 171.0 %reduce_both.1 = (bf16[272,3264]{1,0:T(8,128)(2,1)}, bf16[272,1152]{1,0:T(8,128)(2,1)}, bf16[1088,1088]{1,0:T(8,128)(2,1)}, bf16[272,4352]{1,0:T(8,128)(2,1)}, b...) custom-call(bf16[1088,1152]{1,0:T(8,128)(2,1)} %convolution_convert_fusion.1.q0, ...), custom_call_target="tpu_custom_call" | custom-call | bytes 420000000 | tf_op jit(solution)/shard_map/reduce_both/pallas_call | solution.py:902
  771.7 5.5 collective-permute-done.4.far
  777.3 1.5 copy-done.33
  779.8 13.7 %final_layouts.1 = (f32[272,3264]{1,0:T(8,128)}, f32[272,1088]{1,0:T(8,128)}, f32[1088,1088]{1,0:T(8,128)}, f32[272,4352]{1,0:T(8,128)}, f32[16,272]{1,0:T(8,128...) custom-call(bf16[272,3264]{1,0:T(8,128)(2,1)} %get-tuple-element.161.qkv, ...), custom_call_target="tpu_custom_call" | custom-call | bytes 35000000 | tf_op jit(solution)/shard_map/final_layouts/pallas_call | solution.py:982
  794.1 3.0 copy.32
  797.1 1.4 copy.31
  (138 shorter events, 26.7 us)
Async XLA Ops:
  7.2 84.7 %copy-start = (s32[2,1,1024]{2,1,0:T(1,128)S(1)}, s32[2,1,1024]{2,1,0:T(1,128)}, u32[]{:S(2)}) copy-start(s32[2,1,1024]{2,1,0:T(1,128)} %param.11) | copy-start | bytes 24580
  7.2 3.9 copy-start.15
  7.2 3.9 copy-start.21
  7.2 3.9 copy-start.28
  7.2 3.9 copy-start.26
  7.2 3.9 copy-start.27
  7.2 189.6 %all-gather.2.cloned.1.call-start = ((), (), s32[]{:S(2)}) async-start(), calls=%async_computation.2 | async-start | bytes 11280384 | tf_op jit(solution)/shard_map/all_gather | solution.py:1463
  93.0 26.8 %copy-start.2 = (bf16[1088,1088]{1,0:T(8,128)(2,1)S(1)}, bf16[1088,1088]{1,0:T(8,128)(2,1)}, u32[]{:S(2)}) copy-start(bf16[1088,1088]{1,0:T(8,128)(2,1)} %get-tuple-element.95.up_here) | copy-start | bytes 7102468
  119.8 168.5 %copy-start.6 = (bf16[1,1,256,1088]{3,2,1,0:T(8,128)(2,1)}, bf16[1,1,256,1088]{3,2,1,0:T(8,128)(2,1)S(1)}, u32[]{:S(2)}) copy-start(bf16[1,1,256,1088]{3,2,1,0:T(8,128)(2,1)S(1)} %copy.19) | copy-start | bytes 1671172
  119.8 1.8 copy-start.7
  191.0 2.2 copy-start.9
  194.0 1.4 copy-start.29
  234.4 1.7 copy-start.3
  239.4 48.9 %copy-start.4 = (bf16[1088,1088]{1,0:T(8,128)(2,1)S(1)}, bf16[1088,1088]{1,0:T(8,128)(2,1)}, u32[]{:S(2)}) copy-start(bf16[1088,1088]{1,0:T(8,128)(2,1)} %get-tuple-element.102.up_here) | copy-start | bytes 7102468
  285.3 2.2 copy-start.11
  288.3 2.3 copy-start.12
  338.0 3.2 copy-start.18
  341.3 3.9 collective-permute-start.1
  344.7 3.1 collective-permute-start
  349.2 72.4 %all-to-all-start = ((bf16[4,136,1088]{2,1,0:T(8,128)(2,1)}), bf16[4,136,1088]{2,1,0:T(8,128)(2,1)}, u32[]{:S(2)}, u32[]{:S(2)}) async-start(bf16[4,136,1088]{2,1,0:T(8,128)(2,1)} %fusion.7), calls=%async_computation | async-start | bytes 2506752 | tf_op jit(solution)/shard_map/all_to_all | solution.py:1525
  353.5 226.0 %all-reduce.4.cloned.1.call-start = ((), (), s32[]{:S(2)}) async-start(), calls=%async_computation.3 | async-start | bytes 5013504 | tf_op jit(solution)/shard_map/psum | solution.py:1554
  421.7 3.5 copy-start.13
  425.2 2.3 copy-start.10
  427.5 42.5 %copy-start.32 = (bf16[4,256,1088]{2,1,0:T(8,128)(2,1)S(1)}, bf16[4,256,1088]{2,1,0:T(8,128)(2,1)}, u32[]{:S(2)}) copy-start(bf16[4,256,1088]{2,1,0:T(8,128)(2,1)} %copy-done.31) | copy-start | bytes 6684676
  470.0 3.2 copy-start.17
  473.2 5.7 copy-start.34
  473.2 2.6 copy-start.30
  473.3 7.3 collective-permute-start.3
  478.9 1.5 copy-start.35
  480.5 3.1 collective-permute-start.2
  480.6 3.0 copy-start.36
  486.5 6.1 copy-start.48
  486.5 49.4 %all-to-all-start.1 = ((bf16[4,136,1088]{2,1,0:T(8,128)(2,1)}), bf16[4,136,1088]{2,1,0:T(8,128)(2,1)S(1)}, u32[]{:S(2)}, u32[]{:S(2)}) async-start(bf16[4,136,1088]{2,1,0:T(8,128)(2,1)} %fusion.5), calls=%async_computation.1 | async-start | bytes 2506752 | tf_op jit(solution)/shard_map/all_to_all | solution.py:1525
  490.2 280.2 %all-reduce.6.cloned.1.call-start = ((), (), s32[]{:S(2)}) async-start(), calls=%async_computation.4 | async-start | bytes 5013504 | tf_op jit(solution)/shard_map/psum | solution.py:1554
  492.6 4.3 copy-start.38
  492.6 4.3 copy-start.45
  537.7 41.8 %copy-start.39 = (bf16[768,1088]{1,0:T(8,128)(2,1)S(1)}, bf16[768,1088]{1,0:T(8,128)(2,1)}, u32[]{:S(2)}) copy-start(bf16[768,1088]{1,0:T(8,128)(2,1)} %get-tuple-element.149) | copy-start | bytes 5013508
  537.7 41.8 %copy-start.40 = (bf16[256,1152]{1,0:T(8,128)(2,1)S(1)}, bf16[256,1152]{1,0:T(8,128)(2,1)}, u32[]{:S(2)}) copy-start(bf16[256,1152]{1,0:T(8,128)(2,1)} %get-tuple-element.121) | copy-start | bytes 1769476
  579.6 2.4 copy-start.44
  582.0 4.0 copy-start.37
  582.0 4.0 copy-start.41
  585.9 2.4 copy-start.49
  585.9 2.4 copy-start.50
  588.3 3.1 copy-start.47
  591.4 3.8 copy-start.46
  770.4 6.8 collective-permute-start.4
  777.3 1.5 copy-start.33
  794.1 5.7 copy-start.1
  (13 other events, 12.8 us)
Sparse Core Ops, SparseCore 0:
  92.0 78.5 all-gather.1
  480.7 98.7 all-reduce.3
  581.9 140.7 all-reduce.5

commit v11 on v10

--- a/solution.py
+++ b/solution.py
@@ -221,7 +221,7 @@
             pltpu.SemaphoreType.DMA((10,)),
         ],
         compiler_params=pltpu.CompilerParams(
-            collective_id=ident, has_side_effects=True, vmem_limit_bytes=40 * 1024 * 1024
+            collective_id=ident, has_side_effects=True, vmem_limit_bytes=56 * 1024 * 1024
         ),
         cost_estimate=lasting(40),
     )(*operands)
@@ -549,7 +549,7 @@
             dma((2,)), dma((2,)), *spread_sems(),
         ],
         compiler_params=pltpu.CompilerParams(
-            collective_id=4, has_side_effects=True, vmem_limit_bytes=48 * 1024 * 1024
+            collective_id=4, has_side_effects=True, vmem_limit_bytes=58 * 1024 * 1024
         ),
         cost_estimate=lasting(75),
         name="first_weights",
@@ -984,7 +984,7 @@
         out_shape=tuple(jax.ShapeDtypeStruct(*out) for out in outs),
         in_specs=[VSPEC] * 8,
         out_specs=(VSPEC,) * 7,
-        compiler_params=pltpu.CompilerParams(vmem_limit_bytes=52 * 1024 * 1024),
+        compiler_params=pltpu.CompilerParams(vmem_limit_bytes=58 * 1024 * 1024),
         cost_estimate=lasting(10),
         name="final_layouts",
     )(*values)
@@ -1254,7 +1254,7 @@
         ],
         out_specs=tuple(whole(shape) for shape, _ in outs),
         scratch_shapes=scratch,
-        compiler_params=pltpu.CompilerParams(vmem_limit_bytes=60 * 1024 * 1024, **params),
+        compiler_params=pltpu.CompilerParams(vmem_limit_bytes=62 * 1024 * 1024, **params),
         cost_estimate=lasting(45 if more else 22),
         name="block_forward",
     )(first, weights, weights, weights, weights, bias, *more)
@@ -1421,7 +1421,7 @@
         ],
         out_specs=tuple(whole(shape) for shape, _ in outs),
         scratch_shapes=held,
-        compiler_params=pltpu.CompilerParams(vmem_limit_bytes=60 * 1024 * 1024, **params),
+        compiler_params=pltpu.CompilerParams(vmem_limit_bytes=62 * 1024 * 1024, **params),
         cost_estimate=lasting(58 if ring else 38),
         name="block_backward",
     )(*before, weights, weights, weights, weights, par, bias_t)

time: 815 us -> 817 us (level)
  Pallas kernels: 627 us -> 650 us
  local copies, waits for them, and re-layouts: 48.8 us -> 27.3 us
    unnamed x105 -> x61, local copies, waits for them, and re-layouts: 37 us -> 11.7 us
    pallas_call x4, Pallas kernels: 203 us -> 224 us  [plane_call(): pl.pallas_call(kernel, out_shape=outs, in_specs=[VSPEC, any_spec, any_spe...]
  transfers between devices with their start and end apart: 10 -> 10, of which waited for: 4 -> 4; matrix products, arithmetic and copies ran while one was open for 6% -> 6% of each run, Pallas kernels for 45% -> 46%
where the time goes in v11:
time: 817 us; the launch traced here: 809 us
  Pallas kernels  650 us (80%)
  waiting for transfers between devices  48.6 us (6%)
  matrix products  42.6 us (5%)
  local copies, waits for them, and re-layouts  27.3 us (3%)
  other arithmetic  16.8 us (2%)
  between operations  14.4 us (2%)
  starting transfers between devices  9.3 us (1%)
    pallas_call x4, Pallas kernels, plane_call(): pl.pallas_call(kernel, out_shape=outs, in_specs=[VSPEC, any_spec, any_spe...  224 us
    pallas_call x1, Pallas kernels, reduce_both(): pl.pallas_call(reduce_kernel, out_shape=(*(jax.ShapeDtypeStruct(shape, BF...  171 us
    pallas_call x2, Pallas kernels, block_backward(): pl.pallas_call(functools.partial(block_back_kernel, ring), out_shape=tupl...  98.7 us
    pallas_call x1, Pallas kernels, first_weights(): pl.pallas_call(weights_kernel, out_shape=tuple((jax.ShapeDtypeStruct(shap...  80.2 us
    pallas_call x2, Pallas kernels, block_forward(): pl.pallas_call(functools.partial(block_kernel, bool(more)), out_shape=tup...  61.2 us
    dot_general x12, matrix products, mm_tn(): lax.dot_general(a, b, (((0,), (0,)), ((), ())), preferred_element_type=F32)  42.6 us
    psum x2, waiting for transfers between devices, on_device(): mlp_sums[layer] = lax.psum(halves, 'ctx')  41 us
  transfers between devices with their start and end apart: 10, of which 4 were waited for; matrix products, arithmetic and copies ran while one was open for 6% of the time, Pallas kernels for 46%

profile of v11, /device:TPU:0, one launch (start us, length us, event | category | flops | bytes accessed | tf_op | source)
XLA Modules:
  0.0 808.8 jit_solution(13883441943645843134)
XLA Ops:
  7.2 1.3 constant_dynamic-slice_fusion.1
  8.5 1.1 copy.20
  9.6 80.2 %first_weights.1 = (bf16[4,1088,1152]{2,1,0:T(8,128)(2,1)}, bf16[768,1088]{1,0:T(8,128)(2,1)}, bf16[1088,1088]{1,0:T(8,128)(2,1)}, bf16[4,272,1088]{2,1,0:T(8,12...) custom-call(bf16[272,3264]{1,0:T(8,128)(2,1)} %bitcast.107, bf16[272,1088]{1,0:T(8,128)(2,1)} %bitcast.109, ...), custom_call_target="tpu_custom_call" | custom-call | bytes 262500000 | tf_op jit(solution)/shard_map/first_weights/pallas_call | solution.py:540
  91.0 24.4 %block_forward.2 = (bf16[768,1088]{1,0:T(8,128)(2,1)}, bf16[256,1152]{1,0:T(8,128)(2,1)}, bf16[768,1152]{1,0:T(8,128)(2,1)}, bf16[768,1152]{1,0:T(8,128)(2,1)}, ...) custom-call(bf16[768,1088]{1,0:T(8,128)(2,1)} %get-tuple-element.92.first.wide,, ...), custom_call_target="tpu_custom_call" | custom-call | bytes 77000000 | tf_op jit(solution)/shard_map/block_forward/pallas_call | solution.py:1247
  116.8 1.1 copy.19
  117.9 73.8 %shard_map.169 = (bf16[256,1088]{1,0:T(8,128)(2,1)}, bf16[4,256,1088]{2,1,0:T(8,128)(2,1)}, bf16[4,256,1088]{2,1,0:T(8,128)(2,1)}, f32[4,256,1088]{2,1,0:T(8,128)}) custom-call(bf16[256,1088]{1,0:T(8,128)(2,1)} %get-tuple-element.94.own, bf16[1088,1088]{1,0:T(8,128)(2,1)} %get-tuple-element.95.up_here, bf16[2,1088,1088]{2,1,0:T(8,128)(2,1)} %get-tuple-element.96.down_both, ...), custom_call_target="tpu_custom_call" | custom-call | bytes 140000000 | tf_op jit(solution)/shard_map/pallas_call | solution.py:204
  191.8 36.8 %block_forward.3 = (bf16[768,1088]{1,0:T(8,128)(2,1)}, bf16[256,1152]{1,0:T(8,128)(2,1)}, bf16[768,1152]{1,0:T(8,128)(2,1)}, bf16[768,1152]{1,0:T(8,128)(2,1)}, ...) custom-call(bf16[256,1088]{1,0:T(8,128)(2,1)} %get-tuple-element.99., ...), custom_call_target="tpu_custom_call" | custom-call | bytes 157500000 | tf_op jit(solution)/shard_map/block_forward/pallas_call | solution.py:1247
  230.1 50.7 %shard_map.170 = (bf16[256,1088]{1,0:T(8,128)(2,1)}, bf16[4,256,1088]{2,1,0:T(8,128)(2,1)}, bf16[4,256,1088]{2,1,0:T(8,128)(2,1)}, f32[4,256,1088]{2,1,0:T(8,128)}) custom-call(bf16[256,1088]{1,0:T(8,128)(2,1)} %get-tuple-element.103.own, bf16[1088,1088]{1,0:T(8,128)(2,1)} %get-tuple-element.102.up_here, bf16[2,1088,1088]{2,1,0:T(8,128)(2,1)} %get-tuple-element.96.down_both, ...), custom_call_target="tpu_custom_call" | custom-call | bytes 140000000 | tf_op jit(solution)/shard_map/pallas_call | solution.py:204
  280.7 52.3 %shard_map.171 = (f32[256,1088]{1,0:T(8,128)}, bf16[4,256,1088]{2,1,0:T(8,128)(2,1)}, bf16[4,256,1088]{2,1,0:T(8,128)(2,1)}, f32[1,1088]{1,0:T(1,128)}) custom-call(bf16[256,1088]{1,0:T(8,128)(2,1)} %bitcast.89, bf16[1088,1088]{1,0:T(8,128)(2,1)} %get-tuple-element.102.up_here, bf16[2,1088,1088]{2,1,0:T(8,128)(2,1)} %get-tuple-element.96.down_both, ...), custom_call_target="tpu_custom_call" | custom-call | bytes 140000000 | tf_op jit(solution)/shard_map/pallas_call | solution.py:204
  333.1 4.9 fusion.1
  338.2 1.5 copy-done.17
  339.7 3.1 fusion
  343.0 1.4 fusion.6
  344.4 1.6 collective-permute-done
  346.0 1.4 fusion.7
  347.3 3.7 all-to-all-start
  351.1 1.2 fusion.11.bias_t
  353.6 64.7 %block_backward.2 = (f32[256,1088]{1,0:T(8,128)}, bf16[256,1088]{1,0:T(8,128)(2,1)}, bf16[256,1152]{1,0:T(8,128)(2,1)}, bf16[768,1152]{1,0:T(8,128)(2,1)}, bf16[...) custom-call(f32[256,1088]{1,0:T(8,128)} %get-tuple-element.114.d_second, ...), custom_call_target="tpu_custom_call" | custom-call | bytes 203000000 | tf_op jit(solution)/shard_map/block_backward/pallas_call | solution.py:1414
  418.3 3.1 pad_maximum_fusion
  421.4 47.3 %shard_map.172 = (f32[256,1088]{1,0:T(8,128)}, bf16[4,256,1088]{2,1,0:T(8,128)(2,1)}, bf16[4,256,1088]{2,1,0:T(8,128)(2,1)}, f32[1,1088]{1,0:T(1,128)}) custom-call(bf16[256,1088]{1,0:T(8,128)(2,1)} %get-tuple-element.125.own.up, bf16[1088,1088]{1,0:T(8,128)(2,1)} %get-tuple-element.95.up_here, bf16[2,1088,1088]{2,1,0:T(8,128)(2,1)} %get-tuple-element.96.down_both, ...), custom_call_target="tpu_custom_call" | custom-call | bytes 140000000 | tf_op jit(solution)/shard_map/pallas_call | solution.py:204
  468.7 4.9 fusion.3
  473.7 1.1 dynamic-slice_bitcast_fusion
  475.8 3.1 fusion.2
  479.0 1.4 copy-done.3
  480.4 1.1 dynamic-slice_bitcast_fusion.1
  481.6 2.8 fusion.4
  484.8 2.7 fusion.5
  487.5 3.7 all-to-all-start.1
  491.6 2.0 slice.24.wide
  493.6 3.0 convolution_convert_fusion.6.o1
  496.7 3.8 convolution_convert_fusion.2.v1
  501.7 34.0 %block_backward.3 = (f32[256,1088]{1,0:T(8,128)}, bf16[256,1152]{1,0:T(8,128)(2,1)}, bf16[768,1152]{1,0:T(8,128)(2,1)}, bf16[768,1152]{1,0:T(8,128)(2,1)}, f32[2...) custom-call(f32[256,1088]{1,0:T(8,128)} %get-tuple-element.134.d_second, ...), custom_call_target="tpu_custom_call" | custom-call | bytes 133000000 | tf_op jit(solution)/shard_map/block_backward/pallas_call | solution.py:1414
  535.7 3.2 pad_maximum_fusion.1
  538.9 40.9 %all-reduce.4.cloned.1.call-done.mlp = bf16[2,544,1088]{2,1,0:T(8,128)(2,1)} async-done(((bf16[2,544,1088]{2,1,0:T(8,128)(2,1)}), bf16[2,544,1088]{2,1,0:T(8,128)(2,1)}) %all-reduce.4.cloned.1.call-update) | async-done | bytes 2367504 | tf_op jit(solution)/shard_map/psum | solution.py:1554
  579.9 2.4 convolution_convert_fusion.q1
  582.3 3.8 convolution_convert_fusion.3.k1
  586.2 2.4 convolution_convert_fusion.1.q0
  588.5 3.1 convolution_convert_fusion.7.o0
  591.6 3.8 convolution_convert_fusion.4.v0
  595.4 4.1 convolution_convert_fusion.5.k0
  599.5 171.4 %reduce_both.1 = (bf16[272,3264]{1,0:T(8,128)(2,1)}, bf16[272,1152]{1,0:T(8,128)(2,1)}, bf16[1088,1088]{1,0:T(8,128)(2,1)}, bf16[272,4352]{1,0:T(8,128)(2,1)}, b...) custom-call(bf16[1088,1152]{1,0:T(8,128)(2,1)} %convolution_convert_fusion.1.q0, ...), custom_call_target="tpu_custom_call" | custom-call | bytes 420000000 | tf_op jit(solution)/shard_map/reduce_both/pallas_call | solution.py:902
  771.0 1.3 collective-permute-start.4
  772.3 5.5 collective-permute-done.4.far
  777.8 1.5 copy-done.2
  779.4 14.2 %final_layouts.1 = (f32[272,3264]{1,0:T(8,128)}, f32[272,1088]{1,0:T(8,128)}, f32[1088,1088]{1,0:T(8,128)}, f32[272,4352]{1,0:T(8,128)}, f32[16,272]{1,0:T(8,128...) custom-call(bf16[272,3264]{1,0:T(8,128)(2,1)} %get-tuple-element.161.qkv, ...), custom_call_target="tpu_custom_call" | custom-call | bytes 35000000 | tf_op jit(solution)/shard_map/final_layouts/pallas_call | solution.py:982
  795.1 1.3 slice_bitcast_fusion.1
  796.4 3.0 copy.32
  799.4 1.4 copy.31
  (94 shorter events, 11.9 us)
Async XLA Ops:
  7.2 82.7 %copy-start = (s32[2,1,1024]{2,1,0:T(1,128)S(1)}, s32[2,1,1024]{2,1,0:T(1,128)}, u32[]{:S(2)}) copy-start(s32[2,1,1024]{2,1,0:T(1,128)} %param.11) | copy-start | bytes 24580
  7.2 184.6 %all-gather.2.cloned.1.call-start = ((), (), s32[]{:S(2)}) async-start(), calls=%async_computation.2 | async-start | bytes 11280384 | tf_op jit(solution)/shard_map/all_gather | solution.py:1463
  280.7 52.3 %copy-start.20 = (bf16[4,256,1088]{2,1,0:T(8,128)(2,1)S(1)}, bf16[4,256,1088]{2,1,0:T(8,128)(2,1)}, u32[]{:S(2)}) copy-start(bf16[4,256,1088]{2,1,0:T(8,128)(2,1)} %get-tuple-element.110) | copy-start | bytes 6684676
  333.1 5.2 copy-start.19
  338.0 1.7 copy-start.17
  338.1 4.9 collective-permute-start.1
  342.9 3.0 collective-permute-start
  347.3 4.9 copy-start.14
  347.3 71.0 %all-to-all-start = ((bf16[4,136,1088]{2,1,0:T(8,128)(2,1)}), bf16[4,136,1088]{2,1,0:T(8,128)(2,1)S(1)}, u32[]{:S(2)}, u32[]{:S(2)}) async-start(bf16[4,136,1088]{2,1,0:T(8,128)(2,1)} %fusion.7), calls=%async_computation | async-start | bytes 2506752 | tf_op jit(solution)/shard_map/all_to_all | solution.py:1525
  351.0 228.8 %all-reduce.4.cloned.1.call-start = ((), (), s32[]{:S(2)}) async-start(), calls=%async_computation.3 | async-start | bytes 5013504 | tf_op jit(solution)/shard_map/psum | solution.py:1554
  353.0 0.6 copy-start.12
  421.4 47.3 %copy-start.16 = (bf16[4,256,1088]{2,1,0:T(8,128)(2,1)S(1)}, bf16[4,256,1088]{2,1,0:T(8,128)(2,1)}, u32[]{:S(2)}) copy-start(bf16[4,256,1088]{2,1,0:T(8,128)(2,1)} %get-tuple-element.130) | copy-start | bytes 6684676
  468.7 6.1 copy-start.18
  473.7 2.1 copy-start.15
  474.8 6.7 collective-permute-start.3
  479.0 1.5 copy-start.3
  481.5 3.3 collective-permute-start.2
  481.6 3.3 copy-start.4
  487.5 6.1 copy-start.25
  487.5 6.1 copy-start.26
  487.5 48.2 %all-to-all-start.1 = ((bf16[4,136,1088]{2,1,0:T(8,128)(2,1)}), bf16[4,136,1088]{2,1,0:T(8,128)(2,1)S(1)}, u32[]{:S(2)}, u32[]{:S(2)}) async-start(bf16[4,136,1088]{2,1,0:T(8,128)(2,1)} %fusion.5), calls=%async_computation.1 | async-start | bytes 2506752 | tf_op jit(solution)/shard_map/all_to_all | solution.py:1525
  491.2 279.8 %all-reduce.6.cloned.1.call-start = ((), (), s32[]{:S(2)}) async-start(), calls=%async_computation.4 | async-start | bytes 5013504 | tf_op jit(solution)/shard_map/psum | solution.py:1554
  493.6 3.0 copy-start.7
  493.6 3.0 copy-start.22
  496.7 3.8 copy-start.13
  501.1 0.6 copy-start.11
  538.9 41.0 %copy-start.8 = (bf16[768,1088]{1,0:T(8,128)(2,1)S(1)}, bf16[768,1088]{1,0:T(8,128)(2,1)}, u32[]{:S(2)}) copy-start(bf16[768,1088]{1,0:T(8,128)(2,1)} %get-tuple-element.149) | copy-start | bytes 5013508
  538.9 41.0 %copy-start.9 = (bf16[256,1152]{1,0:T(8,128)(2,1)S(1)}, bf16[256,1152]{1,0:T(8,128)(2,1)}, u32[]{:S(2)}) copy-start(bf16[256,1152]{1,0:T(8,128)(2,1)} %get-tuple-element.121) | copy-start | bytes 1769476
  579.9 2.4 copy-start.21
  582.3 3.8 copy-start.6
  582.3 3.8 copy-start.10
  586.2 2.4 copy-start.27
  586.2 2.4 copy-start.28
  588.5 3.1 copy-start.24
  591.6 3.8 copy-start.23
  771.0 6.8 collective-permute-start.4
  777.8 1.5 copy-start.2
  793.5 5.8 copy-start.5
  796.4 5.7 copy-start.1
Sparse Core Ops, SparseCore 0:
  90.0 80.6 all-gather.1
  481.7 98.1 all-reduce.3
  582.3 140.9 all-reduce.5

commit v12 on v11

--- a/solution.py
+++ b/solution.py
@@ -572,7 +572,7 @@
 
 
 def reduce_kernel(
-    q0, k0, v0, o0, q1, k1, v1, o1, mlp, made0, made1, grad1, halo, d_resid, da_own, wide, par,
+    q0, k0, v0, o0, q1, k1, v1, o1, mlp_down, mlp_up, made0, made1, grad1, halo, d_resid, da_own, wide, par,
     qkv_out, out_out, down_out, up_out, made_out, grad_out,
     own_in, held, up_own, up_far, sent, caught, grad0,
     x1a, y1a, x2a, y2a, sxa, sya, ta, zaa, zba,
@@ -727,10 +727,10 @@
 
     half = down_out.shape[0] // 2
     mine = pl.ds(pl.multiple_of(s * half, 16), half)
-    down_far = to(mlp.at[0], down_out.at[mine], core_s.at[4], core_r.at[4], section=1 - s)
-    down_near = pltpu.make_async_copy(mlp.at[0], down_out.at[mine], load.at[4])
-    far_up = to(mlp.at[1], up_far, core_s.at[5], core_r.at[5], section=1 - s)
-    near_up = pltpu.make_async_copy(mlp.at[1], up_own, load.at[5])
+    down_far = to(mlp_down, down_out.at[mine], core_s.at[4], core_r.at[4], section=1 - s)
+    down_near = pltpu.make_async_copy(mlp_down, down_out.at[mine], load.at[4])
+    far_up = to(mlp_up, up_far, core_s.at[5], core_r.at[5], section=1 - s)
+    near_up = pltpu.make_async_copy(mlp_up, up_own, load.at[5])
 
     def lay_up():
         far_up.wait_recv()
@@ -905,7 +905,7 @@
             *(jax.ShapeDtypeStruct(shape, BF) for shape in shapes),
             jax.ShapeDtypeStruct((2, rows, D), F32),
         ),
-        in_specs=[any_spec] * 12 + [VSPEC] * 5,
+        in_specs=[any_spec] * 13 + [VSPEC] * 5,
         out_specs=(VSPEC,) * 6,
         scratch_shapes=[
             buf(2, D, WIDE), buf(4, D, WIDE), buf(D // 2, D), buf(D // 2, D), buf(rows, D),
@@ -918,15 +918,15 @@
         ),
         cost_estimate=lasting(120),
         name="reduce_both",
-    )(*zero, *one, mlp, *made, grad1, halo, d_resid, da_own, wide, par)
+    )(*zero, *one, *mlp, *made, grad1, halo, d_resid, da_own, wide, par)
 
 
 def final_kernel(
-    qkv, out, mine, far, down_one, up_one, made, grads,
+    qkv, out, down_mine, up_mine, down_far, up_far, down_one, up_one, made, grads,
     qkv_f, out_f, down_f, up_f, small, made_out, grads_out,
 ):
     s = lax.axis_index("section")
-    half = mine.shape[1]
+    half = down_mine.shape[0]
     shard = qkv.shape[0]
     pick_row = (
         lax.broadcasted_iota(jnp.int32, (16, 128), 1)
@@ -955,7 +955,7 @@
     def _():
         for k in range(4):
             at = pl.ds(k * (shard // 2), shard // 2)
-            rows_k = jnp.concatenate([mine[1, at, :], far[1, at, :]], axis=0)
+            rows_k = jnp.concatenate([up_mine[at, :], up_far[at, :]], axis=0)
             up_f[:, pl.ds(k * D, D)] = rows_k.astype(F32)
 
     @pl.loop(0, half // 16)
@@ -965,8 +965,8 @@
 
         @pl.when(s == 0)
         def _():
-            down_f[at, :] = mine[0, at, :].astype(F32)
-            down_f[after, :] = far[0, at, :].astype(F32)
+            down_f[at, :] = down_mine[at, :].astype(F32)
+            down_f[after, :] = down_far[at, :].astype(F32)
 
         @pl.when(s == 1)
         def _():
@@ -975,14 +975,14 @@
 
 
 def final_layouts(*values):
-    qkv, _, _, _, down_one, up_one, made, grads = values
+    qkv, *_, down_one, up_one, made, grads = values
     shard = qkv.shape[0]
     outs = [(shape, F32) for shape in (qkv.shape, (shard, D), down_one.shape, up_one.shape)]
     outs += [((16, shard), F32), (made.shape, BF), (grads.shape, F32)]
     return pl.pallas_call(
         final_kernel,
         out_shape=tuple(jax.ShapeDtypeStruct(*out) for out in outs),
-        in_specs=[VSPEC] * 8,
+        in_specs=[VSPEC] * 10,
         out_specs=(VSPEC,) * 7,
         compiler_params=pltpu.CompilerParams(vmem_limit_bytes=58 * 1024 * 1024),
         cost_estimate=lasting(10),
@@ -999,6 +999,7 @@
 
 def halves_settle(zero, one, nf, shard):
     s = lax.axis_index("section")
+    zero, one = jnp.stack(zero), jnp.stack(one)
     mine, far = pick(s, zero, one), on_chip(pick(s, one, zero))
     first, second = pick(s, mine, far).astype(F32), pick(s, far, mine).astype(F32)
     down = jnp.concatenate([first[0], second[0]], axis=0)
@@ -1546,7 +1547,7 @@
         )
         parts[layer] = pieces
         up_half, down_half, _ = lax.optimization_barrier((up_half, down_half, dq))
-        halves = jnp.stack([down_half, up_half.reshape(ff_here // 2, D)])
+        halves = (down_half, up_half.reshape(ff_here // 2, D))
         if layer == 1:
             _, upstream_next = lax.optimization_barrier((halves, upstream_next))
         else:
@@ -1561,9 +1562,9 @@
             wide[reach:], par,
         )
         late_sum, qkv_g = lax.optimization_barrier((mlp_sums[0], qkv_g))
-        far = lax.ppermute(late_sum, "section", [(1, 0)])
+        far = [lax.ppermute(half, "section", [(1, 0)]) for half in late_sum]
         qkv_g, out_g, grad_down, grad_up, small, made, grads = final_layouts(
-            qkv_g, out_g, late_sum, far, down_one, up_one, made, grads
+            qkv_g, out_g, *late_sum, *far, down_one, up_one, made, grads
         )
         made, grads = made[None, :, None], grads[None, :, None]
     else:

time: 817 us -> 814 us (level)
  transfers between devices with their start and end apart: 10 -> 11, of which waited for: 4 -> 5; matrix products, arithmetic and copies ran while one was open for 6% -> 6% of each run, Pallas kernels for 46% -> 45%
where the time goes in v12:
time: 814 us; the launch traced here: 806 us
  Pallas kernels  648 us (80%)
  waiting for transfers between devices  51.6 us (6%)
  matrix products  43.8 us (5%)
  local copies, waits for them, and re-layouts  26.9 us (3%)
  between operations  14.5 us (2%)
  starting transfers between devices  10.6 us (1%)
  other arithmetic  10.5 us (1%)
    pallas_call x4, Pallas kernels, plane_call(): pl.pallas_call(kernel, out_shape=outs, in_specs=[VSPEC, any_spec, any_spe...  224 us
    pallas_call x1, Pallas kernels, reduce_both(): pl.pallas_call(reduce_kernel, out_shape=(*(jax.ShapeDtypeStruct(shape, BF...  169 us
    pallas_call x2, Pallas kernels, block_backward(): pl.pallas_call(functools.partial(block_back_kernel, ring), out_shape=tupl...  98.8 us
    pallas_call x1, Pallas kernels, first_weights(): pl.pallas_call(weights_kernel, out_shape=tuple((jax.ShapeDtypeStruct(shap...  80.2 us
    pallas_call x2, Pallas kernels, block_forward(): pl.pallas_call(functools.partial(block_kernel, bool(more)), out_shape=tup...  61.2 us
    psum x2, waiting for transfers between devices, on_device(): mlp_sums[layer] = lax.psum(halves, 'ctx')  44.2 us
    dot_general x12, matrix products, mm_tn(): lax.dot_general(a, b, (((0,), (0,)), ((), ())), preferred_element_type=F32)  43.8 us
  transfers between devices with their start and end apart: 11, of which 5 were waited for; matrix products, arithmetic and copies ran while one was open for 6% of the time, Pallas kernels for 45%

profile of v12, /device:TPU:0, one launch (start us, length us, event | category | flops | bytes accessed | tf_op | source)
XLA Modules:
  0.0 806.2 jit_solution(1595075709125888295)
XLA Ops:
  7.2 1.3 constant_dynamic-slice_fusion.1
  8.5 1.1 copy.20
  9.6 80.2 %first_weights.1 = (bf16[4,1088,1152]{2,1,0:T(8,128)(2,1)}, bf16[768,1088]{1,0:T(8,128)(2,1)}, bf16[1088,1088]{1,0:T(8,128)(2,1)}, bf16[4,272,1088]{2,1,0:T(8,12...) custom-call(bf16[272,3264]{1,0:T(8,128)(2,1)} %bitcast.103, bf16[272,1088]{1,0:T(8,128)(2,1)} %bitcast.105, ...), custom_call_target="tpu_custom_call" | custom-call | bytes 262500000 | tf_op jit(solution)/shard_map/first_weights/pallas_call | solution.py:540
  91.0 24.4 %block_forward.2 = (bf16[768,1088]{1,0:T(8,128)(2,1)}, bf16[256,1152]{1,0:T(8,128)(2,1)}, bf16[768,1152]{1,0:T(8,128)(2,1)}, bf16[768,1152]{1,0:T(8,128)(2,1)}, ...) custom-call(bf16[768,1088]{1,0:T(8,128)(2,1)} %get-tuple-element.95.first.wide,, ...), custom_call_target="tpu_custom_call" | custom-call | bytes 77000000 | tf_op jit(solution)/shard_map/block_forward/pallas_call | solution.py:1248
  116.9 1.1 copy.19
  118.0 73.8 %shard_map.169 = (bf16[256,1088]{1,0:T(8,128)(2,1)}, bf16[4,256,1088]{2,1,0:T(8,128)(2,1)}, bf16[4,256,1088]{2,1,0:T(8,128)(2,1)}, f32[4,256,1088]{2,1,0:T(8,128)}) custom-call(bf16[256,1088]{1,0:T(8,128)(2,1)} %get-tuple-element.97.own, bf16[1088,1088]{1,0:T(8,128)(2,1)} %get-tuple-element.98.up_here, bf16[2,1088,1088]{2,1,0:T(8,128)(2,1)} %get-tuple-element.99.down_both, ...), custom_call_target="tpu_custom_call" | custom-call | bytes 140000000 | tf_op jit(solution)/shard_map/pallas_call | solution.py:204
  191.8 36.8 %block_forward.3 = (bf16[768,1088]{1,0:T(8,128)(2,1)}, bf16[256,1152]{1,0:T(8,128)(2,1)}, bf16[768,1152]{1,0:T(8,128)(2,1)}, bf16[768,1152]{1,0:T(8,128)(2,1)}, ...) custom-call(bf16[256,1088]{1,0:T(8,128)(2,1)} %get-tuple-element.102, ...), custom_call_target="tpu_custom_call" | custom-call | bytes 157500000 | tf_op jit(solution)/shard_map/block_forward/pallas_call | solution.py:1248
  230.0 50.7 %shard_map.170 = (bf16[256,1088]{1,0:T(8,128)(2,1)}, bf16[4,256,1088]{2,1,0:T(8,128)(2,1)}, bf16[4,256,1088]{2,1,0:T(8,128)(2,1)}, f32[4,256,1088]{2,1,0:T(8,128)}) custom-call(bf16[256,1088]{1,0:T(8,128)(2,1)} %get-tuple-element.106.own, bf16[1088,1088]{1,0:T(8,128)(2,1)} %get-tuple-element.105.up_here, bf16[2,1088,1088]{2,1,0:T(8,128)(2,1)} %get-tuple-element.99.down_both, ...), custom_call_target="tpu_custom_call" | custom-call | bytes 140000000 | tf_op jit(solution)/shard_map/pallas_call | solution.py:204
  280.8 52.3 %shard_map.171 = (f32[256,1088]{1,0:T(8,128)}, bf16[4,256,1088]{2,1,0:T(8,128)(2,1)}, bf16[4,256,1088]{2,1,0:T(8,128)(2,1)}, f32[1,1088]{1,0:T(1,128)}) custom-call(bf16[256,1088]{1,0:T(8,128)(2,1)} %bitcast.87, bf16[1088,1088]{1,0:T(8,128)(2,1)} %get-tuple-element.105.up_here, bf16[2,1088,1088]{2,1,0:T(8,128)(2,1)} %get-tuple-element.99.down_both, ...), custom_call_target="tpu_custom_call" | custom-call | bytes 140000000 | tf_op jit(solution)/shard_map/pallas_call | solution.py:204
  333.1 4.9 fusion.1
  338.2 1.5 copy-done.20
  339.7 3.1 fusion
  343.0 1.4 fusion.6
  344.4 1.6 collective-permute-done
  346.0 1.4 fusion.7
  347.3 3.7 all-to-all-start
  351.1 1.2 fusion.11.bias_t
  353.6 64.8 %block_backward.2 = (f32[256,1088]{1,0:T(8,128)}, bf16[256,1088]{1,0:T(8,128)(2,1)}, bf16[256,1152]{1,0:T(8,128)(2,1)}, bf16[768,1152]{1,0:T(8,128)(2,1)}, bf16[...) custom-call(f32[256,1088]{1,0:T(8,128)} %get-tuple-element.117.d_second, ...), custom_call_target="tpu_custom_call" | custom-call | bytes 203000000 | tf_op jit(solution)/shard_map/block_backward/pallas_call | solution.py:1415
  418.4 47.7 %shard_map.172 = (f32[256,1088]{1,0:T(8,128)}, bf16[4,256,1088]{2,1,0:T(8,128)(2,1)}, bf16[4,256,1088]{2,1,0:T(8,128)(2,1)}, f32[1,1088]{1,0:T(1,128)}) custom-call(bf16[256,1088]{1,0:T(8,128)(2,1)} %get-tuple-element.128.own.up, bf16[1088,1088]{1,0:T(8,128)(2,1)} %get-tuple-element.98.up_here, bf16[2,1088,1088]{2,1,0:T(8,128)(2,1)} %get-tuple-element.99.down_both, ...), custom_call_target="tpu_custom_call" | custom-call | bytes 140000000 | tf_op jit(solution)/shard_map/pallas_call | solution.py:204
  466.1 4.9 fusion.3
  471.1 1.2 dynamic-slice_bitcast_fusion
  473.2 3.1 fusion.2
  476.4 1.4 copy-done.4
  477.8 1.2 dynamic-slice_bitcast_fusion.1
  479.1 2.8 fusion.4
  482.3 2.7 fusion.5
  485.0 3.7 all-to-all-start.1
  489.1 1.9 slice.24.wide
  491.0 3.1 convolution_convert_fusion.6.o1
  494.1 3.8 convolution_convert_fusion.2.v1
  499.2 34.0 %block_backward.3 = (f32[256,1088]{1,0:T(8,128)}, bf16[256,1152]{1,0:T(8,128)(2,1)}, bf16[768,1152]{1,0:T(8,128)(2,1)}, bf16[768,1152]{1,0:T(8,128)(2,1)}, f32[2...) custom-call(f32[256,1088]{1,0:T(8,128)} %get-tuple-element.137.d_second, ...), custom_call_target="tpu_custom_call" | custom-call | bytes 133000000 | tf_op jit(solution)/shard_map/block_backward/pallas_call | solution.py:1415
  533.2 44.2 %all-reduce.8.cloned.1.call-done = (bf16[544,1088]{1,0:T(8,128)(2,1)}, bf16[544,1088]{1,0:T(8,128)(2,1)}) async-done(((bf16[544,1088]{1,0:T(8,128)(2,1)}, bf16[544,1088]{1,0:T(8,128)(2,1)}), (bf16[544,1088]{1,0:T(8,128)(2,1)}, bf16[544,1088]{1,0:T(8,128)(2,1)})) %all-reduce.8.cloned.1.call-update) | async-done | bytes 2367504 | tf_op jit(solution)/shard_map/psum | solution.py:1555
  577.4 3.6 convolution_convert_fusion.q1
  581.1 3.8 convolution_convert_fusion.3.k1
  584.9 2.4 convolution_convert_fusion.1.q0
  587.3 3.1 convolution_convert_fusion.7.o0
  590.4 3.8 convolution_convert_fusion.4.v0
  594.2 4.1 convolution_convert_fusion.5.k0
  598.3 169.4 %reduce_both.1 = (bf16[272,3264]{1,0:T(8,128)(2,1)}, bf16[272,1152]{1,0:T(8,128)(2,1)}, bf16[1088,1088]{1,0:T(8,128)(2,1)}, bf16[272,4352]{1,0:T(8,128)(2,1)}, b...) custom-call(bf16[1088,1152]{1,0:T(8,128)(2,1)} %convolution_convert_fusion.1.q0, ...), custom_call_target="tpu_custom_call" | custom-call | bytes 420000000 | tf_op jit(solution)/shard_map/reduce_both/pallas_call | solution.py:902
  767.7 1.3 collective-permute-start.4
  769.0 1.3 collective-permute-start.5
  770.3 3.5 collective-permute-done.4.down_far
  773.8 1.8 collective-permute-done.5.up_far
  775.6 1.1 copy-done.7
  776.7 14.2 %final_layouts.1 = (f32[272,3264]{1,0:T(8,128)}, f32[272,1088]{1,0:T(8,128)}, f32[1088,1088]{1,0:T(8,128)}, f32[272,4352]{1,0:T(8,128)}, f32[16,272]{1,0:T(8,128...) custom-call(bf16[272,3264]{1,0:T(8,128)(2,1)} %get-tuple-element.166.qkv, ...), custom_call_target="tpu_custom_call" | custom-call | bytes 35000000 | tf_op jit(solution)/shard_map/final_layouts/pallas_call | solution.py:982
  792.4 1.3 slice_bitcast_fusion.1
  793.7 3.0 copy.32
  796.7 1.4 copy.31
  (100 shorter events, 11.9 us)
Async XLA Ops:
  7.2 82.7 %copy-start = (s32[2,1,1024]{2,1,0:T(1,128)S(1)}, s32[2,1,1024]{2,1,0:T(1,128)}, u32[]{:S(2)}) copy-start(s32[2,1,1024]{2,1,0:T(1,128)} %param.11) | copy-start | bytes 24580
  7.2 184.6 %all-gather.2.cloned.1.call-start = ((), (), s32[]{:S(2)}) async-start(), calls=%async_computation.2 | async-start | bytes 11280384 | tf_op jit(solution)/shard_map/all_gather | solution.py:1464
  280.8 52.3 %copy-start.23 = (bf16[4,256,1088]{2,1,0:T(8,128)(2,1)S(1)}, bf16[4,256,1088]{2,1,0:T(8,128)(2,1)}, u32[]{:S(2)}) copy-start(bf16[4,256,1088]{2,1,0:T(8,128)(2,1)} %get-tuple-element.113) | copy-start | bytes 6684676
  333.1 5.2 copy-start.22
  338.0 1.7 copy-start.20
  338.2 4.9 collective-permute-start.1
  343.0 3.0 collective-permute-start
  347.3 4.9 copy-start.17
  347.3 71.1 %all-to-all-start = ((bf16[4,136,1088]{2,1,0:T(8,128)(2,1)}), bf16[4,136,1088]{2,1,0:T(8,128)(2,1)S(1)}, u32[]{:S(2)}, u32[]{:S(2)}) async-start(bf16[4,136,1088]{2,1,0:T(8,128)(2,1)} %fusion.7), calls=%async_computation | async-start | bytes 2506752 | tf_op jit(solution)/shard_map/all_to_all | solution.py:1526
  351.0 226.4 %all-reduce.8.cloned.1.call-start = ((), (), s32[]{:S(2)}) async-start(), calls=%async_computation.4 | async-start | bytes 5013504 | tf_op jit(solution)/shard_map/psum | solution.py:1555
  353.0 0.6 copy-start.15
  418.4 47.7 %copy-start.2 = (bf16[4,136,1088]{2,1,0:T(8,128)(2,1)}, bf16[4,136,1088]{2,1,0:T(8,128)(2,1)S(1)}, u32[]{:S(2)}) copy-start(bf16[4,136,1088]{2,1,0:T(8,128)(2,1)S(1)} %all-to-all-done) | copy-start | bytes 3551236
  418.4 47.7 %copy-start.19 = (bf16[4,256,1088]{2,1,0:T(8,128)(2,1)S(1)}, bf16[4,256,1088]{2,1,0:T(8,128)(2,1)}, u32[]{:S(2)}) copy-start(bf16[4,256,1088]{2,1,0:T(8,128)(2,1)} %get-tuple-element.133) | copy-start | bytes 6684676
  466.1 6.1 copy-start.21
  471.1 2.1 copy-start.18
  472.3 6.8 collective-permute-start.3
  476.4 1.5 copy-start.4
  479.0 3.3 collective-permute-start.2
  479.1 3.3 copy-start.5
  485.0 6.0 copy-start.28
  485.0 6.0 copy-start.29
  485.0 48.2 %all-to-all-start.1 = ((bf16[4,136,1088]{2,1,0:T(8,128)(2,1)}), bf16[4,136,1088]{2,1,0:T(8,128)(2,1)S(1)}, u32[]{:S(2)}, u32[]{:S(2)}) async-start(bf16[4,136,1088]{2,1,0:T(8,128)(2,1)} %fusion.5), calls=%async_computation.1 | async-start | bytes 2506752 | tf_op jit(solution)/shard_map/all_to_all | solution.py:1526
  488.7 279.0 %all-reduce.6.cloned.1.call-start = ((), (), s32[]{:S(2)}) async-start(), calls=%async_computation.3 | async-start | bytes 5013504 | tf_op jit(solution)/shard_map/psum | solution.py:1555
  491.0 3.1 copy-start.10
  491.0 3.1 copy-start.25
  494.1 3.8 copy-start.16
  498.5 0.6 copy-start.14
  533.1 44.3 %copy-start.12 = (bf16[256,1152]{1,0:T(8,128)(2,1)S(1)}, bf16[256,1152]{1,0:T(8,128)(2,1)}, u32[]{:S(2)}) copy-start(bf16[256,1152]{1,0:T(8,128)(2,1)} %get-tuple-element.124) | copy-start | bytes 1769476
  533.2 44.2 %copy-start.3 = (bf16[4,136,1088]{2,1,0:T(8,128)(2,1)}, bf16[4,136,1088]{2,1,0:T(8,128)(2,1)S(1)}, u32[]{:S(2)}) copy-start(bf16[4,136,1088]{2,1,0:T(8,128)(2,1)S(1)} %all-to-all-done.1) | copy-start | bytes 3551236
  577.4 3.7 copy-start.11
  577.4 3.6 copy-start.24
  581.1 3.8 copy-start.9
  581.1 3.8 copy-start.13
  584.9 2.4 copy-start.30
  584.9 2.4 copy-start.31
  587.3 3.1 copy-start.27
  590.4 3.8 copy-start.26
  767.7 6.1 collective-permute-start.4
  769.0 6.6 collective-permute-start.5
  773.8 1.8 copy-start.6
  775.6 1.1 copy-start.7
  790.9 5.8 copy-start.8
  793.7 5.7 copy-start.1
Sparse Core Ops, SparseCore 0:
  90.0 80.6 all-gather.1
  479.2 98.1 all-reduce.7
  579.9 139.9 all-reduce.5
